TPU v7x, 32 devices: a whole 2x2x4 slice. The times are simulated.
32 devices in a mesh: cell: 2 (over x), blk: 16 (over z, y, core).
Axes of the slice: x: 2, y: 2, z: 4, core: 2. Of those that a mesh axis runs over, the one named last changes fastest.
Arguments:
- psi_val: float32 [256, 64, 64, 64], P('cell', 'blk'), parts along dimension 0, may hold values from -6 to 6
- psi_cond: float32 [6, 64, 64, 64], P('cell', 'blk'), parts along dimension 0, may hold values from -6 to 6
- e_val: float32 [256], P('cell'), parts along dimension 0, may hold values from -8 to -1
- e_cond: float32 [6], P('cell'), parts along dimension 0, may hold values from 1 to 8
- occ: int32 [256], P('cell'), parts along dimension 0, may hold values from 1 to 2
- freq: float32 [10], P('cell'), parts along dimension 0, may hold values from 0.5 to 16
- gmap: int32 [8192], P('cell'), parts along dimension 0, may hold values from 0 to 262143, as said below
Outputs:
- chi_real: float32 [10, 4096, 4096], P('cell', 'blk'), parts along dimension 0
- chi_imag: float32 [10, 4096, 4096], P('cell', 'blk'), parts along dimension 0
There are 2 independent parts, one for each index of `cell`. A program takes and returns all parts, laid end to end along the dimension named above; each array names one. Nothing has to cross between parts.
Inputs may be any that keep to these rules, and one draw needn't show every extreme that they name: `gmap`: the 4096 indices are distinct; index 0 and index 262143 are always among them.
All inputs are finite; a program needn't handle non-finite values.
Results may differ from a plain program's by a relative error of at most 0.0001.
Values sent between devices are 32-bit elements; how exact they have to be, the bound alone decides.
No kernel may reach another device: no remote copies, remote signals or barrier semaphores. Data moves between devices by JAX's collectives and lax.ppermute only.
A program may use at most 256 MiB of HBM per device.

v0:
```python
import math

import jax
import jax.numpy as jnp
from jax import lax
from jax.sharding import PartitionSpec as P

highest = lax.Precision.HIGHEST


def dft_tables(length):
    counter = jnp.arange(length, dtype=jnp.int32)
    angles = (counter[:, None] * counter[None, :] % length).astype(jnp.float32) * (
        2.0 * math.pi / length
    )
    return (jnp.cos(angles), jnp.sin(angles))


def plane_picks(val_part, cond_part, column_idx):
    num_val, planes, size_y, size_z = val_part.shape
    num_cond = cond_part.shape[0]
    pair_count = num_val * num_cond
    density = (val_part[:, None] * cond_part[None]).reshape(pair_count, planes, size_y, size_z)
    cos_z, sin_z = dft_tables(size_z)
    real_a = jnp.einsum("pxyz,zk->ykxp", density, cos_z, precision=highest)
    imag_a = -jnp.einsum("pxyz,zk->ykxp", density, sin_z, precision=highest)
    cos_y, sin_y = dft_tables(size_y)
    real_b = jnp.einsum("ly,ykxp->lkxp", cos_y, real_a, precision=highest) + jnp.einsum(
        "ly,ykxp->lkxp", sin_y, imag_a, precision=highest
    )
    imag_b = jnp.einsum("ly,ykxp->lkxp", cos_y, imag_a, precision=highest) - jnp.einsum(
        "ly,ykxp->lkxp", sin_y, real_a, precision=highest
    )
    return jnp.concatenate(
        [
            jnp.take(real_b.reshape(size_y * size_z, planes, pair_count), column_idx, axis=0),
            jnp.take(imag_b.reshape(size_y * size_z, planes, pair_count), column_idx, axis=0),
        ],
        axis=2,
    )


def phase_sum(values, freq_x, positions, size_x, norm_factor):
    half = values.shape[2] // 2
    angles = (freq_x[:, None] * positions[None, :] % size_x).astype(jnp.float32) * (
        2.0 * math.pi / size_x
    )
    cosine = jnp.cos(angles)[:, :, None]
    sine = jnp.sin(angles)[:, :, None]
    real_v = values[:, :, :half]
    imag_v = values[:, :, half:]
    real_m = jnp.sum(real_v * cosine + imag_v * sine, axis=1)
    imag_m = jnp.sum(imag_v * cosine - real_v * sine, axis=1)
    return jnp.concatenate([real_m, imag_m], axis=1) * norm_factor


def body(psi_val, psi_cond, e_val, e_cond, occ, freq, gmap):
    num_val, planes, size_y, size_z = psi_val.shape
    num_cond = psi_cond.shape[0]
    pairs = num_val * num_cond
    devices_blk = lax.axis_size("blk")
    size_x = planes * devices_blk
    total_points = size_x * size_y * size_z
    norm_factor = 1.0 / math.sqrt(total_points)
    column_idx = gmap % (size_y * size_z)
    plane_freq = gmap // (size_y * size_z)
    picked = plane_picks(psi_val, psi_cond, column_idx)
    positions = lax.axis_index("blk") * planes + jnp.arange(planes, dtype=jnp.int32)
    owned = lax.psum_scatter(
        phase_sum(picked, plane_freq, positions, size_x, norm_factor),
        "blk",
        scatter_dimension=0,
        tiled=True,
    )
    gaps = e_val[:, None] - e_cond[None, :]
    occ_col = occ.astype(jnp.float32)[:, None, None]
    weights = (
        occ_col
        * gaps[:, :, None]
        / (gaps[:, :, None] * gaps[:, :, None] + (freq * freq)[None, None, :])
    )
    weights = weights.reshape(pairs, freq.shape[0]) / math.sqrt(pairs)
    freq_weights = jnp.transpose(weights)[:, None, :]
    real_w = owned[None, :, :pairs] * freq_weights
    imag_w = owned[None, :, pairs:] * freq_weights
    left_side = jnp.stack(
        [jnp.concatenate([real_w, imag_w], axis=2), jnp.concatenate([imag_w, -real_w], axis=2)],
        axis=0,
    )
    chi_both = jnp.einsum(
        "awgk,hk->awgh",
        left_side,
        lax.all_gather(owned, "blk", axis=0, tiled=True),
        precision=highest,
    )
    return (chi_both[0], chi_both[1])


def solution(mesh):
    return jax.shard_map(
        body,
        mesh=mesh,
        in_specs=(
            P("cell", "blk", None, None),
            P("cell", "blk", None, None),
            P("cell"),
            P("cell"),
            P("cell"),
            P("cell"),
            P("cell"),
        ),
        out_specs=(P("cell", "blk", None), P("cell", "blk", None)),
        check_vma=False,
    )
```

profile of v0, /device:TPU:0, one launch (start us, length us, event | category | flops | bytes accessed | tf_op | source)
XLA Modules:
  0.0 1110.7 jit_solution(17548782149290452893)
XLA Ops:
  7.2 0.0 copy-start
  7.2 0.0 reduce-scatter.2.cloned.1.call-start
  7.2 16.3 %copy.40 = f32[128,4,64,64]{3,2,1,0:T(8,128)} copy(f32[128,4,64,64]{0,3,2,1:T(8,128)} %param.9) | data formatting | bytes 16777216 | tf_op args[0]
  23.5 0.0 copy-done
  23.5 23.2 %broadcast_multiply_fusion = f32[128,3,4,64,64]{4,3,2,1,0:T(8,128)} fusion(f32[3,4,64,64]{3,2,1,0:T(8,128)S(1)} %copy-done, f32[128,4,64,64]{3,2,1,0:T(8,128)} %copy.40), kind=kLoop, calls=%fused_computation.5 | loop fusion | flops 6291456 | bytes 33751040 | tf_op jit(solution)/shard_map/mul | solution.py:23
  46.7 40.4 %copy.42 = f32[384,4,64,64]{0,3,2,1:T(8,128)} copy(f32[384,4,64,64]{3,2,1,0:T(8,128)} %bitcast.45) | data formatting | bytes 50331648 | tf_op jit(solution)/shard_map/mul | solution.py:23
  87.1 29.5 %negate_bitcast_fusion = f32[64,64,4,384]{3,1,0,2:T(8,128)} fusion(f32[384,4,64,64]{0,3,2,1:T(8,128)} %copy.42), kind=kOutput, calls=%fused_computation.4 | convolution fusion | flops 4838187008 | bytes 50331648 | tf_op jit(solution)/shard_map/pxyz,zk->ykxp/dot_general | solution.py:26
  116.6 29.9 %convolution_bitcast_fusion = f32[64,64,4,384]{3,1,0,2:T(8,128)} fusion(f32[384,4,64,64]{0,3,2,1:T(8,128)} %copy.42), kind=kOutput, calls=%fused_computation.19 | convolution fusion | flops 4831895552 | bytes 50331648 | tf_op jit(solution)/shard_map/pxyz,zk->ykxp/dot_general | solution.py:25
  146.6 52.3 %fusion.2 = f32[64,64,4,384]{3,0,2,1:T(8,128)} fusion(f32[64,64,4,384]{3,1,0,2:T(8,128)} %negate_bitcast_fusion), kind=kOutput, calls=%fused_computation.8 | convolution fusion | flops 4831895552 | bytes 50331648 | tf_op jit(solution)/shard_map/ly,ykxp->lkxp/dot_general | solution.py:28
  198.9 0.0 copy-start.1
  198.9 51.7 %fusion = f32[64,64,4,384]{3,0,2,1:T(8,128)} fusion(f32[64,64,4,384]{3,1,0,2:T(8,128)} %negate_bitcast_fusion), kind=kOutput, calls=%fused_computation.6 | convolution fusion | flops 4831895552 | bytes 50331648 | tf_op jit(solution)/shard_map/ly,ykxp->lkxp/dot_general | solution.py:31
  250.7 0.0 copy-done.1
  250.7 54.9 %fusion.10 = f32[64,64,4,384]{3,0,2,1:T(8,128)} fusion(f32[64,64,4,384]{3,0,2,1:T(8,128)} %fusion.2, f32[64,64,4,384]{3,1,0,2:T(8,128)} %convolution_bitcast_fusion), kind=kOutput, calls=%fused_computation.20 | convolution fusion | flops 4838187008 | bytes 75497472 | tf_op jit(solution)/shard_map/ly,ykxp->lkxp/dot_general | solution.py:28
  305.7 21.8 %copy.47 = f32[64,64,4,384]{3,1,0,2:T(8,128)S(1)} copy(f32[64,64,4,384]{3,0,2,1:T(8,128)} %fusion.10) | data formatting | bytes 50331648 | tf_op jit(solution)/shard_map/add | solution.py:28
  327.5 59.9 %copy.48 = f32[4096,4,384]{2,1,0:T(4,128)} copy(f32[4096,4,384]{2,0,1:T(8,128)S(1)} %bitcast.46) | data formatting | bytes 50331648 | tf_op jit(solution)/shard_map/reshape | solution.py:36
  387.3 54.7 %fusion.13 = f32[64,64,4,384]{3,0,2,1:T(8,128)} fusion(f32[64,64,4,384]{3,0,2,1:T(8,128)} %fusion, f32[64,64,4,384]{3,1,0,2:T(8,128)} %convolution_bitcast_fusion), kind=kOutput, calls=%fused_computation.21 | convolution fusion | flops 4838187008 | bytes 75497472 | tf_op jit(solution)/shard_map/ly,ykxp->lkxp/dot_general | solution.py:31
  442.0 21.8 %copy.52 = f32[64,64,4,384]{3,1,0,2:T(8,128)S(1)} copy(f32[64,64,4,384]{3,0,2,1:T(8,128)} %fusion.13) | data formatting | bytes 50331648 | tf_op jit(solution)/shard_map/sub | solution.py:31
  463.8 59.8 %copy.53 = f32[4096,4,384]{2,1,0:T(4,128)} copy(f32[4096,4,384]{2,0,1:T(8,128)S(1)} %bitcast.47) | data formatting | bytes 50331648 | tf_op jit(solution)/shard_map/reshape | solution.py:37
  523.7 53.5 %gather_fusion = f32[4096,4,384]{2,1,0:T(4,128)} fusion(f32[4096,4,384]{2,1,0:T(4,128)} %copy.48, s32[4096]{0:T(1024)S(1)} %get-tuple-element.16), kind=kCustom, calls=%fused_computation.clone | custom fusion | bytes 50348032 | tf_op jit(solution)/shard_map/jit(_take)/gather | solution.py:36
  577.2 53.5 %gather_fusion.1 = f32[4096,4,384]{2,1,0:T(4,128)} fusion(f32[4096,4,384]{2,1,0:T(4,128)} %copy.53, s32[4096]{0:T(1024)S(1)} %get-tuple-element.16), kind=kCustom, calls=%fused_computation.1.clone | custom fusion | bytes 50348032 | tf_op jit(solution)/shard_map/jit(_take)/gather | solution.py:37
  630.7 0.6 fusion.33
  631.3 0.6 copy.49
  631.9 2.0 copy.54
  633.9 82.4 %add_reduce_fusion = (f32[4096,384]{1,0:T(8,128)}, f32[4096,384]{1,0:T(8,128)}) fusion(f32[4096,4,384]{2,1,0:T(4,128)} %gather_fusion.1, f32[4096,4,384]{2,1,0:T(4,128)} %gather_fusion, f32[4096,4]{1,0:T(8,128)} %copy.54, f32[4096,4]{1,0:T(8,128)S(1)} %copy.49, pred[4096]{0:T(1024)(128)(4,1)S(1)} %compare_and_fusion), kind=kLoop, calls=%fused_computation.3 | loop fusion | flops 59768832 | bytes 63049728 | tf_op jit(solution)/shard_map/reduce_sum | solution.py:52
  716.3 0.0 copy-start.4
  716.3 0.0 copy-start.2
  716.3 0.0 copy-start.3
  716.3 0.0 copy-start.5
  716.4 10.3 maximum_multiply_fusion
  726.7 0.0 reduce-scatter.2.cloned.1.call-update
  726.7 0.0 all-gather.2.cloned.1.call-start
  726.8 137.7 %reduce-scatter.2.cloned.1.call-done = f32[256,768]{1,0:T(8,128)} async-done(((f32[4096,768]{1,0:T(8,128)}), f32[256,768]{1,0:T(8,128)}) %reduce-scatter.2.cloned.1.call-update) | async-done | bytes 786448 | tf_op jit(solution)/shard_map/reduce_scatter | solution.py:69
  864.5 0.0 all-gather.2.cloned.1.call-update
  864.5 0.0 copy-done.4
  864.5 0.1 mul.224
  864.6 0.2 mul.225
  864.8 0.0 copy-done.2
  864.9 0.1 sub.39
  864.9 0.2 sub.40
  865.1 0.0 copy-done.3
  865.2 0.2 sub.42
  865.4 0.0 copy-done.5
  865.4 0.1 divide_multiply_fusion
  865.5 1.2 fusion.72
  866.7 0.5 broadcast_multiply_fusion.2
  867.2 3.9 maximum_bitcast_fusion
  871.1 95.4 %all-gather.2.cloned.1.call-done = f32[4096,768]{1,0:T(8,128)} async-done(((f32[256,768]{1,0:T(8,128)}), f32[4096,768]{1,0:T(8,128)}) %all-gather.2.cloned.1.call-update) | async-done | bytes 12582928 | tf_op jit(solution)/shard_map/all_gather | solution.py:93
  966.5 108.3 %fusion.8 = f32[2,5,256,4096]{3,2,1,0:T(8,128)} fusion(f32[4096,768]{1,0:T(8,128)} %all-gather.2.cloned.1.call-done, f32[1,5,256,768]{3,2,1,0:T(8,128)} %get-tuple-element.8, f32[1,5,256,768]{3,2,1,0:T(8,128)} %get-tuple-element.7), kind=kOutput, calls=%fused_computation.17 | convolution fusion | flops 96638730240 | bytes 62390272 | tf_op jit(solution)/shard_map/awgk,hk->awgh/dot_general | solution.py:90
  1074.8 28.8 %slice_bitcast_fusion = (f32[5,256,4096]{2,1,0:T(8,128)}, f32[5,256,4096]{2,1,0:T(8,128)}) fusion(f32[2,5,256,4096]{3,2,1,0:T(8,128)} %fusion.8), kind=kLoop, calls=%fused_computation.14 | loop fusion | bytes 83886080 | tf_op jit(solution)/shard_map/squeeze | solution.py:96
  (7 shorter events, 0.1 us)
Async XLA Ops:
  7.2 16.3 %copy-start = (f32[3,4,64,64]{3,2,1,0:T(8,128)S(1)}, f32[3,4,64,64]{3,2,1,0:T(8,128)}, u32[]{:S(2)}) copy-start(f32[3,4,64,64]{3,2,1,0:T(8,128)} %param.10) | copy-start | bytes 589828
  7.2 857.3 %reduce-scatter.2.cloned.1.call-start = ((), (), s32[]{:S(2)}) async-start(), calls=%async_computation.1 | async-start | bytes 13369344 | tf_op jit(solution)/shard_map/reduce_scatter | solution.py:69
  198.9 51.8 %copy-start.1 = (s32[4096]{0:T(1024)S(1)}, s32[4096]{0:T(1024)}, u32[]{:S(2)}) copy-start(s32[4096]{0:T(1024)} %param.15) | copy-start | bytes 49156
  716.3 148.2 %copy-start.4 = (s32[128]{0:T(128)S(1)}, s32[128]{0:T(128)}, u32[]{:S(2)}) copy-start(s32[128]{0:T(128)} %param.13) | copy-start | bytes 1540
  716.3 148.5 %copy-start.2 = (f32[128]{0:T(128)S(1)}, f32[128]{0:T(128)}, u32[]{:S(2)}) copy-start(f32[128]{0:T(128)} %param.11) | copy-start | bytes 1540
  716.3 148.8 %copy-start.3 = (f32[3]{0:T(128)S(1)}, f32[3]{0:T(128)}, u32[]{:S(2)}) copy-start(f32[3]{0:T(128)} %param.12) | copy-start | bytes 40
  716.3 149.0 %copy-start.5 = (f32[5]{0:T(128)S(1)}, f32[5]{0:T(128)}, u32[]{:S(2)}) copy-start(f32[5]{0:T(128)} %param.14) | copy-start | bytes 64
  726.7 239.8 %all-gather.2.cloned.1.call-start = ((), (), s32[]{:S(2)}) async-start(), calls=%async_computation.2 | async-start | bytes 13369344 | tf_op jit(solution)/shard_map/all_gather | solution.py:93
Sparse Core Ops, SparseCore 0:
  726.8 137.6 reduce-scatter.1
  866.8 99.6 all-gather.1
where the time goes:
time: 1120 us; the launch traced here: 1110 us
  matrix products  382 us (34%)
  local copies, waits for them, and re-layouts  360 us (32%)
  waiting for transfers between devices  233 us (21%)
  other arithmetic  121 us (11%)
  between operations  14.4 us (1%)
    reduce_scatter x1, waiting for transfers between devices, body(): lax.psum_scatter(phase_sum(picked, plane_freq, positions, size_x, norm_fa...  138 us
    dot_general x1, matrix products, body(): jnp.einsum('awgk,hk->awgh', left_side, lax.all_gather(owned, 'blk', axis=...  108 us
    all_gather x1, waiting for transfers between devices, body(): lax.all_gather(owned, 'blk', axis=0, tiled=True)  95.4 us
    reduce_sum x1, other arithmetic, phase_sum(): real_m = jnp.sum(real_v * cosine + imag_v * sine, axis=1)  82.4 us
    reshape x1, local copies, waits for them, and re-layouts, plane_picks(): real_b.reshape(size_y * size_z, planes, pair_count)  59.9 us
    reshape x1, local copies, waits for them, and re-layouts, plane_picks(): imag_b.reshape(size_y * size_z, planes, pair_count)  59.8 us
    dot_general x1, matrix products, plane_picks(): jnp.einsum('ly,ykxp->lkxp', cos_y, real_a, precision=highest)  54.9 us
    dot_general x1, matrix products, plane_picks(): jnp.einsum('ly,ykxp->lkxp', sin_y, real_a, precision=highest)  54.7 us
  transfers between devices with their start and end apart: 2, of which 2 were waited for; matrix products, arithmetic and copies ran while one was open for 1% of the time, Pallas kernels for 0%

commit v1 on v0

v1 whole, which is shorter than its diff:
```python
import functools
import math

import jax
import jax.numpy as jnp
import ml_dtypes
import numpy as np
from jax import lax
from jax.experimental import pallas as pl
from jax.experimental.pallas import tpu as pltpu
from jax.sharding import PartitionSpec as P

LANES = 128
SUB = 8
SLOTS = 4
f32 = jnp.float32
bf16 = jnp.bfloat16


def split_np(table):
    high = table.astype(ml_dtypes.bfloat16)
    low = (table - high.astype(np.float64)).astype(ml_dtypes.bfloat16)
    return np.concatenate([high, high, low], axis=1)


def split3(block):
    high = block.astype(bf16)
    low = (block - high.astype(f32)).astype(bf16)
    return jnp.concatenate([high, low, high], axis=0)


def z_table(size_z):
    half = size_z // 2
    z = np.arange(size_z)
    cos_rows = np.cos(2 * np.pi * ((np.arange(half + 1)[:, None] * z) % size_z) / size_z)
    sin_rows = -np.sin(2 * np.pi * ((np.arange(1, half)[:, None] * z) % size_z) / size_z)
    return np.concatenate([cos_rows, sin_rows], axis=0)


def y_tables(size_y):
    k = np.arange(size_y)
    ang = 2 * np.pi * ((k[:, None] * k[None, :]) % size_y) / size_y
    cos_t, sin_t = np.cos(ang), np.sin(ang)
    real_rows = np.concatenate([cos_t, sin_t], axis=1)
    imag_rows = np.concatenate([-sin_t, cos_t], axis=1)
    full = np.stack([real_rows, imag_rows], axis=0).reshape(2, size_y // 4, 4, 2 * size_y)
    full = full.transpose(1, 0, 2, 3).reshape(2 * size_y, 2 * size_y)
    return full, full[:, :size_y]


def roll_sub(x, shift):
    return pltpu.roll(x, shift % SUB, axis=x.ndim - 2)


def transform_kernel(
    pick_ref, val_ref, cond_ref, dz_ref, dy_ref, dyr_ref, cs_ref, out_ref, z_scr, tab_scr
):
    slots, size_y, size_z, lanes = val_ref.shape
    half = size_z // 2
    groups_y = size_y // SUB

    def z_stage(step, carry):
        x = step // groups_y
        yg = step % groups_y
        cond = cond_ref[x, yg]
        parts = []
        for j in range(SUB):
            block = val_ref[x, yg * SUB + j]
            parts.append(block * jnp.broadcast_to(cond[:, j : j + 1], (size_z, lanes)))
        rhs = split3(jnp.concatenate(parts, axis=1))
        got = jnp.dot(dz_ref[...], rhs, preferred_element_type=f32)
        for j in range(SUB):
            z_scr[x, pl.ds(yg * SUB + j, size_z, stride=size_y), :] = got[
                :, j * lanes : (j + 1) * lanes
            ]
        return carry

    lax.fori_loop(0, slots * groups_y, z_stage, 0)

    shape = (size_y // 4, SUB, lanes)
    sub = lax.broadcasted_iota(jnp.int32, shape, 1)
    low2 = (sub % 4) < 2
    low1 = (sub % 2) == 0

    def put(kz, got):
        a = [got[:, x * lanes : (x + 1) * lanes].reshape(shape) for x in range(slots)]
        p0 = jnp.where(low2, a[0], roll_sub(a[2], 2))
        p2 = jnp.where(low2, roll_sub(a[0], -2), a[2])
        p1 = jnp.where(low2, a[1], roll_sub(a[3], 2))
        p3 = jnp.where(low2, roll_sub(a[1], -2), a[3])
        tab_scr[kz, :, 0] = jnp.where(low1, p0, roll_sub(p1, 1))
        tab_scr[kz, :, 1] = jnp.where(low1, roll_sub(p0, -1), p1)
        tab_scr[kz, :, 2] = jnp.where(low1, p2, roll_sub(p3, 1))
        tab_scr[kz, :, 3] = jnp.where(low1, roll_sub(p2, -1), p3)

    def rows(k):
        start = pl.multiple_of(k * size_y, size_y)
        return jnp.concatenate([z_scr[x, pl.ds(start, size_y), :] for x in range(slots)], axis=1)

    for kz in (0, half):
        put(kz, jnp.dot(dyr_ref[...], split3(rows(kz)), preferred_element_type=f32))

    def y_stage(kz, carry):
        block = jnp.concatenate([rows(kz), rows(half + kz)], axis=0)
        put(kz, jnp.dot(dy_ref[...], split3(block), preferred_element_type=f32))
        return carry

    lax.fori_loop(1, half, y_stage, 0)

    sub1 = lax.broadcasted_iota(jnp.int32, (SUB, lanes), 0)
    m2 = (sub1 % 4) < 2
    m1 = (sub1 % 2) == 0
    kzs, kyq, _, _, _ = tab_scr.shape
    tab = tab_scr.reshape(kzs * kyq * 4, SUB, lanes)
    quads = out_ref.shape[0]

    def quad(q):
        t = []
        for i in range(4):
            word = pick_ref[q * 4 + i]
            col = lax.shift_right_logical(word, 8)
            ph = word & 255
            d = tab[col]
            t.append(d * cs_ref[0, ph] + roll_sub(d, 4) * cs_ref[1, ph])
        v0 = jnp.where(m2, t[0], roll_sub(t[2], 2)) + jnp.where(m2, roll_sub(t[0], -2), t[2])
        v1 = jnp.where(m2, t[1], roll_sub(t[3], 2)) + jnp.where(m2, roll_sub(t[1], -2), t[3])
        out_ref[q] = jnp.where(m1, v0, roll_sub(v1, 1)) + jnp.where(m1, roll_sub(v0, -1), v1)

    def gather(step, carry):
        for u in range(4):
            quad(step * 4 + u)
        return carry

    lax.fori_loop(0, quads // 4, gather, 0)


def transform(pick, val, cond, cs, num_g):
    slots, size_y, size_z, lanes = val.shape
    dz = jnp.asarray(split_np(z_table(size_z)))
    full, real_only = y_tables(size_y)
    dy, dyr = jnp.asarray(split_np(full)), jnp.asarray(split_np(real_only))
    vmem = pl.BlockSpec(memory_space=pltpu.VMEM)
    return pl.pallas_call(
        transform_kernel,
        out_shape=jax.ShapeDtypeStruct((num_g // 4, SUB, lanes), f32),
        in_specs=[pl.BlockSpec(memory_space=pltpu.SMEM)] + [vmem] * 6,
        out_specs=vmem,
        scratch_shapes=[
            pltpu.VMEM((slots, size_z * size_y, lanes), f32),
            pltpu.VMEM((size_z // 2 + 1, size_y // 4, 4, SUB, lanes), f32),
        ],
        name="transform",
    )(pick, val, cond, dz, dy, dyr, cs)


def split_lanes(block):
    high = block.astype(bf16)
    low = (block - high.astype(f32)).astype(bf16)
    return high, low


def chi_kernel(w_ref, own_ref, all_ref, real_ref, imag_ref, left_scr):
    freqs, rows, _ = real_ref.shape
    pairs2 = own_ref.shape[1]
    pairs = pairs2 // 2

    @pl.when(pl.program_id(0) == 0)
    def _():
        own = own_ref[...]
        for w in range(freqs):
            a = own[:, :pairs] * w_ref[w : w + 1, :]
            b = own[:, pairs:] * w_ref[w : w + 1, :]
            ah, al = split_lanes(a)
            bh, bl = split_lanes(b)
            for half, parts in enumerate(([ah, bh, ah, bh, al, bl], [bh, -ah, bh, -ah, bl, -al])):
                r0 = (half * freqs + w) * rows
                for n, part in enumerate(parts):
                    left_scr[r0 : r0 + rows, n * pairs : (n + 1) * pairs] = part

    high, low = split_lanes(all_ref[...])
    right = jnp.concatenate([high, low, high], axis=1)
    got = lax.dot_general(
        left_scr[...], right, (((1,), (1,)), ((), ())), preferred_element_type=f32
    )
    for w in range(freqs):
        real_ref[w] = got[w * rows : (w + 1) * rows]
        imag_ref[w] = got[(freqs + w) * rows : (freqs + w + 1) * rows]


def chi(weights, own, everyone, tile=512):
    freqs, pairs = weights.shape
    rows = own.shape[0]
    num_g = everyone.shape[0]
    out = jax.ShapeDtypeStruct((freqs, rows, num_g), f32)
    out_spec = pl.BlockSpec((freqs, rows, tile), lambda t: (0, 0, t))
    return pl.pallas_call(
        chi_kernel,
        grid=(num_g // tile,),
        out_shape=(out, out),
        in_specs=[
            pl.BlockSpec((freqs, pairs), lambda t: (0, 0)),
            pl.BlockSpec((rows, 2 * pairs), lambda t: (0, 0)),
            pl.BlockSpec((tile, 2 * pairs), lambda t: (t, 0)),
        ],
        out_specs=(out_spec, out_spec),
        scratch_shapes=[pltpu.VMEM((2 * freqs * rows, 6 * pairs), bf16)],
        name="chi",
    )(weights, own, everyone)


def phase_table(size_x, first, planes, norm):
    x = first + jnp.arange(SLOTS, dtype=jnp.int32)
    k = jnp.arange(size_x, dtype=jnp.int32)
    ang = (k[:, None] * x[None, :] % size_x).astype(f32) * (2.0 * math.pi / size_x)
    live = (jnp.arange(SLOTS) < planes).astype(f32) * norm
    cos_t, sin_t = jnp.cos(ang) * live, jnp.sin(ang) * live
    plain = jnp.stack(
        [jnp.concatenate([cos_t, cos_t], 1), jnp.concatenate([sin_t, -sin_t], 1)]
    )
    mirror = jnp.stack(
        [jnp.concatenate([cos_t, -cos_t], 1), jnp.concatenate([-sin_t, -sin_t], 1)]
    )
    table = jnp.concatenate([plain, mirror], axis=1)
    return jnp.broadcast_to(table[..., None], table.shape + (LANES,))


def body(psi_val, psi_cond, e_val, e_cond, occ, freq, gmap):
    num_val, planes, size_y, size_z = psi_val.shape
    num_cond = psi_cond.shape[0]
    num_g = gmap.shape[0]
    pairs = num_val * num_cond
    size_x = planes * lax.axis_size("blk")
    norm = 1.0 / math.sqrt(size_x * size_y * size_z)

    val = jnp.transpose(psi_val, (1, 2, 3, 0))
    cond = jnp.transpose(
        psi_cond.reshape(num_cond, planes, size_y // SUB, SUB, size_z), (0, 1, 2, 4, 3)
    )
    if planes < SLOTS:
        val = jnp.pad(val, ((0, SLOTS - planes), (0, 0), (0, 0), (0, 0)))
        cond = jnp.pad(cond, ((0, 0), (0, SLOTS - planes), (0, 0), (0, 0), (0, 0)))

    kz = gmap % size_z
    ky = gmap // size_z % size_y
    kx = gmap // (size_z * size_y)
    mirrored = kz > size_z // 2
    col = jnp.where(mirrored, size_z - kz, kz) * size_y + jnp.where(
        mirrored, (size_y - ky) % size_y, ky
    )
    pick = col * 256 + kx + jnp.where(mirrored, size_x, 0)
    cs = phase_table(size_x, lax.axis_index("blk") * planes, planes, norm)

    owned = []
    for c in range(num_cond):
        part = transform(pick, val, cond[c], cs, num_g)
        owned.append(lax.psum_scatter(part, "blk", scatter_dimension=0, tiled=True))
    own = jnp.stack(owned).reshape(num_cond, -1, 2, 4, num_val)
    own = jnp.transpose(own, (1, 3, 2, 0, 4)).reshape(-1, 2 * pairs)

    gaps = e_val[None, :] - e_cond[:, None]
    gaps = gaps.reshape(1, pairs)
    occ_row = jnp.broadcast_to(occ.astype(f32)[None, :], (num_cond, num_val)).reshape(1, pairs)
    weights = occ_row * gaps / (gaps * gaps + (freq * freq)[:, None]) / math.sqrt(pairs)

    return chi(weights, own, lax.all_gather(own, "blk", axis=0, tiled=True))


def solution(mesh):
    return jax.shard_map(
        body,
        mesh=mesh,
        in_specs=(
            P("cell", "blk", None, None),
            P("cell", "blk", None, None),
            P("cell"),
            P("cell"),
            P("cell"),
            P("cell"),
            P("cell"),
        ),
        out_specs=(P("cell", "blk", None), P("cell", "blk", None)),
        check_vma=False,
    )
```

time: 1120 us -> 447 us (0.40)
  matrix products: 382 us -> 0 us
  local copies, waits for them, and re-layouts: 360 us -> 10.2 us
  Pallas kernels: 0 us -> 172 us
  other arithmetic: 121 us -> 3.01 us
  waiting for transfers between devices: 233 us -> 247 us
    dot_general x7 -> x0, matrix products: 382 us -> none  [the longest x1 108 us: body(): jnp.einsum('awgk,hk->awgh', left_side, lax.all_gather(owned, 'blk', axis=...]
    pallas_call x0 -> x4, Pallas kernels: none -> 172 us  [the longest x3 116 us: transform(): pl.pallas_call(transform_kernel, out_shape=jax.ShapeDtypeStruct((num_g //...]
    reshape x2, local copies, waits for them, and re-layouts: 120 us -> 3.3 us  [the longest x1 1.94 us: body(): psi_cond.reshape(num_cond, planes, size_y // SUB, SUB, size_z)]
    gather x2 -> x0, local copies, waits for them, and re-layouts: 107 us -> none  [the longest x1 53.5 us: plane_picks(): jnp.take(real_b.reshape(size_y * size_z, planes, pair_count), column_idx,...]
    reduce_sum x1 -> x0, other arithmetic: 82.4 us -> none  [phase_sum(): real_m = jnp.sum(real_v * cosine + imag_v * sine, axis=1)]
    mul x3 -> x0, local copies, waits for them, and re-layouts: 40.7 us -> none  [the longest x1 40.4 us: plane_picks(): val_part[:, None] * cond_part[None]]
    mul x4 -> x3, other arithmetic: 34.1 us -> 0.19 us  [the longest x1 0.12 us: phase_table(): cos_t, sin_t = (jnp.cos(ang) * live, jnp.sin(ang) * live)]
    squeeze x1, local copies, waits for them, and re-layouts: 28.8 us -> 1.73 us  [body(): part = transform(pick, val, cond[c], cs, num_g)]
  transfers between devices with their start and end apart: 2 -> 4, of which waited for: 2 -> 3; matrix products, arithmetic and copies ran while one was open for 1% -> 1% of each run, Pallas kernels for 0% -> 17%
where the time goes in v1:
time: 447 us; the launch traced here: 446 us
  waiting for transfers between devices  247 us (55%)
  Pallas kernels  172 us (38%)
  between operations  13.9 us (3%)
  local copies, waits for them, and re-layouts  10.2 us (2%)
    reduce_scatter x3, waiting for transfers between devices, body(): owned.append(lax.psum_scatter(part, 'blk', scatter_dimension=0, tiled=True))  148 us
    pallas_call x3, Pallas kernels, transform(): pl.pallas_call(transform_kernel, out_shape=jax.ShapeDtypeStruct((num_g //...  116 us
    all_gather x1, waiting for transfers between devices, body(): return chi(weights, own, lax.all_gather(own, 'blk', axis=0, tiled=True))  98.9 us
    pallas_call x1, Pallas kernels, chi(): pl.pallas_call(chi_kernel, grid=(num_g // tile,), out_shape=(out, out), i...  55.9 us
  transfers between devices with their start and end apart: 4, of which 3 were waited for; matrix products, arithmetic and copies ran while one was open for 1% of the time, Pallas kernels for 17%

profile of v1, /device:TPU:0, one launch (start us, length us, event | category | flops | bytes accessed | tf_op | source)
XLA Modules:
  0.0 446.4 jit_solution(16580708534134148817)
XLA Ops:
  7.2 0.0 reduce-scatter.4.cloned.1.call-start
  7.2 1.4 fusion.4.pick_ref
  8.6 0.1 sine_multiply_fusion
  8.7 0.1 maximum_maximum_fusion
  8.8 0.1 copy.26
  9.0 1.9 copy.25
  10.9 1.7 slice_bitcast_fusion.2
  12.6 1.3 broadcast_in_dim.9.cs_ref
  14.0 38.8 %transform.3 = f32[1024,8,128]{2,1,0:T(8,128)} custom-call(s32[4096]{0:T(1024)} %fusion.4.pick_ref, f32[4,64,64,128]{3,2,1,0:T(8,128)} %bitcast.26, f32[4,8,64,8]{3,2,1,0:T(8,128)} %get-tuple-element.2.cond_ref, bf16[64,192]{1,0:T(8,128)(2,1)} %constant.85.clone.dz_ref, bf16[128,384]{1,0:T(8,128)(2,1)} %constant.86.clone.dy_ref, ...), custom_call_target="tpu_custom_call" | custom-call | tf_op jit(solution)/shard_map/transform/pallas_call | solution.py:143
  52.8 0.0 reduce-scatter.4.cloned.1.call-update
  52.8 0.0 reduce-scatter.8.cloned.1.call-start
  52.8 38.9 %transform.5 = f32[1024,8,128]{2,1,0:T(8,128)} custom-call(s32[4096]{0:T(1024)} %fusion.4.pick_ref, f32[4,64,64,128]{3,2,1,0:T(8,128)} %bitcast.27, f32[4,8,64,8]{3,2,1,0:T(8,128)} %get-tuple-element.3.cond_ref, bf16[64,192]{1,0:T(8,128)(2,1)} %constant.85.clone.dz_ref, bf16[128,384]{1,0:T(8,128)(2,1)} %constant.86.clone.dy_ref, ...), custom_call_target="tpu_custom_call" | custom-call | tf_op jit(solution)/shard_map/transform/pallas_call | solution.py:143
  91.7 0.0 reduce-scatter.8.cloned.1.call-update
  91.7 0.0 reduce-scatter.6.cloned.1.call-start
  91.8 38.8 %transform.4 = f32[1024,8,128]{2,1,0:T(8,128)} custom-call(s32[4096]{0:T(1024)} %fusion.4.pick_ref, f32[4,64,64,128]{3,2,1,0:T(8,128)} %bitcast.28, f32[4,8,64,8]{3,2,1,0:T(8,128)} %get-tuple-element.4.cond_ref, bf16[64,192]{1,0:T(8,128)(2,1)} %constant.85.clone.dz_ref, bf16[128,384]{1,0:T(8,128)(2,1)} %constant.86.clone.dy_ref, ...), custom_call_target="tpu_custom_call" | custom-call | tf_op jit(solution)/shard_map/transform/pallas_call | solution.py:143
  130.6 0.0 copy-start.2
  130.6 0.0 copy-start.3
  130.6 0.0 copy-start
  130.6 0.0 copy-start.1
  130.6 0.0 reduce-scatter.6.cloned.1.call-update
  130.6 0.2 all-gather.2.cloned.1.call-start
  130.9 0.0 reduce-scatter.4.cloned.1.call-done
  130.9 1.2 copy.27
  132.1 72.6 %reduce-scatter.8.cloned.1.call-done = f32[64,8,128]{2,1,0:T(8,128)} async-done(((f32[1024,8,128]{2,1,0:T(8,128)}), f32[64,8,128]{2,1,0:T(8,128)}) %reduce-scatter.8.cloned.1.call-update) | async-done | bytes 262160 | tf_op jit(solution)/shard_map/reduce_scatter | solution.py:256
  204.8 1.2 copy.29
  206.0 75.1 %reduce-scatter.6.cloned.1.call-done = f32[64,8,128]{2,1,0:T(8,128)} async-done(((f32[1024,8,128]{2,1,0:T(8,128)}), f32[64,8,128]{2,1,0:T(8,128)}) %reduce-scatter.6.cloned.1.call-update) | async-done | bytes 262160 | tf_op jit(solution)/shard_map/reduce_scatter | solution.py:256
  281.0 1.2 copy.28
  282.3 0.7 maximum_bitcast_fusion
  283.0 1.4 reshape.67.own_ref
  284.3 0.0 all-gather.2.cloned.1.call-update
  284.3 0.0 copy-done.2
  284.4 0.0 copy-done.3
  284.4 0.0 copy-done
  284.4 0.0 copy-done.1
  284.4 0.1 fusion.18
  284.5 0.7 divide_multiply_fusion.w_ref
  285.1 98.9 %all-gather.2.cloned.1.call-done.all_ref = f32[4096,768]{1,0:T(8,128)} async-done(((f32[256,768]{1,0:T(8,128)}), f32[4096,768]{1,0:T(8,128)}) %all-gather.2.cloned.1.call-update) | async-done | bytes 12582928 | tf_op jit(solution)/shard_map/all_gather | solution.py:265
  384.0 55.9 %chi.1 = (f32[5,256,4096]{2,1,0:T(8,128)}, f32[5,256,4096]{2,1,0:T(8,128)}) custom-call(f32[5,384]{1,0:T(8,128)} %divide_multiply_fusion.w_ref, f32[256,768]{1,0:T(8,128)} %reshape.67.own_ref, f32[4096,768]{1,0:T(8,128)} %all-gather.2.cloned.1.call-done.all_ref), custom_call_target="tpu_custom_call" | custom-call | tf_op jit(solution)/shard_map/chi/pallas_call | solution.py:196
  (5 shorter events, 0.0 us)
Async XLA Ops:
  7.2 123.7 %reduce-scatter.4.cloned.1.call-start = ((), (), s32[]{:S(2)}) async-start(), calls=%async_computation.3 | async-start | bytes 4456448 | tf_op jit(solution)/shard_map/reduce_scatter | solution.py:256
  52.8 152.0 %reduce-scatter.8.cloned.1.call-start = ((), (), s32[]{:S(2)}) async-start(), calls=%async_computation.5 | async-start | bytes 4456448 | tf_op jit(solution)/shard_map/reduce_scatter | solution.py:256
  91.7 189.3 %reduce-scatter.6.cloned.1.call-start = ((), (), s32[]{:S(2)}) async-start(), calls=%async_computation.4 | async-start | bytes 4456448 | tf_op jit(solution)/shard_map/reduce_scatter | solution.py:256
  130.6 153.8 %copy-start.2 = (s32[128]{0:T(128)S(1)}, s32[128]{0:T(128)}, u32[]{:S(2)}) copy-start(s32[128]{0:T(128)} %param.20) | copy-start | bytes 1540
  130.6 153.8 %copy-start.3 = (f32[5]{0:T(128)S(1)}, f32[5]{0:T(128)}, u32[]{:S(2)}) copy-start(f32[5]{0:T(128)} %param.21) | copy-start | bytes 64
  130.6 153.8 %copy-start = (f32[3]{0:T(128)S(1)}, f32[3]{0:T(128)}, u32[]{:S(2)}) copy-start(f32[3]{0:T(128)} %param.19) | copy-start | bytes 40
  130.6 153.8 %copy-start.1 = (f32[128]{0:T(128)S(1)}, f32[128]{0:T(128)}, u32[]{:S(2)}) copy-start(f32[128]{0:T(128)} %param.18) | copy-start | bytes 1540
  130.6 253.4 %all-gather.2.cloned.1.call-start = ((), (), s32[]{:S(2)}) async-start(), calls=%async_computation.6 | async-start | bytes 13369344 | tf_op jit(solution)/shard_map/all_gather | solution.py:265
Sparse Core Ops, SparseCore 0:
  52.9 75.5 reduce-scatter.3
  132.9 71.8 reduce-scatter.7
  209.2 71.8 reduce-scatter.5
  284.5 99.5 all-gather.1

commit v2 on v1

--- a/solution.py
+++ b/solution.py
@@ -9,6 +9,7 @@
 from jax.experimental import pallas as pl
 from jax.experimental.pallas import tpu as pltpu
 from jax.sharding import PartitionSpec as P
+
 
 LANES = 128
 SUB = 8
@@ -53,7 +54,7 @@
 
 
 def transform_kernel(
-    pick_ref, val_ref, cond_ref, dz_ref, dy_ref, dyr_ref, cs_ref, out_ref, z_scr, tab_scr
+    pick_ref, val_ref, cond_ref, dz_ref, dy_ref, dyr_ref, cs_ref, keep_ref, send_ref, z_scr, tab_scr
 ):
     slots, size_y, size_z, lanes = val_ref.shape
     half = size_z // 2
@@ -112,12 +113,12 @@
     m1 = (sub1 % 2) == 0
     kzs, kyq, _, _, _ = tab_scr.shape
     tab = tab_scr.reshape(kzs * kyq * 4, SUB, lanes)
-    quads = out_ref.shape[0]
-
-    def quad(q):
+    quads = keep_ref.shape[0]
+
+    def quad(out_ref, first, q):
         t = []
         for i in range(4):
-            word = pick_ref[q * 4 + i]
+            word = pick_ref[first + q * 4 + i]
             col = lax.shift_right_logical(word, 8)
             ph = word & 255
             d = tab[col]
@@ -126,12 +127,14 @@
         v1 = jnp.where(m2, t[1], roll_sub(t[3], 2)) + jnp.where(m2, roll_sub(t[1], -2), t[3])
         out_ref[q] = jnp.where(m1, v0, roll_sub(v1, 1)) + jnp.where(m1, roll_sub(v0, -1), v1)
 
-    def gather(step, carry):
-        for u in range(4):
-            quad(step * 4 + u)
-        return carry
-
-    lax.fori_loop(0, quads // 4, gather, 0)
+    for out_ref, first in ((send_ref, quads * 4), (keep_ref, 0)):
+
+        def gather(step, carry, out_ref=out_ref, first=first):
+            for u in range(4):
+                quad(out_ref, first, step * 4 + u)
+            return carry
+
+        lax.fori_loop(0, quads // 4, gather, 0)
 
 
 def transform(pick, val, cond, cs, num_g):
@@ -142,9 +145,9 @@
     vmem = pl.BlockSpec(memory_space=pltpu.VMEM)
     return pl.pallas_call(
         transform_kernel,
-        out_shape=jax.ShapeDtypeStruct((num_g // 4, SUB, lanes), f32),
+        out_shape=(jax.ShapeDtypeStruct((num_g // 8, SUB, lanes), f32),) * 2,
         in_specs=[pl.BlockSpec(memory_space=pltpu.SMEM)] + [vmem] * 6,
-        out_specs=vmem,
+        out_specs=(vmem, vmem),
         scratch_shapes=[
             pltpu.VMEM((slots, size_z * size_y, lanes), f32),
             pltpu.VMEM((size_z // 2 + 1, size_y // 4, 4, SUB, lanes), f32),
@@ -159,38 +162,48 @@
     return high, low
 
 
+def fill_left(w_ref, own_ref, left_scr):
+    freqs = w_ref.shape[0]
+    rows, pairs2 = own_ref.shape
+
+    def fill(w, carry):
+        row = w_ref[pl.ds(w, 1), :]
+        high, low = split_lanes(own_ref[...] * jnp.concatenate([row, row], axis=1))
+        at = pl.ds(pl.multiple_of(w * rows, rows), rows)
+        left_scr[at, :pairs2] = high
+        left_scr[at, pairs2 : 2 * pairs2] = high
+        left_scr[at, 2 * pairs2 :] = low
+        return carry
+
+    lax.fori_loop(0, freqs, fill, 0)
+
+
+def chi_tile(block, left_scr, real_ref, imag_ref):
+    freqs, rows, _ = real_ref.shape
+    pairs = block.shape[1] // 2
+    turned = jnp.concatenate([-block[:, pairs:], block[:, :pairs]], axis=1)
+    for value, out_ref in ((block, real_ref), (turned, imag_ref)):
+        high, low = split_lanes(value)
+        right = jnp.concatenate([high, low, high], axis=1)
+        got = lax.dot_general(
+            left_scr[...], right, (((1,), (1,)), ((), ())), preferred_element_type=f32
+        )
+        out_ref[...] = got.reshape(freqs, rows, -1)
+
+
 def chi_kernel(w_ref, own_ref, all_ref, real_ref, imag_ref, left_scr):
-    freqs, rows, _ = real_ref.shape
-    pairs2 = own_ref.shape[1]
-    pairs = pairs2 // 2
-
     @pl.when(pl.program_id(0) == 0)
     def _():
-        own = own_ref[...]
-        for w in range(freqs):
-            a = own[:, :pairs] * w_ref[w : w + 1, :]
-            b = own[:, pairs:] * w_ref[w : w + 1, :]
-            ah, al = split_lanes(a)
-            bh, bl = split_lanes(b)
-            for half, parts in enumerate(([ah, bh, ah, bh, al, bl], [bh, -ah, bh, -ah, bl, -al])):
-                r0 = (half * freqs + w) * rows
-                for n, part in enumerate(parts):
-                    left_scr[r0 : r0 + rows, n * pairs : (n + 1) * pairs] = part
-
-    high, low = split_lanes(all_ref[...])
-    right = jnp.concatenate([high, low, high], axis=1)
-    got = lax.dot_general(
-        left_scr[...], right, (((1,), (1,)), ((), ())), preferred_element_type=f32
-    )
-    for w in range(freqs):
-        real_ref[w] = got[w * rows : (w + 1) * rows]
-        imag_ref[w] = got[(freqs + w) * rows : (freqs + w + 1) * rows]
-
-
-def chi(weights, own, everyone, tile=512):
+        fill_left(w_ref, own_ref, left_scr)
+
+    chi_tile(all_ref[...], left_scr, real_ref, imag_ref)
+
+
+def chi(weights, own, everyone):
     freqs, pairs = weights.shape
     rows = own.shape[0]
     num_g = everyone.shape[0]
+    tile = min(num_g, 4 * LANES)
     out = jax.ShapeDtypeStruct((freqs, rows, num_g), f32)
     out_spec = pl.BlockSpec((freqs, rows, tile), lambda t: (0, 0, t))
     return pl.pallas_call(
@@ -203,9 +216,159 @@
             pl.BlockSpec((tile, 2 * pairs), lambda t: (t, 0)),
         ],
         out_specs=(out_spec, out_spec),
-        scratch_shapes=[pltpu.VMEM((2 * freqs * rows, 6 * pairs), bf16)],
+        scratch_shapes=[pltpu.VMEM((freqs * rows, 6 * pairs), bf16)],
         name="chi",
     )(weights, own, everyone)
+
+
+def chi_group_kernel(counts, with_old, *refs):
+    total = sum(counts)
+    n = len(counts)
+    _, w_ref, own_ref = refs[:3]
+    pieces = refs[3 : 3 + total]
+    rest = refs[3 + total + (2 if with_old else 0) :]
+    real_ref, imag_ref, left_scr, got_scr, sems = rest
+    step = pl.program_id(0)
+
+    def copies(i):
+        at, first = 0, sum(counts[:i])
+        for j in range(counts[i]):
+            ref = pieces[first + j]
+            yield pltpu.make_async_copy(
+                ref, got_scr.at[i, pl.ds(at, ref.shape[0])], sems.at[first + j]
+            )
+            at += ref.shape[0]
+
+    @pl.when(step == 0)
+    def _():
+        for i in range(n):
+            for copy in copies(i):
+                copy.start()
+        fill_left(w_ref, own_ref, left_scr)
+
+    for i in range(n):
+
+        @pl.when(step == i)
+        def _(i=i):
+            for copy in copies(i):
+                copy.wait()
+
+    chi_tile(got_scr[step], left_scr, real_ref, imag_ref)
+
+
+def chi_group(weights, own, blocks, ids, num_g, old):
+    freqs, pairs = weights.shape
+    rows = own.shape[0]
+    counts = tuple(len(b) for b in blocks)
+    pieces = [p for b in blocks for p in b]
+    out = jax.ShapeDtypeStruct((freqs, rows, num_g), f32)
+    out_spec = pl.BlockSpec((freqs, rows, rows), lambda t, ids: (0, 0, ids[t]))
+    hbm = pl.BlockSpec(memory_space=pl.ANY)
+    olds = () if old is None else old
+    return pl.pallas_call(
+        functools.partial(chi_group_kernel, counts, old is not None),
+        grid_spec=pltpu.PrefetchScalarGridSpec(
+            num_scalar_prefetch=1,
+            grid=(len(blocks),),
+            in_specs=[
+                pl.BlockSpec((freqs, pairs), lambda t, ids: (0, 0)),
+                pl.BlockSpec((rows, 2 * pairs), lambda t, ids: (0, 0)),
+            ]
+            + [hbm] * (len(pieces) + len(olds)),
+            out_specs=(out_spec, out_spec),
+            scratch_shapes=[
+                pltpu.VMEM((freqs * rows, 6 * pairs), bf16),
+                pltpu.VMEM((len(blocks), rows, 2 * pairs), f32),
+                pltpu.SemaphoreType.DMA((len(pieces),)),
+            ],
+        ),
+        out_shape=(out, out),
+        input_output_aliases={3 + len(pieces) + i: i for i in range(len(olds))},
+        name="chi",
+    )(ids, weights, own, *pieces, *olds)
+
+
+RING = (0, 2, 3, 1)
+
+
+class Links:
+    def __init__(self, count):
+        def place(i):
+            return i // 4, i // 2 % 2, i % 2
+
+        def at(z, y, core):
+            return z * 4 + y * 2 + core
+
+        def turn(i, by):
+            z, y, core = place(i)
+            return at(RING[(RING.index(z) + by) % 4], y, core)
+
+        every = range(count)
+        self.core = [(i, i ^ 1) for i in every]
+        self.y = [(i, i ^ 2) for i in every]
+        self.cw = [(i, turn(i, 1)) for i in every]
+        self.ccw = [(i, turn(i, -1)) for i in every]
+        self.near = np.array(
+            [
+                [[[turn(i ^ (2 * b) ^ a, r) for r in range(4)] for b in range(2)] for a in range(2)]
+                for i in every
+            ],
+            dtype=np.int32,
+        )
+
+    @staticmethod
+    def fits(count):
+        return count == len(RING) * 4
+
+
+def send(value, pairs):
+    return lax.ppermute(value, "blk", pairs)
+
+
+def reduce_scatter(keep, other, links):
+    half = keep.shape[0] // 2
+    got = send(other, links.core)
+    far = send(keep[half:] + got[half:], links.y)
+    near = keep[:half] + got[:half] + far
+    block = half // 4
+    part = block // 2
+    cw = send(near[2 * block : 2 * block + part], links.cw)
+    ccw = send(near[2 * block + part : 3 * block], links.ccw)
+    cw, ccw = lax.optimization_barrier((cw, ccw))
+    from_cw = send(
+        jnp.concatenate([near[block : block + part] + cw, near[block + part : 2 * block]]), links.cw
+    )
+    from_ccw = send(
+        jnp.concatenate([near[3 * block : 3 * block + part], near[3 * block + part :] + ccw]),
+        links.ccw,
+    )
+    from_cw, from_ccw = lax.optimization_barrier((from_cw, from_ccw))
+    return near[:block] + from_cw + from_ccw
+
+
+GROUPS = (((0, 0),), ((1, 0),), ((0, 1), (0, 3)), ((0, 2),), ((1, 1), (1, 3)), ((1, 2),))
+
+
+def gather_and_chi(weights, own, links, near, num_g):
+    part = own.shape[0] // 2
+
+    def over(pieces, pairs):
+        return [send(p, pairs) for p in pieces]
+
+    mine = {(0, 0): [own]}
+    mine[0, 3] = over([own], links.cw)
+    mine[0, 1] = over([own], links.ccw)
+    mine[0, 2] = [send(mine[0, 3][0][:part], links.cw), send(mine[0, 1][0][part:], links.ccw)]
+    for r in range(4):
+        mine[1, r] = over(mine[0, r], links.y)
+    old = None
+    for group in GROUPS:
+        blocks, ids = [], []
+        for b, r in group:
+            blocks += [mine[b, r], over(mine[b, r], links.core)]
+            ids += [near[0, b, r], near[1, b, r]]
+        old = chi_group(weights, own, blocks, jnp.stack(ids), num_g, old)
+    return old
 
 
 def phase_table(size_x, first, planes, norm):
@@ -224,7 +387,7 @@
     return jnp.broadcast_to(table[..., None], table.shape + (LANES,))
 
 
-def body(psi_val, psi_cond, e_val, e_cond, occ, freq, gmap):
+def polarizability(psi_val, psi_cond, e_val, e_cond, occ, freq, gmap):
     num_val, planes, size_y, size_z = psi_val.shape
     num_cond = psi_cond.shape[0]
     num_g = gmap.shape[0]
@@ -250,10 +413,19 @@
     pick = col * 256 + kx + jnp.where(mirrored, size_x, 0)
     cs = phase_table(size_x, lax.axis_index("blk") * planes, planes, norm)
 
+    count = lax.axis_size("blk")
+    links = Links(count) if Links.fits(count) else None
+    if links is not None:
+        near = jnp.asarray(links.near)[lax.axis_index("blk")]
+        pick = pick.reshape(count, -1)[near.reshape(-1)].reshape(-1)
     owned = []
     for c in range(num_cond):
-        part = transform(pick, val, cond[c], cs, num_g)
-        owned.append(lax.psum_scatter(part, "blk", scatter_dimension=0, tiled=True))
+        keep, other = transform(pick, val, cond[c], cs, num_g)
+        if links is not None:
+            owned.append(reduce_scatter(keep, other, links))
+        else:
+            whole = jnp.concatenate([keep, other])
+            owned.append(lax.psum_scatter(whole, "blk", scatter_dimension=0, tiled=True))
     own = jnp.stack(owned).reshape(num_cond, -1, 2, 4, num_val)
     own = jnp.transpose(own, (1, 3, 2, 0, 4)).reshape(-1, 2 * pairs)
 
@@ -262,12 +434,14 @@
     occ_row = jnp.broadcast_to(occ.astype(f32)[None, :], (num_cond, num_val)).reshape(1, pairs)
     weights = occ_row * gaps / (gaps * gaps + (freq * freq)[:, None]) / math.sqrt(pairs)
 
+    if links is not None:
+        return gather_and_chi(weights, own, links, near, num_g)
     return chi(weights, own, lax.all_gather(own, "blk", axis=0, tiled=True))
 
 
 def solution(mesh):
-    return jax.shard_map(
-        body,
+    step = jax.shard_map(
+        polarizability,
         mesh=mesh,
         in_specs=(
             P("cell", "blk", None, None),
@@ -281,3 +455,6 @@
         out_specs=(P("cell", "blk", None), P("cell", "blk", None)),
         check_vma=False,
     )
+    if not Links.fits(mesh.shape["blk"]):
+        return step
+    return step

time: 447 us -> 428 us (0.957)
  waiting for transfers between devices: 247 us -> 161 us
  starting transfers between devices: 0.35 us -> 38.1 us
  Pallas kernels: 172 us -> 196 us
  other arithmetic: 3.01 us -> 21 us
  between operations: 13.9 us -> 1.27 us
    ppermute x0 -> x37, waiting for transfers between devices: none -> 161 us  [send(): return lax.ppermute(value, 'blk', pairs)]
    reduce_scatter x3 -> x0, waiting for transfers between devices: 148 us -> none  [body(): owned.append(lax.psum_scatter(part, 'blk', scatter_dimension=0, tiled=True))]
    all_gather x1 -> x0, waiting for transfers between devices: 98.9 us -> none  [body(): return chi(weights, own, lax.all_gather(own, 'blk', axis=0, tiled=True))]
    ppermute x0 -> x37, starting transfers between devices: none -> 38.1 us  [send(): return lax.ppermute(value, 'blk', pairs)]
    pallas_call x4 -> x9, Pallas kernels: 172 us -> 196 us  [the longest x3 116 us: transform(): pl.pallas_call(transform_kernel, out_shape=(jax.ShapeDtypeStruct((num_g /...]
    another operation x0 -> x6, other arithmetic: none -> 13.7 us  [gather_and_chi(): old = chi_group(weights, own, blocks, jnp.stack(ids), num_g, old)]
  transfers between devices with their start and end apart: 4 -> 37, of which waited for: 3 -> 18; matrix products, arithmetic and copies ran while one was open for 1% -> 5% of each run, Pallas kernels for 17% -> 34%
where the time goes in v2:
time: 428 us
  Pallas kernels  196 us (46%)
  waiting for transfers between devices  161 us (38%)
  starting transfers between devices  38.1 us (9%)
  other arithmetic  21 us (5%)
  local copies, waits for them, and re-layouts  9.24 us (2%)
    ppermute x37, waiting for transfers between devices, send(): return lax.ppermute(value, 'blk', pairs)  161 us
    pallas_call x3, Pallas kernels, transform(): pl.pallas_call(transform_kernel, out_shape=(jax.ShapeDtypeStruct((num_g /...  116 us
    pallas_call x6, Pallas kernels, chi_group(): pl.pallas_call(functools.partial(chi_group_kernel, counts, old is not Non...  80.2 us
    ppermute x37, starting transfers between devices, send(): return lax.ppermute(value, 'blk', pairs)  38.1 us
    another operation x6, other arithmetic, gather_and_chi(): old = chi_group(weights, own, blocks, jnp.stack(ids), num_g, old)  13.7 us
  transfers between devices with their start and end apart: 37, of which 18 were waited for; matrix products, arithmetic and copies ran while one was open for 5% of the time, Pallas kernels for 34%

profile of v2, /device:TPU:0, one launch (start us, length us, event | category | flops | bytes accessed | tf_op | source)
XLA Modules:
  0.0 427.5 jit_solution(7941247072676755767)
XLA Ops:
  1.0 0.7 constant_dynamic-slice_fusion
  1.8 0.8 fusion.10
  2.6 0.6 gather_fusion
  3.2 0.6 copy.41
  3.8 1.9 copy.36
  5.7 1.7 slice_bitcast_fusion.2
  7.4 1.4 broadcast_in_dim.9.cs_ref
  8.8 38.7 %transform.3 = (f32[512,8,128]{2,1,0:T(8,128)}, f32[512,8,128]{2,1,0:T(8,128)}) custom-call(s32[4096]{0:T(1024)} %bitcast.56, f32[4,64,64,128]{3,2,1,0:T(8,128)} %bitcast.48, f32[4,8,64,8]{3,2,1,0:T(8,128)} %get-tuple-element.58.cond_ref, bf16[64,192]{1,0:T(8,128)(2,1)} %constant.92.clone.dz_ref, bf16[128,384]{1,0:T(8,128)(2,1)} %constant.93.clone.dy_ref, ...), custom_call_target="tpu_custom_call" | custom-call | tf_op jit(solution)/shard_map/transform/pallas_call | solution.py:146
  48.0 38.8 %transform.4 = (f32[512,8,128]{2,1,0:T(8,128)}, f32[512,8,128]{2,1,0:T(8,128)}) custom-call(s32[4096]{0:T(1024)} %bitcast.57, f32[4,64,64,128]{3,2,1,0:T(8,128)} %bitcast.49, f32[4,8,64,8]{3,2,1,0:T(8,128)} %get-tuple-element.60.cond_ref, bf16[64,192]{1,0:T(8,128)(2,1)} %constant.92.clone.dz_ref, bf16[128,384]{1,0:T(8,128)(2,1)} %constant.93.clone.dy_ref, ...), custom_call_target="tpu_custom_call" | custom-call | tf_op jit(solution)/shard_map/transform/pallas_call | solution.py:146
  86.8 38.7 %transform.5 = (f32[512,8,128]{2,1,0:T(8,128)}, f32[512,8,128]{2,1,0:T(8,128)}) custom-call(s32[4096]{0:T(1024)} %bitcast.58, f32[4,64,64,128]{3,2,1,0:T(8,128)} %bitcast.50, f32[4,8,64,8]{3,2,1,0:T(8,128)} %get-tuple-element.59.cond_ref, bf16[64,192]{1,0:T(8,128)(2,1)} %constant.92.clone.dz_ref, bf16[128,384]{1,0:T(8,128)(2,1)} %constant.93.clone.dy_ref, ...), custom_call_target="tpu_custom_call" | custom-call | tf_op jit(solution)/shard_map/transform/pallas_call | solution.py:146
  126.0 1.8 slice_add_fusion.4
  127.8 2.6 collective-permute-start.1
  131.1 2.0 collective-permute-start.13
  133.1 21.4 %collective-permute-done.1 = f32[256,8,128]{2,1,0:T(8,128)S(1)} collective-permute-done((f32[256,8,128]{2,1,0:T(8,128)S(1)}, f32[256,8,128]{2,1,0:T(8,128)S(1)}, u32[]{:S(2)}, u32[]{:S(2)}) %collective-permute-start.1) | collective-permute-done | bytes 1048608 | tf_op jit(solution)/shard_map/ppermute | solution.py:325
  154.4 1.4 fusion.2
  155.8 3.1 collective-permute-start.2
  159.0 17.9 %collective-permute-done.7 = f32[256,8,128]{2,1,0:T(8,128)S(1)} collective-permute-done((f32[256,8,128]{2,1,0:T(8,128)S(1)}, f32[256,8,128]{2,1,0:T(8,128)S(1)}, u32[]{:S(2)}, u32[]{:S(2)}) %collective-permute-start.7) | collective-permute-done | bytes 1048608 | tf_op jit(solution)/shard_map/ppermute | solution.py:325
  177.1 3.1 collective-permute-start.8
  180.3 18.9 %collective-permute-done.13 = f32[256,8,128]{2,1,0:T(8,128)S(1)} collective-permute-done((f32[256,8,128]{2,1,0:T(8,128)S(1)}, f32[256,8,128]{2,1,0:T(8,128)S(1)}, u32[]{:S(2)}, u32[]{:S(2)}) %collective-permute-start.13) | collective-permute-done | bytes 1048608 | tf_op jit(solution)/shard_map/ppermute | solution.py:325
  199.3 2.9 collective-permute-start.14
  202.3 2.0 collective-permute-start.5
  204.3 1.1 collective-permute-start.4
  205.4 1.0 collective-permute-start.11
  206.5 2.9 collective-permute-start.10
  209.5 0.7 collective-permute-done.15
  210.3 1.2 collective-permute-start.17
  211.5 9.2 %collective-permute-done.5 = f32[64,8,128]{2,1,0:T(8,128)S(1)} collective-permute-done((f32[64,8,128]{2,1,0:T(8,128)S(1)}, f32[64,8,128]{2,1,0:T(8,128)S(1)}, u32[]{:S(2)}, u32[]{:S(2)}) %collective-permute-start.5) | collective-permute-done | bytes 262176 | tf_op jit(solution)/shard_map/ppermute | solution.py:325
  220.7 1.1 collective-permute-done.4
  222.2 9.8 %collective-permute-done.11 = f32[64,8,128]{2,1,0:T(8,128)S(1)} collective-permute-done((f32[64,8,128]{2,1,0:T(8,128)S(1)}, f32[64,8,128]{2,1,0:T(8,128)S(1)}, u32[]{:S(2)}, u32[]{:S(2)}) %collective-permute-start.11) | collective-permute-done | bytes 262176 | tf_op jit(solution)/shard_map/ppermute | solution.py:325
  232.0 1.0 collective-permute-done.10
  233.4 5.5 %collective-permute-done.17 = f32[64,8,128]{2,1,0:T(8,128)S(1)} collective-permute-done((f32[64,8,128]{2,1,0:T(8,128)S(1)}, f32[64,8,128]{2,1,0:T(8,128)S(1)}, u32[]{:S(2)}, u32[]{:S(2)}) %collective-permute-start.17) | collective-permute-done | bytes 262176 | tf_op jit(solution)/shard_map/ppermute | solution.py:325
  238.9 3.0 collective-permute-done.16
  242.3 0.7 maximum_bitcast_fusion
  243.4 2.8 collective-permute-start.18
  246.3 1.5 collective-permute-start.34
  247.8 16.4 %collective-permute-done.18.refs_5_ = f32[256,768]{1,0:T(8,128)S(1)} collective-permute-done((f32[256,768]{1,0:T(8,128)S(1)}, f32[256,768]{1,0:T(8,128)S(1)}, u32[]{:S(2)}, u32[]{:S(2)}) %collective-permute-start.18) | collective-permute-done | bytes 786464 | tf_op jit(solution)/shard_map/ppermute | solution.py:325
  264.3 3.4 collective-permute-start.19
  267.7 15.2 %collective-permute-done.21.refs_3_ = f32[256,768]{1,0:T(8,128)S(1)} collective-permute-done((f32[256,768]{1,0:T(8,128)S(1)}, f32[256,768]{1,0:T(8,128)S(1)}, u32[]{:S(2)}, u32[]{:S(2)}) %collective-permute-start.21) | collective-permute-done | bytes 786464 | tf_op jit(solution)/shard_map/ppermute | solution.py:325
  283.0 0.7 collective-permute-start.22
  284.2 5.3 %collective-permute-done.19.refs_3_ = f32[128,768]{1,0:T(8,128)S(1)} collective-permute-done((f32[128,768]{1,0:T(8,128)S(1)}, f32[128,768]{1,0:T(8,128)S(1)}, u32[]{:S(2)}, u32[]{:S(2)}) %collective-permute-start.19) | collective-permute-done | bytes 393248 | tf_op jit(solution)/shard_map/ppermute | solution.py:325
  289.5 1.5 collective-permute-start.26
  291.0 6.6 %collective-permute-done.22.refs_4_ = f32[128,768]{1,0:T(8,128)} collective-permute-done((f32[128,768]{1,0:T(8,128)S(1)}, f32[128,768]{1,0:T(8,128)}, u32[]{:S(2)}, u32[]{:S(2)}) %collective-permute-start.22) | collective-permute-done | bytes 393248 | tf_op jit(solution)/shard_map/ppermute | solution.py:325
  297.6 1.5 collective-permute-start.28
  299.2 0.7 fusion.38
  299.9 2.0 pad_add_fusion.5.refs_0_
  301.8 1.8 pad_add_fusion.4.refs_0_
  303.7 0.6 collective-permute-start.20
  304.2 1.5 collective-permute-start.23
  305.8 2.0 pad_add_fusion.2.refs_0_
  307.7 2.3 collective-permute-done.26.refs_3_
  310.0 16.8 %collective-permute-done.28.refs_5_ = f32[256,768]{1,0:T(8,128)} collective-permute-done((f32[256,768]{1,0:T(8,128)S(1)}, f32[256,768]{1,0:T(8,128)}, u32[]{:S(2)}, u32[]{:S(2)}) %collective-permute-start.28) | collective-permute-done | bytes 786464 | tf_op jit(solution)/shard_map/ppermute | solution.py:325
  326.9 1.9 pad_add_fusion.refs_0_
  329.4 5.9 %collective-permute-done.20.refs_3_ = f32[128,768]{1,0:T(8,128)} collective-permute-done((f32[128,768]{1,0:T(8,128)S(1)}, f32[128,768]{1,0:T(8,128)}, u32[]{:S(2)}, u32[]{:S(2)}) %collective-permute-start.20) | collective-permute-done | bytes 393248 | tf_op jit(solution)/shard_map/ppermute | solution.py:325
  335.2 4.2 collective-permute-done.23.refs_4_
  339.4 3.1 pad_add_fusion.3.refs_0_
  342.6 0.7 mul.81
  343.3 3.0 pad_add_fusion.1.refs_0_
  346.3 0.7 divide_multiply_fusion.refs_1_
  347.0 11.3 %chi.6 = (f32[5,256,4096]{2,1,0:T(8,128)}, f32[5,256,4096]{2,1,0:T(8,128)}) custom-call(s32[2]{0:T(128)} %pad_add_fusion.5.refs_0_, f32[5,384]{1,0:T(8,128)} %divide_multiply_fusion.refs_1_, f32[256,768]{1,0:T(8,128)} %copy-done, f32[256,768]{1,0:T(8,128)} %copy-done, f32[256,768]{1,0:T(8,128)} %copy-done.6), custom_call_target="tpu_custom_call" | custom-call | tf_op jit(solution)/shard_map/chi/pallas_call | solution.py:268
  358.2 11.1 %chi.7 = (f32[5,256,4096]{2,1,0:T(8,128)}, f32[5,256,4096]{2,1,0:T(8,128)}) custom-call(s32[2]{0:T(128)} %pad_add_fusion.4.refs_0_, f32[5,384]{1,0:T(8,128)} %divide_multiply_fusion.refs_1_, f32[256,768]{1,0:T(8,128)} %copy-done, f32[256,768]{1,0:T(8,128)} %copy-done.7, f32[256,768]{1,0:T(8,128)} %copy-done.9, ...), custom_call_target="tpu_custom_call", output_to_operand_aliasing={{0}: (5, {}), {1}: (6, {})} | custom-call | tf_op jit(solution)/shard_map/chi/pallas_call | solution.py:268
  369.4 17.7 %chi.8 = (f32[5,256,4096]{2,1,0:T(8,128)}, f32[5,256,4096]{2,1,0:T(8,128)}) custom-call(s32[4]{0:T(128)} %pad_add_fusion.3.refs_0_, f32[5,384]{1,0:T(8,128)} %divide_multiply_fusion.refs_1_, f32[256,768]{1,0:T(8,128)} %copy-done, f32[256,768]{1,0:T(8,128)} %copy-done.5, f32[256,768]{1,0:T(8,128)} %copy-done.8, ...), custom_call_target="tpu_custom_call", output_to_operand_aliasing={{0}: (7, {}), {1}: (8, {})} | custom-call | tf_op jit(solution)/shard_map/chi/pallas_call | solution.py:268
  387.1 11.1 %chi.9 = (f32[5,256,4096]{2,1,0:T(8,128)}, f32[5,256,4096]{2,1,0:T(8,128)}) custom-call(s32[2]{0:T(128)} %pad_add_fusion.2.refs_0_, f32[5,384]{1,0:T(8,128)} %divide_multiply_fusion.refs_1_, f32[256,768]{1,0:T(8,128)} %copy-done, f32[128,768]{1,0:T(8,128)} %copy-done.11, ...), custom_call_target="tpu_custom_call", output_to_operand_aliasing={{0}: (7, {}), {1}: (8, {})} | custom-call | tf_op jit(solution)/shard_map/chi/pallas_call | solution.py:268
  398.2 18.0 %chi.10 = (f32[5,256,4096]{2,1,0:T(8,128)}, f32[5,256,4096]{2,1,0:T(8,128)}) custom-call(s32[4]{0:T(128)} %pad_add_fusion.1.refs_0_, f32[5,384]{1,0:T(8,128)} %divide_multiply_fusion.refs_1_, f32[256,768]{1,0:T(8,128)} %copy-done, f32[256,768]{1,0:T(8,128)} %collective-permute-done.26.refs_3_, ...), custom_call_target="tpu_custom_call", output_to_operand_aliasing={{0}: (7, {}), {1}: (8, {})} | custom-call | tf_op jit(solution)/shard_map/chi/pallas_call | solution.py:268
  416.2 11.1 %chi.11 = (f32[5,256,4096]{2,1,0:T(8,128)}, f32[5,256,4096]{2,1,0:T(8,128)}) custom-call(s32[2]{0:T(128)} %pad_add_fusion.refs_0_, f32[5,384]{1,0:T(8,128)} %divide_multiply_fusion.refs_1_, f32[256,768]{1,0:T(8,128)} %copy-done, f32[128,768]{1,0:T(8,128)} %collective-permute-done.20.refs_3_, ...), custom_call_target="tpu_custom_call", output_to_operand_aliasing={{0}: (7, {}), {1}: (8, {})} | custom-call | tf_op jit(solution)/shard_map/chi/pallas_call | solution.py:268
  (107 shorter events, 5.5 us)
Async XLA Ops:
  47.5 78.5 %collective-permute-start = (f32[512,8,128]{2,1,0:T(8,128)}, f32[512,8,128]{2,1,0:T(8,128)}, u32[]{:S(2)}, u32[]{:S(2)}) collective-permute-start(f32[512,8,128]{2,1,0:T(8,128)} %get-tuple-element.31), channel_id=1, source_target_pairs={{0,1},{1,0},{2,3},{3,2},{4,5},{5,4},{6,7},{7,6},{8,9},{9,8},{10,11... | collective-permute-start | bytes 6291464 | tf_op jit(solution)/shard_map/ppermute | solution.py:325
  86.8 43.7 %collective-permute-start.6 = (f32[512,8,128]{2,1,0:T(8,128)}, f32[512,8,128]{2,1,0:T(8,128)S(1)}, u32[]{:S(2)}, u32[]{:S(2)}) collective-permute-start(f32[512,8,128]{2,1,0:T(8,128)} %get-tuple-element.37), channel_id=1, source_target_pairs={{0,1},{1,0},{2,3},{3,2},{4,5},{5,4},{6,7},{7,6},{8,9},{9,8},{10,11... | collective-permute-start | bytes 6291464 | tf_op jit(solution)/shard_map/ppermute | solution.py:325
  125.5 4.9 %copy-start.2 = (f32[512,8,128]{2,1,0:T(8,128)S(1)}, f32[512,8,128]{2,1,0:T(8,128)}, u32[]{:S(2)}) copy-start(f32[512,8,128]{2,1,0:T(8,128)} %get-tuple-element.36) | copy-start | bytes 6291460
  125.5 5.5 %collective-permute-start.12 = (f32[512,8,128]{2,1,0:T(8,128)}, f32[512,8,128]{2,1,0:T(8,128)S(1)}, u32[]{:S(2)}, u32[]{:S(2)}) collective-permute-start(f32[512,8,128]{2,1,0:T(8,128)} %get-tuple-element.43), channel_id=1, source_target_pairs={{0,1},{1,0},{2,3},{3,2},{4,5},{5,4},{6,7},{7,6},{8,9},{9,8},{10,11... | collective-permute-start | bytes 6291464 | tf_op jit(solution)/shard_map/ppermute | solution.py:325
  127.8 3.2 copy-start.1
  127.8 26.6 %collective-permute-start.1 = (f32[256,8,128]{2,1,0:T(8,128)S(1)}, f32[256,8,128]{2,1,0:T(8,128)S(1)}, u32[]{:S(2)}, u32[]{:S(2)}) collective-permute-start(f32[256,8,128]{2,1,0:T(8,128)S(1)} %slice_add_fusion.4), channel_id=1, source_target_pairs={{0,2},{1,3},{2,0},{3,1},{4,6},{5,7},{6,4},{7,5},{8,10},{9,11},{10,... | collective-permute-start | bytes 3145736 | tf_op jit(solution)/shard_map/ppermute | solution.py:325
  130.6 23.9 %copy-start.3 = (f32[512,8,128]{2,1,0:T(8,128)S(1)}, f32[512,8,128]{2,1,0:T(8,128)}, u32[]{:S(2)}) copy-start(f32[512,8,128]{2,1,0:T(8,128)} %get-tuple-element.30) | copy-start | bytes 6291460
  130.6 46.3 %collective-permute-start.7 = (f32[256,8,128]{2,1,0:T(8,128)S(1)}, f32[256,8,128]{2,1,0:T(8,128)S(1)}, u32[]{:S(2)}, u32[]{:S(2)}) collective-permute-start(f32[256,8,128]{2,1,0:T(8,128)S(1)} %slice_add_fusion.2), channel_id=1, source_target_pairs={{0,2},{1,3},{2,0},{3,1},{4,6},{5,7},{6,4},{7,5},{8,10},{9,11},{10,... | collective-permute-start | bytes 3145736 | tf_op jit(solution)/shard_map/ppermute | solution.py:325
  131.1 68.1 %collective-permute-start.13 = (f32[256,8,128]{2,1,0:T(8,128)S(1)}, f32[256,8,128]{2,1,0:T(8,128)S(1)}, u32[]{:S(2)}, u32[]{:S(2)}) collective-permute-start(f32[256,8,128]{2,1,0:T(8,128)S(1)} %slice_add_fusion), channel_id=1, source_target_pairs={{0,2},{1,3},{2,0},{3,1},{4,6},{5,7},{6,4},{7,5},{8,10},{9,11},{10,... | collective-permute-start | bytes 3145736 | tf_op jit(solution)/shard_map/ppermute | solution.py:325
  155.8 46.4 %collective-permute-start.2 = (f32[32,8,128]{2,1,0:T(8,128)S(1)}, f32[32,8,128]{2,1,0:T(8,128)S(1)}, u32[]{:S(2)}, u32[]{:S(2)}) collective-permute-start(f32[32,8,128]{2,1,0:T(8,128)S(1)} %get-tuple-element.66), channel_id=1, source_target_pairs={{0,8},{1,9},{2,10},{3,11},{4,0},{5,1},{6,2},{7,3},{8,12},{9,13},{1... | collective-permute-start | bytes 393224 | tf_op jit(solution)/shard_map/ppermute | solution.py:325
  159.0 43.2 %collective-permute-start.3 = (f32[32,8,128]{2,1,0:T(8,128)S(1)}, f32[32,8,128]{2,1,0:T(8,128)S(1)}, u32[]{:S(2)}, u32[]{:S(2)}) collective-permute-start(f32[32,8,128]{2,1,0:T(8,128)S(1)} %get-tuple-element.65), channel_id=1, source_target_pairs={{0,4},{1,5},{2,6},{3,7},{4,12},{5,13},{6,14},{7,15},{8,0},{9,1},{1... | collective-permute-start | bytes 393224 | tf_op jit(solution)/shard_map/ppermute | solution.py:325
  177.1 27.1 %collective-permute-start.8 = (f32[32,8,128]{2,1,0:T(8,128)S(1)}, f32[32,8,128]{2,1,0:T(8,128)S(1)}, u32[]{:S(2)}, u32[]{:S(2)}) collective-permute-start(f32[32,8,128]{2,1,0:T(8,128)S(1)} %get-tuple-element.72), channel_id=1, source_target_pairs={{0,8},{1,9},{2,10},{3,11},{4,0},{5,1},{6,2},{7,3},{8,12},{9,13},{1... | collective-permute-start | bytes 393224 | tf_op jit(solution)/shard_map/ppermute | solution.py:325
  180.2 25.1 %collective-permute-start.9 = (f32[32,8,128]{2,1,0:T(8,128)S(1)}, f32[32,8,128]{2,1,0:T(8,128)S(1)}, u32[]{:S(2)}, u32[]{:S(2)}) collective-permute-start(f32[32,8,128]{2,1,0:T(8,128)S(1)} %get-tuple-element.71), channel_id=1, source_target_pairs={{0,4},{1,5},{2,6},{3,7},{4,12},{5,13},{6,14},{7,15},{8,0},{9,1},{1... | collective-permute-start | bytes 393224 | tf_op jit(solution)/shard_map/ppermute | solution.py:325
  199.3 7.2 %collective-permute-start.14 = (f32[32,8,128]{2,1,0:T(8,128)S(1)}, f32[32,8,128]{2,1,0:T(8,128)S(1)}, u32[]{:S(2)}, u32[]{:S(2)}) collective-permute-start(f32[32,8,128]{2,1,0:T(8,128)S(1)} %get-tuple-element.78), channel_id=1, source_target_pairs={{0,8},{1,9},{2,10},{3,11},{4,0},{5,1},{6,2},{7,3},{8,12},{9,13},{1... | collective-permute-start | bytes 393224 | tf_op jit(solution)/shard_map/ppermute | solution.py:325
  202.2 8.0 %collective-permute-start.15 = (f32[32,8,128]{2,1,0:T(8,128)S(1)}, f32[32,8,128]{2,1,0:T(8,128)S(1)}, u32[]{:S(2)}, u32[]{:S(2)}) collective-permute-start(f32[32,8,128]{2,1,0:T(8,128)S(1)} %get-tuple-element.77), channel_id=1, source_target_pairs={{0,4},{1,5},{2,6},{3,7},{4,12},{5,13},{6,14},{7,15},{8,0},{9,1},{1... | collective-permute-start | bytes 393224 | tf_op jit(solution)/shard_map/ppermute | solution.py:325
  202.3 18.5 %collective-permute-start.5 = (f32[64,8,128]{2,1,0:T(8,128)S(1)}, f32[64,8,128]{2,1,0:T(8,128)S(1)}, u32[]{:S(2)}, u32[]{:S(2)}) collective-permute-start(f32[64,8,128]{2,1,0:T(8,128)S(1)} %pad_maximum_fusion.1), channel_id=1, source_target_pairs={{0,4},{1,5},{2,6},{3,7},{4,12},{5,13},{6,14},{7,15},{8,0},{9,1},{1... | collective-permute-start | bytes 786440 | tf_op jit(solution)/shard_map/ppermute | solution.py:325
  204.3 17.6 %collective-permute-start.4 = (f32[64,8,128]{2,1,0:T(8,128)S(1)}, f32[64,8,128]{2,1,0:T(8,128)S(1)}, u32[]{:S(2)}, u32[]{:S(2)}) collective-permute-start(f32[64,8,128]{2,1,0:T(8,128)S(1)} %pad_maximum_fusion), channel_id=1, source_target_pairs={{0,8},{1,9},{2,10},{3,11},{4,0},{5,1},{6,2},{7,3},{8,12},{9,13},{1... | collective-permute-start | bytes 786440 | tf_op jit(solution)/shard_map/ppermute | solution.py:325
  205.4 26.6 %collective-permute-start.11 = (f32[64,8,128]{2,1,0:T(8,128)S(1)}, f32[64,8,128]{2,1,0:T(8,128)S(1)}, u32[]{:S(2)}, u32[]{:S(2)}) collective-permute-start(f32[64,8,128]{2,1,0:T(8,128)S(1)} %pad_maximum_fusion.3), channel_id=1, source_target_pairs={{0,4},{1,5},{2,6},{3,7},{4,12},{5,13},{6,14},{7,15},{8,0},{9,1},{1... | collective-permute-start | bytes 786440 | tf_op jit(solution)/shard_map/ppermute | solution.py:325
  206.5 26.6 %collective-permute-start.10 = (f32[64,8,128]{2,1,0:T(8,128)S(1)}, f32[64,8,128]{2,1,0:T(8,128)S(1)}, u32[]{:S(2)}, u32[]{:S(2)}) collective-permute-start(f32[64,8,128]{2,1,0:T(8,128)S(1)} %pad_maximum_fusion.2), channel_id=1, source_target_pairs={{0,8},{1,9},{2,10},{3,11},{4,0},{5,1},{6,2},{7,3},{8,12},{9,13},{1... | collective-permute-start | bytes 786440 | tf_op jit(solution)/shard_map/ppermute | solution.py:325
  210.3 28.7 %collective-permute-start.17 = (f32[64,8,128]{2,1,0:T(8,128)S(1)}, f32[64,8,128]{2,1,0:T(8,128)S(1)}, u32[]{:S(2)}, u32[]{:S(2)}) collective-permute-start(f32[64,8,128]{2,1,0:T(8,128)S(1)} %pad_maximum_fusion.5), channel_id=1, source_target_pairs={{0,4},{1,5},{2,6},{3,7},{4,12},{5,13},{6,14},{7,15},{8,0},{9,1},{1... | collective-permute-start | bytes 786440 | tf_op jit(solution)/shard_map/ppermute | solution.py:325
  220.7 21.2 %collective-permute-start.16 = (f32[64,8,128]{2,1,0:T(8,128)S(1)}, f32[64,8,128]{2,1,0:T(8,128)S(1)}, u32[]{:S(2)}, u32[]{:S(2)}) collective-permute-start(f32[64,8,128]{2,1,0:T(8,128)S(1)} %pad_maximum_fusion.4), channel_id=1, source_target_pairs={{0,8},{1,9},{2,10},{3,11},{4,0},{5,1},{6,2},{7,3},{8,12},{9,13},{1... | collective-permute-start | bytes 786440 | tf_op jit(solution)/shard_map/ppermute | solution.py:325
  243.0 56.2 %copy-start.15 = (s32[128]{0:T(128)S(1)}, s32[128]{0:T(128)}, u32[]{:S(2)}) copy-start(s32[128]{0:T(128)} %param.21) | copy-start | bytes 1540
  243.0 85.8 %copy-start.13 = (f32[3]{0:T(128)S(1)}, f32[3]{0:T(128)}, u32[]{:S(2)}) copy-start(f32[3]{0:T(128)} %param.20) | copy-start | bytes 40
  243.0 85.8 %copy-start.14 = (f32[128]{0:T(128)S(1)}, f32[128]{0:T(128)}, u32[]{:S(2)}) copy-start(f32[128]{0:T(128)} %param.19) | copy-start | bytes 1540
  243.4 103.5 %copy-start = (f32[256,768]{1,0:T(8,128)}, f32[256,768]{1,0:T(8,128)S(1)}, u32[]{:S(2)}) copy-start(f32[256,768]{1,0:T(8,128)S(1)} %reshape.103.refs_2_.refs_3_) | copy-start | bytes 2359300
  243.4 20.8 %collective-permute-start.18 = (f32[256,768]{1,0:T(8,128)S(1)}, f32[256,768]{1,0:T(8,128)S(1)}, u32[]{:S(2)}, u32[]{:S(2)}) collective-permute-start(f32[256,768]{1,0:T(8,128)S(1)} %reshape.103.refs_2_.refs_3_), channel_id=1, source_target_pairs={{0,8},{1,9},{2,10},{3,11},{4,0},{5,1},{6,2},{7,3},{8,12},{9,13},{1... | collective-permute-start | bytes 2359304 | tf_op jit(solution)/shard_map/ppermute | solution.py:325
  246.3 36.6 %collective-permute-start.21 = (f32[256,768]{1,0:T(8,128)S(1)}, f32[256,768]{1,0:T(8,128)S(1)}, u32[]{:S(2)}, u32[]{:S(2)}) collective-permute-start(f32[256,768]{1,0:T(8,128)S(1)} %reshape.103.refs_2_.refs_3_), channel_id=1, source_target_pairs={{0,4},{1,5},{2,6},{3,7},{4,12},{5,13},{6,14},{7,15},{8,0},{9,1},{1... | collective-permute-start | bytes 2359304 | tf_op jit(solution)/shard_map/ppermute | solution.py:325
  246.3 37.4 %collective-permute-start.34 = (f32[256,768]{1,0:T(8,128)S(1)}, f32[256,768]{1,0:T(8,128)S(1)}, u32[]{:S(2)}, u32[]{:S(2)}) collective-permute-start(f32[256,768]{1,0:T(8,128)S(1)} %reshape.103.refs_2_.refs_3_), channel_id=1, source_target_pairs={{0,2},{1,3},{2,0},{3,1},{4,6},{5,7},{6,4},{7,5},{8,10},{9,11},{10,... | collective-permute-start | bytes 2359304 | tf_op jit(solution)/shard_map/ppermute | solution.py:325
  247.8 36.4 %collective-permute-start.36 = (f32[256,768]{1,0:T(8,128)S(1)}, f32[256,768]{1,0:T(8,128)S(1)}, u32[]{:S(2)}, u32[]{:S(2)}) collective-permute-start(f32[256,768]{1,0:T(8,128)S(1)} %reshape.103.refs_2_.refs_3_), channel_id=1, source_target_pairs={{0,1},{1,0},{2,3},{3,2},{4,5},{5,4},{6,7},{7,6},{8,9},{9,8},{10,11... | collective-permute-start | bytes 2359304 | tf_op jit(solution)/shard_map/ppermute | solution.py:325
  264.2 105.1 %copy-start.4 = (f32[256,768]{1,0:T(8,128)}, f32[256,768]{1,0:T(8,128)S(1)}, u32[]{:S(2)}) copy-start(f32[256,768]{1,0:T(8,128)S(1)} %collective-permute-done.18.refs_5_) | copy-start | bytes 2359300
  264.3 25.2 %collective-permute-start.19 = (f32[128,768]{1,0:T(8,128)S(1)}, f32[128,768]{1,0:T(8,128)S(1)}, u32[]{:S(2)}, u32[]{:S(2)}) collective-permute-start(f32[128,768]{1,0:T(8,128)S(1)} %slice.250), channel_id=1, source_target_pairs={{0,8},{1,9},{2,10},{3,11},{4,0},{5,1},{6,2},{7,3},{8,12},{9,13},{1... | collective-permute-start | bytes 1179656 | tf_op jit(solution)/shard_map/ppermute | solution.py:325
  282.9 86.4 %copy-start.5 = (f32[256,768]{1,0:T(8,128)}, f32[256,768]{1,0:T(8,128)S(1)}, u32[]{:S(2)}) copy-start(f32[256,768]{1,0:T(8,128)S(1)} %collective-permute-done.21.refs_3_) | copy-start | bytes 2359300
  283.0 14.7 %collective-permute-start.22 = (f32[128,768]{1,0:T(8,128)S(1)}, f32[128,768]{1,0:T(8,128)}, u32[]{:S(2)}, u32[]{:S(2)}) collective-permute-start(f32[128,768]{1,0:T(8,128)S(1)} %slice.251), channel_id=1, source_target_pairs={{0,4},{1,5},{2,6},{3,7},{4,12},{5,13},{6,14},{7,15},{8,0},{9,1},{1... | collective-permute-start | bytes 1179656 | tf_op jit(solution)/shard_map/ppermute | solution.py:325
  283.7 43.2 %copy-start.7 = (f32[256,768]{1,0:T(8,128)}, f32[256,768]{1,0:T(8,128)S(1)}, u32[]{:S(2)}) copy-start(f32[256,768]{1,0:T(8,128)S(1)} %collective-permute-done.34.refs_3_) | copy-start | bytes 2359300
  283.7 20.0 %collective-permute-start.35 = (f32[256,768]{1,0:T(8,128)S(1)}, f32[256,768]{1,0:T(8,128)S(1)}, u32[]{:S(2)}, u32[]{:S(2)}) collective-permute-start(f32[256,768]{1,0:T(8,128)S(1)} %collective-permute-done.34.refs_3_), channel_id=1, source_target_pairs={{0,1},{1,0},{2,3},{3,2},{4,5},{5,4},{6,7},{7,6},{8,9},{9,8},{10,11... | collective-permute-start | bytes 2359304 | tf_op jit(solution)/shard_map/ppermute | solution.py:325
  283.7 20.0 %collective-permute-start.32 = (f32[256,768]{1,0:T(8,128)S(1)}, f32[256,768]{1,0:T(8,128)S(1)}, u32[]{:S(2)}, u32[]{:S(2)}) collective-permute-start(f32[256,768]{1,0:T(8,128)S(1)} %collective-permute-done.21.refs_3_), channel_id=1, source_target_pairs={{0,1},{1,0},{2,3},{3,2},{4,5},{5,4},{6,7},{7,6},{8,9},{9,8},{10,11... | collective-permute-start | bytes 2359304 | tf_op jit(solution)/shard_map/ppermute | solution.py:325
  284.2 62.8 %copy-start.6 = (f32[256,768]{1,0:T(8,128)}, f32[256,768]{1,0:T(8,128)S(1)}, u32[]{:S(2)}) copy-start(f32[256,768]{1,0:T(8,128)S(1)} %collective-permute-done.36.refs_4_) | copy-start | bytes 2359300
  284.2 20.1 %collective-permute-start.33 = (f32[256,768]{1,0:T(8,128)S(1)}, f32[256,768]{1,0:T(8,128)S(1)}, u32[]{:S(2)}, u32[]{:S(2)}) collective-permute-start(f32[256,768]{1,0:T(8,128)S(1)} %collective-permute-done.18.refs_5_), channel_id=1, source_target_pairs={{0,1},{1,0},{2,3},{3,2},{4,5},{5,4},{6,7},{7,6},{8,9},{9,8},{10,11... | collective-permute-start | bytes 2359304 | tf_op jit(solution)/shard_map/ppermute | solution.py:325
  289.5 79.8 %copy-start.11 = (f32[128,768]{1,0:T(8,128)}, f32[128,768]{1,0:T(8,128)S(1)}, u32[]{:S(2)}) copy-start(f32[128,768]{1,0:T(8,128)S(1)} %collective-permute-done.19.refs_3_) | copy-start | bytes 1179652
  289.5 20.5 %collective-permute-start.26 = (f32[256,768]{1,0:T(8,128)S(1)}, f32[256,768]{1,0:T(8,128)}, u32[]{:S(2)}, u32[]{:S(2)}) collective-permute-start(f32[256,768]{1,0:T(8,128)S(1)} %collective-permute-done.21.refs_3_), channel_id=1, source_target_pairs={{0,2},{1,3},{2,0},{3,1},{4,6},{5,7},{6,4},{7,5},{8,10},{9,11},{10,... | collective-permute-start | bytes 2359304 | tf_op jit(solution)/shard_map/ppermute | solution.py:325
  297.6 29.2 %collective-permute-start.28 = (f32[256,768]{1,0:T(8,128)S(1)}, f32[256,768]{1,0:T(8,128)}, u32[]{:S(2)}, u32[]{:S(2)}) collective-permute-start(f32[256,768]{1,0:T(8,128)S(1)} %collective-permute-done.18.refs_5_), channel_id=1, source_target_pairs={{0,2},{1,3},{2,0},{3,1},{4,6},{5,7},{6,4},{7,5},{8,10},{9,11},{10,... | collective-permute-start | bytes 2359304 | tf_op jit(solution)/shard_map/ppermute | solution.py:325
  303.6 23.3 %copy-start.9 = (f32[256,768]{1,0:T(8,128)}, f32[256,768]{1,0:T(8,128)S(1)}, u32[]{:S(2)}) copy-start(f32[256,768]{1,0:T(8,128)S(1)} %collective-permute-done.35.refs_4_) | copy-start | bytes 2359300
  303.6 25.2 %collective-permute-start.30 = (f32[128,768]{1,0:T(8,128)S(1)}, f32[128,768]{1,0:T(8,128)S(1)}, u32[]{:S(2)}, u32[]{:S(2)}) collective-permute-start(f32[128,768]{1,0:T(8,128)S(1)} %collective-permute-done.19.refs_3_), channel_id=1, source_target_pairs={{0,1},{1,0},{2,3},{3,2},{4,5},{5,4},{6,7},{7,6},{8,9},{9,8},{10,11... | collective-permute-start | bytes 1179656 | tf_op jit(solution)/shard_map/ppermute | solution.py:325
  303.6 23.2 %copy-start.8 = (f32[256,768]{1,0:T(8,128)}, f32[256,768]{1,0:T(8,128)S(1)}, u32[]{:S(2)}) copy-start(f32[256,768]{1,0:T(8,128)S(1)} %collective-permute-done.32.refs_4_) | copy-start | bytes 2359300
  303.7 31.6 %collective-permute-start.20 = (f32[128,768]{1,0:T(8,128)S(1)}, f32[128,768]{1,0:T(8,128)}, u32[]{:S(2)}, u32[]{:S(2)}) collective-permute-start(f32[128,768]{1,0:T(8,128)S(1)} %collective-permute-done.19.refs_3_), channel_id=1, source_target_pairs={{0,2},{1,3},{2,0},{3,1},{4,6},{5,7},{6,4},{7,5},{8,10},{9,11},{10,... | collective-permute-start | bytes 1179656 | tf_op jit(solution)/shard_map/ppermute | solution.py:325
  304.2 22.7 %copy-start.10 = (f32[256,768]{1,0:T(8,128)}, f32[256,768]{1,0:T(8,128)S(1)}, u32[]{:S(2)}) copy-start(f32[256,768]{1,0:T(8,128)S(1)} %collective-permute-done.33.refs_6_) | copy-start | bytes 2359300
  304.2 35.2 %collective-permute-start.23 = (f32[128,768]{1,0:T(8,128)}, f32[128,768]{1,0:T(8,128)}, u32[]{:S(2)}, u32[]{:S(2)}) collective-permute-start(f32[128,768]{1,0:T(8,128)} %collective-permute-done.22.refs_4_), channel_id=1, source_target_pairs={{0,2},{1,3},{2,0},{3,1},{4,6},{5,7},{6,4},{7,5},{8,10},{9,11},{10,... | collective-permute-start | bytes 1179656 | tf_op jit(solution)/shard_map/ppermute | solution.py:325
  310.0 88.2 %collective-permute-start.27 = (f32[256,768]{1,0:T(8,128)}, f32[256,768]{1,0:T(8,128)}, u32[]{:S(2)}, u32[]{:S(2)}) collective-permute-start(f32[256,768]{1,0:T(8,128)} %collective-permute-done.26.refs_3_), channel_id=1, source_target_pairs={{0,1},{1,0},{2,3},{3,2},{4,5},{5,4},{6,7},{7,6},{8,9},{9,8},{10,11... | collective-permute-start | bytes 2359304 | tf_op jit(solution)/shard_map/ppermute | solution.py:325
  326.9 71.4 %collective-permute-start.29 = (f32[256,768]{1,0:T(8,128)}, f32[256,768]{1,0:T(8,128)}, u32[]{:S(2)}, u32[]{:S(2)}) collective-permute-start(f32[256,768]{1,0:T(8,128)} %collective-permute-done.28.refs_5_), channel_id=1, source_target_pairs={{0,1},{1,0},{2,3},{3,2},{4,5},{5,4},{6,7},{7,6},{8,9},{9,8},{10,11... | collective-permute-start | bytes 2359304 | tf_op jit(solution)/shard_map/ppermute | solution.py:325
  328.8 6.4 %copy-start.12 = (f32[128,768]{1,0:T(8,128)}, f32[128,768]{1,0:T(8,128)S(1)}, u32[]{:S(2)}) copy-start(f32[128,768]{1,0:T(8,128)S(1)} %collective-permute-done.30.refs_5_) | copy-start | bytes 1179652
  328.9 58.3 %collective-permute-start.31 = (f32[128,768]{1,0:T(8,128)}, f32[128,768]{1,0:T(8,128)}, u32[]{:S(2)}, u32[]{:S(2)}) collective-permute-start(f32[128,768]{1,0:T(8,128)} %collective-permute-done.22.refs_4_), channel_id=1, source_target_pairs={{0,1},{1,0},{2,3},{3,2},{4,5},{5,4},{6,7},{7,6},{8,9},{9,8},{10,11... | collective-permute-start | bytes 1179656 | tf_op jit(solution)/shard_map/ppermute | solution.py:325
  335.2 81.0 %collective-permute-start.24 = (f32[128,768]{1,0:T(8,128)}, f32[128,768]{1,0:T(8,128)}, u32[]{:S(2)}, u32[]{:S(2)}) collective-permute-start(f32[128,768]{1,0:T(8,128)} %collective-permute-done.20.refs_3_), channel_id=1, source_target_pairs={{0,1},{1,0},{2,3},{3,2},{4,5},{5,4},{6,7},{7,6},{8,9},{9,8},{10,11... | collective-permute-start | bytes 1179656 | tf_op jit(solution)/shard_map/ppermute | solution.py:325
  339.4 76.8 %collective-permute-start.25 = (f32[128,768]{1,0:T(8,128)}, f32[128,768]{1,0:T(8,128)}, u32[]{:S(2)}, u32[]{:S(2)}) collective-permute-start(f32[128,768]{1,0:T(8,128)} %collective-permute-done.23.refs_4_), channel_id=1, source_target_pairs={{0,1},{1,0},{2,3},{3,2},{4,5},{5,4},{6,7},{7,6},{8,9},{9,8},{10,11... | collective-permute-start | bytes 1179656 | tf_op jit(solution)/shard_map/ppermute | solution.py:325

commit v3 on v2

--- a/solution.py
+++ b/solution.py
@@ -53,30 +53,67 @@
     return pltpu.roll(x, shift % SUB, axis=x.ndim - 2)
 
 
+def in_steps(count, at_once, step):
+    def several(i, carry):
+        for u in range(at_once):
+            step(i * at_once + u)
+        return carry
+
+    lax.fori_loop(0, count // at_once, several, 0)
+    for i in range(count // at_once * at_once, count):
+        step(i)
+
+
 def transform_kernel(
-    pick_ref, val_ref, cond_ref, dz_ref, dy_ref, dyr_ref, cs_ref, keep_ref, send_ref, z_scr, tab_scr
+    col_ref,
+    phase_ref,
+    val_hbm,
+    cond_ref,
+    dz_ref,
+    dy_ref,
+    dyr_ref,
+    cs_hbm,
+    keep_hbm,
+    send_hbm,
+    val_scr,
+    cs_scr,
+    z_scr,
+    tab_scr,
+    out_scr,
+    in_sems,
+    out_sems,
 ):
-    slots, size_y, size_z, lanes = val_ref.shape
+    slots, size_y, size_z, lanes = val_hbm.shape
     half = size_z // 2
     groups_y = size_y // SUB
-
-    def z_stage(step, carry):
-        x = step // groups_y
-        yg = step % groups_y
+    pitch = size_z + SUB
+
+    def plane(x):
+        return pltpu.make_async_copy(val_hbm.at[x], val_scr.at[x], in_sems.at[x])
+
+    phases = pltpu.make_async_copy(cs_hbm, cs_scr, in_sems.at[slots])
+    for x in range(slots):
+        plane(x).start()
+    phases.start()
+
+    def z_stage(x, yg):
         cond = cond_ref[x, yg]
         parts = []
         for j in range(SUB):
-            block = val_ref[x, yg * SUB + j]
+            block = val_scr[x, yg * SUB + j]
             parts.append(block * jnp.broadcast_to(cond[:, j : j + 1], (size_z, lanes)))
         rhs = split3(jnp.concatenate(parts, axis=1))
         got = jnp.dot(dz_ref[...], rhs, preferred_element_type=f32)
         for j in range(SUB):
-            z_scr[x, pl.ds(yg * SUB + j, size_z, stride=size_y), :] = got[
-                :, j * lanes : (j + 1) * lanes
-            ]
+            at = pl.multiple_of((yg * SUB + j) * pitch, SUB)
+            z_scr[x, pl.ds(at, size_z), :] = got[:, j * lanes : (j + 1) * lanes]
+
+    def z_plane(x, carry):
+        plane(x).wait()
+        in_steps(groups_y, 4, functools.partial(z_stage, x))
         return carry
 
-    lax.fori_loop(0, slots * groups_y, z_stage, 0)
+    lax.fori_loop(0, slots, z_plane, 0)
 
     shape = (size_y // 4, SUB, lanes)
     sub = lax.broadcasted_iota(jnp.int32, shape, 1)
@@ -95,65 +132,82 @@
         tab_scr[kz, :, 3] = jnp.where(low1, roll_sub(p2, -1), p3)
 
     def rows(k):
-        start = pl.multiple_of(k * size_y, size_y)
-        return jnp.concatenate([z_scr[x, pl.ds(start, size_y), :] for x in range(slots)], axis=1)
+        return jnp.concatenate(
+            [z_scr[x, pl.ds(k, size_y, stride=pitch), :] for x in range(slots)], axis=1
+        )
 
     for kz in (0, half):
         put(kz, jnp.dot(dyr_ref[...], split3(rows(kz)), preferred_element_type=f32))
 
-    def y_stage(kz, carry):
+    def y_stage(step):
+        kz = step + 1
         block = jnp.concatenate([rows(kz), rows(half + kz)], axis=0)
         put(kz, jnp.dot(dy_ref[...], split3(block), preferred_element_type=f32))
-        return carry
-
-    lax.fori_loop(1, half, y_stage, 0)
+
+    in_steps(half - 1, 3, y_stage)
 
     sub1 = lax.broadcasted_iota(jnp.int32, (SUB, lanes), 0)
     m2 = (sub1 % 4) < 2
     m1 = (sub1 % 2) == 0
     kzs, kyq, _, _, _ = tab_scr.shape
-    tab = tab_scr.reshape(kzs * kyq * 4, SUB, lanes)
-    quads = keep_ref.shape[0]
-
-    def quad(out_ref, first, q):
+    tab = tab_scr.reshape(kzs * kyq * 4 * SUB, lanes)
+    quads = keep_hbm.shape[0]
+    phases.wait()
+
+    def quad(q):
         t = []
         for i in range(4):
-            word = pick_ref[first + q * 4 + i]
-            col = lax.shift_right_logical(word, 8)
-            ph = word & 255
-            d = tab[col]
-            t.append(d * cs_ref[0, ph] + roll_sub(d, 4) * cs_ref[1, ph])
+            d = tab[pl.ds(pl.multiple_of(col_ref[q * 4 + i], SUB), SUB), :]
+            at = pl.ds(pl.multiple_of(phase_ref[q * 4 + i], SUB), SUB)
+            t.append(d * cs_scr[0, at, :] + roll_sub(d, 4) * cs_scr[1, at, :])
         v0 = jnp.where(m2, t[0], roll_sub(t[2], 2)) + jnp.where(m2, roll_sub(t[0], -2), t[2])
         v1 = jnp.where(m2, t[1], roll_sub(t[3], 2)) + jnp.where(m2, roll_sub(t[1], -2), t[3])
-        out_ref[q] = jnp.where(m1, v0, roll_sub(v1, 1)) + jnp.where(m1, roll_sub(v0, -1), v1)
-
-    for out_ref, first in ((send_ref, quads * 4), (keep_ref, 0)):
-
-        def gather(step, carry, out_ref=out_ref, first=first):
-            for u in range(4):
-                quad(out_ref, first, step * 4 + u)
-            return carry
-
-        lax.fori_loop(0, quads // 4, gather, 0)
-
-
-def transform(pick, val, cond, cs, num_g):
+        out_scr[q] = jnp.where(m1, v0, roll_sub(v1, 1)) + jnp.where(m1, roll_sub(v0, -1), v1)
+
+    at_once = math.gcd(quads // 2, SUB)
+    copies = []
+    for n, (out_hbm, first, at, size) in enumerate(
+        (
+            (send_hbm, quads, 0, quads),
+            (keep_hbm, 0, 0, quads // 2),
+            (keep_hbm, 0, quads // 2, quads // 2),
+        )
+    ):
+        in_steps(size, at_once, lambda q, start=first + at: quad(start + q))
+        copies.append(
+            pltpu.make_async_copy(
+                out_scr.at[pl.ds(first + at, size)], out_hbm.at[pl.ds(at, size)], out_sems.at[n]
+            )
+        )
+        copies[-1].start()
+    for copy in copies:
+        copy.wait()
+
+
+def transform(col, phase, val, cond, cs, num_g):
     slots, size_y, size_z, lanes = val.shape
     dz = jnp.asarray(split_np(z_table(size_z)))
     full, real_only = y_tables(size_y)
     dy, dyr = jnp.asarray(split_np(full)), jnp.asarray(split_np(real_only))
     vmem = pl.BlockSpec(memory_space=pltpu.VMEM)
+    smem = pl.BlockSpec(memory_space=pltpu.SMEM)
+    hbm = pl.BlockSpec(memory_space=pl.ANY)
     return pl.pallas_call(
         transform_kernel,
         out_shape=(jax.ShapeDtypeStruct((num_g // 8, SUB, lanes), f32),) * 2,
-        in_specs=[pl.BlockSpec(memory_space=pltpu.SMEM)] + [vmem] * 6,
-        out_specs=(vmem, vmem),
+        in_specs=[smem, smem, hbm, vmem, vmem, vmem, vmem, hbm],
+        out_specs=(hbm, hbm),
         scratch_shapes=[
-            pltpu.VMEM((slots, size_z * size_y, lanes), f32),
+            pltpu.VMEM(val.shape, f32),
+            pltpu.VMEM(cs.shape, f32),
+            pltpu.VMEM((slots, (size_z + SUB) * size_y, lanes), f32),
             pltpu.VMEM((size_z // 2 + 1, size_y // 4, 4, SUB, lanes), f32),
+            pltpu.VMEM((num_g // 4, SUB, lanes), f32),
+            pltpu.SemaphoreType.DMA((slots + 1,)),
+            pltpu.SemaphoreType.DMA((3,)),
         ],
         name="transform",
-    )(pick, val, cond, dz, dy, dyr, cs)
+    )(col, phase, val, cond, dz, dy, dyr, cs)
 
 
 def split_lanes(block):
@@ -256,13 +310,13 @@
     chi_tile(got_scr[step], left_scr, real_ref, imag_ref)
 
 
-def chi_group(weights, own, blocks, ids, num_g, old):
+def chi_group(weights, own, blocks, ids, first, num_g, old):
     freqs, pairs = weights.shape
     rows = own.shape[0]
     counts = tuple(len(b) for b in blocks)
     pieces = [p for b in blocks for p in b]
     out = jax.ShapeDtypeStruct((freqs, rows, num_g), f32)
-    out_spec = pl.BlockSpec((freqs, rows, rows), lambda t, ids: (0, 0, ids[t]))
+    out_spec = pl.BlockSpec((freqs, rows, rows), lambda t, ids: (0, 0, ids[first + t]))
     hbm = pl.BlockSpec(memory_space=pl.ANY)
     olds = () if old is None else old
     return pl.pallas_call(
@@ -288,6 +342,7 @@
     )(ids, weights, own, *pieces, *olds)
 
 
+GROUPS = (((0, 0),), ((1, 0),), ((0, 1), (0, 3)), ((0, 2),), ((1, 1), (1, 3)), ((1, 2),))
 RING = (0, 2, 3, 1)
 
 
@@ -315,6 +370,7 @@
             ],
             dtype=np.int32,
         )
+        self.order = np.stack([self.near[:, :, b, r] for g in GROUPS for b, r in g], axis=1)
 
     @staticmethod
     def fits(count):
@@ -325,31 +381,27 @@
     return lax.ppermute(value, "blk", pairs)
 
 
-def reduce_scatter(keep, other, links):
+def reduce_scatter(keep, other, links, ahead):
     half = keep.shape[0] // 2
     got = send(other, links.core)
     far = send(keep[half:] + got[half:], links.y)
+    if ahead:
+        far, ahead = lax.optimization_barrier((far, ahead))
     near = keep[:half] + got[:half] + far
     block = half // 4
     part = block // 2
     cw = send(near[2 * block : 2 * block + part], links.cw)
     ccw = send(near[2 * block + part : 3 * block], links.ccw)
     cw, ccw = lax.optimization_barrier((cw, ccw))
-    from_cw = send(
-        jnp.concatenate([near[block : block + part] + cw, near[block + part : 2 * block]]), links.cw
-    )
-    from_ccw = send(
-        jnp.concatenate([near[3 * block : 3 * block + part], near[3 * block + part :] + ccw]),
-        links.ccw,
-    )
+    to_cw = jnp.concatenate([near[block : block + part] + cw, near[block + part : 2 * block]])
+    to_ccw = jnp.concatenate([near[3 * block : 3 * block + part], near[3 * block + part :] + ccw])
+    from_cw = send(to_cw, links.cw)
+    from_ccw = send(to_ccw, links.ccw)
     from_cw, from_ccw = lax.optimization_barrier((from_cw, from_ccw))
-    return near[:block] + from_cw + from_ccw
-
-
-GROUPS = (((0, 0),), ((1, 0),), ((0, 1), (0, 3)), ((0, 2),), ((1, 1), (1, 3)), ((1, 2),))
-
-
-def gather_and_chi(weights, own, links, near, num_g):
+    return near[:block], from_cw, from_ccw
+
+
+def gather_and_chi(weights, own, links, ids, num_g):
     part = own.shape[0] // 2
 
     def over(pieces, pairs):
@@ -362,12 +414,13 @@
     for r in range(4):
         mine[1, r] = over(mine[0, r], links.y)
     old = None
+    first = 0
     for group in GROUPS:
-        blocks, ids = [], []
+        blocks = []
         for b, r in group:
             blocks += [mine[b, r], over(mine[b, r], links.core)]
-            ids += [near[0, b, r], near[1, b, r]]
-        old = chi_group(weights, own, blocks, jnp.stack(ids), num_g, old)
+        old = chi_group(weights, own, blocks, ids, first, num_g, old)
+        first += len(blocks)
     return old
 
 
@@ -384,7 +437,7 @@
         [jnp.concatenate([cos_t, -cos_t], 1), jnp.concatenate([-sin_t, -sin_t], 1)]
     )
     table = jnp.concatenate([plain, mirror], axis=1)
-    return jnp.broadcast_to(table[..., None], table.shape + (LANES,))
+    return jnp.broadcast_to(table.reshape(2, -1, 1), (2, table[0].size, LANES))
 
 
 def polarizability(psi_val, psi_cond, e_val, e_cond, occ, freq, gmap):
@@ -410,23 +463,25 @@
     col = jnp.where(mirrored, size_z - kz, kz) * size_y + jnp.where(
         mirrored, (size_y - ky) % size_y, ky
     )
-    pick = col * 256 + kx + jnp.where(mirrored, size_x, 0)
+    pick = jnp.stack([col, kx + jnp.where(mirrored, size_x, 0)]) * SUB
     cs = phase_table(size_x, lax.axis_index("blk") * planes, planes, norm)
 
     count = lax.axis_size("blk")
     links = Links(count) if Links.fits(count) else None
     if links is not None:
         near = jnp.asarray(links.near)[lax.axis_index("blk")]
-        pick = pick.reshape(count, -1)[near.reshape(-1)].reshape(-1)
+        ids = jnp.asarray(links.order.reshape(count, -1))[lax.axis_index("blk")]
+        pick = pick.reshape(2, count, -1)[:, near.reshape(-1)].reshape(2, -1)
     owned = []
     for c in range(num_cond):
-        keep, other = transform(pick, val, cond[c], cs, num_g)
+        keep, other = transform(pick[0], pick[1], val, cond[c], cs, num_g)
         if links is not None:
-            owned.append(reduce_scatter(keep, other, links))
+            ahead = owned[-1][1:] if c == num_cond - 1 else ()
+            owned.append(reduce_scatter(keep, other, links, ahead))
         else:
             whole = jnp.concatenate([keep, other])
-            owned.append(lax.psum_scatter(whole, "blk", scatter_dimension=0, tiled=True))
-    own = jnp.stack(owned).reshape(num_cond, -1, 2, 4, num_val)
+            owned.append((lax.psum_scatter(whole, "blk", scatter_dimension=0, tiled=True),))
+    own = jnp.stack([sum(parts) for parts in owned]).reshape(num_cond, -1, 2, 4, num_val)
     own = jnp.transpose(own, (1, 3, 2, 0, 4)).reshape(-1, 2 * pairs)
 
     gaps = e_val[None, :] - e_cond[:, None]
@@ -435,7 +490,7 @@
     weights = occ_row * gaps / (gaps * gaps + (freq * freq)[:, None]) / math.sqrt(pairs)
 
     if links is not None:
-        return gather_and_chi(weights, own, links, near, num_g)
+        return gather_and_chi(weights, own, links, ids, num_g)
     return chi(weights, own, lax.all_gather(own, "blk", axis=0, tiled=True))
 
 

time: 428 us -> 347 us (0.81)
  Pallas kernels: 196 us -> 149 us
  waiting for transfers between devices: 161 us -> 144 us
  other arithmetic: 21 us -> 9.01 us
  starting transfers between devices: 38.1 us -> 32.7 us
    pallas_call x3, Pallas kernels: 116 us -> 68.8 us  [transform(): pl.pallas_call(transform_kernel, out_shape=(jax.ShapeDtypeStruct((num_g /...]
    ppermute x37, waiting for transfers between devices: 161 us -> 144 us  [send(): return lax.ppermute(value, 'blk', pairs)]
    another operation x6 -> x0, other arithmetic: 13.7 us -> none  [gather_and_chi(): old = chi_group(weights, own, blocks, jnp.stack(ids), num_g, old)]
    ppermute x37, starting transfers between devices: 38.1 us -> 32.7 us  [send(): return lax.ppermute(value, 'blk', pairs)]
  transfers between devices with their start and end apart: 37 -> 37, of which waited for: 18 -> 17; matrix products, arithmetic and copies ran while one was open for 5% -> 3% of each run, Pallas kernels for 34% -> 33%
where the time goes in v3:
time: 347 us; the launch traced here: 346 us
  Pallas kernels  149 us (43%)
  waiting for transfers between devices  144 us (41%)
  starting transfers between devices  32.7 us (9%)
  local copies, waits for them, and re-layouts  10.2 us (3%)
  other arithmetic  9.01 us (3%)
    ppermute x37, waiting for transfers between devices, send(): return lax.ppermute(value, 'blk', pairs)  144 us
    pallas_call x6, Pallas kernels, chi_group(): pl.pallas_call(functools.partial(chi_group_kernel, counts, old is not Non...  79.8 us
    pallas_call x3, Pallas kernels, transform(): pl.pallas_call(transform_kernel, out_shape=(jax.ShapeDtypeStruct((num_g /...  68.8 us
    ppermute x37, starting transfers between devices, send(): return lax.ppermute(value, 'blk', pairs)  32.7 us
  transfers between devices with their start and end apart: 37, of which 17 were waited for; matrix products, arithmetic and copies ran while one was open for 3% of the time, Pallas kernels for 33%

profile of v3, /device:TPU:0, one launch (start us, length us, event | category | flops | bytes accessed | tf_op | source)
XLA Modules:
  0.0 346.2 jit_solution(17919435443330557156)
XLA Ops:
  1.1 0.7 constant_dynamic-slice_fusion
  1.9 0.8 fusion.7
  2.7 0.6 gather_fusion
  3.3 0.6 fusion.34
  4.0 1.9 copy.37
  5.9 1.8 slice_bitcast_fusion.2
  7.7 1.4 broadcast_in_dim.12.cs_hbm
  9.0 22.9 %transform.3 = (f32[512,8,128]{2,1,0:T(8,128)}, f32[512,8,128]{2,1,0:T(8,128)}) custom-call(s32[4096]{0:T(1024)} %bitcast.46, s32[4096]{0:T(1024)} %bitcast.43, f32[4,64,64,128]{3,2,1,0:T(8,128)} %bitcast.35, f32[4,8,64,8]{3,2,1,0:T(8,128)} %get-tuple-element.60.cond_ref, bf16[64,192]{1,0:T(8,128)(2,1)} %constant.95.clone.dz_ref, ...), custom_call_target="tpu_custom_call" | custom-call | tf_op jit(solution)/shard_map/transform/pallas_call | solution.py:195
  31.9 0.6 collective-permute-start
  32.5 23.0 %transform.4 = (f32[512,8,128]{2,1,0:T(8,128)}, f32[512,8,128]{2,1,0:T(8,128)}) custom-call(s32[4096]{0:T(1024)} %bitcast.47, s32[4096]{0:T(1024)} %bitcast.44, f32[4,64,64,128]{3,2,1,0:T(8,128)} %bitcast.36, f32[4,8,64,8]{3,2,1,0:T(8,128)} %get-tuple-element.62.cond_ref, bf16[64,192]{1,0:T(8,128)(2,1)} %constant.95.clone.dz_ref, ...), custom_call_target="tpu_custom_call" | custom-call | tf_op jit(solution)/shard_map/transform/pallas_call | solution.py:195
  55.6 1.3 slice_add_fusion.4
  57.0 3.0 collective-permute-start.1
  59.9 22.9 %transform.5 = (f32[512,8,128]{2,1,0:T(8,128)}, f32[512,8,128]{2,1,0:T(8,128)}) custom-call(s32[4096]{0:T(1024)} %bitcast.48, s32[4096]{0:T(1024)} %bitcast.45, f32[4,64,64,128]{3,2,1,0:T(8,128)} %bitcast.37, f32[4,8,64,8]{3,2,1,0:T(8,128)} %get-tuple-element.61.cond_ref, bf16[64,192]{1,0:T(8,128)(2,1)} %constant.95.clone.dz_ref, ...), custom_call_target="tpu_custom_call" | custom-call | tf_op jit(solution)/shard_map/transform/pallas_call | solution.py:195
  83.0 1.5 slice_add_fusion.2
  84.8 1.7 fusion.2
  86.5 3.0 collective-permute-start.2
  89.5 20.4 %collective-permute-done.7 = f32[256,8,128]{2,1,0:T(8,128)S(1)} collective-permute-done((f32[256,8,128]{2,1,0:T(8,128)S(1)}, f32[256,8,128]{2,1,0:T(8,128)S(1)}, u32[]{:S(2)}, u32[]{:S(2)}) %collective-permute-start.7) | collective-permute-done | bytes 1048608 | tf_op jit(solution)/shard_map/ppermute | solution.py:381
  109.9 1.4 fusion.1
  111.3 2.7 collective-permute-start.8
  114.2 0.6 collective-permute-start.13
  114.7 3.1 collective-permute-done.8
  117.9 3.2 collective-permute-done.9
  121.1 0.8 collective-permute-start.11
  121.9 2.3 collective-permute-start.10
  124.5 2.8 collective-permute-start.4
  127.3 9.7 %collective-permute-done.11 = f32[64,8,128]{2,1,0:T(8,128)S(1)} collective-permute-done((f32[64,8,128]{2,1,0:T(8,128)S(1)}, f32[64,8,128]{2,1,0:T(8,128)S(1)}, u32[]{:S(2)}, u32[]{:S(2)}) %collective-permute-start.11) | collective-permute-done | bytes 262176 | tf_op jit(solution)/shard_map/ppermute | solution.py:381
  137.0 1.5 collective-permute-done.13
  138.7 2.7 collective-permute-start.14
  141.4 5.2 %collective-permute-done.4 = f32[64,8,128]{2,1,0:T(8,128)S(1)} collective-permute-done((f32[64,8,128]{2,1,0:T(8,128)S(1)}, f32[64,8,128]{2,1,0:T(8,128)S(1)}, u32[]{:S(2)}, u32[]{:S(2)}) %collective-permute-start.4) | collective-permute-done | bytes 262176 | tf_op jit(solution)/shard_map/ppermute | solution.py:381
  146.5 2.9 collective-permute-done.14
  149.5 3.0 collective-permute-done.15
  152.7 3.0 collective-permute-start.16
  155.7 0.3 copy.39
  156.3 11.1 %collective-permute-done.17 = f32[64,8,128]{2,1,0:T(8,128)S(1)} collective-permute-done((f32[64,8,128]{2,1,0:T(8,128)S(1)}, f32[64,8,128]{2,1,0:T(8,128)S(1)}, u32[]{:S(2)}, u32[]{:S(2)}) %collective-permute-start.17) | collective-permute-done | bytes 262176 | tf_op jit(solution)/shard_map/ppermute | solution.py:381
  167.5 0.3 copy.41
  167.8 0.7 maximum_bitcast_fusion
  168.5 0.4 reshape.106.refs_2_.refs_3_
  168.9 0.4 collective-permute-start.18
  169.3 1.7 collective-permute-start.21
  171.0 0.5 collective-permute-start.34
  171.5 15.8 %collective-permute-done.18.refs_5_ = f32[256,768]{1,0:T(8,128)S(1)} collective-permute-done((f32[256,768]{1,0:T(8,128)S(1)}, f32[256,768]{1,0:T(8,128)S(1)}, u32[]{:S(2)}, u32[]{:S(2)}) %collective-permute-start.18) | collective-permute-done | bytes 786464 | tf_op jit(solution)/shard_map/ppermute | solution.py:381
  187.3 3.4 collective-permute-start.19
  190.8 15.6 %collective-permute-done.21.refs_3_ = f32[256,768]{1,0:T(8,128)S(1)} collective-permute-done((f32[256,768]{1,0:T(8,128)S(1)}, f32[256,768]{1,0:T(8,128)S(1)}, u32[]{:S(2)}, u32[]{:S(2)}) %collective-permute-start.21) | collective-permute-done | bytes 786464 | tf_op jit(solution)/shard_map/ppermute | solution.py:381
  206.3 0.5 collective-permute-start.22
  206.9 0.5 collective-permute-start.32
  207.5 5.1 %collective-permute-done.19.refs_3_ = f32[128,768]{1,0:T(8,128)S(1)} collective-permute-done((f32[128,768]{1,0:T(8,128)S(1)}, f32[128,768]{1,0:T(8,128)S(1)}, u32[]{:S(2)}, u32[]{:S(2)}) %collective-permute-start.19) | collective-permute-done | bytes 393248 | tf_op jit(solution)/shard_map/ppermute | solution.py:381
  212.6 0.6 collective-permute-start.26
  213.2 8.2 %collective-permute-done.22.refs_4_ = f32[128,768]{1,0:T(8,128)} collective-permute-done((f32[128,768]{1,0:T(8,128)S(1)}, f32[128,768]{1,0:T(8,128)}, u32[]{:S(2)}, u32[]{:S(2)}) %collective-permute-start.22) | collective-permute-done | bytes 393248 | tf_op jit(solution)/shard_map/ppermute | solution.py:381
  221.4 0.5 collective-permute-start.28
  222.0 1.6 collective-permute-start.20
  223.6 0.5 collective-permute-start.23
  224.1 9.0 %collective-permute-done.26.refs_3_ = f32[256,768]{1,0:T(8,128)} collective-permute-done((f32[256,768]{1,0:T(8,128)S(1)}, f32[256,768]{1,0:T(8,128)}, u32[]{:S(2)}, u32[]{:S(2)}) %collective-permute-start.26) | collective-permute-done | bytes 786464 | tf_op jit(solution)/shard_map/ppermute | solution.py:381
  233.1 16.8 %collective-permute-done.28.refs_5_ = f32[256,768]{1,0:T(8,128)} collective-permute-done((f32[256,768]{1,0:T(8,128)S(1)}, f32[256,768]{1,0:T(8,128)}, u32[]{:S(2)}, u32[]{:S(2)}) %collective-permute-start.28) | collective-permute-done | bytes 786464 | tf_op jit(solution)/shard_map/ppermute | solution.py:381
  250.1 0.5 collective-permute-start.31
  250.6 7.7 %collective-permute-done.20.refs_3_ = f32[128,768]{1,0:T(8,128)} collective-permute-done((f32[128,768]{1,0:T(8,128)S(1)}, f32[128,768]{1,0:T(8,128)}, u32[]{:S(2)}, u32[]{:S(2)}) %collective-permute-start.20) | collective-permute-done | bytes 393248 | tf_op jit(solution)/shard_map/ppermute | solution.py:381
  258.4 5.7 %collective-permute-done.23.refs_4_ = f32[128,768]{1,0:T(8,128)} collective-permute-done((f32[128,768]{1,0:T(8,128)}, f32[128,768]{1,0:T(8,128)}, u32[]{:S(2)}, u32[]{:S(2)}) %collective-permute-start.23) | collective-permute-done | bytes 393248 | tf_op jit(solution)/shard_map/ppermute | solution.py:381
  264.2 1.2 dynamic-slice_bitcast_fusion.refs_0_
  265.4 0.7 divide_multiply_fusion.refs_1_
  266.1 11.0 %chi.6 = (f32[5,256,4096]{2,1,0:T(8,128)}, f32[5,256,4096]{2,1,0:T(8,128)}) custom-call(s32[16]{0:T(128)} %dynamic-slice_bitcast_fusion.refs_0_, f32[5,384]{1,0:T(8,128)} %divide_multiply_fusion.refs_1_, f32[256,768]{1,0:T(8,128)} %copy-done, f32[256,768]{1,0:T(8,128)} %copy-done, f32[256,768]{1,0:T(8,128)} %copy-done.7), custom_call_target="tpu_custom_call" | custom-call | tf_op jit(solution)/shard_map/chi/pallas_call | solution.py:322
  277.1 11.1 %chi.7 = (f32[5,256,4096]{2,1,0:T(8,128)}, f32[5,256,4096]{2,1,0:T(8,128)}) custom-call(s32[16]{0:T(128)} %dynamic-slice_bitcast_fusion.refs_0_, f32[5,384]{1,0:T(8,128)} %divide_multiply_fusion.refs_1_, f32[256,768]{1,0:T(8,128)} %copy-done, f32[256,768]{1,0:T(8,128)} %copy-done.8, ...), custom_call_target="tpu_custom_call", output_to_operand_aliasing={{0}: (5, {}), {1}: (6, {})} | custom-call | tf_op jit(solution)/shard_map/chi/pallas_call | solution.py:322
  288.2 17.7 %chi.8 = (f32[5,256,4096]{2,1,0:T(8,128)}, f32[5,256,4096]{2,1,0:T(8,128)}) custom-call(s32[16]{0:T(128)} %dynamic-slice_bitcast_fusion.refs_0_, f32[5,384]{1,0:T(8,128)} %divide_multiply_fusion.refs_1_, f32[256,768]{1,0:T(8,128)} %copy-done, f32[256,768]{1,0:T(8,128)} %copy-done.6, ...), custom_call_target="tpu_custom_call", output_to_operand_aliasing={{0}: (7, {}), {1}: (8, {})} | custom-call | tf_op jit(solution)/shard_map/chi/pallas_call | solution.py:322
  305.9 11.1 %chi.9 = (f32[5,256,4096]{2,1,0:T(8,128)}, f32[5,256,4096]{2,1,0:T(8,128)}) custom-call(s32[16]{0:T(128)} %dynamic-slice_bitcast_fusion.refs_0_, f32[5,384]{1,0:T(8,128)} %divide_multiply_fusion.refs_1_, f32[256,768]{1,0:T(8,128)} %copy-done, f32[128,768]{1,0:T(8,128)} %copy-done.12, ...), custom_call_target="tpu_custom_call", output_to_operand_aliasing={{0}: (7, {}), {1}: (8, {})} | custom-call | tf_op jit(solution)/shard_map/chi/pallas_call | solution.py:322
  317.0 17.9 %chi.10 = (f32[5,256,4096]{2,1,0:T(8,128)}, f32[5,256,4096]{2,1,0:T(8,128)}) custom-call(s32[16]{0:T(128)} %dynamic-slice_bitcast_fusion.refs_0_, f32[5,384]{1,0:T(8,128)} %divide_multiply_fusion.refs_1_, f32[256,768]{1,0:T(8,128)} %copy-done, f32[256,768]{1,0:T(8,128)} %collective-permute-done.26.refs_3_, ...), custom_call_target="tpu_custom_call", output_to_operand_aliasing={{0}: (7, {}), {1}: (8, {})} | custom-call | tf_op jit(solution)/shard_map/chi/pallas_call | solution.py:322
  335.0 11.1 %chi.11 = (f32[5,256,4096]{2,1,0:T(8,128)}, f32[5,256,4096]{2,1,0:T(8,128)}) custom-call(s32[16]{0:T(128)} %dynamic-slice_bitcast_fusion.refs_0_, f32[5,384]{1,0:T(8,128)} %divide_multiply_fusion.refs_1_, f32[256,768]{1,0:T(8,128)} %copy-done, f32[128,768]{1,0:T(8,128)} %collective-permute-done.20.refs_3_, ...), custom_call_target="tpu_custom_call", output_to_operand_aliasing={{0}: (7, {}), {1}: (8, {})} | custom-call | tf_op jit(solution)/shard_map/chi/pallas_call | solution.py:322
  (106 shorter events, 2.8 us)
Async XLA Ops:
  31.9 23.7 %collective-permute-start = (f32[512,8,128]{2,1,0:T(8,128)}, f32[512,8,128]{2,1,0:T(8,128)}, u32[]{:S(2)}, u32[]{:S(2)}) collective-permute-start(f32[512,8,128]{2,1,0:T(8,128)} %get-tuple-element.32), channel_id=1, source_target_pairs={{0,1},{1,0},{2,3},{3,2},{4,5},{5,4},{6,7},{7,6},{8,9},{9,8},{10,11... | collective-permute-start | bytes 6291464 | tf_op jit(solution)/shard_map/ppermute | solution.py:381
  32.5 23.1 %copy-start.3 = (f32[512,8,128]{2,1,0:T(8,128)S(1)}, f32[512,8,128]{2,1,0:T(8,128)}, u32[]{:S(2)}) copy-start(f32[512,8,128]{2,1,0:T(8,128)} %get-tuple-element.31) | copy-start | bytes 6291460
  55.5 27.4 %collective-permute-start.6 = (f32[512,8,128]{2,1,0:T(8,128)}, f32[512,8,128]{2,1,0:T(8,128)}, u32[]{:S(2)}, u32[]{:S(2)}) collective-permute-start(f32[512,8,128]{2,1,0:T(8,128)} %get-tuple-element.38), channel_id=1, source_target_pairs={{0,1},{1,0},{2,3},{3,2},{4,5},{5,4},{6,7},{7,6},{8,9},{9,8},{10,11... | collective-permute-start | bytes 6291464 | tf_op jit(solution)/shard_map/ppermute | solution.py:381
  57.0 27.6 %collective-permute-start.1 = (f32[256,8,128]{2,1,0:T(8,128)S(1)}, f32[256,8,128]{2,1,0:T(8,128)}, u32[]{:S(2)}, u32[]{:S(2)}) collective-permute-start(f32[256,8,128]{2,1,0:T(8,128)S(1)} %slice_add_fusion.4), channel_id=1, source_target_pairs={{0,2},{1,3},{2,0},{3,1},{4,6},{5,7},{6,4},{7,5},{8,10},{9,11},{10,... | collective-permute-start | bytes 3145736 | tf_op jit(solution)/shard_map/ppermute | solution.py:381
  59.9 23.0 %copy-start.2 = (f32[512,8,128]{2,1,0:T(8,128)S(1)}, f32[512,8,128]{2,1,0:T(8,128)}, u32[]{:S(2)}) copy-start(f32[512,8,128]{2,1,0:T(8,128)} %get-tuple-element.37) | copy-start | bytes 6291460
  82.9 1.9 copy-start.4
  82.9 31.2 %collective-permute-start.12 = (f32[512,8,128]{2,1,0:T(8,128)}, f32[512,8,128]{2,1,0:T(8,128)S(1)}, u32[]{:S(2)}, u32[]{:S(2)}) collective-permute-start(f32[512,8,128]{2,1,0:T(8,128)} %get-tuple-element.44), channel_id=1, source_target_pairs={{0,1},{1,0},{2,3},{3,2},{4,5},{5,4},{6,7},{7,6},{8,9},{9,8},{10,11... | collective-permute-start | bytes 6291464 | tf_op jit(solution)/shard_map/ppermute | solution.py:381
  84.4 25.5 %collective-permute-start.7 = (f32[256,8,128]{2,1,0:T(8,128)S(1)}, f32[256,8,128]{2,1,0:T(8,128)S(1)}, u32[]{:S(2)}, u32[]{:S(2)}) collective-permute-start(f32[256,8,128]{2,1,0:T(8,128)S(1)} %slice_add_fusion.2), channel_id=1, source_target_pairs={{0,2},{1,3},{2,0},{3,1},{4,6},{5,7},{6,4},{7,5},{8,10},{9,11},{10,... | collective-permute-start | bytes 3145736 | tf_op jit(solution)/shard_map/ppermute | solution.py:381
  86.5 28.2 %collective-permute-start.2 = (f32[32,8,128]{2,1,0:T(8,128)S(1)}, f32[32,8,128]{2,1,0:T(8,128)S(1)}, u32[]{:S(2)}, u32[]{:S(2)}) collective-permute-start(f32[32,8,128]{2,1,0:T(8,128)S(1)} %get-tuple-element.68), channel_id=1, source_target_pairs={{0,8},{1,9},{2,10},{3,11},{4,0},{5,1},{6,2},{7,3},{8,12},{9,13},{1... | collective-permute-start | bytes 393224 | tf_op jit(solution)/shard_map/ppermute | solution.py:381
  89.5 24.6 %copy-start.1 = (f32[512,8,128]{2,1,0:T(8,128)S(1)}, f32[512,8,128]{2,1,0:T(8,128)}, u32[]{:S(2)}) copy-start(f32[512,8,128]{2,1,0:T(8,128)} %get-tuple-element.43) | copy-start | bytes 6291460
  89.5 25.2 %collective-permute-start.3 = (f32[32,8,128]{2,1,0:T(8,128)S(1)}, f32[32,8,128]{2,1,0:T(8,128)S(1)}, u32[]{:S(2)}, u32[]{:S(2)}) collective-permute-start(f32[32,8,128]{2,1,0:T(8,128)S(1)} %get-tuple-element.67), channel_id=1, source_target_pairs={{0,4},{1,5},{2,6},{3,7},{4,12},{5,13},{6,14},{7,15},{8,0},{9,1},{1... | collective-permute-start | bytes 393224 | tf_op jit(solution)/shard_map/ppermute | solution.py:381
  111.3 6.5 %collective-permute-start.8 = (f32[32,8,128]{2,1,0:T(8,128)S(1)}, f32[32,8,128]{2,1,0:T(8,128)S(1)}, u32[]{:S(2)}, u32[]{:S(2)}) collective-permute-start(f32[32,8,128]{2,1,0:T(8,128)S(1)} %get-tuple-element.80), channel_id=1, source_target_pairs={{0,8},{1,9},{2,10},{3,11},{4,0},{5,1},{6,2},{7,3},{8,12},{9,13},{1... | collective-permute-start | bytes 393224 | tf_op jit(solution)/shard_map/ppermute | solution.py:381
  114.0 7.0 %collective-permute-start.9 = (f32[32,8,128]{2,1,0:T(8,128)S(1)}, f32[32,8,128]{2,1,0:T(8,128)S(1)}, u32[]{:S(2)}, u32[]{:S(2)}) collective-permute-start(f32[32,8,128]{2,1,0:T(8,128)S(1)} %get-tuple-element.79), channel_id=1, source_target_pairs={{0,4},{1,5},{2,6},{3,7},{4,12},{5,13},{6,14},{7,15},{8,0},{9,1},{1... | collective-permute-start | bytes 393224 | tf_op jit(solution)/shard_map/ppermute | solution.py:381
  114.2 24.3 %collective-permute-start.13 = (f32[256,8,128]{2,1,0:T(8,128)S(1)}, f32[256,8,128]{2,1,0:T(8,128)S(1)}, u32[]{:S(2)}, u32[]{:S(2)}) collective-permute-start(f32[256,8,128]{2,1,0:T(8,128)S(1)} %slice_add_fusion), channel_id=1, source_target_pairs={{0,2},{1,3},{2,0},{3,1},{4,6},{5,7},{6,4},{7,5},{8,10},{9,11},{10,... | collective-permute-start | bytes 3145736 | tf_op jit(solution)/shard_map/ppermute | solution.py:381
  121.1 15.9 %collective-permute-start.11 = (f32[64,8,128]{2,1,0:T(8,128)S(1)}, f32[64,8,128]{2,1,0:T(8,128)S(1)}, u32[]{:S(2)}, u32[]{:S(2)}) collective-permute-start(f32[64,8,128]{2,1,0:T(8,128)S(1)} %pad_maximum_fusion.3), channel_id=1, source_target_pairs={{0,4},{1,5},{2,6},{3,7},{4,12},{5,13},{6,14},{7,15},{8,0},{9,1},{1... | collective-permute-start | bytes 786440 | tf_op jit(solution)/shard_map/ppermute | solution.py:381
  121.9 15.1 %collective-permute-start.10 = (f32[64,8,128]{2,1,0:T(8,128)S(1)}, f32[64,8,128]{2,1,0:T(8,128)S(1)}, u32[]{:S(2)}, u32[]{:S(2)}) collective-permute-start(f32[64,8,128]{2,1,0:T(8,128)S(1)} %pad_maximum_fusion.2), channel_id=1, source_target_pairs={{0,8},{1,9},{2,10},{3,11},{4,0},{5,1},{6,2},{7,3},{8,12},{9,13},{1... | collective-permute-start | bytes 786440 | tf_op jit(solution)/shard_map/ppermute | solution.py:381
  124.2 17.2 %collective-permute-start.5 = (f32[64,8,128]{2,1,0:T(8,128)S(1)}, f32[64,8,128]{2,1,0:T(8,128)S(1)}, u32[]{:S(2)}, u32[]{:S(2)}) collective-permute-start(f32[64,8,128]{2,1,0:T(8,128)S(1)} %pad_maximum_fusion.1), channel_id=1, source_target_pairs={{0,4},{1,5},{2,6},{3,7},{4,12},{5,13},{6,14},{7,15},{8,0},{9,1},{1... | collective-permute-start | bytes 786440 | tf_op jit(solution)/shard_map/ppermute | solution.py:381
  124.5 22.1 %collective-permute-start.4 = (f32[64,8,128]{2,1,0:T(8,128)S(1)}, f32[64,8,128]{2,1,0:T(8,128)S(1)}, u32[]{:S(2)}, u32[]{:S(2)}) collective-permute-start(f32[64,8,128]{2,1,0:T(8,128)S(1)} %pad_maximum_fusion), channel_id=1, source_target_pairs={{0,8},{1,9},{2,10},{3,11},{4,0},{5,1},{6,2},{7,3},{8,12},{9,13},{1... | collective-permute-start | bytes 786440 | tf_op jit(solution)/shard_map/ppermute | solution.py:381
  138.7 10.8 %collective-permute-start.14 = (f32[32,8,128]{2,1,0:T(8,128)S(1)}, f32[32,8,128]{2,1,0:T(8,128)S(1)}, u32[]{:S(2)}, u32[]{:S(2)}) collective-permute-start(f32[32,8,128]{2,1,0:T(8,128)S(1)} %get-tuple-element.74), channel_id=1, source_target_pairs={{0,8},{1,9},{2,10},{3,11},{4,0},{5,1},{6,2},{7,3},{8,12},{9,13},{1... | collective-permute-start | bytes 393224 | tf_op jit(solution)/shard_map/ppermute | solution.py:381
  141.4 11.1 %collective-permute-start.15 = (f32[32,8,128]{2,1,0:T(8,128)S(1)}, f32[32,8,128]{2,1,0:T(8,128)S(1)}, u32[]{:S(2)}, u32[]{:S(2)}) collective-permute-start(f32[32,8,128]{2,1,0:T(8,128)S(1)} %get-tuple-element.73), channel_id=1, source_target_pairs={{0,4},{1,5},{2,6},{3,7},{4,12},{5,13},{6,14},{7,15},{8,0},{9,1},{1... | collective-permute-start | bytes 393224 | tf_op jit(solution)/shard_map/ppermute | solution.py:381
  152.6 14.8 %collective-permute-start.17 = (f32[64,8,128]{2,1,0:T(8,128)S(1)}, f32[64,8,128]{2,1,0:T(8,128)S(1)}, u32[]{:S(2)}, u32[]{:S(2)}) collective-permute-start(f32[64,8,128]{2,1,0:T(8,128)S(1)} %pad_maximum_fusion.5), channel_id=1, source_target_pairs={{0,4},{1,5},{2,6},{3,7},{4,12},{5,13},{6,14},{7,15},{8,0},{9,1},{1... | collective-permute-start | bytes 786440 | tf_op jit(solution)/shard_map/ppermute | solution.py:381
  152.7 14.8 %collective-permute-start.16 = (f32[64,8,128]{2,1,0:T(8,128)S(1)}, f32[64,8,128]{2,1,0:T(8,128)S(1)}, u32[]{:S(2)}, u32[]{:S(2)}) collective-permute-start(f32[64,8,128]{2,1,0:T(8,128)S(1)} %pad_maximum_fusion.4), channel_id=1, source_target_pairs={{0,8},{1,9},{2,10},{3,11},{4,0},{5,1},{6,2},{7,3},{8,12},{9,13},{1... | collective-permute-start | bytes 786440 | tf_op jit(solution)/shard_map/ppermute | solution.py:381
  168.4 81.6 %copy-start.16 = (s32[128]{0:T(128)S(1)}, s32[128]{0:T(128)}, u32[]{:S(2)}) copy-start(s32[128]{0:T(128)} %param.22) | copy-start | bytes 1540
  168.5 95.7 %copy-start.14 = (f32[3]{0:T(128)S(1)}, f32[3]{0:T(128)}, u32[]{:S(2)}) copy-start(f32[3]{0:T(128)} %param.21) | copy-start | bytes 40
  168.5 95.7 %copy-start.15 = (f32[128]{0:T(128)S(1)}, f32[128]{0:T(128)}, u32[]{:S(2)}) copy-start(f32[128]{0:T(128)} %param.20) | copy-start | bytes 1540
  168.5 95.7 %copy-start.17 = (f32[5]{0:T(128)S(1)}, f32[5]{0:T(128)}, u32[]{:S(2)}) copy-start(f32[5]{0:T(128)} %param.23) | copy-start | bytes 64
  168.9 97.2 %copy-start = (f32[256,768]{1,0:T(8,128)}, f32[256,768]{1,0:T(8,128)S(1)}, u32[]{:S(2)}) copy-start(f32[256,768]{1,0:T(8,128)S(1)} %reshape.106.refs_2_.refs_3_) | copy-start | bytes 2359300
  168.9 18.4 %collective-permute-start.18 = (f32[256,768]{1,0:T(8,128)S(1)}, f32[256,768]{1,0:T(8,128)S(1)}, u32[]{:S(2)}, u32[]{:S(2)}) collective-permute-start(f32[256,768]{1,0:T(8,128)S(1)} %reshape.106.refs_2_.refs_3_), channel_id=1, source_target_pairs={{0,8},{1,9},{2,10},{3,11},{4,0},{5,1},{6,2},{7,3},{8,12},{9,13},{1... | collective-permute-start | bytes 2359304 | tf_op jit(solution)/shard_map/ppermute | solution.py:381
  169.3 37.0 %collective-permute-start.21 = (f32[256,768]{1,0:T(8,128)S(1)}, f32[256,768]{1,0:T(8,128)S(1)}, u32[]{:S(2)}, u32[]{:S(2)}) collective-permute-start(f32[256,768]{1,0:T(8,128)S(1)} %reshape.106.refs_2_.refs_3_), channel_id=1, source_target_pairs={{0,4},{1,5},{2,6},{3,7},{4,12},{5,13},{6,14},{7,15},{8,0},{9,1},{1... | collective-permute-start | bytes 2359304 | tf_op jit(solution)/shard_map/ppermute | solution.py:381
  171.0 35.9 %collective-permute-start.34 = (f32[256,768]{1,0:T(8,128)S(1)}, f32[256,768]{1,0:T(8,128)S(1)}, u32[]{:S(2)}, u32[]{:S(2)}) collective-permute-start(f32[256,768]{1,0:T(8,128)S(1)} %reshape.106.refs_2_.refs_3_), channel_id=1, source_target_pairs={{0,2},{1,3},{2,0},{3,1},{4,6},{5,7},{6,4},{7,5},{8,10},{9,11},{10,... | collective-permute-start | bytes 2359304 | tf_op jit(solution)/shard_map/ppermute | solution.py:381
  171.5 35.9 %collective-permute-start.36 = (f32[256,768]{1,0:T(8,128)S(1)}, f32[256,768]{1,0:T(8,128)S(1)}, u32[]{:S(2)}, u32[]{:S(2)}) collective-permute-start(f32[256,768]{1,0:T(8,128)S(1)} %reshape.106.refs_2_.refs_3_), channel_id=1, source_target_pairs={{0,1},{1,0},{2,3},{3,2},{4,5},{5,4},{6,7},{7,6},{8,9},{9,8},{10,11... | collective-permute-start | bytes 2359304 | tf_op jit(solution)/shard_map/ppermute | solution.py:381
  187.3 100.9 %copy-start.5 = (f32[256,768]{1,0:T(8,128)}, f32[256,768]{1,0:T(8,128)S(1)}, u32[]{:S(2)}) copy-start(f32[256,768]{1,0:T(8,128)S(1)} %collective-permute-done.18.refs_5_) | copy-start | bytes 2359300
  187.3 25.3 %collective-permute-start.19 = (f32[128,768]{1,0:T(8,128)S(1)}, f32[128,768]{1,0:T(8,128)S(1)}, u32[]{:S(2)}, u32[]{:S(2)}) collective-permute-start(f32[128,768]{1,0:T(8,128)S(1)} %slice.200), channel_id=1, source_target_pairs={{0,8},{1,9},{2,10},{3,11},{4,0},{5,1},{6,2},{7,3},{8,12},{9,13},{1... | collective-permute-start | bytes 1179656 | tf_op jit(solution)/shard_map/ppermute | solution.py:381
  206.3 81.9 %copy-start.6 = (f32[256,768]{1,0:T(8,128)}, f32[256,768]{1,0:T(8,128)S(1)}, u32[]{:S(2)}) copy-start(f32[256,768]{1,0:T(8,128)S(1)} %collective-permute-done.21.refs_3_) | copy-start | bytes 2359300
  206.3 15.1 %collective-permute-start.22 = (f32[128,768]{1,0:T(8,128)S(1)}, f32[128,768]{1,0:T(8,128)}, u32[]{:S(2)}, u32[]{:S(2)}) collective-permute-start(f32[128,768]{1,0:T(8,128)S(1)} %slice.201), channel_id=1, source_target_pairs={{0,4},{1,5},{2,6},{3,7},{4,12},{5,13},{6,14},{7,15},{8,0},{9,1},{1... | collective-permute-start | bytes 1179656 | tf_op jit(solution)/shard_map/ppermute | solution.py:381
  206.9 43.1 %copy-start.8 = (f32[256,768]{1,0:T(8,128)}, f32[256,768]{1,0:T(8,128)S(1)}, u32[]{:S(2)}) copy-start(f32[256,768]{1,0:T(8,128)S(1)} %collective-permute-done.34.refs_3_) | copy-start | bytes 2359300
  206.9 15.1 %collective-permute-start.35 = (f32[256,768]{1,0:T(8,128)S(1)}, f32[256,768]{1,0:T(8,128)S(1)}, u32[]{:S(2)}, u32[]{:S(2)}) collective-permute-start(f32[256,768]{1,0:T(8,128)S(1)} %collective-permute-done.34.refs_3_), channel_id=1, source_target_pairs={{0,1},{1,0},{2,3},{3,2},{4,5},{5,4},{6,7},{7,6},{8,9},{9,8},{10,11... | collective-permute-start | bytes 2359304 | tf_op jit(solution)/shard_map/ppermute | solution.py:381
  206.9 15.1 %collective-permute-start.32 = (f32[256,768]{1,0:T(8,128)S(1)}, f32[256,768]{1,0:T(8,128)S(1)}, u32[]{:S(2)}, u32[]{:S(2)}) collective-permute-start(f32[256,768]{1,0:T(8,128)S(1)} %collective-permute-done.21.refs_3_), channel_id=1, source_target_pairs={{0,1},{1,0},{2,3},{3,2},{4,5},{5,4},{6,7},{7,6},{8,9},{9,8},{10,11... | collective-permute-start | bytes 2359304 | tf_op jit(solution)/shard_map/ppermute | solution.py:381
  207.4 58.7 %copy-start.7 = (f32[256,768]{1,0:T(8,128)}, f32[256,768]{1,0:T(8,128)S(1)}, u32[]{:S(2)}) copy-start(f32[256,768]{1,0:T(8,128)S(1)} %collective-permute-done.36.refs_4_) | copy-start | bytes 2359300
  207.4 16.1 %collective-permute-start.33 = (f32[256,768]{1,0:T(8,128)S(1)}, f32[256,768]{1,0:T(8,128)S(1)}, u32[]{:S(2)}, u32[]{:S(2)}) collective-permute-start(f32[256,768]{1,0:T(8,128)S(1)} %collective-permute-done.18.refs_5_), channel_id=1, source_target_pairs={{0,1},{1,0},{2,3},{3,2},{4,5},{5,4},{6,7},{7,6},{8,9},{9,8},{10,11... | collective-permute-start | bytes 2359304 | tf_op jit(solution)/shard_map/ppermute | solution.py:381
  212.6 75.6 %copy-start.12 = (f32[128,768]{1,0:T(8,128)}, f32[128,768]{1,0:T(8,128)S(1)}, u32[]{:S(2)}) copy-start(f32[128,768]{1,0:T(8,128)S(1)} %collective-permute-done.19.refs_3_) | copy-start | bytes 1179652
  212.6 20.5 %collective-permute-start.26 = (f32[256,768]{1,0:T(8,128)S(1)}, f32[256,768]{1,0:T(8,128)}, u32[]{:S(2)}, u32[]{:S(2)}) collective-permute-start(f32[256,768]{1,0:T(8,128)S(1)} %collective-permute-done.21.refs_3_), channel_id=1, source_target_pairs={{0,2},{1,3},{2,0},{3,1},{4,6},{5,7},{6,4},{7,5},{8,10},{9,11},{10,... | collective-permute-start | bytes 2359304 | tf_op jit(solution)/shard_map/ppermute | solution.py:381
  221.4 28.5 %collective-permute-start.28 = (f32[256,768]{1,0:T(8,128)S(1)}, f32[256,768]{1,0:T(8,128)}, u32[]{:S(2)}, u32[]{:S(2)}) collective-permute-start(f32[256,768]{1,0:T(8,128)S(1)} %collective-permute-done.18.refs_5_), channel_id=1, source_target_pairs={{0,2},{1,3},{2,0},{3,1},{4,6},{5,7},{6,4},{7,5},{8,10},{9,11},{10,... | collective-permute-start | bytes 2359304 | tf_op jit(solution)/shard_map/ppermute | solution.py:381
  222.0 28.0 %copy-start.10 = (f32[256,768]{1,0:T(8,128)}, f32[256,768]{1,0:T(8,128)S(1)}, u32[]{:S(2)}) copy-start(f32[256,768]{1,0:T(8,128)S(1)} %collective-permute-done.35.refs_4_) | copy-start | bytes 2359300
  222.0 28.1 %collective-permute-start.30 = (f32[128,768]{1,0:T(8,128)S(1)}, f32[128,768]{1,0:T(8,128)S(1)}, u32[]{:S(2)}, u32[]{:S(2)}) collective-permute-start(f32[128,768]{1,0:T(8,128)S(1)} %collective-permute-done.19.refs_3_), channel_id=1, source_target_pairs={{0,1},{1,0},{2,3},{3,2},{4,5},{5,4},{6,7},{7,6},{8,9},{9,8},{10,11... | collective-permute-start | bytes 1179656 | tf_op jit(solution)/shard_map/ppermute | solution.py:381
  222.0 28.0 %copy-start.9 = (f32[256,768]{1,0:T(8,128)}, f32[256,768]{1,0:T(8,128)S(1)}, u32[]{:S(2)}) copy-start(f32[256,768]{1,0:T(8,128)S(1)} %collective-permute-done.32.refs_4_) | copy-start | bytes 2359300
  222.0 36.4 %collective-permute-start.20 = (f32[128,768]{1,0:T(8,128)S(1)}, f32[128,768]{1,0:T(8,128)}, u32[]{:S(2)}, u32[]{:S(2)}) collective-permute-start(f32[128,768]{1,0:T(8,128)S(1)} %collective-permute-done.19.refs_3_), channel_id=1, source_target_pairs={{0,2},{1,3},{2,0},{3,1},{4,6},{5,7},{6,4},{7,5},{8,10},{9,11},{10,... | collective-permute-start | bytes 1179656 | tf_op jit(solution)/shard_map/ppermute | solution.py:381
  223.6 26.4 %copy-start.11 = (f32[256,768]{1,0:T(8,128)}, f32[256,768]{1,0:T(8,128)S(1)}, u32[]{:S(2)}) copy-start(f32[256,768]{1,0:T(8,128)S(1)} %collective-permute-done.33.refs_6_) | copy-start | bytes 2359300
  223.6 40.6 %collective-permute-start.23 = (f32[128,768]{1,0:T(8,128)}, f32[128,768]{1,0:T(8,128)}, u32[]{:S(2)}, u32[]{:S(2)}) collective-permute-start(f32[128,768]{1,0:T(8,128)} %collective-permute-done.22.refs_4_), channel_id=1, source_target_pairs={{0,2},{1,3},{2,0},{3,1},{4,6},{5,7},{6,4},{7,5},{8,10},{9,11},{10,... | collective-permute-start | bytes 1179656 | tf_op jit(solution)/shard_map/ppermute | solution.py:381
  233.1 83.9 %collective-permute-start.27 = (f32[256,768]{1,0:T(8,128)}, f32[256,768]{1,0:T(8,128)}, u32[]{:S(2)}, u32[]{:S(2)}) collective-permute-start(f32[256,768]{1,0:T(8,128)} %collective-permute-done.26.refs_3_), channel_id=1, source_target_pairs={{0,1},{1,0},{2,3},{3,2},{4,5},{5,4},{6,7},{7,6},{8,9},{9,8},{10,11... | collective-permute-start | bytes 2359304 | tf_op jit(solution)/shard_map/ppermute | solution.py:381
  250.0 67.0 %collective-permute-start.29 = (f32[256,768]{1,0:T(8,128)}, f32[256,768]{1,0:T(8,128)}, u32[]{:S(2)}, u32[]{:S(2)}) collective-permute-start(f32[256,768]{1,0:T(8,128)} %collective-permute-done.28.refs_5_), channel_id=1, source_target_pairs={{0,1},{1,0},{2,3},{3,2},{4,5},{5,4},{6,7},{7,6},{8,9},{9,8},{10,11... | collective-permute-start | bytes 2359304 | tf_op jit(solution)/shard_map/ppermute | solution.py:381
  250.1 8.3 %copy-start.13 = (f32[128,768]{1,0:T(8,128)}, f32[128,768]{1,0:T(8,128)S(1)}, u32[]{:S(2)}) copy-start(f32[128,768]{1,0:T(8,128)S(1)} %collective-permute-done.30.refs_5_) | copy-start | bytes 1179652
  250.1 55.8 %collective-permute-start.31 = (f32[128,768]{1,0:T(8,128)}, f32[128,768]{1,0:T(8,128)}, u32[]{:S(2)}, u32[]{:S(2)}) collective-permute-start(f32[128,768]{1,0:T(8,128)} %collective-permute-done.22.refs_4_), channel_id=1, source_target_pairs={{0,1},{1,0},{2,3},{3,2},{4,5},{5,4},{6,7},{7,6},{8,9},{9,8},{10,11... | collective-permute-start | bytes 1179656 | tf_op jit(solution)/shard_map/ppermute | solution.py:381
  258.4 76.6 %collective-permute-start.24 = (f32[128,768]{1,0:T(8,128)}, f32[128,768]{1,0:T(8,128)}, u32[]{:S(2)}, u32[]{:S(2)}) collective-permute-start(f32[128,768]{1,0:T(8,128)} %collective-permute-done.20.refs_3_), channel_id=1, source_target_pairs={{0,1},{1,0},{2,3},{3,2},{4,5},{5,4},{6,7},{7,6},{8,9},{9,8},{10,11... | collective-permute-start | bytes 1179656 | tf_op jit(solution)/shard_map/ppermute | solution.py:381
  264.1 70.8 %collective-permute-start.25 = (f32[128,768]{1,0:T(8,128)}, f32[128,768]{1,0:T(8,128)}, u32[]{:S(2)}, u32[]{:S(2)}) collective-permute-start(f32[128,768]{1,0:T(8,128)} %collective-permute-done.23.refs_4_), channel_id=1, source_target_pairs={{0,1},{1,0},{2,3},{3,2},{4,5},{5,4},{6,7},{7,6},{8,9},{9,8},{10,11... | collective-permute-start | bytes 1179656 | tf_op jit(solution)/shard_map/ppermute | solution.py:381

commit v4 on v3

--- a/solution.py
+++ b/solution.py
@@ -11,6 +11,7 @@
 from jax.sharding import PartitionSpec as P
 
 
+VMEM_BYTES = 64 * 2**20
 LANES = 128
 SUB = 8
 SLOTS = 4
@@ -206,6 +207,7 @@
             pltpu.SemaphoreType.DMA((slots + 1,)),
             pltpu.SemaphoreType.DMA((3,)),
         ],
+        compiler_params=pltpu.CompilerParams(vmem_limit_bytes=VMEM_BYTES),
         name="transform",
     )(col, phase, val, cond, dz, dy, dyr, cs)
 
@@ -338,11 +340,12 @@
         ),
         out_shape=(out, out),
         input_output_aliases={3 + len(pieces) + i: i for i in range(len(olds))},
+        compiler_params=pltpu.CompilerParams(vmem_limit_bytes=VMEM_BYTES),
         name="chi",
     )(ids, weights, own, *pieces, *olds)
 
 
-GROUPS = (((0, 0),), ((1, 0),), ((0, 1), (0, 3)), ((0, 2),), ((1, 1), (1, 3)), ((1, 2),))
+GROUPS = (((0, 0),), ((1, 0), (0, 3)), ((0, 1), (1, 3)), ((0, 2), (1, 1)), ((1, 2),))
 RING = (0, 2, 3, 1)
 
 
@@ -370,6 +373,11 @@
             ],
             dtype=np.int32,
         )
+        whole = np.arange(2 * count).reshape(count, 2)[self.near]
+        first = whole[..., 0].reshape(count, 2, -1)
+        second = whole[..., 1].swapaxes(2, 3).reshape(count, 2, -1)
+        self.whole = whole.reshape(count, -1)
+        self.halved = np.concatenate([first, second], axis=2).reshape(count, -1)
         self.order = np.stack([self.near[:, :, b, r] for g in GROUPS for b, r in g], axis=1)
 
     @staticmethod
@@ -381,24 +389,38 @@
     return lax.ppermute(value, "blk", pairs)
 
 
-def reduce_scatter(keep, other, links, ahead):
-    half = keep.shape[0] // 2
-    got = send(other, links.core)
-    far = send(keep[half:] + got[half:], links.y)
-    if ahead:
-        far, ahead = lax.optimization_barrier((far, ahead))
-    near = keep[:half] + got[:half] + far
-    block = half // 4
+def ring(near, links):
+    block = near.shape[0] // 4
     part = block // 2
-    cw = send(near[2 * block : 2 * block + part], links.cw)
-    ccw = send(near[2 * block + part : 3 * block], links.ccw)
-    cw, ccw = lax.optimization_barrier((cw, ccw))
+    to_cw, to_ccw, near = lax.optimization_barrier(
+        (near[2 * block : 2 * block + part], near[2 * block + part : 3 * block], near)
+    )
+    cw = send(to_cw, links.cw)
+    ccw = send(to_ccw, links.ccw)
     to_cw = jnp.concatenate([near[block : block + part] + cw, near[block + part : 2 * block]])
     to_ccw = jnp.concatenate([near[3 * block : 3 * block + part], near[3 * block + part :] + ccw])
     from_cw = send(to_cw, links.cw)
     from_ccw = send(to_ccw, links.ccw)
-    from_cw, from_ccw = lax.optimization_barrier((from_cw, from_ccw))
     return near[:block], from_cw, from_ccw
+
+
+def reduce_scatter(keep, other, links):
+    half = keep.shape[0] // 2
+    got = send(other, links.core)
+    far = send(keep[half:] + got[half:], links.y)
+    return ring(keep[:half] + got[:half] + far, links)
+
+
+def reduce_scatter_halves(keep, other, links):
+    half = keep.shape[0] // 2
+    part = half // 2
+    got = send(other, links.core)
+    far = send(keep[part:half] + got[part:half], links.y)
+    mine, cw, ccw = ring(keep[half:] + got[half:], links)
+    last = mine.shape[0] // 2
+    late = send(mine[last:] + cw[last:] + ccw[last:], links.y)
+    first = sum(ring(keep[:part] + got[:part] + far, links))
+    return jnp.concatenate([first, mine[:last] + cw[:last] + ccw[:last] + late])
 
 
 def gather_and_chi(weights, own, links, ids, num_g):
@@ -407,10 +429,12 @@
     def over(pieces, pairs):
         return [send(p, pairs) for p in pieces]
 
-    mine = {(0, 0): [own]}
-    mine[0, 3] = over([own], links.cw)
-    mine[0, 1] = over([own], links.ccw)
-    mine[0, 2] = [send(mine[0, 3][0][:part], links.cw), send(mine[0, 1][0][part:], links.ccw)]
+    cw = send(own, links.cw)
+    later, cw = lax.optimization_barrier((own, cw))
+    ccw = send(later, links.ccw)
+    cw_later, ccw = lax.optimization_barrier((cw, ccw))
+    mine = {(0, 0): [own], (0, 3): [cw], (0, 1): [ccw]}
+    mine[0, 2] = [send(cw_later[:part], links.cw), send(ccw[part:], links.ccw)]
     for r in range(4):
         mine[1, r] = over(mine[0, r], links.y)
     old = None
@@ -469,19 +493,25 @@
     count = lax.axis_size("blk")
     links = Links(count) if Links.fits(count) else None
     if links is not None:
-        near = jnp.asarray(links.near)[lax.axis_index("blk")]
-        ids = jnp.asarray(links.order.reshape(count, -1))[lax.axis_index("blk")]
-        pick = pick.reshape(2, count, -1)[:, near.reshape(-1)].reshape(2, -1)
+        tables = np.concatenate([links.whole, links.halved, links.order.reshape(count, -1)], axis=1)
+        table = jnp.asarray(tables)[lax.axis_index("blk")]
+        picks = pick.reshape(2, 2 * count, -1)[:, table[: 4 * count]].reshape(2, 2, -1)
+        ids = table[4 * count :]
     owned = []
     for c in range(num_cond):
-        keep, other = transform(pick[0], pick[1], val, cond[c], cs, num_g)
-        if links is not None:
-            ahead = owned[-1][1:] if c == num_cond - 1 else ()
-            owned.append(reduce_scatter(keep, other, links, ahead))
-        else:
+        last = c == num_cond - 1
+        chosen = pick if links is None else picks[:, int(last)]
+        keep, other = transform(chosen[0], chosen[1], val, cond[c], cs, num_g)
+        if links is None:
             whole = jnp.concatenate([keep, other])
             owned.append((lax.psum_scatter(whole, "blk", scatter_dimension=0, tiled=True),))
-    own = jnp.stack([sum(parts) for parts in owned]).reshape(num_cond, -1, 2, 4, num_val)
+        elif last:
+            owned.append((reduce_scatter_halves(keep, other, links),))
+        else:
+            owned.append(reduce_scatter(keep, other, links))
+    for c, parts in enumerate(owned):
+        owned[c] = sum(parts[1:], parts[0])
+    own = jnp.stack(owned).reshape(num_cond, -1, 2, 4, num_val)
     own = jnp.transpose(own, (1, 3, 2, 0, 4)).reshape(-1, 2 * pairs)
 
     gaps = e_val[None, :] - e_cond[:, None]

time: 347 us -> 338 us (0.974)
  waiting for transfers between devices: 144 us -> 130 us
  starting transfers between devices: 32.7 us -> 41.1 us
  Pallas kernels: 149 us -> 144 us
    ppermute x37 -> x42, waiting for transfers between devices: 144 us -> 130 us  [send(): return lax.ppermute(value, 'blk', pairs)]
    ppermute x37 -> x42, starting transfers between devices: 32.7 us -> 41.1 us  [send(): return lax.ppermute(value, 'blk', pairs)]
    pallas_call x6 -> x5, Pallas kernels: 79.8 us -> 75.4 us  [chi_group(): pl.pallas_call(functools.partial(chi_group_kernel, counts, old is not Non...]
  transfers between devices with their start and end apart: 37 -> 42, of which waited for: 17 -> 19; matrix products, arithmetic and copies ran while one was open for 3% -> 3% of each run, Pallas kernels for 33% -> 33%
where the time goes in v4:
time: 338 us; the launch traced here: 337 us
  Pallas kernels  144 us (43%)
  waiting for transfers between devices  130 us (38%)
  starting transfers between devices  41.1 us (12%)
  other arithmetic  10.1 us (3%)
  local copies, waits for them, and re-layouts  9.95 us (3%)
    ppermute x42, waiting for transfers between devices, send(): return lax.ppermute(value, 'blk', pairs)  130 us
    pallas_call x5, Pallas kernels, chi_group(): pl.pallas_call(functools.partial(chi_group_kernel, counts, old is not Non...  75.4 us
    pallas_call x3, Pallas kernels, transform(): pl.pallas_call(transform_kernel, out_shape=(jax.ShapeDtypeStruct((num_g /...  68.4 us
    ppermute x42, starting transfers between devices, send(): return lax.ppermute(value, 'blk', pairs)  41.1 us
  transfers between devices with their start and end apart: 42, of which 19 were waited for; matrix products, arithmetic and copies ran while one was open for 3% of the time, Pallas kernels for 33%

profile of v4, /device:TPU:0, one launch (start us, length us, event | category | flops | bytes accessed | tf_op | source)
XLA Modules:
  0.0 336.9 jit_solution(13474523040468208400)
XLA Ops:
  1.1 0.7 constant_dynamic-slice_fusion
  1.8 0.6 copy-done.17
  2.4 0.8 fusion.5
  3.2 0.7 gather_fusion
  3.9 0.7 fusion.30
  4.6 1.9 copy.40
  6.5 1.7 slice_bitcast_fusion.2
  8.3 1.3 broadcast_in_dim.12.cs_hbm
  9.6 22.8 %transform.3 = (f32[512,8,128]{2,1,0:T(8,128)}, f32[512,8,128]{2,1,0:T(8,128)}) custom-call(s32[4096]{0:T(1024)} %bitcast.50, s32[4096]{0:T(1024)} %bitcast.48, f32[4,64,64,128]{3,2,1,0:T(8,128)} %bitcast.39, f32[4,8,64,8]{3,2,1,0:T(8,128)} %get-tuple-element.62.cond_ref, bf16[64,192]{1,0:T(8,128)(2,1)} %constant.92.clone.dz_ref, ...), custom_call_target="tpu_custom_call" | custom-call | tf_op jit(solution)/shard_map/transform/pallas_call | solution.py:196
  32.4 0.6 collective-permute-start
  33.0 22.8 %transform.5 = (f32[512,8,128]{2,1,0:T(8,128)}, f32[512,8,128]{2,1,0:T(8,128)}) custom-call(s32[4096]{0:T(1024)} %bitcast.53, s32[4096]{0:T(1024)} %bitcast.52, f32[4,64,64,128]{3,2,1,0:T(8,128)} %bitcast.40, f32[4,8,64,8]{3,2,1,0:T(8,128)} %get-tuple-element.63.cond_ref, bf16[64,192]{1,0:T(8,128)(2,1)} %constant.92.clone.dz_ref, ...), custom_call_target="tpu_custom_call" | custom-call | tf_op jit(solution)/shard_map/transform/pallas_call | solution.py:196
  55.9 22.8 %transform.4 = (f32[512,8,128]{2,1,0:T(8,128)}, f32[512,8,128]{2,1,0:T(8,128)}) custom-call(s32[4096]{0:T(1024)} %bitcast.51, s32[4096]{0:T(1024)} %bitcast.49, f32[4,64,64,128]{3,2,1,0:T(8,128)} %bitcast.41, f32[4,8,64,8]{3,2,1,0:T(8,128)} %get-tuple-element.64.cond_ref, bf16[64,192]{1,0:T(8,128)(2,1)} %constant.92.clone.dz_ref, ...), custom_call_target="tpu_custom_call" | custom-call | tf_op jit(solution)/shard_map/transform/pallas_call | solution.py:196
  79.3 1.7 slice_add_fusion.3
  81.0 2.6 collective-permute-start.1
  83.7 1.1 slice_add_fusion.5
  85.1 1.5 slice_add_fusion
  86.6 2.9 collective-permute-start.18
  89.7 1.5 collective-permute-start.7
  91.2 2.2 collective-permute-done.18
  93.4 3.6 %collective-permute-done.20 = f32[32,8,128]{2,1,0:T(8,128)S(1)} collective-permute-done((f32[32,8,128]{2,1,0:T(8,128)S(1)}, f32[32,8,128]{2,1,0:T(8,128)S(1)}, u32[]{:S(2)}, u32[]{:S(2)}) %collective-permute-start.20) | collective-permute-done | bytes 131104 | tf_op jit(solution)/shard_map/ppermute | solution.py:389
  97.2 0.6 collective-permute-start.19
  97.8 1.5 collective-permute-start.21
  99.3 19.6 %collective-permute-done.13 = f32[128,8,128]{2,1,0:T(8,128)S(1)} collective-permute-done((f32[128,8,128]{2,1,0:T(8,128)S(1)}, f32[128,8,128]{2,1,0:T(8,128)S(1)}, u32[]{:S(2)}, u32[]{:S(2)}) %collective-permute-start.13) | collective-permute-done | bytes 524320 | tf_op jit(solution)/shard_map/ppermute | solution.py:389
  118.9 1.1 fusion.2
  120.1 3.2 collective-permute-start.14
  123.3 1.6 collective-permute-start.22
  125.2 3.3 collective-permute-done.16
  128.5 0.7 collective-permute-start.15
  129.3 1.4 collective-permute-start.17
  130.7 13.3 %collective-permute-done.22 = f32[32,8,128]{2,1,0:T(8,128)S(1)} collective-permute-done((f32[32,8,128]{2,1,0:T(8,128)S(1)}, f32[32,8,128]{2,1,0:T(8,128)S(1)}, u32[]{:S(2)}, u32[]{:S(2)}) %collective-permute-start.22) | collective-permute-done | bytes 131104 | tf_op jit(solution)/shard_map/ppermute | solution.py:389
  144.0 1.4 fusion.1
  145.5 2.9 collective-permute-start.2
  148.6 2.0 collective-permute-start.10
  150.6 1.1 collective-permute-start.8
  151.6 0.7 collective-permute-done.2
  152.3 4.1 %collective-permute-done.4 = f32[32,8,128]{2,1,0:T(8,128)S(1)} collective-permute-done((f32[32,8,128]{2,1,0:T(8,128)S(1)}, f32[32,8,128]{2,1,0:T(8,128)S(1)}, u32[]{:S(2)}, u32[]{:S(2)}) %collective-permute-start.4) | collective-permute-done | bytes 131104 | tf_op jit(solution)/shard_map/ppermute | solution.py:389
  156.5 1.1 collective-permute-start.3
  157.6 1.0 collective-permute-start.5
  158.6 7.3 %collective-permute-done.10 = f32[32,8,128]{2,1,0:T(8,128)S(1)} collective-permute-done((f32[32,8,128]{2,1,0:T(8,128)S(1)}, f32[32,8,128]{2,1,0:T(8,128)S(1)}, u32[]{:S(2)}, u32[]{:S(2)}) %collective-permute-start.10) | collective-permute-done | bytes 131104 | tf_op jit(solution)/shard_map/ppermute | solution.py:389
  166.1 2.1 collective-permute-start.11
  168.5 8.7 %collective-permute-done.5 = f32[64,8,128]{2,1,0:T(8,128)S(1)} collective-permute-done((f32[64,8,128]{2,1,0:T(8,128)S(1)}, f32[64,8,128]{2,1,0:T(8,128)S(1)}, u32[]{:S(2)}, u32[]{:S(2)}) %collective-permute-start.5) | collective-permute-done | bytes 262176 | tf_op jit(solution)/shard_map/ppermute | solution.py:389
  177.7 6.0 %collective-permute-done.11 = f32[64,8,128]{2,1,0:T(8,128)S(1)} collective-permute-done((f32[64,8,128]{2,1,0:T(8,128)S(1)}, f32[64,8,128]{2,1,0:T(8,128)S(1)}, u32[]{:S(2)}, u32[]{:S(2)}) %collective-permute-start.11) | collective-permute-done | bytes 262176 | tf_op jit(solution)/shard_map/ppermute | solution.py:389
  184.0 0.7 maximum_bitcast_fusion
  185.2 0.6 collective-permute-start.23
  185.8 1.5 collective-permute-start.38
  187.3 17.3 %collective-permute-done.23.refs_5_ = f32[256,768]{1,0:T(8,128)S(1)} collective-permute-done((f32[256,768]{1,0:T(8,128)S(1)}, f32[256,768]{1,0:T(8,128)S(1)}, u32[]{:S(2)}, u32[]{:S(2)}) %collective-permute-start.23) | collective-permute-done | bytes 786464 | tf_op jit(solution)/shard_map/ppermute | solution.py:389
  204.6 1.4 collective-permute-start.24
  205.9 1.6 collective-permute-start.36
  208.0 15.9 %collective-permute-done.24.refs_3_ = f32[256,768]{1,0:T(8,128)S(1)} collective-permute-done((f32[256,768]{1,0:T(8,128)S(1)}, f32[256,768]{1,0:T(8,128)S(1)}, u32[]{:S(2)}, u32[]{:S(2)}) %collective-permute-start.24) | collective-permute-done | bytes 786464 | tf_op jit(solution)/shard_map/ppermute | solution.py:389
  223.9 1.6 collective-permute-start.33
  225.7 0.7 collective-permute-done.36.refs_5_
  226.4 1.6 collective-permute-start.25
  228.5 9.7 %collective-permute-done.25.refs_3_ = f32[128,768]{1,0:T(8,128)} collective-permute-done((f32[128,768]{1,0:T(8,128)S(1)}, f32[128,768]{1,0:T(8,128)}, u32[]{:S(2)}, u32[]{:S(2)}) %collective-permute-start.25) | collective-permute-done | bytes 393248 | tf_op jit(solution)/shard_map/ppermute | solution.py:389
  238.1 1.6 collective-permute-start.26
  239.7 8.8 %collective-permute-done.27.refs_4_ = f32[128,768]{1,0:T(8,128)} collective-permute-done((f32[128,768]{1,0:T(8,128)S(1)}, f32[128,768]{1,0:T(8,128)}, u32[]{:S(2)}, u32[]{:S(2)}) %collective-permute-start.27) | collective-permute-done | bytes 393248 | tf_op jit(solution)/shard_map/ppermute | solution.py:389
  248.5 1.6 collective-permute-start.28
  251.5 8.5 %collective-permute-done.28.refs_4_ = f32[128,768]{1,0:T(8,128)} collective-permute-done((f32[128,768]{1,0:T(8,128)}, f32[128,768]{1,0:T(8,128)}, u32[]{:S(2)}, u32[]{:S(2)}) %collective-permute-start.28) | collective-permute-done | bytes 393248 | tf_op jit(solution)/shard_map/ppermute | solution.py:389
  259.9 0.7 slice_bitcast_fusion.3.refs_0_
  260.6 0.7 divide_multiply_fusion.refs_1_
  261.3 11.0 %chi.5 = (f32[5,256,4096]{2,1,0:T(8,128)}, f32[5,256,4096]{2,1,0:T(8,128)}) custom-call(s32[16]{0:T(128)} %slice_bitcast_fusion.3.refs_0_, f32[5,384]{1,0:T(8,128)} %divide_multiply_fusion.refs_1_, f32[256,768]{1,0:T(8,128)} %copy-done, f32[256,768]{1,0:T(8,128)} %copy-done, f32[256,768]{1,0:T(8,128)} %copy-done.6), custom_call_target="tpu_custom_call" | custom-call | tf_op jit(solution)/shard_map/chi/pallas_call | solution.py:324
  272.3 17.7 %chi.6 = (f32[5,256,4096]{2,1,0:T(8,128)}, f32[5,256,4096]{2,1,0:T(8,128)}) custom-call(s32[16]{0:T(128)} %slice_bitcast_fusion.3.refs_0_, f32[5,384]{1,0:T(8,128)} %divide_multiply_fusion.refs_1_, f32[256,768]{1,0:T(8,128)} %copy-done, f32[256,768]{1,0:T(8,128)} %copy-done.7, f32[256,768]{1,0:T(8,128)} %copy-done.10, ...), custom_call_target="tpu_custom_call", output_to_operand_aliasing={{0}: (7, {}), {1}: (8, {})} | custom-call | tf_op jit(solution)/shard_map/chi/pallas_call | solution.py:324
  290.0 17.7 %chi.7 = (f32[5,256,4096]{2,1,0:T(8,128)}, f32[5,256,4096]{2,1,0:T(8,128)}) custom-call(s32[16]{0:T(128)} %slice_bitcast_fusion.3.refs_0_, f32[5,384]{1,0:T(8,128)} %divide_multiply_fusion.refs_1_, f32[256,768]{1,0:T(8,128)} %copy-done, f32[256,768]{1,0:T(8,128)} %copy-done.5, f32[256,768]{1,0:T(8,128)} %copy-done.11, ...), custom_call_target="tpu_custom_call", output_to_operand_aliasing={{0}: (7, {}), {1}: (8, {})} | custom-call | tf_op jit(solution)/shard_map/chi/pallas_call | solution.py:324
  307.7 17.7 %chi.8 = (f32[5,256,4096]{2,1,0:T(8,128)}, f32[5,256,4096]{2,1,0:T(8,128)}) custom-call(s32[16]{0:T(128)} %slice_bitcast_fusion.3.refs_0_, f32[5,384]{1,0:T(8,128)} %divide_multiply_fusion.refs_1_, f32[256,768]{1,0:T(8,128)} %copy-done, f32[128,768]{1,0:T(8,128)} %collective-permute-done.25.refs_3_, ...), custom_call_target="tpu_custom_call", output_to_operand_aliasing={{0}: (9, {}), {1}: (10, {})} | custom-call | tf_op jit(solution)/shard_map/chi/pallas_call | solution.py:324
  325.5 11.3 %chi.9 = (f32[5,256,4096]{2,1,0:T(8,128)}, f32[5,256,4096]{2,1,0:T(8,128)}) custom-call(s32[16]{0:T(128)} %slice_bitcast_fusion.3.refs_0_, f32[5,384]{1,0:T(8,128)} %divide_multiply_fusion.refs_1_, f32[256,768]{1,0:T(8,128)} %copy-done, f32[128,768]{1,0:T(8,128)} %collective-permute-done.26.refs_3_, ...), custom_call_target="tpu_custom_call", output_to_operand_aliasing={{0}: (7, {}), {1}: (8, {})} | custom-call | tf_op jit(solution)/shard_map/chi/pallas_call | solution.py:324
  (126 shorter events, 6.6 us)
Async XLA Ops:
  1.8 0.6 copy-start.17
  32.4 46.9 %collective-permute-start = (f32[512,8,128]{2,1,0:T(8,128)}, f32[512,8,128]{2,1,0:T(8,128)}, u32[]{:S(2)}, u32[]{:S(2)}) collective-permute-start(f32[512,8,128]{2,1,0:T(8,128)} %get-tuple-element.33), channel_id=1, source_target_pairs={{0,1},{1,0},{2,3},{3,2},{4,5},{5,4},{6,7},{7,6},{8,9},{9,8},{10,11... | collective-permute-start | bytes 6291464 | tf_op jit(solution)/shard_map/ppermute | solution.py:389
  55.8 27.9 %collective-permute-start.12 = (f32[512,8,128]{2,1,0:T(8,128)}, f32[512,8,128]{2,1,0:T(8,128)}, u32[]{:S(2)}, u32[]{:S(2)}) collective-permute-start(f32[512,8,128]{2,1,0:T(8,128)} %get-tuple-element.43), channel_id=1, source_target_pairs={{0,1},{1,0},{2,3},{3,2},{4,5},{5,4},{6,7},{7,6},{8,9},{9,8},{10,11... | collective-permute-start | bytes 6291464 | tf_op jit(solution)/shard_map/ppermute | solution.py:389
  78.7 4.9 %copy-start.1 = (f32[512,8,128]{2,1,0:T(8,128)S(1)}, f32[512,8,128]{2,1,0:T(8,128)}, u32[]{:S(2)}) copy-start(f32[512,8,128]{2,1,0:T(8,128)} %get-tuple-element.42) | copy-start | bytes 6291460
  78.8 10.8 %collective-permute-start.6 = (f32[512,8,128]{2,1,0:T(8,128)}, f32[512,8,128]{2,1,0:T(8,128)S(1)}, u32[]{:S(2)}, u32[]{:S(2)}) collective-permute-start(f32[512,8,128]{2,1,0:T(8,128)} %get-tuple-element.38), channel_id=1, source_target_pairs={{0,1},{1,0},{2,3},{3,2},{4,5},{5,4},{6,7},{7,6},{8,9},{9,8},{10,11... | collective-permute-start | bytes 6291464 | tf_op jit(solution)/shard_map/ppermute | solution.py:389
  81.0 63.0 %collective-permute-start.1 = (f32[256,8,128]{2,1,0:T(8,128)S(1)}, f32[256,8,128]{2,1,0:T(8,128)S(1)}, u32[]{:S(2)}, u32[]{:S(2)}) collective-permute-start(f32[256,8,128]{2,1,0:T(8,128)S(1)} %slice_add_fusion.3), channel_id=1, source_target_pairs={{0,2},{1,3},{2,0},{3,1},{4,6},{5,7},{6,4},{7,5},{8,10},{9,11},{10,... | collective-permute-start | bytes 3145736 | tf_op jit(solution)/shard_map/ppermute | solution.py:389
  84.8 4.8 %copy-start.3 = (f32[512,8,128]{2,1,0:T(8,128)S(1)}, f32[512,8,128]{2,1,0:T(8,128)}, u32[]{:S(2)}) copy-start(f32[512,8,128]{2,1,0:T(8,128)} %get-tuple-element.37) | copy-start | bytes 6291460
  84.8 34.1 %collective-permute-start.13 = (f32[128,8,128]{2,1,0:T(8,128)S(1)}, f32[128,8,128]{2,1,0:T(8,128)S(1)}, u32[]{:S(2)}, u32[]{:S(2)}) collective-permute-start(f32[128,8,128]{2,1,0:T(8,128)S(1)} %slice_add_fusion.5), channel_id=1, source_target_pairs={{0,2},{1,3},{2,0},{3,1},{4,6},{5,7},{6,4},{7,5},{8,10},{9,11},{10,... | collective-permute-start | bytes 1572872 | tf_op jit(solution)/shard_map/ppermute | solution.py:389
  86.6 6.8 %collective-permute-start.18 = (f32[32,8,128]{2,1,0:T(8,128)S(1)}, f32[32,8,128]{2,1,0:T(8,128)S(1)}, u32[]{:S(2)}, u32[]{:S(2)}) collective-permute-start(f32[32,8,128]{2,1,0:T(8,128)S(1)} %get-tuple-element.48), channel_id=1, source_target_pairs={{0,8},{1,9},{2,10},{3,11},{4,0},{5,1},{6,2},{7,3},{8,12},{9,13},{1... | collective-permute-start | bytes 393224 | tf_op jit(solution)/shard_map/ppermute | solution.py:389
  89.5 7.5 %collective-permute-start.20 = (f32[32,8,128]{2,1,0:T(8,128)S(1)}, f32[32,8,128]{2,1,0:T(8,128)S(1)}, u32[]{:S(2)}, u32[]{:S(2)}) collective-permute-start(f32[32,8,128]{2,1,0:T(8,128)S(1)} %get-tuple-element.49), channel_id=1, source_target_pairs={{0,4},{1,5},{2,6},{3,7},{4,12},{5,13},{6,14},{7,15},{8,0},{9,1},{1... | collective-permute-start | bytes 393224 | tf_op jit(solution)/shard_map/ppermute | solution.py:389
  89.7 58.8 %collective-permute-start.7 = (f32[256,8,128]{2,1,0:T(8,128)S(1)}, f32[256,8,128]{2,1,0:T(8,128)S(1)}, u32[]{:S(2)}, u32[]{:S(2)}) collective-permute-start(f32[256,8,128]{2,1,0:T(8,128)S(1)} %slice_add_fusion.1), channel_id=1, source_target_pairs={{0,2},{1,3},{2,0},{3,1},{4,6},{5,7},{6,4},{7,5},{8,10},{9,11},{10,... | collective-permute-start | bytes 3145736 | tf_op jit(solution)/shard_map/ppermute | solution.py:389
  97.2 26.1 %collective-permute-start.19 = (f32[64,8,128]{2,1,0:T(8,128)S(1)}, f32[64,8,128]{2,1,0:T(8,128)S(1)}, u32[]{:S(2)}, u32[]{:S(2)}) collective-permute-start(f32[64,8,128]{2,1,0:T(8,128)S(1)} %pad_maximum_fusion.4), channel_id=1, source_target_pairs={{0,8},{1,9},{2,10},{3,11},{4,0},{5,1},{6,2},{7,3},{8,12},{9,13},{1... | collective-permute-start | bytes 786440 | tf_op jit(solution)/shard_map/ppermute | solution.py:389
  97.8 25.5 %collective-permute-start.21 = (f32[64,8,128]{2,1,0:T(8,128)S(1)}, f32[64,8,128]{2,1,0:T(8,128)S(1)}, u32[]{:S(2)}, u32[]{:S(2)}) collective-permute-start(f32[64,8,128]{2,1,0:T(8,128)S(1)} %pad_maximum_fusion.5), channel_id=1, source_target_pairs={{0,4},{1,5},{2,6},{3,7},{4,12},{5,13},{6,14},{7,15},{8,0},{9,1},{1... | collective-permute-start | bytes 786440 | tf_op jit(solution)/shard_map/ppermute | solution.py:389
  120.1 24.0 %copy-start.2 = (f32[512,8,128]{2,1,0:T(8,128)S(1)}, f32[512,8,128]{2,1,0:T(8,128)}, u32[]{:S(2)}) copy-start(f32[512,8,128]{2,1,0:T(8,128)} %get-tuple-element.32) | copy-start | bytes 6291460
  120.1 5.1 %collective-permute-start.14 = (f32[16,8,128]{2,1,0:T(8,128)S(1)}, f32[16,8,128]{2,1,0:T(8,128)S(1)}, u32[]{:S(2)}, u32[]{:S(2)}) collective-permute-start(f32[16,8,128]{2,1,0:T(8,128)S(1)} %get-tuple-element.45), channel_id=1, source_target_pairs={{0,8},{1,9},{2,10},{3,11},{4,0},{5,1},{6,2},{7,3},{8,12},{9,13},{1... | collective-permute-start | bytes 196616 | tf_op jit(solution)/shard_map/ppermute | solution.py:389
  123.3 5.2 %collective-permute-start.16 = (f32[16,8,128]{2,1,0:T(8,128)S(1)}, f32[16,8,128]{2,1,0:T(8,128)S(1)}, u32[]{:S(2)}, u32[]{:S(2)}) collective-permute-start(f32[16,8,128]{2,1,0:T(8,128)S(1)} %get-tuple-element.46), channel_id=1, source_target_pairs={{0,4},{1,5},{2,6},{3,7},{4,12},{5,13},{6,14},{7,15},{8,0},{9,1},{1... | collective-permute-start | bytes 196616 | tf_op jit(solution)/shard_map/ppermute | solution.py:389
  123.3 20.6 %collective-permute-start.22 = (f32[32,8,128]{2,1,0:T(8,128)S(1)}, f32[32,8,128]{2,1,0:T(8,128)S(1)}, u32[]{:S(2)}, u32[]{:S(2)}) collective-permute-start(f32[32,8,128]{2,1,0:T(8,128)S(1)} %slice_add_fusion.7), channel_id=1, source_target_pairs={{0,2},{1,3},{2,0},{3,1},{4,6},{5,7},{6,4},{7,5},{8,10},{9,11},{10,... | collective-permute-start | bytes 393224 | tf_op jit(solution)/shard_map/ppermute | solution.py:389
  128.5 15.5 %collective-permute-start.15 = (f32[32,8,128]{2,1,0:T(8,128)S(1)}, f32[32,8,128]{2,1,0:T(8,128)S(1)}, u32[]{:S(2)}, u32[]{:S(2)}) collective-permute-start(f32[32,8,128]{2,1,0:T(8,128)S(1)} %pad_maximum_fusion.7), channel_id=1, source_target_pairs={{0,8},{1,9},{2,10},{3,11},{4,0},{5,1},{6,2},{7,3},{8,12},{9,13},{1... | collective-permute-start | bytes 393224 | tf_op jit(solution)/shard_map/ppermute | solution.py:389
  129.3 14.7 %collective-permute-start.17 = (f32[32,8,128]{2,1,0:T(8,128)S(1)}, f32[32,8,128]{2,1,0:T(8,128)S(1)}, u32[]{:S(2)}, u32[]{:S(2)}) collective-permute-start(f32[32,8,128]{2,1,0:T(8,128)S(1)} %pad_maximum_fusion.8), channel_id=1, source_target_pairs={{0,4},{1,5},{2,6},{3,7},{4,12},{5,13},{6,14},{7,15},{8,0},{9,1},{1... | collective-permute-start | bytes 393224 | tf_op jit(solution)/shard_map/ppermute | solution.py:389
  145.5 6.8 %collective-permute-start.2 = (f32[32,8,128]{2,1,0:T(8,128)S(1)}, f32[32,8,128]{2,1,0:T(8,128)S(1)}, u32[]{:S(2)}, u32[]{:S(2)}) collective-permute-start(f32[32,8,128]{2,1,0:T(8,128)S(1)} %get-tuple-element.35), channel_id=1, source_target_pairs={{0,8},{1,9},{2,10},{3,11},{4,0},{5,1},{6,2},{7,3},{8,12},{9,13},{1... | collective-permute-start | bytes 393224 | tf_op jit(solution)/shard_map/ppermute | solution.py:389
  148.4 8.0 %collective-permute-start.4 = (f32[32,8,128]{2,1,0:T(8,128)S(1)}, f32[32,8,128]{2,1,0:T(8,128)S(1)}, u32[]{:S(2)}, u32[]{:S(2)}) collective-permute-start(f32[32,8,128]{2,1,0:T(8,128)S(1)} %get-tuple-element.36), channel_id=1, source_target_pairs={{0,4},{1,5},{2,6},{3,7},{4,12},{5,13},{6,14},{7,15},{8,0},{9,1},{1... | collective-permute-start | bytes 393224 | tf_op jit(solution)/shard_map/ppermute | solution.py:389
  148.6 17.3 %collective-permute-start.10 = (f32[32,8,128]{2,1,0:T(8,128)S(1)}, f32[32,8,128]{2,1,0:T(8,128)S(1)}, u32[]{:S(2)}, u32[]{:S(2)}) collective-permute-start(f32[32,8,128]{2,1,0:T(8,128)S(1)} %get-tuple-element.41), channel_id=1, source_target_pairs={{0,4},{1,5},{2,6},{3,7},{4,12},{5,13},{6,14},{7,15},{8,0},{9,1},{1... | collective-permute-start | bytes 393224 | tf_op jit(solution)/shard_map/ppermute | solution.py:389
  150.6 15.4 %collective-permute-start.8 = (f32[32,8,128]{2,1,0:T(8,128)S(1)}, f32[32,8,128]{2,1,0:T(8,128)S(1)}, u32[]{:S(2)}, u32[]{:S(2)}) collective-permute-start(f32[32,8,128]{2,1,0:T(8,128)S(1)} %get-tuple-element.40), channel_id=1, source_target_pairs={{0,8},{1,9},{2,10},{3,11},{4,0},{5,1},{6,2},{7,3},{8,12},{9,13},{1... | collective-permute-start | bytes 393224 | tf_op jit(solution)/shard_map/ppermute | solution.py:389
  156.5 12.0 %collective-permute-start.3 = (f32[64,8,128]{2,1,0:T(8,128)S(1)}, f32[64,8,128]{2,1,0:T(8,128)S(1)}, u32[]{:S(2)}, u32[]{:S(2)}) collective-permute-start(f32[64,8,128]{2,1,0:T(8,128)S(1)} %pad_maximum_fusion), channel_id=1, source_target_pairs={{0,8},{1,9},{2,10},{3,11},{4,0},{5,1},{6,2},{7,3},{8,12},{9,13},{1... | collective-permute-start | bytes 786440 | tf_op jit(solution)/shard_map/ppermute | solution.py:389
  157.6 19.6 %collective-permute-start.5 = (f32[64,8,128]{2,1,0:T(8,128)S(1)}, f32[64,8,128]{2,1,0:T(8,128)S(1)}, u32[]{:S(2)}, u32[]{:S(2)}) collective-permute-start(f32[64,8,128]{2,1,0:T(8,128)S(1)} %pad_maximum_fusion.1), channel_id=1, source_target_pairs={{0,4},{1,5},{2,6},{3,7},{4,12},{5,13},{6,14},{7,15},{8,0},{9,1},{1... | collective-permute-start | bytes 786440 | tf_op jit(solution)/shard_map/ppermute | solution.py:389
  166.0 11.7 %collective-permute-start.9 = (f32[64,8,128]{2,1,0:T(8,128)S(1)}, f32[64,8,128]{2,1,0:T(8,128)S(1)}, u32[]{:S(2)}, u32[]{:S(2)}) collective-permute-start(f32[64,8,128]{2,1,0:T(8,128)S(1)} %pad_maximum_fusion.2), channel_id=1, source_target_pairs={{0,8},{1,9},{2,10},{3,11},{4,0},{5,1},{6,2},{7,3},{8,12},{9,13},{1... | collective-permute-start | bytes 786440 | tf_op jit(solution)/shard_map/ppermute | solution.py:389
  166.1 17.6 %collective-permute-start.11 = (f32[64,8,128]{2,1,0:T(8,128)S(1)}, f32[64,8,128]{2,1,0:T(8,128)S(1)}, u32[]{:S(2)}, u32[]{:S(2)}) collective-permute-start(f32[64,8,128]{2,1,0:T(8,128)S(1)} %pad_maximum_fusion.3), channel_id=1, source_target_pairs={{0,4},{1,5},{2,6},{3,7},{4,12},{5,13},{6,14},{7,15},{8,0},{9,1},{1... | collective-permute-start | bytes 786440 | tf_op jit(solution)/shard_map/ppermute | solution.py:389
  184.7 65.4 %copy-start.15 = (s32[128]{0:T(128)S(1)}, s32[128]{0:T(128)}, u32[]{:S(2)}) copy-start(s32[128]{0:T(128)} %param.21) | copy-start | bytes 1540
  184.7 65.4 %copy-start.16 = (f32[5]{0:T(128)S(1)}, f32[5]{0:T(128)}, u32[]{:S(2)}) copy-start(f32[5]{0:T(128)} %param.22) | copy-start | bytes 64
  184.7 65.4 %copy-start.13 = (f32[3]{0:T(128)S(1)}, f32[3]{0:T(128)}, u32[]{:S(2)}) copy-start(f32[3]{0:T(128)} %param.20) | copy-start | bytes 40
  184.8 65.4 %copy-start.14 = (f32[128]{0:T(128)S(1)}, f32[128]{0:T(128)}, u32[]{:S(2)}) copy-start(f32[128]{0:T(128)} %param.19) | copy-start | bytes 1540
  184.8 75.2 %copy-start.18 = (s32[1,80]{1,0:T(1,128)S(1)}, s32[1,80]{1,0:T(1,128)}, u32[]{:S(2)}) copy-start(s32[1,80]{1,0:T(1,128)} %copy-done.17) | copy-start | bytes 964
  185.2 20.7 %copy-start = (f32[256,768]{1,0:T(8,128)}, f32[256,768]{1,0:T(8,128)S(1)}, u32[]{:S(2)}) copy-start(f32[256,768]{1,0:T(8,128)S(1)} %reshape.115.refs_2_.refs_3_) | copy-start | bytes 2359300
  185.2 19.4 %collective-permute-start.23 = (f32[256,768]{1,0:T(8,128)S(1)}, f32[256,768]{1,0:T(8,128)S(1)}, u32[]{:S(2)}, u32[]{:S(2)}) collective-permute-start(f32[256,768]{1,0:T(8,128)S(1)} %reshape.115.refs_2_.refs_3_), channel_id=1, source_target_pairs={{0,8},{1,9},{2,10},{3,11},{4,0},{5,1},{6,2},{7,3},{8,12},{9,13},{1... | collective-permute-start | bytes 2359304 | tf_op jit(solution)/shard_map/ppermute | solution.py:389
  185.8 21.9 %collective-permute-start.38 = (f32[256,768]{1,0:T(8,128)S(1)}, f32[256,768]{1,0:T(8,128)S(1)}, u32[]{:S(2)}, u32[]{:S(2)}) collective-permute-start(f32[256,768]{1,0:T(8,128)S(1)} %reshape.115.refs_2_.refs_3_), channel_id=1, source_target_pairs={{0,2},{1,3},{2,0},{3,1},{4,6},{5,7},{6,4},{7,5},{8,10},{9,11},{10,... | collective-permute-start | bytes 2359304 | tf_op jit(solution)/shard_map/ppermute | solution.py:389
  204.6 21.0 %copy-start.4 = (f32[256,768]{1,0:T(8,128)}, f32[256,768]{1,0:T(8,128)S(1)}, u32[]{:S(2)}) copy-start(f32[256,768]{1,0:T(8,128)S(1)} %collective-permute-done.23.refs_5_) | copy-start | bytes 2359300
  204.6 19.3 %collective-permute-start.24 = (f32[256,768]{1,0:T(8,128)S(1)}, f32[256,768]{1,0:T(8,128)S(1)}, u32[]{:S(2)}, u32[]{:S(2)}) collective-permute-start(f32[256,768]{1,0:T(8,128)S(1)} %reshape.115.refs_2_.refs_3_), channel_id=1, source_target_pairs={{0,4},{1,5},{2,6},{3,7},{4,12},{5,13},{6,14},{7,15},{8,0},{9,1},{1... | collective-permute-start | bytes 2359304 | tf_op jit(solution)/shard_map/ppermute | solution.py:389
  205.9 19.7 %collective-permute-start.41 = (f32[256,768]{1,0:T(8,128)S(1)}, f32[256,768]{1,0:T(8,128)S(1)}, u32[]{:S(2)}, u32[]{:S(2)}) collective-permute-start(f32[256,768]{1,0:T(8,128)S(1)} %reshape.115.refs_2_.refs_3_), channel_id=1, source_target_pairs={{0,1},{1,0},{2,3},{3,2},{4,5},{5,4},{6,7},{7,6},{8,9},{9,8},{10,11... | collective-permute-start | bytes 2359304 | tf_op jit(solution)/shard_map/ppermute | solution.py:389
  205.9 20.4 %collective-permute-start.36 = (f32[256,768]{1,0:T(8,128)S(1)}, f32[256,768]{1,0:T(8,128)S(1)}, u32[]{:S(2)}, u32[]{:S(2)}) collective-permute-start(f32[256,768]{1,0:T(8,128)S(1)} %collective-permute-done.23.refs_5_), channel_id=1, source_target_pairs={{0,2},{1,3},{2,0},{3,1},{4,6},{5,7},{6,4},{7,5},{8,10},{9,11},{10,... | collective-permute-start | bytes 2359304 | tf_op jit(solution)/shard_map/ppermute | solution.py:389
  207.5 18.9 %collective-permute-start.40 = (f32[256,768]{1,0:T(8,128)S(1)}, f32[256,768]{1,0:T(8,128)S(1)}, u32[]{:S(2)}, u32[]{:S(2)}) collective-permute-start(f32[256,768]{1,0:T(8,128)S(1)} %collective-permute-done.23.refs_5_), channel_id=1, source_target_pairs={{0,1},{1,0},{2,3},{3,2},{4,5},{5,4},{6,7},{7,6},{8,9},{9,8},{10,11... | collective-permute-start | bytes 2359304 | tf_op jit(solution)/shard_map/ppermute | solution.py:389
  207.7 43.1 %copy-start.7 = (f32[256,768]{1,0:T(8,128)}, f32[256,768]{1,0:T(8,128)S(1)}, u32[]{:S(2)}) copy-start(f32[256,768]{1,0:T(8,128)S(1)} %collective-permute-done.38.refs_3_) | copy-start | bytes 2359300
  207.7 20.3 %collective-permute-start.39 = (f32[256,768]{1,0:T(8,128)S(1)}, f32[256,768]{1,0:T(8,128)S(1)}, u32[]{:S(2)}, u32[]{:S(2)}) collective-permute-start(f32[256,768]{1,0:T(8,128)S(1)} %collective-permute-done.38.refs_3_), channel_id=1, source_target_pairs={{0,1},{1,0},{2,3},{3,2},{4,5},{5,4},{6,7},{7,6},{8,9},{9,8},{10,11... | collective-permute-start | bytes 2359304 | tf_op jit(solution)/shard_map/ppermute | solution.py:389
  223.9 2.4 copy-start.5
  223.9 26.2 %collective-permute-start.33 = (f32[256,768]{1,0:T(8,128)S(1)}, f32[256,768]{1,0:T(8,128)}, u32[]{:S(2)}, u32[]{:S(2)}) collective-permute-start(f32[256,768]{1,0:T(8,128)S(1)} %collective-permute-done.24.refs_3_), channel_id=1, source_target_pairs={{0,2},{1,3},{2,0},{3,1},{4,6},{5,7},{6,4},{7,5},{8,10},{9,11},{10,... | collective-permute-start | bytes 2359304 | tf_op jit(solution)/shard_map/ppermute | solution.py:389
  225.6 24.6 %copy-start.6 = (f32[256,768]{1,0:T(8,128)}, f32[256,768]{1,0:T(8,128)S(1)}, u32[]{:S(2)}) copy-start(f32[256,768]{1,0:T(8,128)S(1)} %collective-permute-done.41.refs_4_) | copy-start | bytes 2359300
  225.6 24.6 %collective-permute-start.35 = (f32[256,768]{1,0:T(8,128)S(1)}, f32[256,768]{1,0:T(8,128)S(1)}, u32[]{:S(2)}, u32[]{:S(2)}) collective-permute-start(f32[256,768]{1,0:T(8,128)S(1)} %collective-permute-done.24.refs_3_), channel_id=1, source_target_pairs={{0,1},{1,0},{2,3},{3,2},{4,5},{5,4},{6,7},{7,6},{8,9},{9,8},{10,11... | collective-permute-start | bytes 2359304 | tf_op jit(solution)/shard_map/ppermute | solution.py:389
  226.3 24.5 %copy-start.8 = (f32[256,768]{1,0:T(8,128)}, f32[256,768]{1,0:T(8,128)S(1)}, u32[]{:S(2)}) copy-start(f32[256,768]{1,0:T(8,128)S(1)} %collective-permute-done.36.refs_5_) | copy-start | bytes 2359300
  226.3 24.4 %collective-permute-start.37 = (f32[256,768]{1,0:T(8,128)S(1)}, f32[256,768]{1,0:T(8,128)S(1)}, u32[]{:S(2)}, u32[]{:S(2)}) collective-permute-start(f32[256,768]{1,0:T(8,128)S(1)} %collective-permute-done.36.refs_5_), channel_id=1, source_target_pairs={{0,1},{1,0},{2,3},{3,2},{4,5},{5,4},{6,7},{7,6},{8,9},{9,8},{10,11... | collective-permute-start | bytes 2359304 | tf_op jit(solution)/shard_map/ppermute | solution.py:389
  226.4 24.5 %copy-start.9 = (f32[256,768]{1,0:T(8,128)}, f32[256,768]{1,0:T(8,128)S(1)}, u32[]{:S(2)}) copy-start(f32[256,768]{1,0:T(8,128)S(1)} %collective-permute-done.40.refs_6_) | copy-start | bytes 2359300
  226.4 11.8 %collective-permute-start.25 = (f32[128,768]{1,0:T(8,128)S(1)}, f32[128,768]{1,0:T(8,128)}, u32[]{:S(2)}, u32[]{:S(2)}) collective-permute-start(f32[128,768]{1,0:T(8,128)S(1)} %slice.254), channel_id=1, source_target_pairs={{0,8},{1,9},{2,10},{3,11},{4,0},{5,1},{6,2},{7,3},{8,12},{9,13},{1... | collective-permute-start | bytes 1179656 | tf_op jit(solution)/shard_map/ppermute | solution.py:389
  228.0 23.3 %copy-start.10 = (f32[256,768]{1,0:T(8,128)}, f32[256,768]{1,0:T(8,128)S(1)}, u32[]{:S(2)}) copy-start(f32[256,768]{1,0:T(8,128)S(1)} %collective-permute-done.39.refs_4_) | copy-start | bytes 2359300
  228.0 20.5 %collective-permute-start.27 = (f32[128,768]{1,0:T(8,128)S(1)}, f32[128,768]{1,0:T(8,128)}, u32[]{:S(2)}, u32[]{:S(2)}) collective-permute-start(f32[128,768]{1,0:T(8,128)S(1)} %slice.255), channel_id=1, source_target_pairs={{0,4},{1,5},{2,6},{3,7},{4,12},{5,13},{6,14},{7,15},{8,0},{9,1},{1... | collective-permute-start | bytes 1179656 | tf_op jit(solution)/shard_map/ppermute | solution.py:389
  238.1 13.1 %collective-permute-start.26 = (f32[128,768]{1,0:T(8,128)}, f32[128,768]{1,0:T(8,128)}, u32[]{:S(2)}, u32[]{:S(2)}) collective-permute-start(f32[128,768]{1,0:T(8,128)} %collective-permute-done.25.refs_3_), channel_id=1, source_target_pairs={{0,2},{1,3},{2,0},{3,1},{4,6},{5,7},{6,4},{7,5},{8,10},{9,11},{10,... | collective-permute-start | bytes 1179656 | tf_op jit(solution)/shard_map/ppermute | solution.py:389
  248.5 11.4 %collective-permute-start.28 = (f32[128,768]{1,0:T(8,128)}, f32[128,768]{1,0:T(8,128)}, u32[]{:S(2)}, u32[]{:S(2)}) collective-permute-start(f32[128,768]{1,0:T(8,128)} %collective-permute-done.27.refs_4_), channel_id=1, source_target_pairs={{0,2},{1,3},{2,0},{3,1},{4,6},{5,7},{6,4},{7,5},{8,10},{9,11},{10,... | collective-permute-start | bytes 1179656 | tf_op jit(solution)/shard_map/ppermute | solution.py:389
  250.1 57.6 %collective-permute-start.34 = (f32[256,768]{1,0:T(8,128)}, f32[256,768]{1,0:T(8,128)}, u32[]{:S(2)}, u32[]{:S(2)}) collective-permute-start(f32[256,768]{1,0:T(8,128)} %collective-permute-done.33.refs_7_), channel_id=1, source_target_pairs={{0,1},{1,0},{2,3},{3,2},{4,5},{5,4},{6,7},{7,6},{8,9},{9,8},{10,11... | collective-permute-start | bytes 2359304 | tf_op jit(solution)/shard_map/ppermute | solution.py:389
  250.2 1.2 copy-start.11
  250.2 57.5 %collective-permute-start.31 = (f32[128,768]{1,0:T(8,128)}, f32[128,768]{1,0:T(8,128)}, u32[]{:S(2)}, u32[]{:S(2)}) collective-permute-start(f32[128,768]{1,0:T(8,128)} %collective-permute-done.25.refs_3_), channel_id=1, source_target_pairs={{0,1},{1,0},{2,3},{3,2},{4,5},{5,4},{6,7},{7,6},{8,9},{9,8},{10,11... | collective-permute-start | bytes 1179656 | tf_op jit(solution)/shard_map/ppermute | solution.py:389
  250.8 9.1 %copy-start.12 = (f32[256,768]{1,0:T(8,128)}, f32[256,768]{1,0:T(8,128)S(1)}, u32[]{:S(2)}) copy-start(f32[256,768]{1,0:T(8,128)S(1)} %collective-permute-done.37.refs_6_) | copy-start | bytes 2359300
  250.8 56.9 %collective-permute-start.32 = (f32[128,768]{1,0:T(8,128)}, f32[128,768]{1,0:T(8,128)}, u32[]{:S(2)}, u32[]{:S(2)}) collective-permute-start(f32[128,768]{1,0:T(8,128)} %collective-permute-done.27.refs_4_), channel_id=1, source_target_pairs={{0,1},{1,0},{2,3},{3,2},{4,5},{5,4},{6,7},{7,6},{8,9},{9,8},{10,11... | collective-permute-start | bytes 1179656 | tf_op jit(solution)/shard_map/ppermute | solution.py:389
  251.3 74.2 %collective-permute-start.29 = (f32[128,768]{1,0:T(8,128)}, f32[128,768]{1,0:T(8,128)}, u32[]{:S(2)}, u32[]{:S(2)}) collective-permute-start(f32[128,768]{1,0:T(8,128)} %collective-permute-done.26.refs_3_), channel_id=1, source_target_pairs={{0,1},{1,0},{2,3},{3,2},{4,5},{5,4},{6,7},{7,6},{8,9},{9,8},{10,11... | collective-permute-start | bytes 1179656 | tf_op jit(solution)/shard_map/ppermute | solution.py:389
  259.9 65.5 %collective-permute-start.30 = (f32[128,768]{1,0:T(8,128)}, f32[128,768]{1,0:T(8,128)}, u32[]{:S(2)}, u32[]{:S(2)}) collective-permute-start(f32[128,768]{1,0:T(8,128)} %collective-permute-done.28.refs_4_), channel_id=1, source_target_pairs={{0,1},{1,0},{2,3},{3,2},{4,5},{5,4},{6,7},{7,6},{8,9},{9,8},{10,11... | collective-permute-start | bytes 1179656 | tf_op jit(solution)/shard_map/ppermute | solution.py:389

commit v5 on v3

--- a/solution.py
+++ b/solution.py
@@ -11,6 +11,7 @@
 from jax.sharding import PartitionSpec as P
 
 
+VMEM_BYTES = 64 * 2**20
 LANES = 128
 SUB = 8
 SLOTS = 4
@@ -206,6 +207,7 @@
             pltpu.SemaphoreType.DMA((slots + 1,)),
             pltpu.SemaphoreType.DMA((3,)),
         ],
+        compiler_params=pltpu.CompilerParams(vmem_limit_bytes=VMEM_BYTES),
         name="transform",
     )(col, phase, val, cond, dz, dy, dyr, cs)
 
@@ -275,74 +277,80 @@
     )(weights, own, everyone)
 
 
-def chi_group_kernel(counts, with_old, *refs):
-    total = sum(counts)
-    n = len(counts)
-    _, w_ref, own_ref = refs[:3]
-    pieces = refs[3 : 3 + total]
-    rest = refs[3 + total + (2 if with_old else 0) :]
-    real_ref, imag_ref, left_scr, got_scr, sems = rest
-    step = pl.program_id(0)
-
-    def copies(i):
-        at, first = 0, sum(counts[:i])
-        for j in range(counts[i]):
-            ref = pieces[first + j]
-            yield pltpu.make_async_copy(
-                ref, got_scr.at[i, pl.ds(at, ref.shape[0])], sems.at[first + j]
+def chi_group_kernel(n, first, ids_ref, w_ref, own_ref, *refs):
+    pieces = refs[:n]
+    outs = refs[-7:-5]
+    left_scr, got_scr, out_scr, in_sems, out_sems = refs[-5:]
+    rows, pairs2 = own_ref.shape
+    freqs = w_ref.shape[0]
+
+    def piece(i):
+        return pltpu.make_async_copy(pieces[i], got_scr.at[i], in_sems.at[i])
+
+    def result(i, half):
+        at = pl.ds(pl.multiple_of(ids_ref[first + i] * rows, rows), rows)
+        slot = i % 2
+        return pltpu.make_async_copy(
+            out_scr.at[slot, half], outs[half].at[:, :, at], out_sems.at[slot, half]
+        )
+
+    for i in range(n):
+        piece(i).start()
+    fill_left(w_ref, own_ref, left_scr)
+    for i in range(n):
+        piece(i).wait()
+
+    def block(i, carry):
+        value = got_scr[i]
+        turned = jnp.concatenate([-value[:, pairs2 // 2 :], value[:, : pairs2 // 2]], axis=1)
+        for half, side in enumerate((value, turned)):
+            high, low = split_lanes(side)
+            right = jnp.concatenate([high, low, high], axis=1)
+
+            @pl.when(i >= 2)
+            def _(half=half):
+                result(i - 2, half).wait()
+
+            got = lax.dot_general(
+                left_scr[...], right, (((1,), (1,)), ((), ())), preferred_element_type=f32
             )
-            at += ref.shape[0]
-
-    @pl.when(step == 0)
-    def _():
-        for i in range(n):
-            for copy in copies(i):
-                copy.start()
-        fill_left(w_ref, own_ref, left_scr)
-
-    for i in range(n):
-
-        @pl.when(step == i)
-        def _(i=i):
-            for copy in copies(i):
-                copy.wait()
-
-    chi_tile(got_scr[step], left_scr, real_ref, imag_ref)
+            out_scr[i % 2, half] = got.reshape(freqs, rows, rows)
+            result(i, half).start()
+        return carry
+
+    lax.fori_loop(0, n, block, 0)
+    for i in range(max(n - 2, 0), n):
+        for half in range(2):
+            result(i, half).wait()
 
 
 def chi_group(weights, own, blocks, ids, first, num_g, old):
     freqs, pairs = weights.shape
     rows = own.shape[0]
-    counts = tuple(len(b) for b in blocks)
-    pieces = [p for b in blocks for p in b]
+    n = len(blocks)
     out = jax.ShapeDtypeStruct((freqs, rows, num_g), f32)
-    out_spec = pl.BlockSpec((freqs, rows, rows), lambda t, ids: (0, 0, ids[first + t]))
     hbm = pl.BlockSpec(memory_space=pl.ANY)
+    vmem = pl.BlockSpec(memory_space=pltpu.VMEM)
     olds = () if old is None else old
     return pl.pallas_call(
-        functools.partial(chi_group_kernel, counts, old is not None),
-        grid_spec=pltpu.PrefetchScalarGridSpec(
-            num_scalar_prefetch=1,
-            grid=(len(blocks),),
-            in_specs=[
-                pl.BlockSpec((freqs, pairs), lambda t, ids: (0, 0)),
-                pl.BlockSpec((rows, 2 * pairs), lambda t, ids: (0, 0)),
-            ]
-            + [hbm] * (len(pieces) + len(olds)),
-            out_specs=(out_spec, out_spec),
-            scratch_shapes=[
-                pltpu.VMEM((freqs * rows, 6 * pairs), bf16),
-                pltpu.VMEM((len(blocks), rows, 2 * pairs), f32),
-                pltpu.SemaphoreType.DMA((len(pieces),)),
-            ],
-        ),
+        functools.partial(chi_group_kernel, n, first),
+        in_specs=[pl.BlockSpec(memory_space=pltpu.SMEM), vmem, vmem] + [hbm] * (n + len(olds)),
+        out_specs=(hbm, hbm),
+        scratch_shapes=[
+            pltpu.VMEM((freqs * rows, 6 * pairs), bf16),
+            pltpu.VMEM((n, rows, 2 * pairs), f32),
+            pltpu.VMEM((2, 2, freqs, rows, rows), f32),
+            pltpu.SemaphoreType.DMA((n,)),
+            pltpu.SemaphoreType.DMA((2, 2)),
+        ],
         out_shape=(out, out),
-        input_output_aliases={3 + len(pieces) + i: i for i in range(len(olds))},
+        input_output_aliases={3 + n + i: i for i in range(len(olds))},
+        compiler_params=pltpu.CompilerParams(vmem_limit_bytes=VMEM_BYTES),
         name="chi",
-    )(ids, weights, own, *pieces, *olds)
-
-
-GROUPS = (((0, 0),), ((1, 0),), ((0, 1), (0, 3)), ((0, 2),), ((1, 1), (1, 3)), ((1, 2),))
+    )(ids, weights, own, *blocks, *olds)
+
+
+GROUPS = (((0, 0),), ((1, 0), (0, 3)), ((0, 1), (1, 3)), ((0, 2), (1, 1)), ((1, 2),))
 RING = (0, 2, 3, 1)
 
 
@@ -381,44 +389,38 @@
     return lax.ppermute(value, "blk", pairs)
 
 
-def reduce_scatter(keep, other, links, ahead):
+def reduce_scatter(keep, other, links, before):
     half = keep.shape[0] // 2
     got = send(other, links.core)
     far = send(keep[half:] + got[half:], links.y)
-    if ahead:
-        far, ahead = lax.optimization_barrier((far, ahead))
+    if before:
+        far, *_ = lax.optimization_barrier((far, *before))
     near = keep[:half] + got[:half] + far
     block = half // 4
-    part = block // 2
-    cw = send(near[2 * block : 2 * block + part], links.cw)
-    ccw = send(near[2 * block + part : 3 * block], links.ccw)
-    cw, ccw = lax.optimization_barrier((cw, ccw))
-    to_cw = jnp.concatenate([near[block : block + part] + cw, near[block + part : 2 * block]])
-    to_ccw = jnp.concatenate([near[3 * block : 3 * block + part], near[3 * block + part :] + ccw])
-    from_cw = send(to_cw, links.cw)
-    from_ccw = send(to_ccw, links.ccw)
-    from_cw, from_ccw = lax.optimization_barrier((from_cw, from_ccw))
-    return near[:block], from_cw, from_ccw
+    to_cw, to_ccw, next_cw, mine = lax.optimization_barrier(
+        tuple(near[i * block : (i + 1) * block] for i in (2, 3, 1, 0))
+    )
+    two_back = send(to_cw, links.cw)
+    ahead = send(to_ccw, links.ccw)
+    next_cw = next_cw + two_back
+    back = send(next_cw, links.cw)
+    return mine, ahead, back
 
 
 def gather_and_chi(weights, own, links, ids, num_g):
-    part = own.shape[0] // 2
-
-    def over(pieces, pairs):
-        return [send(p, pairs) for p in pieces]
-
-    mine = {(0, 0): [own]}
-    mine[0, 3] = over([own], links.cw)
-    mine[0, 1] = over([own], links.ccw)
-    mine[0, 2] = [send(mine[0, 3][0][:part], links.cw), send(mine[0, 1][0][part:], links.ccw)]
+    cw = send(own, links.cw)
+    later, cw = lax.optimization_barrier((own, cw))
+    ccw = send(later, links.ccw)
+    cw_later, ccw = lax.optimization_barrier((cw, ccw))
+    mine = {(0, 0): own, (0, 3): cw, (0, 1): ccw, (0, 2): send(cw_later, links.cw)}
     for r in range(4):
-        mine[1, r] = over(mine[0, r], links.y)
+        mine[1, r] = send(mine[0, r], links.y)
     old = None
     first = 0
     for group in GROUPS:
         blocks = []
         for b, r in group:
-            blocks += [mine[b, r], over(mine[b, r], links.core)]
+            blocks += [mine[b, r], send(mine[b, r], links.core)]
         old = chi_group(weights, own, blocks, ids, first, num_g, old)
         first += len(blocks)
     return old
@@ -469,19 +471,22 @@
     count = lax.axis_size("blk")
     links = Links(count) if Links.fits(count) else None
     if links is not None:
-        near = jnp.asarray(links.near)[lax.axis_index("blk")]
-        ids = jnp.asarray(links.order.reshape(count, -1))[lax.axis_index("blk")]
-        pick = pick.reshape(2, count, -1)[:, near.reshape(-1)].reshape(2, -1)
+        tables = np.concatenate([x.reshape(count, -1) for x in (links.near, links.order)], axis=1)
+        table = jnp.asarray(tables)[lax.axis_index("blk")]
+        pick = pick.reshape(2, count, -1)[:, table[:count]].reshape(2, -1)
+        ids = table[count:]
     owned = []
     for c in range(num_cond):
         keep, other = transform(pick[0], pick[1], val, cond[c], cs, num_g)
-        if links is not None:
-            ahead = owned[-1][1:] if c == num_cond - 1 else ()
-            owned.append(reduce_scatter(keep, other, links, ahead))
-        else:
+        if links is None:
             whole = jnp.concatenate([keep, other])
             owned.append((lax.psum_scatter(whole, "blk", scatter_dimension=0, tiled=True),))
-    own = jnp.stack([sum(parts) for parts in owned]).reshape(num_cond, -1, 2, 4, num_val)
+        else:
+            before = owned[-1][1:] if c == num_cond - 1 else ()
+            owned.append(reduce_scatter(keep, other, links, before))
+    for c, parts in enumerate(owned):
+        owned[c] = sum(parts[1:], parts[0])
+    own = jnp.stack(owned).reshape(num_cond, -1, 2, 4, num_val)
     own = jnp.transpose(own, (1, 3, 2, 0, 4)).reshape(-1, 2 * pairs)
 
     gaps = e_val[None, :] - e_cond[:, None]

time: 347 us -> 407 us (1.17)
  Pallas kernels: 149 us -> 194 us
  starting transfers between devices: 32.7 us -> 40.6 us
  waiting for transfers between devices: 144 us -> 150 us
    pallas_call x6 -> x5, Pallas kernels: 79.8 us -> 126 us  [chi_group(): pl.pallas_call(functools.partial(chi_group_kernel, n, first), in_specs=[p...]
    ppermute x37 -> x30, starting transfers between devices: 32.7 us -> 40.6 us  [send(): return lax.ppermute(value, 'blk', pairs)]
    ppermute x37 -> x30, waiting for transfers between devices: 144 us -> 150 us  [send(): return lax.ppermute(value, 'blk', pairs)]
  transfers between devices with their start and end apart: 37 -> 30, of which waited for: 17 -> 15; matrix products, arithmetic and copies ran while one was open for 3% -> 2% of each run, Pallas kernels for 33% -> 38%
where the time goes in v5:
time: 407 us; the launch traced here: 406 us
  Pallas kernels  194 us (48%)
  waiting for transfers between devices  150 us (37%)
  starting transfers between devices  40.6 us (10%)
  local copies, waits for them, and re-layouts  11.1 us (3%)
  other arithmetic  8.91 us (2%)
    ppermute x30, waiting for transfers between devices, send(): return lax.ppermute(value, 'blk', pairs)  150 us
    pallas_call x5, Pallas kernels, chi_group(): pl.pallas_call(functools.partial(chi_group_kernel, n, first), in_specs=[p...  126 us
    pallas_call x3, Pallas kernels, transform(): pl.pallas_call(transform_kernel, out_shape=(jax.ShapeDtypeStruct((num_g /...  68.5 us
    ppermute x30, starting transfers between devices, send(): return lax.ppermute(value, 'blk', pairs)  40.6 us
  transfers between devices with their start and end apart: 30, of which 15 were waited for; matrix products, arithmetic and copies ran while one was open for 2% of the time, Pallas kernels for 38%

profile of v5, /device:TPU:0, one launch (start us, length us, event | category | flops | bytes accessed | tf_op | source)
XLA Modules:
  0.0 406.1 jit_solution(3886949644500271590)
XLA Ops:
  1.1 0.7 constant_dynamic-slice_fusion
  1.8 0.5 copy-done.13
  2.4 0.8 fusion.4
  3.2 0.6 gather_fusion
  3.8 0.7 fusion.28
  4.4 1.9 copy.34
  6.4 1.7 slice_bitcast_fusion.2
  8.1 1.3 broadcast_in_dim.12.cs_hbm
  9.4 22.8 %transform.4 = (f32[512,8,128]{2,1,0:T(8,128)}, f32[512,8,128]{2,1,0:T(8,128)}) custom-call(s32[4096]{0:T(1024)} %bitcast.48, s32[4096]{0:T(1024)} %bitcast.45, f32[4,64,64,128]{3,2,1,0:T(8,128)} %bitcast.37, f32[4,8,64,8]{3,2,1,0:T(8,128)} %get-tuple-element.66.cond_ref, bf16[64,192]{1,0:T(8,128)(2,1)} %constant.92.clone.dz_ref, ...), custom_call_target="tpu_custom_call" | custom-call | tf_op jit(solution)/shard_map/transform/pallas_call | solution.py:196
  32.2 0.6 collective-permute-start.5
  32.8 22.9 %transform.3 = (f32[512,8,128]{2,1,0:T(8,128)}, f32[512,8,128]{2,1,0:T(8,128)}) custom-call(s32[4096]{0:T(1024)} %bitcast.49, s32[4096]{0:T(1024)} %bitcast.46, f32[4,64,64,128]{3,2,1,0:T(8,128)} %bitcast.38, f32[4,8,64,8]{3,2,1,0:T(8,128)} %get-tuple-element.64.cond_ref, bf16[64,192]{1,0:T(8,128)(2,1)} %constant.92.clone.dz_ref, ...), custom_call_target="tpu_custom_call" | custom-call | tf_op jit(solution)/shard_map/transform/pallas_call | solution.py:196
  55.7 22.9 %transform.5 = (f32[512,8,128]{2,1,0:T(8,128)}, f32[512,8,128]{2,1,0:T(8,128)}) custom-call(s32[4096]{0:T(1024)} %bitcast.50, s32[4096]{0:T(1024)} %bitcast.47, f32[4,64,64,128]{3,2,1,0:T(8,128)} %bitcast.39, f32[4,8,64,8]{3,2,1,0:T(8,128)} %get-tuple-element.65.cond_ref, bf16[64,192]{1,0:T(8,128)(2,1)} %constant.92.clone.dz_ref, ...), custom_call_target="tpu_custom_call" | custom-call | tf_op jit(solution)/shard_map/transform/pallas_call | solution.py:196
  78.6 0.5 collective-permute-start.10
  79.1 1.8 slice_add_fusion.2
  80.9 2.7 collective-permute-start.6
  83.6 1.4 slice_add_fusion.4
  85.0 0.5 collective-permute-start.1
  85.6 1.7 collective-permute-start.11
  87.3 20.3 %collective-permute-done.6 = f32[256,8,128]{2,1,0:T(8,128)S(1)} collective-permute-done((f32[256,8,128]{2,1,0:T(8,128)S(1)}, f32[256,8,128]{2,1,0:T(8,128)S(1)}, u32[]{:S(2)}, u32[]{:S(2)}) %collective-permute-start.6) | collective-permute-done | bytes 1048608 | tf_op jit(solution)/shard_map/ppermute | solution.py:389
  107.6 1.4 fusion.1
  109.1 3.1 collective-permute-start.8
  112.2 6.7 %collective-permute-done.8 = f32[64,8,128]{2,1,0:T(8,128)S(1)} collective-permute-done((f32[64,8,128]{2,1,0:T(8,128)S(1)}, f32[64,8,128]{2,1,0:T(8,128)S(1)}, u32[]{:S(2)}, u32[]{:S(2)}) %collective-permute-start.8) | collective-permute-done | bytes 262176 | tf_op jit(solution)/shard_map/ppermute | solution.py:389
  118.9 3.4 collective-permute-start.9
  122.4 7.7 %collective-permute-done.1 = f32[256,8,128]{2,1,0:T(8,128)S(1)} collective-permute-done((f32[256,8,128]{2,1,0:T(8,128)S(1)}, f32[256,8,128]{2,1,0:T(8,128)S(1)}, u32[]{:S(2)}, u32[]{:S(2)}) %collective-permute-start.1) | collective-permute-done | bytes 1048608 | tf_op jit(solution)/shard_map/ppermute | solution.py:389
  130.1 1.4 fusion.2
  131.6 3.1 collective-permute-start.3
  134.7 17.6 %collective-permute-done.11 = f32[256,8,128]{2,1,0:T(8,128)S(1)} collective-permute-done((f32[256,8,128]{2,1,0:T(8,128)S(1)}, f32[256,8,128]{2,1,0:T(8,128)S(1)}, u32[]{:S(2)}, u32[]{:S(2)}) %collective-permute-start.11) | collective-permute-done | bytes 1048608 | tf_op jit(solution)/shard_map/ppermute | solution.py:389
  152.5 2.8 collective-permute-start.13
  155.4 3.0 collective-permute-start.4
  158.4 4.1 %collective-permute-done.13 = f32[64,8,128]{2,1,0:T(8,128)S(1)} collective-permute-done((f32[64,8,128]{2,1,0:T(8,128)S(1)}, f32[64,8,128]{2,1,0:T(8,128)S(1)}, u32[]{:S(2)}, u32[]{:S(2)}) %collective-permute-start.13) | collective-permute-done | bytes 262176 | tf_op jit(solution)/shard_map/ppermute | solution.py:389
  162.5 5.4 %collective-permute-start.14 = (f32[64,8,128]{2,1,0:T(8,128)S(1)}, f32[64,8,128]{2,1,0:T(8,128)S(1)}, u32[]{:S(2)}, u32[]{:S(2)}) collective-permute-start(f32[64,8,128]{2,1,0:T(8,128)S(1)} %add.147), channel_id=1, source_target_pairs={{0,8},{1,9},{2,10},{3,11},{4,0},{5,1},{6,2},{7,3},{8,12},{9,13},{1... | collective-permute-start | bytes 786440 | tf_op jit(solution)/shard_map/ppermute | solution.py:389
  167.9 1.8 collective-permute-done.2
  169.7 4.0 collective-permute-done.4
  173.7 0.3 copy.36
  174.1 0.3 copy.37
  174.3 6.5 %collective-permute-done.12 = f32[64,8,128]{2,1,0:T(8,128)S(1)} collective-permute-done((f32[64,8,128]{2,1,0:T(8,128)S(1)}, f32[64,8,128]{2,1,0:T(8,128)S(1)}, u32[]{:S(2)}, u32[]{:S(2)}) %collective-permute-start.12) | collective-permute-done | bytes 262176 | tf_op jit(solution)/shard_map/ppermute | solution.py:389
  180.9 2.3 collective-permute-done.14
  183.3 0.3 copy.38
  183.6 0.7 maximum_bitcast_fusion
  184.3 0.4 reshape.108.own_ref.refs_0_
  184.7 3.4 collective-permute-start.15
  188.1 15.7 %collective-permute-done.15.refs_2_ = f32[256,768]{1,0:T(8,128)S(1)} collective-permute-done((f32[256,768]{1,0:T(8,128)S(1)}, f32[256,768]{1,0:T(8,128)S(1)}, u32[]{:S(2)}, u32[]{:S(2)}) %collective-permute-start.15) | collective-permute-done | bytes 786464 | tf_op jit(solution)/shard_map/ppermute | solution.py:389
  203.8 2.4 collective-permute-start.16
  206.2 1.5 collective-permute-start.26
  207.8 15.1 %collective-permute-done.16.refs_0_ = f32[256,768]{1,0:T(8,128)} collective-permute-done((f32[256,768]{1,0:T(8,128)S(1)}, f32[256,768]{1,0:T(8,128)}, u32[]{:S(2)}, u32[]{:S(2)}) %collective-permute-start.16) | collective-permute-done | bytes 786464 | tf_op jit(solution)/shard_map/ppermute | solution.py:389
  222.8 2.1 collective-permute-start.17
  224.9 1.7 collective-permute-start.24
  226.6 0.2 collective-permute-start.27
  226.8 0.9 copy-done.4
  227.8 0.3 collective-permute-start.21
  228.1 11.6 %collective-permute-done.17.refs_0_ = f32[256,768]{1,0:T(8,128)} collective-permute-done((f32[256,768]{1,0:T(8,128)S(1)}, f32[256,768]{1,0:T(8,128)}, u32[]{:S(2)}, u32[]{:S(2)}) %collective-permute-start.17) | collective-permute-done | bytes 786464 | tf_op jit(solution)/shard_map/ppermute | solution.py:389
  239.7 1.6 collective-permute-start.18
  241.3 4.2 %collective-permute-done.24.refs_2_ = f32[256,768]{1,0:T(8,128)} collective-permute-done((f32[256,768]{1,0:T(8,128)S(1)}, f32[256,768]{1,0:T(8,128)}, u32[]{:S(2)}, u32[]{:S(2)}) %collective-permute-start.24) | collective-permute-done | bytes 786464 | tf_op jit(solution)/shard_map/ppermute | solution.py:389
  245.5 0.6 collective-permute-start.20
  246.0 0.4 copy-done.8
  246.4 15.9 %collective-permute-done.21.refs_2_ = f32[256,768]{1,0:T(8,128)} collective-permute-done((f32[256,768]{1,0:T(8,128)}, f32[256,768]{1,0:T(8,128)}, u32[]{:S(2)}, u32[]{:S(2)}) %collective-permute-start.21) | collective-permute-done | bytes 786464 | tf_op jit(solution)/shard_map/ppermute | solution.py:389
  262.3 16.4 %collective-permute-done.18.refs_0_ = f32[256,768]{1,0:T(8,128)} collective-permute-done((f32[256,768]{1,0:T(8,128)}, f32[256,768]{1,0:T(8,128)}, u32[]{:S(2)}, u32[]{:S(2)}) %collective-permute-start.18) | collective-permute-done | bytes 786464 | tf_op jit(solution)/shard_map/ppermute | solution.py:389
  278.7 0.6 slice_bitcast_fusion.3.ids_ref
  279.4 0.7 divide_multiply_fusion.w_ref
  280.1 16.9 %chi.5 = (f32[5,256,4096]{2,1,0:T(8,128)}, f32[5,256,4096]{2,1,0:T(8,128)}) custom-call(s32[16]{0:T(128)} %slice_bitcast_fusion.3.ids_ref, f32[5,384]{1,0:T(8,128)} %divide_multiply_fusion.w_ref, f32[256,768]{1,0:T(8,128)} %copy-done, f32[256,768]{1,0:T(8,128)} %copy-done, f32[256,768]{1,0:T(8,128)} %copy-done.4), custom_call_target="tpu_custom_call" | custom-call | tf_op jit(solution)/shard_map/chi/pallas_call | solution.py:335
  297.0 30.6 %chi.6 = (f32[5,256,4096]{2,1,0:T(8,128)}, f32[5,256,4096]{2,1,0:T(8,128)}) custom-call(s32[16]{0:T(128)} %slice_bitcast_fusion.3.ids_ref, f32[5,384]{1,0:T(8,128)} %divide_multiply_fusion.w_ref, f32[256,768]{1,0:T(8,128)} %copy-done, f32[256,768]{1,0:T(8,128)} %copy-done.6, f32[256,768]{1,0:T(8,128)} %copy-done.8, ...), custom_call_target="tpu_custom_call", output_to_operand_aliasing={{0}: (7, {}), {1}: (8, {})} | custom-call | tf_op jit(solution)/shard_map/chi/pallas_call | solution.py:335
  327.6 30.7 %chi.7 = (f32[5,256,4096]{2,1,0:T(8,128)}, f32[5,256,4096]{2,1,0:T(8,128)}) custom-call(s32[16]{0:T(128)} %slice_bitcast_fusion.3.ids_ref, f32[5,384]{1,0:T(8,128)} %divide_multiply_fusion.w_ref, f32[256,768]{1,0:T(8,128)} %copy-done, f32[256,768]{1,0:T(8,128)} %collective-permute-done.16.refs_0_, ...), custom_call_target="tpu_custom_call", output_to_operand_aliasing={{0}: (7, {}), {1}: (8, {})} | custom-call | tf_op jit(solution)/shard_map/chi/pallas_call | solution.py:335
  358.4 30.6 %chi.8 = (f32[5,256,4096]{2,1,0:T(8,128)}, f32[5,256,4096]{2,1,0:T(8,128)}) custom-call(s32[16]{0:T(128)} %slice_bitcast_fusion.3.ids_ref, f32[5,384]{1,0:T(8,128)} %divide_multiply_fusion.w_ref, f32[256,768]{1,0:T(8,128)} %copy-done, f32[256,768]{1,0:T(8,128)} %collective-permute-done.17.refs_0_, ...), custom_call_target="tpu_custom_call", output_to_operand_aliasing={{0}: (7, {}), {1}: (8, {})} | custom-call | tf_op jit(solution)/shard_map/chi/pallas_call | solution.py:335
  389.0 16.9 %chi.9 = (f32[5,256,4096]{2,1,0:T(8,128)}, f32[5,256,4096]{2,1,0:T(8,128)}) custom-call(s32[16]{0:T(128)} %slice_bitcast_fusion.3.ids_ref, f32[5,384]{1,0:T(8,128)} %divide_multiply_fusion.w_ref, f32[256,768]{1,0:T(8,128)} %copy-done, f32[256,768]{1,0:T(8,128)} %collective-permute-done.18.refs_0_, ...), custom_call_target="tpu_custom_call", output_to_operand_aliasing={{0}: (5, {}), {1}: (6, {})} | custom-call | tf_op jit(solution)/shard_map/chi/pallas_call | solution.py:335
  (76 shorter events, 1.5 us)
Async XLA Ops:
  1.8 0.5 copy-start.13
  32.2 46.9 %collective-permute-start.5 = (f32[512,8,128]{2,1,0:T(8,128)}, f32[512,8,128]{2,1,0:T(8,128)}, u32[]{:S(2)}, u32[]{:S(2)}) collective-permute-start(f32[512,8,128]{2,1,0:T(8,128)} %get-tuple-element.40), channel_id=1, source_target_pairs={{0,1},{1,0},{2,3},{3,2},{4,5},{5,4},{6,7},{7,6},{8,9},{9,8},{10,11... | collective-permute-start | bytes 6291464 | tf_op jit(solution)/shard_map/ppermute | solution.py:389
  55.6 28.0 %collective-permute-start = (f32[512,8,128]{2,1,0:T(8,128)}, f32[512,8,128]{2,1,0:T(8,128)}, u32[]{:S(2)}, u32[]{:S(2)}) collective-permute-start(f32[512,8,128]{2,1,0:T(8,128)} %get-tuple-element.34), channel_id=1, source_target_pairs={{0,1},{1,0},{2,3},{3,2},{4,5},{5,4},{6,7},{7,6},{8,9},{9,8},{10,11... | collective-permute-start | bytes 6291464 | tf_op jit(solution)/shard_map/ppermute | solution.py:389
  78.6 5.0 %copy-start.2 = (f32[512,8,128]{2,1,0:T(8,128)S(1)}, f32[512,8,128]{2,1,0:T(8,128)}, u32[]{:S(2)}) copy-start(f32[512,8,128]{2,1,0:T(8,128)} %get-tuple-element.33) | copy-start | bytes 6291460
  78.6 6.9 %collective-permute-start.10 = (f32[512,8,128]{2,1,0:T(8,128)}, f32[512,8,128]{2,1,0:T(8,128)S(1)}, u32[]{:S(2)}, u32[]{:S(2)}) collective-permute-start(f32[512,8,128]{2,1,0:T(8,128)} %get-tuple-element.46), channel_id=1, source_target_pairs={{0,1},{1,0},{2,3},{3,2},{4,5},{5,4},{6,7},{7,6},{8,9},{9,8},{10,11... | collective-permute-start | bytes 6291464 | tf_op jit(solution)/shard_map/ppermute | solution.py:389
  80.9 4.6 %copy-start.1 = (f32[512,8,128]{2,1,0:T(8,128)S(1)}, f32[512,8,128]{2,1,0:T(8,128)}, u32[]{:S(2)}) copy-start(f32[512,8,128]{2,1,0:T(8,128)} %get-tuple-element.45) | copy-start | bytes 6291460
  80.9 26.7 %collective-permute-start.6 = (f32[256,8,128]{2,1,0:T(8,128)S(1)}, f32[256,8,128]{2,1,0:T(8,128)S(1)}, u32[]{:S(2)}, u32[]{:S(2)}) collective-permute-start(f32[256,8,128]{2,1,0:T(8,128)S(1)} %slice_add_fusion.2), channel_id=1, source_target_pairs={{0,2},{1,3},{2,0},{3,1},{4,6},{5,7},{6,4},{7,5},{8,10},{9,11},{10,... | collective-permute-start | bytes 3145736 | tf_op jit(solution)/shard_map/ppermute | solution.py:389
  85.0 22.6 %copy-start.3 = (f32[512,8,128]{2,1,0:T(8,128)S(1)}, f32[512,8,128]{2,1,0:T(8,128)}, u32[]{:S(2)}) copy-start(f32[512,8,128]{2,1,0:T(8,128)} %get-tuple-element.39) | copy-start | bytes 6291460
  85.0 45.1 %collective-permute-start.1 = (f32[256,8,128]{2,1,0:T(8,128)S(1)}, f32[256,8,128]{2,1,0:T(8,128)S(1)}, u32[]{:S(2)}, u32[]{:S(2)}) collective-permute-start(f32[256,8,128]{2,1,0:T(8,128)S(1)} %slice_add_fusion.4), channel_id=1, source_target_pairs={{0,2},{1,3},{2,0},{3,1},{4,6},{5,7},{6,4},{7,5},{8,10},{9,11},{10,... | collective-permute-start | bytes 3145736 | tf_op jit(solution)/shard_map/ppermute | solution.py:389
  85.6 66.7 %collective-permute-start.11 = (f32[256,8,128]{2,1,0:T(8,128)S(1)}, f32[256,8,128]{2,1,0:T(8,128)S(1)}, u32[]{:S(2)}, u32[]{:S(2)}) collective-permute-start(f32[256,8,128]{2,1,0:T(8,128)S(1)} %slice_add_fusion), channel_id=1, source_target_pairs={{0,2},{1,3},{2,0},{3,1},{4,6},{5,7},{6,4},{7,5},{8,10},{9,11},{10,... | collective-permute-start | bytes 3145736 | tf_op jit(solution)/shard_map/ppermute | solution.py:389
  109.1 9.8 %collective-permute-start.8 = (f32[64,8,128]{2,1,0:T(8,128)S(1)}, f32[64,8,128]{2,1,0:T(8,128)S(1)}, u32[]{:S(2)}, u32[]{:S(2)}) collective-permute-start(f32[64,8,128]{2,1,0:T(8,128)S(1)} %get-tuple-element.44), channel_id=1, source_target_pairs={{0,8},{1,9},{2,10},{3,11},{4,0},{5,1},{6,2},{7,3},{8,12},{9,13},{1... | collective-permute-start | bytes 786440 | tf_op jit(solution)/shard_map/ppermute | solution.py:389
  112.2 40.1 %collective-permute-start.7 = (f32[64,8,128]{2,1,0:T(8,128)S(1)}, f32[64,8,128]{2,1,0:T(8,128)S(1)}, u32[]{:S(2)}, u32[]{:S(2)}) collective-permute-start(f32[64,8,128]{2,1,0:T(8,128)S(1)} %get-tuple-element.42), channel_id=1, source_target_pairs={{0,4},{1,5},{2,6},{3,7},{4,12},{5,13},{6,14},{7,15},{8,0},{9,1},{1... | collective-permute-start | bytes 786440 | tf_op jit(solution)/shard_map/ppermute | solution.py:389
  118.9 33.4 %collective-permute-start.9 = (f32[64,8,128]{2,1,0:T(8,128)S(1)}, f32[64,8,128]{2,1,0:T(8,128)S(1)}, u32[]{:S(2)}, u32[]{:S(2)}) collective-permute-start(f32[64,8,128]{2,1,0:T(8,128)S(1)} %add.141), channel_id=1, source_target_pairs={{0,8},{1,9},{2,10},{3,11},{4,0},{5,1},{6,2},{7,3},{8,12},{9,13},{1... | collective-permute-start | bytes 786440 | tf_op jit(solution)/shard_map/ppermute | solution.py:389
  131.6 23.8 %collective-permute-start.3 = (f32[64,8,128]{2,1,0:T(8,128)S(1)}, f32[64,8,128]{2,1,0:T(8,128)S(1)}, u32[]{:S(2)}, u32[]{:S(2)}) collective-permute-start(f32[64,8,128]{2,1,0:T(8,128)S(1)} %get-tuple-element.38), channel_id=1, source_target_pairs={{0,8},{1,9},{2,10},{3,11},{4,0},{5,1},{6,2},{7,3},{8,12},{9,13},{1... | collective-permute-start | bytes 786440 | tf_op jit(solution)/shard_map/ppermute | solution.py:389
  152.5 9.9 %collective-permute-start.13 = (f32[64,8,128]{2,1,0:T(8,128)S(1)}, f32[64,8,128]{2,1,0:T(8,128)S(1)}, u32[]{:S(2)}, u32[]{:S(2)}) collective-permute-start(f32[64,8,128]{2,1,0:T(8,128)S(1)} %get-tuple-element.51), channel_id=1, source_target_pairs={{0,8},{1,9},{2,10},{3,11},{4,0},{5,1},{6,2},{7,3},{8,12},{9,13},{1... | collective-permute-start | bytes 786440 | tf_op jit(solution)/shard_map/ppermute | solution.py:389
  155.3 14.3 %collective-permute-start.2 = (f32[64,8,128]{2,1,0:T(8,128)S(1)}, f32[64,8,128]{2,1,0:T(8,128)S(1)}, u32[]{:S(2)}, u32[]{:S(2)}) collective-permute-start(f32[64,8,128]{2,1,0:T(8,128)S(1)} %get-tuple-element.36), channel_id=1, source_target_pairs={{0,4},{1,5},{2,6},{3,7},{4,12},{5,13},{6,14},{7,15},{8,0},{9,1},{1... | collective-permute-start | bytes 786440 | tf_op jit(solution)/shard_map/ppermute | solution.py:389
  155.4 18.3 %collective-permute-start.4 = (f32[64,8,128]{2,1,0:T(8,128)S(1)}, f32[64,8,128]{2,1,0:T(8,128)S(1)}, u32[]{:S(2)}, u32[]{:S(2)}) collective-permute-start(f32[64,8,128]{2,1,0:T(8,128)S(1)} %add.135), channel_id=1, source_target_pairs={{0,8},{1,9},{2,10},{3,11},{4,0},{5,1},{6,2},{7,3},{8,12},{9,13},{1... | collective-permute-start | bytes 786440 | tf_op jit(solution)/shard_map/ppermute | solution.py:389
  158.4 22.5 %collective-permute-start.12 = (f32[64,8,128]{2,1,0:T(8,128)S(1)}, f32[64,8,128]{2,1,0:T(8,128)S(1)}, u32[]{:S(2)}, u32[]{:S(2)}) collective-permute-start(f32[64,8,128]{2,1,0:T(8,128)S(1)} %get-tuple-element.49), channel_id=1, source_target_pairs={{0,4},{1,5},{2,6},{3,7},{4,12},{5,13},{6,14},{7,15},{8,0},{9,1},{1... | collective-permute-start | bytes 786440 | tf_op jit(solution)/shard_map/ppermute | solution.py:389
  162.5 20.7 %collective-permute-start.14 = (f32[64,8,128]{2,1,0:T(8,128)S(1)}, f32[64,8,128]{2,1,0:T(8,128)S(1)}, u32[]{:S(2)}, u32[]{:S(2)}) collective-permute-start(f32[64,8,128]{2,1,0:T(8,128)S(1)} %add.147), channel_id=1, source_target_pairs={{0,8},{1,9},{2,10},{3,11},{4,0},{5,1},{6,2},{7,3},{8,12},{9,13},{1... | collective-permute-start | bytes 786440 | tf_op jit(solution)/shard_map/ppermute | solution.py:389
  183.2 95.5 %copy-start.11 = (s32[128]{0:T(128)S(1)}, s32[128]{0:T(128)}, u32[]{:S(2)}) copy-start(s32[128]{0:T(128)} %param.21) | copy-start | bytes 1540
  183.2 95.5 %copy-start.12 = (f32[5]{0:T(128)S(1)}, f32[5]{0:T(128)}, u32[]{:S(2)}) copy-start(f32[5]{0:T(128)} %param.22) | copy-start | bytes 64
  183.3 95.5 %copy-start.14 = (s32[1,32]{1,0:T(1,128)S(1)}, s32[1,32]{1,0:T(1,128)}, u32[]{:S(2)}) copy-start(s32[1,32]{1,0:T(1,128)} %copy-done.13) | copy-start | bytes 388
  183.3 96.1 %copy-start.9 = (f32[3]{0:T(128)S(1)}, f32[3]{0:T(128)}, u32[]{:S(2)}) copy-start(f32[3]{0:T(128)} %param.20) | copy-start | bytes 40
  183.3 96.1 %copy-start.10 = (f32[128]{0:T(128)S(1)}, f32[128]{0:T(128)}, u32[]{:S(2)}) copy-start(f32[128]{0:T(128)} %param.19) | copy-start | bytes 1540
  184.7 23.1 %copy-start = (f32[256,768]{1,0:T(8,128)}, f32[256,768]{1,0:T(8,128)S(1)}, u32[]{:S(2)}) copy-start(f32[256,768]{1,0:T(8,128)S(1)} %reshape.108.own_ref.refs_0_) | copy-start | bytes 2359300
  184.7 19.1 %collective-permute-start.15 = (f32[256,768]{1,0:T(8,128)S(1)}, f32[256,768]{1,0:T(8,128)S(1)}, u32[]{:S(2)}, u32[]{:S(2)}) collective-permute-start(f32[256,768]{1,0:T(8,128)S(1)} %reshape.108.own_ref.refs_0_), channel_id=1, source_target_pairs={{0,8},{1,9},{2,10},{3,11},{4,0},{5,1},{6,2},{7,3},{8,12},{9,13},{1... | collective-permute-start | bytes 2359304 | tf_op jit(solution)/shard_map/ppermute | solution.py:389
  203.8 24.3 %copy-start.5 = (f32[256,768]{1,0:T(8,128)}, f32[256,768]{1,0:T(8,128)S(1)}, u32[]{:S(2)}) copy-start(f32[256,768]{1,0:T(8,128)S(1)} %collective-permute-done.15.refs_2_) | copy-start | bytes 2359300
  203.8 19.0 %collective-permute-start.16 = (f32[256,768]{1,0:T(8,128)S(1)}, f32[256,768]{1,0:T(8,128)}, u32[]{:S(2)}, u32[]{:S(2)}) collective-permute-start(f32[256,768]{1,0:T(8,128)S(1)} %reshape.108.own_ref.refs_0_), channel_id=1, source_target_pairs={{0,4},{1,5},{2,6},{3,7},{4,12},{5,13},{6,14},{7,15},{8,0},{9,1},{1... | collective-permute-start | bytes 2359304 | tf_op jit(solution)/shard_map/ppermute | solution.py:389
  206.2 20.4 %collective-permute-start.26 = (f32[256,768]{1,0:T(8,128)S(1)}, f32[256,768]{1,0:T(8,128)S(1)}, u32[]{:S(2)}, u32[]{:S(2)}) collective-permute-start(f32[256,768]{1,0:T(8,128)S(1)} %reshape.108.own_ref.refs_0_), channel_id=1, source_target_pairs={{0,2},{1,3},{2,0},{3,1},{4,6},{5,7},{6,4},{7,5},{8,10},{9,11},{10,... | collective-permute-start | bytes 2359304 | tf_op jit(solution)/shard_map/ppermute | solution.py:389
  207.8 19.1 %collective-permute-start.29 = (f32[256,768]{1,0:T(8,128)S(1)}, f32[256,768]{1,0:T(8,128)S(1)}, u32[]{:S(2)}, u32[]{:S(2)}) collective-permute-start(f32[256,768]{1,0:T(8,128)S(1)} %reshape.108.own_ref.refs_0_), channel_id=1, source_target_pairs={{0,1},{1,0},{2,3},{3,2},{4,5},{5,4},{6,7},{7,6},{8,9},{9,8},{10,11... | collective-permute-start | bytes 2359304 | tf_op jit(solution)/shard_map/ppermute | solution.py:389
  222.8 16.8 %collective-permute-start.17 = (f32[256,768]{1,0:T(8,128)S(1)}, f32[256,768]{1,0:T(8,128)}, u32[]{:S(2)}, u32[]{:S(2)}) collective-permute-start(f32[256,768]{1,0:T(8,128)S(1)} %collective-permute-done.15.refs_2_), channel_id=1, source_target_pairs={{0,8},{1,9},{2,10},{3,11},{4,0},{5,1},{6,2},{7,3},{8,12},{9,13},{1... | collective-permute-start | bytes 2359304 | tf_op jit(solution)/shard_map/ppermute | solution.py:389
  224.9 16.4 %collective-permute-start.28 = (f32[256,768]{1,0:T(8,128)S(1)}, f32[256,768]{1,0:T(8,128)S(1)}, u32[]{:S(2)}, u32[]{:S(2)}) collective-permute-start(f32[256,768]{1,0:T(8,128)S(1)} %collective-permute-done.15.refs_2_), channel_id=1, source_target_pairs={{0,1},{1,0},{2,3},{3,2},{4,5},{5,4},{6,7},{7,6},{8,9},{9,8},{10,11... | collective-permute-start | bytes 2359304 | tf_op jit(solution)/shard_map/ppermute | solution.py:389
  224.9 20.5 %collective-permute-start.24 = (f32[256,768]{1,0:T(8,128)S(1)}, f32[256,768]{1,0:T(8,128)}, u32[]{:S(2)}, u32[]{:S(2)}) collective-permute-start(f32[256,768]{1,0:T(8,128)S(1)} %collective-permute-done.15.refs_2_), channel_id=1, source_target_pairs={{0,2},{1,3},{2,0},{3,1},{4,6},{5,7},{6,4},{7,5},{8,10},{9,11},{10,... | collective-permute-start | bytes 2359304 | tf_op jit(solution)/shard_map/ppermute | solution.py:389
  226.6 18.8 %copy-start.6 = (f32[256,768]{1,0:T(8,128)}, f32[256,768]{1,0:T(8,128)S(1)}, u32[]{:S(2)}) copy-start(f32[256,768]{1,0:T(8,128)S(1)} %collective-permute-done.26.refs_0_) | copy-start | bytes 2359300
  226.6 18.8 %collective-permute-start.27 = (f32[256,768]{1,0:T(8,128)S(1)}, f32[256,768]{1,0:T(8,128)S(1)}, u32[]{:S(2)}, u32[]{:S(2)}) collective-permute-start(f32[256,768]{1,0:T(8,128)S(1)} %collective-permute-done.26.refs_0_), channel_id=1, source_target_pairs={{0,1},{1,0},{2,3},{3,2},{4,5},{5,4},{6,7},{7,6},{8,9},{9,8},{10,11... | collective-permute-start | bytes 2359304 | tf_op jit(solution)/shard_map/ppermute | solution.py:389
  226.8 0.9 copy-start.4
  227.8 34.6 %collective-permute-start.21 = (f32[256,768]{1,0:T(8,128)}, f32[256,768]{1,0:T(8,128)}, u32[]{:S(2)}, u32[]{:S(2)}) collective-permute-start(f32[256,768]{1,0:T(8,128)} %collective-permute-done.16.refs_0_), channel_id=1, source_target_pairs={{0,2},{1,3},{2,0},{3,1},{4,6},{5,7},{6,4},{7,5},{8,10},{9,11},{10,... | collective-permute-start | bytes 2359304 | tf_op jit(solution)/shard_map/ppermute | solution.py:389
  239.7 39.0 %collective-permute-start.18 = (f32[256,768]{1,0:T(8,128)}, f32[256,768]{1,0:T(8,128)}, u32[]{:S(2)}, u32[]{:S(2)}) collective-permute-start(f32[256,768]{1,0:T(8,128)} %collective-permute-done.17.refs_0_), channel_id=1, source_target_pairs={{0,2},{1,3},{2,0},{3,1},{4,6},{5,7},{6,4},{7,5},{8,10},{9,11},{10,... | collective-permute-start | bytes 2359304 | tf_op jit(solution)/shard_map/ppermute | solution.py:389
  241.3 4.2 %copy-start.7 = (f32[256,768]{1,0:T(8,128)}, f32[256,768]{1,0:T(8,128)S(1)}, u32[]{:S(2)}) copy-start(f32[256,768]{1,0:T(8,128)S(1)} %collective-permute-done.28.refs_3_) | copy-start | bytes 2359300
  241.3 86.3 %collective-permute-start.23 = (f32[256,768]{1,0:T(8,128)}, f32[256,768]{1,0:T(8,128)}, u32[]{:S(2)}, u32[]{:S(2)}) collective-permute-start(f32[256,768]{1,0:T(8,128)} %collective-permute-done.16.refs_0_), channel_id=1, source_target_pairs={{0,1},{1,0},{2,3},{3,2},{4,5},{5,4},{6,7},{7,6},{8,9},{9,8},{10,11... | collective-permute-start | bytes 2359304 | tf_op jit(solution)/shard_map/ppermute | solution.py:389
  245.5 82.2 %collective-permute-start.25 = (f32[256,768]{1,0:T(8,128)}, f32[256,768]{1,0:T(8,128)}, u32[]{:S(2)}, u32[]{:S(2)}) collective-permute-start(f32[256,768]{1,0:T(8,128)} %collective-permute-done.24.refs_2_), channel_id=1, source_target_pairs={{0,1},{1,0},{2,3},{3,2},{4,5},{5,4},{6,7},{7,6},{8,9},{9,8},{10,11... | collective-permute-start | bytes 2359304 | tf_op jit(solution)/shard_map/ppermute | solution.py:389
  245.5 1.0 copy-start.8
  245.5 112.8 %collective-permute-start.20 = (f32[256,768]{1,0:T(8,128)}, f32[256,768]{1,0:T(8,128)}, u32[]{:S(2)}, u32[]{:S(2)}) collective-permute-start(f32[256,768]{1,0:T(8,128)} %collective-permute-done.17.refs_0_), channel_id=1, source_target_pairs={{0,1},{1,0},{2,3},{3,2},{4,5},{5,4},{6,7},{7,6},{8,9},{9,8},{10,11... | collective-permute-start | bytes 2359304 | tf_op jit(solution)/shard_map/ppermute | solution.py:389
  262.3 96.0 %collective-permute-start.22 = (f32[256,768]{1,0:T(8,128)}, f32[256,768]{1,0:T(8,128)}, u32[]{:S(2)}, u32[]{:S(2)}) collective-permute-start(f32[256,768]{1,0:T(8,128)} %collective-permute-done.21.refs_2_), channel_id=1, source_target_pairs={{0,1},{1,0},{2,3},{3,2},{4,5},{5,4},{6,7},{7,6},{8,9},{9,8},{10,11... | collective-permute-start | bytes 2359304 | tf_op jit(solution)/shard_map/ppermute | solution.py:389
  278.7 110.3 %collective-permute-start.19 = (f32[256,768]{1,0:T(8,128)}, f32[256,768]{1,0:T(8,128)}, u32[]{:S(2)}, u32[]{:S(2)}) collective-permute-start(f32[256,768]{1,0:T(8,128)} %collective-permute-done.18.refs_0_), channel_id=1, source_target_pairs={{0,1},{1,0},{2,3},{3,2},{4,5},{5,4},{6,7},{7,6},{8,9},{9,8},{10,11... | collective-permute-start | bytes 2359304 | tf_op jit(solution)/shard_map/ppermute | solution.py:389

commit v6 on v3

--- a/solution.py
+++ b/solution.py
@@ -11,6 +11,7 @@
 from jax.sharding import PartitionSpec as P
 
 
+VMEM_BYTES = 64 * 2**20
 LANES = 128
 SUB = 8
 SLOTS = 4
@@ -206,6 +207,7 @@
             pltpu.SemaphoreType.DMA((slots + 1,)),
             pltpu.SemaphoreType.DMA((3,)),
         ],
+        compiler_params=pltpu.CompilerParams(vmem_limit_bytes=VMEM_BYTES),
         name="transform",
     )(col, phase, val, cond, dz, dy, dyr, cs)
 
@@ -338,11 +340,12 @@
         ),
         out_shape=(out, out),
         input_output_aliases={3 + len(pieces) + i: i for i in range(len(olds))},
+        compiler_params=pltpu.CompilerParams(vmem_limit_bytes=VMEM_BYTES),
         name="chi",
     )(ids, weights, own, *pieces, *olds)
 
 
-GROUPS = (((0, 0),), ((1, 0),), ((0, 1), (0, 3)), ((0, 2),), ((1, 1), (1, 3)), ((1, 2),))
+GROUPS = (((0, 0),), ((1, 0), (0, 3)), ((0, 1), (1, 3)), ((0, 2), (1, 1)), ((1, 2),))
 RING = (0, 2, 3, 1)
 
 
@@ -381,44 +384,38 @@
     return lax.ppermute(value, "blk", pairs)
 
 
-def reduce_scatter(keep, other, links, ahead):
+def reduce_scatter(keep, other, links, before):
     half = keep.shape[0] // 2
     got = send(other, links.core)
     far = send(keep[half:] + got[half:], links.y)
-    if ahead:
-        far, ahead = lax.optimization_barrier((far, ahead))
+    if before:
+        far, *_ = lax.optimization_barrier((far, *before))
     near = keep[:half] + got[:half] + far
     block = half // 4
-    part = block // 2
-    cw = send(near[2 * block : 2 * block + part], links.cw)
-    ccw = send(near[2 * block + part : 3 * block], links.ccw)
-    cw, ccw = lax.optimization_barrier((cw, ccw))
-    to_cw = jnp.concatenate([near[block : block + part] + cw, near[block + part : 2 * block]])
-    to_ccw = jnp.concatenate([near[3 * block : 3 * block + part], near[3 * block + part :] + ccw])
-    from_cw = send(to_cw, links.cw)
-    from_ccw = send(to_ccw, links.ccw)
-    from_cw, from_ccw = lax.optimization_barrier((from_cw, from_ccw))
-    return near[:block], from_cw, from_ccw
+    to_cw, to_ccw, next_cw, mine = lax.optimization_barrier(
+        tuple(near[i * block : (i + 1) * block] for i in (2, 3, 1, 0))
+    )
+    two_back = send(to_cw, links.cw)
+    ahead = send(to_ccw, links.ccw)
+    next_cw = next_cw + two_back
+    back = send(next_cw, links.cw)
+    return mine, ahead, back
 
 
 def gather_and_chi(weights, own, links, ids, num_g):
-    part = own.shape[0] // 2
-
-    def over(pieces, pairs):
-        return [send(p, pairs) for p in pieces]
-
-    mine = {(0, 0): [own]}
-    mine[0, 3] = over([own], links.cw)
-    mine[0, 1] = over([own], links.ccw)
-    mine[0, 2] = [send(mine[0, 3][0][:part], links.cw), send(mine[0, 1][0][part:], links.ccw)]
+    cw = send(own, links.cw)
+    later, cw = lax.optimization_barrier((own, cw))
+    ccw = send(later, links.ccw)
+    cw_later, ccw = lax.optimization_barrier((cw, ccw))
+    mine = {(0, 0): own, (0, 3): cw, (0, 1): ccw, (0, 2): send(cw_later, links.cw)}
     for r in range(4):
-        mine[1, r] = over(mine[0, r], links.y)
+        mine[1, r] = send(mine[0, r], links.y)
     old = None
     first = 0
     for group in GROUPS:
         blocks = []
         for b, r in group:
-            blocks += [mine[b, r], over(mine[b, r], links.core)]
+            blocks += [[mine[b, r]], [send(mine[b, r], links.core)]]
         old = chi_group(weights, own, blocks, ids, first, num_g, old)
         first += len(blocks)
     return old
@@ -469,19 +466,22 @@
     count = lax.axis_size("blk")
     links = Links(count) if Links.fits(count) else None
     if links is not None:
-        near = jnp.asarray(links.near)[lax.axis_index("blk")]
-        ids = jnp.asarray(links.order.reshape(count, -1))[lax.axis_index("blk")]
-        pick = pick.reshape(2, count, -1)[:, near.reshape(-1)].reshape(2, -1)
+        tables = np.concatenate([x.reshape(count, -1) for x in (links.near, links.order)], axis=1)
+        table = jnp.asarray(tables)[lax.axis_index("blk")]
+        pick = pick.reshape(2, count, -1)[:, table[:count]].reshape(2, -1)
+        ids = table[count:]
     owned = []
     for c in range(num_cond):
         keep, other = transform(pick[0], pick[1], val, cond[c], cs, num_g)
-        if links is not None:
-            ahead = owned[-1][1:] if c == num_cond - 1 else ()
-            owned.append(reduce_scatter(keep, other, links, ahead))
-        else:
+        if links is None:
             whole = jnp.concatenate([keep, other])
             owned.append((lax.psum_scatter(whole, "blk", scatter_dimension=0, tiled=True),))
-    own = jnp.stack([sum(parts) for parts in owned]).reshape(num_cond, -1, 2, 4, num_val)
+        else:
+            before = owned[-1][1:] if c == num_cond - 1 else ()
+            owned.append(reduce_scatter(keep, other, links, before))
+    for c, parts in enumerate(owned):
+        owned[c] = sum(parts[1:], parts[0])
+    own = jnp.stack(owned).reshape(num_cond, -1, 2, 4, num_val)
     own = jnp.transpose(own, (1, 3, 2, 0, 4)).reshape(-1, 2 * pairs)
 
     gaps = e_val[None, :] - e_cond[:, None]

time: 347 us -> 357 us (1.029)
  starting transfers between devices: 32.7 us -> 40.6 us
  waiting for transfers between devices: 144 us -> 150 us
  Pallas kernels: 149 us -> 144 us
    ppermute x37 -> x30, starting transfers between devices: 32.7 us -> 40.6 us  [send(): return lax.ppermute(value, 'blk', pairs)]
    ppermute x37 -> x30, waiting for transfers between devices: 144 us -> 150 us  [send(): return lax.ppermute(value, 'blk', pairs)]
    pallas_call x6 -> x5, Pallas kernels: 79.8 us -> 75.6 us  [chi_group(): pl.pallas_call(functools.partial(chi_group_kernel, counts, old is not Non...]
  transfers between devices with their start and end apart: 37 -> 30, of which waited for: 17 -> 15; matrix products, arithmetic and copies ran while one was open for 3% -> 2% of each run, Pallas kernels for 33% -> 31%
where the time goes in v6:
time: 357 us; the launch traced here: 356 us
  waiting for transfers between devices  150 us (42%)
  Pallas kernels  144 us (40%)
  starting transfers between devices  40.6 us (11%)
  local copies, waits for them, and re-layouts  11.1 us (3%)
  other arithmetic  8.91 us (2%)
    ppermute x30, waiting for transfers between devices, send(): return lax.ppermute(value, 'blk', pairs)  150 us
    pallas_call x5, Pallas kernels, chi_group(): pl.pallas_call(functools.partial(chi_group_kernel, counts, old is not Non...  75.6 us
    pallas_call x3, Pallas kernels, transform(): pl.pallas_call(transform_kernel, out_shape=(jax.ShapeDtypeStruct((num_g /...  68.5 us
    ppermute x30, starting transfers between devices, send(): return lax.ppermute(value, 'blk', pairs)  40.6 us
  transfers between devices with their start and end apart: 30, of which 15 were waited for; matrix products, arithmetic and copies ran while one was open for 2% of the time, Pallas kernels for 31%

profile of v6, /device:TPU:0, one launch (start us, length us, event | category | flops | bytes accessed | tf_op | source)
XLA Modules:
  0.0 355.9 jit_solution(14480019482817254742)
XLA Ops:
  1.1 0.7 constant_dynamic-slice_fusion
  1.8 0.5 copy-done.13
  2.4 0.8 fusion.4
  3.2 0.6 gather_fusion
  3.8 0.7 fusion.28
  4.4 1.9 copy.34
  6.4 1.7 slice_bitcast_fusion.2
  8.1 1.3 broadcast_in_dim.12.cs_hbm
  9.4 22.8 %transform.4 = (f32[512,8,128]{2,1,0:T(8,128)}, f32[512,8,128]{2,1,0:T(8,128)}) custom-call(s32[4096]{0:T(1024)} %bitcast.48, s32[4096]{0:T(1024)} %bitcast.45, f32[4,64,64,128]{3,2,1,0:T(8,128)} %bitcast.37, f32[4,8,64,8]{3,2,1,0:T(8,128)} %get-tuple-element.66.cond_ref, bf16[64,192]{1,0:T(8,128)(2,1)} %constant.92.clone.dz_ref, ...), custom_call_target="tpu_custom_call" | custom-call | tf_op jit(solution)/shard_map/transform/pallas_call | solution.py:196
  32.2 0.6 collective-permute-start.5
  32.8 22.9 %transform.3 = (f32[512,8,128]{2,1,0:T(8,128)}, f32[512,8,128]{2,1,0:T(8,128)}) custom-call(s32[4096]{0:T(1024)} %bitcast.49, s32[4096]{0:T(1024)} %bitcast.46, f32[4,64,64,128]{3,2,1,0:T(8,128)} %bitcast.38, f32[4,8,64,8]{3,2,1,0:T(8,128)} %get-tuple-element.64.cond_ref, bf16[64,192]{1,0:T(8,128)(2,1)} %constant.92.clone.dz_ref, ...), custom_call_target="tpu_custom_call" | custom-call | tf_op jit(solution)/shard_map/transform/pallas_call | solution.py:196
  55.7 22.9 %transform.5 = (f32[512,8,128]{2,1,0:T(8,128)}, f32[512,8,128]{2,1,0:T(8,128)}) custom-call(s32[4096]{0:T(1024)} %bitcast.50, s32[4096]{0:T(1024)} %bitcast.47, f32[4,64,64,128]{3,2,1,0:T(8,128)} %bitcast.39, f32[4,8,64,8]{3,2,1,0:T(8,128)} %get-tuple-element.65.cond_ref, bf16[64,192]{1,0:T(8,128)(2,1)} %constant.92.clone.dz_ref, ...), custom_call_target="tpu_custom_call" | custom-call | tf_op jit(solution)/shard_map/transform/pallas_call | solution.py:196
  78.6 0.5 collective-permute-start.10
  79.1 1.8 slice_add_fusion.2
  80.9 2.7 collective-permute-start.6
  83.6 1.4 slice_add_fusion.4
  85.0 0.5 collective-permute-start.1
  85.6 1.7 collective-permute-start.11
  87.3 20.3 %collective-permute-done.6 = f32[256,8,128]{2,1,0:T(8,128)S(1)} collective-permute-done((f32[256,8,128]{2,1,0:T(8,128)S(1)}, f32[256,8,128]{2,1,0:T(8,128)S(1)}, u32[]{:S(2)}, u32[]{:S(2)}) %collective-permute-start.6) | collective-permute-done | bytes 1048608 | tf_op jit(solution)/shard_map/ppermute | solution.py:384
  107.6 1.4 fusion.1
  109.1 3.1 collective-permute-start.8
  112.2 6.7 %collective-permute-done.8 = f32[64,8,128]{2,1,0:T(8,128)S(1)} collective-permute-done((f32[64,8,128]{2,1,0:T(8,128)S(1)}, f32[64,8,128]{2,1,0:T(8,128)S(1)}, u32[]{:S(2)}, u32[]{:S(2)}) %collective-permute-start.8) | collective-permute-done | bytes 262176 | tf_op jit(solution)/shard_map/ppermute | solution.py:384
  118.9 3.4 collective-permute-start.9
  122.4 7.7 %collective-permute-done.1 = f32[256,8,128]{2,1,0:T(8,128)S(1)} collective-permute-done((f32[256,8,128]{2,1,0:T(8,128)S(1)}, f32[256,8,128]{2,1,0:T(8,128)S(1)}, u32[]{:S(2)}, u32[]{:S(2)}) %collective-permute-start.1) | collective-permute-done | bytes 1048608 | tf_op jit(solution)/shard_map/ppermute | solution.py:384
  130.1 1.4 fusion.2
  131.6 3.1 collective-permute-start.3
  134.7 17.6 %collective-permute-done.11 = f32[256,8,128]{2,1,0:T(8,128)S(1)} collective-permute-done((f32[256,8,128]{2,1,0:T(8,128)S(1)}, f32[256,8,128]{2,1,0:T(8,128)S(1)}, u32[]{:S(2)}, u32[]{:S(2)}) %collective-permute-start.11) | collective-permute-done | bytes 1048608 | tf_op jit(solution)/shard_map/ppermute | solution.py:384
  152.5 2.8 collective-permute-start.13
  155.4 3.0 collective-permute-start.4
  158.4 4.1 %collective-permute-done.13 = f32[64,8,128]{2,1,0:T(8,128)S(1)} collective-permute-done((f32[64,8,128]{2,1,0:T(8,128)S(1)}, f32[64,8,128]{2,1,0:T(8,128)S(1)}, u32[]{:S(2)}, u32[]{:S(2)}) %collective-permute-start.13) | collective-permute-done | bytes 262176 | tf_op jit(solution)/shard_map/ppermute | solution.py:384
  162.5 5.4 %collective-permute-start.14 = (f32[64,8,128]{2,1,0:T(8,128)S(1)}, f32[64,8,128]{2,1,0:T(8,128)S(1)}, u32[]{:S(2)}, u32[]{:S(2)}) collective-permute-start(f32[64,8,128]{2,1,0:T(8,128)S(1)} %add.147), channel_id=1, source_target_pairs={{0,8},{1,9},{2,10},{3,11},{4,0},{5,1},{6,2},{7,3},{8,12},{9,13},{1... | collective-permute-start | bytes 786440 | tf_op jit(solution)/shard_map/ppermute | solution.py:384
  167.9 1.8 collective-permute-done.2
  169.7 4.0 %collective-permute-done.4 = f32[64,8,128]{2,1,0:T(8,128)S(1)} collective-permute-done((f32[64,8,128]{2,1,0:T(8,128)S(1)}, f32[64,8,128]{2,1,0:T(8,128)S(1)}, u32[]{:S(2)}, u32[]{:S(2)}) %collective-permute-start.4) | collective-permute-done | bytes 262176 | tf_op jit(solution)/shard_map/ppermute | solution.py:384
  173.7 0.3 copy.36
  174.1 0.3 copy.37
  174.3 6.5 %collective-permute-done.12 = f32[64,8,128]{2,1,0:T(8,128)S(1)} collective-permute-done((f32[64,8,128]{2,1,0:T(8,128)S(1)}, f32[64,8,128]{2,1,0:T(8,128)S(1)}, u32[]{:S(2)}, u32[]{:S(2)}) %collective-permute-start.12) | collective-permute-done | bytes 262176 | tf_op jit(solution)/shard_map/ppermute | solution.py:384
  180.9 2.3 collective-permute-done.14
  183.3 0.3 copy.38
  183.6 0.7 maximum_bitcast_fusion
  184.3 0.4 reshape.108.refs_2_.refs_3_
  184.7 3.4 collective-permute-start.15
  188.1 15.7 %collective-permute-done.15.refs_5_ = f32[256,768]{1,0:T(8,128)S(1)} collective-permute-done((f32[256,768]{1,0:T(8,128)S(1)}, f32[256,768]{1,0:T(8,128)S(1)}, u32[]{:S(2)}, u32[]{:S(2)}) %collective-permute-start.15) | collective-permute-done | bytes 786464 | tf_op jit(solution)/shard_map/ppermute | solution.py:384
  203.8 2.4 collective-permute-start.16
  206.2 1.5 collective-permute-start.26
  207.8 15.1 %collective-permute-done.16.refs_3_ = f32[256,768]{1,0:T(8,128)} collective-permute-done((f32[256,768]{1,0:T(8,128)S(1)}, f32[256,768]{1,0:T(8,128)}, u32[]{:S(2)}, u32[]{:S(2)}) %collective-permute-start.16) | collective-permute-done | bytes 786464 | tf_op jit(solution)/shard_map/ppermute | solution.py:384
  222.8 2.1 collective-permute-start.17
  224.9 1.7 collective-permute-start.24
  226.6 0.2 collective-permute-start.27
  226.8 0.9 copy-done.4
  227.8 0.3 collective-permute-start.21
  228.1 11.6 %collective-permute-done.17.refs_3_ = f32[256,768]{1,0:T(8,128)} collective-permute-done((f32[256,768]{1,0:T(8,128)S(1)}, f32[256,768]{1,0:T(8,128)}, u32[]{:S(2)}, u32[]{:S(2)}) %collective-permute-start.17) | collective-permute-done | bytes 786464 | tf_op jit(solution)/shard_map/ppermute | solution.py:384
  239.7 1.6 collective-permute-start.18
  241.3 4.2 %collective-permute-done.24.refs_5_ = f32[256,768]{1,0:T(8,128)} collective-permute-done((f32[256,768]{1,0:T(8,128)S(1)}, f32[256,768]{1,0:T(8,128)}, u32[]{:S(2)}, u32[]{:S(2)}) %collective-permute-start.24) | collective-permute-done | bytes 786464 | tf_op jit(solution)/shard_map/ppermute | solution.py:384
  245.5 0.6 collective-permute-start.20
  246.0 0.4 copy-done.8
  246.4 15.9 %collective-permute-done.21.refs_5_ = f32[256,768]{1,0:T(8,128)} collective-permute-done((f32[256,768]{1,0:T(8,128)}, f32[256,768]{1,0:T(8,128)}, u32[]{:S(2)}, u32[]{:S(2)}) %collective-permute-start.21) | collective-permute-done | bytes 786464 | tf_op jit(solution)/shard_map/ppermute | solution.py:384
  262.3 16.4 %collective-permute-done.18.refs_3_ = f32[256,768]{1,0:T(8,128)} collective-permute-done((f32[256,768]{1,0:T(8,128)}, f32[256,768]{1,0:T(8,128)}, u32[]{:S(2)}, u32[]{:S(2)}) %collective-permute-start.18) | collective-permute-done | bytes 786464 | tf_op jit(solution)/shard_map/ppermute | solution.py:384
  278.7 0.6 slice_bitcast_fusion.3.refs_0_
  279.4 0.7 divide_multiply_fusion.refs_1_
  280.1 11.2 %chi.5 = (f32[5,256,4096]{2,1,0:T(8,128)}, f32[5,256,4096]{2,1,0:T(8,128)}) custom-call(s32[16]{0:T(128)} %slice_bitcast_fusion.3.refs_0_, f32[5,384]{1,0:T(8,128)} %divide_multiply_fusion.refs_1_, f32[256,768]{1,0:T(8,128)} %copy-done, f32[256,768]{1,0:T(8,128)} %copy-done, f32[256,768]{1,0:T(8,128)} %copy-done.4), custom_call_target="tpu_custom_call" | custom-call | tf_op jit(solution)/shard_map/chi/pallas_call | solution.py:324
  291.3 17.7 %chi.6 = (f32[5,256,4096]{2,1,0:T(8,128)}, f32[5,256,4096]{2,1,0:T(8,128)}) custom-call(s32[16]{0:T(128)} %slice_bitcast_fusion.3.refs_0_, f32[5,384]{1,0:T(8,128)} %divide_multiply_fusion.refs_1_, f32[256,768]{1,0:T(8,128)} %copy-done, f32[256,768]{1,0:T(8,128)} %copy-done.6, f32[256,768]{1,0:T(8,128)} %copy-done.8, ...), custom_call_target="tpu_custom_call", output_to_operand_aliasing={{0}: (7, {}), {1}: (8, {})} | custom-call | tf_op jit(solution)/shard_map/chi/pallas_call | solution.py:324
  309.0 17.7 %chi.7 = (f32[5,256,4096]{2,1,0:T(8,128)}, f32[5,256,4096]{2,1,0:T(8,128)}) custom-call(s32[16]{0:T(128)} %slice_bitcast_fusion.3.refs_0_, f32[5,384]{1,0:T(8,128)} %divide_multiply_fusion.refs_1_, f32[256,768]{1,0:T(8,128)} %copy-done, f32[256,768]{1,0:T(8,128)} %collective-permute-done.16.refs_3_, ...), custom_call_target="tpu_custom_call", output_to_operand_aliasing={{0}: (7, {}), {1}: (8, {})} | custom-call | tf_op jit(solution)/shard_map/chi/pallas_call | solution.py:324
  326.7 17.7 %chi.8 = (f32[5,256,4096]{2,1,0:T(8,128)}, f32[5,256,4096]{2,1,0:T(8,128)}) custom-call(s32[16]{0:T(128)} %slice_bitcast_fusion.3.refs_0_, f32[5,384]{1,0:T(8,128)} %divide_multiply_fusion.refs_1_, f32[256,768]{1,0:T(8,128)} %copy-done, f32[256,768]{1,0:T(8,128)} %collective-permute-done.17.refs_3_, ...), custom_call_target="tpu_custom_call", output_to_operand_aliasing={{0}: (7, {}), {1}: (8, {})} | custom-call | tf_op jit(solution)/shard_map/chi/pallas_call | solution.py:324
  344.4 11.3 %chi.9 = (f32[5,256,4096]{2,1,0:T(8,128)}, f32[5,256,4096]{2,1,0:T(8,128)}) custom-call(s32[16]{0:T(128)} %slice_bitcast_fusion.3.refs_0_, f32[5,384]{1,0:T(8,128)} %divide_multiply_fusion.refs_1_, f32[256,768]{1,0:T(8,128)} %copy-done, f32[256,768]{1,0:T(8,128)} %collective-permute-done.18.refs_3_, ...), custom_call_target="tpu_custom_call", output_to_operand_aliasing={{0}: (5, {}), {1}: (6, {})} | custom-call | tf_op jit(solution)/shard_map/chi/pallas_call | solution.py:324
  (76 shorter events, 1.5 us)
Async XLA Ops:
  1.8 0.5 copy-start.13
  32.2 46.9 %collective-permute-start.5 = (f32[512,8,128]{2,1,0:T(8,128)}, f32[512,8,128]{2,1,0:T(8,128)}, u32[]{:S(2)}, u32[]{:S(2)}) collective-permute-start(f32[512,8,128]{2,1,0:T(8,128)} %get-tuple-element.40), channel_id=1, source_target_pairs={{0,1},{1,0},{2,3},{3,2},{4,5},{5,4},{6,7},{7,6},{8,9},{9,8},{10,11... | collective-permute-start | bytes 6291464 | tf_op jit(solution)/shard_map/ppermute | solution.py:384
  55.6 28.0 %collective-permute-start = (f32[512,8,128]{2,1,0:T(8,128)}, f32[512,8,128]{2,1,0:T(8,128)}, u32[]{:S(2)}, u32[]{:S(2)}) collective-permute-start(f32[512,8,128]{2,1,0:T(8,128)} %get-tuple-element.34), channel_id=1, source_target_pairs={{0,1},{1,0},{2,3},{3,2},{4,5},{5,4},{6,7},{7,6},{8,9},{9,8},{10,11... | collective-permute-start | bytes 6291464 | tf_op jit(solution)/shard_map/ppermute | solution.py:384
  78.6 5.0 %copy-start.2 = (f32[512,8,128]{2,1,0:T(8,128)S(1)}, f32[512,8,128]{2,1,0:T(8,128)}, u32[]{:S(2)}) copy-start(f32[512,8,128]{2,1,0:T(8,128)} %get-tuple-element.33) | copy-start | bytes 6291460
  78.6 6.9 %collective-permute-start.10 = (f32[512,8,128]{2,1,0:T(8,128)}, f32[512,8,128]{2,1,0:T(8,128)S(1)}, u32[]{:S(2)}, u32[]{:S(2)}) collective-permute-start(f32[512,8,128]{2,1,0:T(8,128)} %get-tuple-element.46), channel_id=1, source_target_pairs={{0,1},{1,0},{2,3},{3,2},{4,5},{5,4},{6,7},{7,6},{8,9},{9,8},{10,11... | collective-permute-start | bytes 6291464 | tf_op jit(solution)/shard_map/ppermute | solution.py:384
  80.9 4.6 %copy-start.1 = (f32[512,8,128]{2,1,0:T(8,128)S(1)}, f32[512,8,128]{2,1,0:T(8,128)}, u32[]{:S(2)}) copy-start(f32[512,8,128]{2,1,0:T(8,128)} %get-tuple-element.45) | copy-start | bytes 6291460
  80.9 26.7 %collective-permute-start.6 = (f32[256,8,128]{2,1,0:T(8,128)S(1)}, f32[256,8,128]{2,1,0:T(8,128)S(1)}, u32[]{:S(2)}, u32[]{:S(2)}) collective-permute-start(f32[256,8,128]{2,1,0:T(8,128)S(1)} %slice_add_fusion.2), channel_id=1, source_target_pairs={{0,2},{1,3},{2,0},{3,1},{4,6},{5,7},{6,4},{7,5},{8,10},{9,11},{10,... | collective-permute-start | bytes 3145736 | tf_op jit(solution)/shard_map/ppermute | solution.py:384
  85.0 22.6 %copy-start.3 = (f32[512,8,128]{2,1,0:T(8,128)S(1)}, f32[512,8,128]{2,1,0:T(8,128)}, u32[]{:S(2)}) copy-start(f32[512,8,128]{2,1,0:T(8,128)} %get-tuple-element.39) | copy-start | bytes 6291460
  85.0 45.1 %collective-permute-start.1 = (f32[256,8,128]{2,1,0:T(8,128)S(1)}, f32[256,8,128]{2,1,0:T(8,128)S(1)}, u32[]{:S(2)}, u32[]{:S(2)}) collective-permute-start(f32[256,8,128]{2,1,0:T(8,128)S(1)} %slice_add_fusion.4), channel_id=1, source_target_pairs={{0,2},{1,3},{2,0},{3,1},{4,6},{5,7},{6,4},{7,5},{8,10},{9,11},{10,... | collective-permute-start | bytes 3145736 | tf_op jit(solution)/shard_map/ppermute | solution.py:384
  85.6 66.7 %collective-permute-start.11 = (f32[256,8,128]{2,1,0:T(8,128)S(1)}, f32[256,8,128]{2,1,0:T(8,128)S(1)}, u32[]{:S(2)}, u32[]{:S(2)}) collective-permute-start(f32[256,8,128]{2,1,0:T(8,128)S(1)} %slice_add_fusion), channel_id=1, source_target_pairs={{0,2},{1,3},{2,0},{3,1},{4,6},{5,7},{6,4},{7,5},{8,10},{9,11},{10,... | collective-permute-start | bytes 3145736 | tf_op jit(solution)/shard_map/ppermute | solution.py:384
  109.1 9.8 %collective-permute-start.8 = (f32[64,8,128]{2,1,0:T(8,128)S(1)}, f32[64,8,128]{2,1,0:T(8,128)S(1)}, u32[]{:S(2)}, u32[]{:S(2)}) collective-permute-start(f32[64,8,128]{2,1,0:T(8,128)S(1)} %get-tuple-element.44), channel_id=1, source_target_pairs={{0,8},{1,9},{2,10},{3,11},{4,0},{5,1},{6,2},{7,3},{8,12},{9,13},{1... | collective-permute-start | bytes 786440 | tf_op jit(solution)/shard_map/ppermute | solution.py:384
  112.2 40.1 %collective-permute-start.7 = (f32[64,8,128]{2,1,0:T(8,128)S(1)}, f32[64,8,128]{2,1,0:T(8,128)S(1)}, u32[]{:S(2)}, u32[]{:S(2)}) collective-permute-start(f32[64,8,128]{2,1,0:T(8,128)S(1)} %get-tuple-element.42), channel_id=1, source_target_pairs={{0,4},{1,5},{2,6},{3,7},{4,12},{5,13},{6,14},{7,15},{8,0},{9,1},{1... | collective-permute-start | bytes 786440 | tf_op jit(solution)/shard_map/ppermute | solution.py:384
  118.9 33.4 %collective-permute-start.9 = (f32[64,8,128]{2,1,0:T(8,128)S(1)}, f32[64,8,128]{2,1,0:T(8,128)S(1)}, u32[]{:S(2)}, u32[]{:S(2)}) collective-permute-start(f32[64,8,128]{2,1,0:T(8,128)S(1)} %add.141), channel_id=1, source_target_pairs={{0,8},{1,9},{2,10},{3,11},{4,0},{5,1},{6,2},{7,3},{8,12},{9,13},{1... | collective-permute-start | bytes 786440 | tf_op jit(solution)/shard_map/ppermute | solution.py:384
  131.6 23.8 %collective-permute-start.3 = (f32[64,8,128]{2,1,0:T(8,128)S(1)}, f32[64,8,128]{2,1,0:T(8,128)S(1)}, u32[]{:S(2)}, u32[]{:S(2)}) collective-permute-start(f32[64,8,128]{2,1,0:T(8,128)S(1)} %get-tuple-element.38), channel_id=1, source_target_pairs={{0,8},{1,9},{2,10},{3,11},{4,0},{5,1},{6,2},{7,3},{8,12},{9,13},{1... | collective-permute-start | bytes 786440 | tf_op jit(solution)/shard_map/ppermute | solution.py:384
  152.5 9.9 %collective-permute-start.13 = (f32[64,8,128]{2,1,0:T(8,128)S(1)}, f32[64,8,128]{2,1,0:T(8,128)S(1)}, u32[]{:S(2)}, u32[]{:S(2)}) collective-permute-start(f32[64,8,128]{2,1,0:T(8,128)S(1)} %get-tuple-element.51), channel_id=1, source_target_pairs={{0,8},{1,9},{2,10},{3,11},{4,0},{5,1},{6,2},{7,3},{8,12},{9,13},{1... | collective-permute-start | bytes 786440 | tf_op jit(solution)/shard_map/ppermute | solution.py:384
  155.3 14.3 %collective-permute-start.2 = (f32[64,8,128]{2,1,0:T(8,128)S(1)}, f32[64,8,128]{2,1,0:T(8,128)S(1)}, u32[]{:S(2)}, u32[]{:S(2)}) collective-permute-start(f32[64,8,128]{2,1,0:T(8,128)S(1)} %get-tuple-element.36), channel_id=1, source_target_pairs={{0,4},{1,5},{2,6},{3,7},{4,12},{5,13},{6,14},{7,15},{8,0},{9,1},{1... | collective-permute-start | bytes 786440 | tf_op jit(solution)/shard_map/ppermute | solution.py:384
  155.4 18.3 %collective-permute-start.4 = (f32[64,8,128]{2,1,0:T(8,128)S(1)}, f32[64,8,128]{2,1,0:T(8,128)S(1)}, u32[]{:S(2)}, u32[]{:S(2)}) collective-permute-start(f32[64,8,128]{2,1,0:T(8,128)S(1)} %add.135), channel_id=1, source_target_pairs={{0,8},{1,9},{2,10},{3,11},{4,0},{5,1},{6,2},{7,3},{8,12},{9,13},{1... | collective-permute-start | bytes 786440 | tf_op jit(solution)/shard_map/ppermute | solution.py:384
  158.4 22.5 %collective-permute-start.12 = (f32[64,8,128]{2,1,0:T(8,128)S(1)}, f32[64,8,128]{2,1,0:T(8,128)S(1)}, u32[]{:S(2)}, u32[]{:S(2)}) collective-permute-start(f32[64,8,128]{2,1,0:T(8,128)S(1)} %get-tuple-element.49), channel_id=1, source_target_pairs={{0,4},{1,5},{2,6},{3,7},{4,12},{5,13},{6,14},{7,15},{8,0},{9,1},{1... | collective-permute-start | bytes 786440 | tf_op jit(solution)/shard_map/ppermute | solution.py:384
  162.5 20.7 %collective-permute-start.14 = (f32[64,8,128]{2,1,0:T(8,128)S(1)}, f32[64,8,128]{2,1,0:T(8,128)S(1)}, u32[]{:S(2)}, u32[]{:S(2)}) collective-permute-start(f32[64,8,128]{2,1,0:T(8,128)S(1)} %add.147), channel_id=1, source_target_pairs={{0,8},{1,9},{2,10},{3,11},{4,0},{5,1},{6,2},{7,3},{8,12},{9,13},{1... | collective-permute-start | bytes 786440 | tf_op jit(solution)/shard_map/ppermute | solution.py:384
  183.2 95.5 %copy-start.11 = (s32[128]{0:T(128)S(1)}, s32[128]{0:T(128)}, u32[]{:S(2)}) copy-start(s32[128]{0:T(128)} %param.21) | copy-start | bytes 1540
  183.2 95.5 %copy-start.12 = (f32[5]{0:T(128)S(1)}, f32[5]{0:T(128)}, u32[]{:S(2)}) copy-start(f32[5]{0:T(128)} %param.22) | copy-start | bytes 64
  183.3 95.5 %copy-start.14 = (s32[1,32]{1,0:T(1,128)S(1)}, s32[1,32]{1,0:T(1,128)}, u32[]{:S(2)}) copy-start(s32[1,32]{1,0:T(1,128)} %copy-done.13) | copy-start | bytes 388
  183.3 96.1 %copy-start.9 = (f32[3]{0:T(128)S(1)}, f32[3]{0:T(128)}, u32[]{:S(2)}) copy-start(f32[3]{0:T(128)} %param.20) | copy-start | bytes 40
  183.3 96.1 %copy-start.10 = (f32[128]{0:T(128)S(1)}, f32[128]{0:T(128)}, u32[]{:S(2)}) copy-start(f32[128]{0:T(128)} %param.19) | copy-start | bytes 1540
  184.7 23.1 %copy-start = (f32[256,768]{1,0:T(8,128)}, f32[256,768]{1,0:T(8,128)S(1)}, u32[]{:S(2)}) copy-start(f32[256,768]{1,0:T(8,128)S(1)} %reshape.108.refs_2_.refs_3_) | copy-start | bytes 2359300
  184.7 19.1 %collective-permute-start.15 = (f32[256,768]{1,0:T(8,128)S(1)}, f32[256,768]{1,0:T(8,128)S(1)}, u32[]{:S(2)}, u32[]{:S(2)}) collective-permute-start(f32[256,768]{1,0:T(8,128)S(1)} %reshape.108.refs_2_.refs_3_), channel_id=1, source_target_pairs={{0,8},{1,9},{2,10},{3,11},{4,0},{5,1},{6,2},{7,3},{8,12},{9,13},{1... | collective-permute-start | bytes 2359304 | tf_op jit(solution)/shard_map/ppermute | solution.py:384
  203.8 24.3 %copy-start.5 = (f32[256,768]{1,0:T(8,128)}, f32[256,768]{1,0:T(8,128)S(1)}, u32[]{:S(2)}) copy-start(f32[256,768]{1,0:T(8,128)S(1)} %collective-permute-done.15.refs_5_) | copy-start | bytes 2359300
  203.8 19.0 %collective-permute-start.16 = (f32[256,768]{1,0:T(8,128)S(1)}, f32[256,768]{1,0:T(8,128)}, u32[]{:S(2)}, u32[]{:S(2)}) collective-permute-start(f32[256,768]{1,0:T(8,128)S(1)} %reshape.108.refs_2_.refs_3_), channel_id=1, source_target_pairs={{0,4},{1,5},{2,6},{3,7},{4,12},{5,13},{6,14},{7,15},{8,0},{9,1},{1... | collective-permute-start | bytes 2359304 | tf_op jit(solution)/shard_map/ppermute | solution.py:384
  206.2 20.4 %collective-permute-start.26 = (f32[256,768]{1,0:T(8,128)S(1)}, f32[256,768]{1,0:T(8,128)S(1)}, u32[]{:S(2)}, u32[]{:S(2)}) collective-permute-start(f32[256,768]{1,0:T(8,128)S(1)} %reshape.108.refs_2_.refs_3_), channel_id=1, source_target_pairs={{0,2},{1,3},{2,0},{3,1},{4,6},{5,7},{6,4},{7,5},{8,10},{9,11},{10,... | collective-permute-start | bytes 2359304 | tf_op jit(solution)/shard_map/ppermute | solution.py:384
  207.8 19.1 %collective-permute-start.29 = (f32[256,768]{1,0:T(8,128)S(1)}, f32[256,768]{1,0:T(8,128)S(1)}, u32[]{:S(2)}, u32[]{:S(2)}) collective-permute-start(f32[256,768]{1,0:T(8,128)S(1)} %reshape.108.refs_2_.refs_3_), channel_id=1, source_target_pairs={{0,1},{1,0},{2,3},{3,2},{4,5},{5,4},{6,7},{7,6},{8,9},{9,8},{10,11... | collective-permute-start | bytes 2359304 | tf_op jit(solution)/shard_map/ppermute | solution.py:384
  222.8 16.8 %collective-permute-start.17 = (f32[256,768]{1,0:T(8,128)S(1)}, f32[256,768]{1,0:T(8,128)}, u32[]{:S(2)}, u32[]{:S(2)}) collective-permute-start(f32[256,768]{1,0:T(8,128)S(1)} %collective-permute-done.15.refs_5_), channel_id=1, source_target_pairs={{0,8},{1,9},{2,10},{3,11},{4,0},{5,1},{6,2},{7,3},{8,12},{9,13},{1... | collective-permute-start | bytes 2359304 | tf_op jit(solution)/shard_map/ppermute | solution.py:384
  224.9 16.4 %collective-permute-start.28 = (f32[256,768]{1,0:T(8,128)S(1)}, f32[256,768]{1,0:T(8,128)S(1)}, u32[]{:S(2)}, u32[]{:S(2)}) collective-permute-start(f32[256,768]{1,0:T(8,128)S(1)} %collective-permute-done.15.refs_5_), channel_id=1, source_target_pairs={{0,1},{1,0},{2,3},{3,2},{4,5},{5,4},{6,7},{7,6},{8,9},{9,8},{10,11... | collective-permute-start | bytes 2359304 | tf_op jit(solution)/shard_map/ppermute | solution.py:384
  224.9 20.5 %collective-permute-start.24 = (f32[256,768]{1,0:T(8,128)S(1)}, f32[256,768]{1,0:T(8,128)}, u32[]{:S(2)}, u32[]{:S(2)}) collective-permute-start(f32[256,768]{1,0:T(8,128)S(1)} %collective-permute-done.15.refs_5_), channel_id=1, source_target_pairs={{0,2},{1,3},{2,0},{3,1},{4,6},{5,7},{6,4},{7,5},{8,10},{9,11},{10,... | collective-permute-start | bytes 2359304 | tf_op jit(solution)/shard_map/ppermute | solution.py:384
  226.6 18.8 %copy-start.6 = (f32[256,768]{1,0:T(8,128)}, f32[256,768]{1,0:T(8,128)S(1)}, u32[]{:S(2)}) copy-start(f32[256,768]{1,0:T(8,128)S(1)} %collective-permute-done.26.refs_3_) | copy-start | bytes 2359300
  226.6 18.8 %collective-permute-start.27 = (f32[256,768]{1,0:T(8,128)S(1)}, f32[256,768]{1,0:T(8,128)S(1)}, u32[]{:S(2)}, u32[]{:S(2)}) collective-permute-start(f32[256,768]{1,0:T(8,128)S(1)} %collective-permute-done.26.refs_3_), channel_id=1, source_target_pairs={{0,1},{1,0},{2,3},{3,2},{4,5},{5,4},{6,7},{7,6},{8,9},{9,8},{10,11... | collective-permute-start | bytes 2359304 | tf_op jit(solution)/shard_map/ppermute | solution.py:384
  226.8 0.9 copy-start.4
  227.8 34.6 %collective-permute-start.21 = (f32[256,768]{1,0:T(8,128)}, f32[256,768]{1,0:T(8,128)}, u32[]{:S(2)}, u32[]{:S(2)}) collective-permute-start(f32[256,768]{1,0:T(8,128)} %collective-permute-done.16.refs_3_), channel_id=1, source_target_pairs={{0,2},{1,3},{2,0},{3,1},{4,6},{5,7},{6,4},{7,5},{8,10},{9,11},{10,... | collective-permute-start | bytes 2359304 | tf_op jit(solution)/shard_map/ppermute | solution.py:384
  239.7 39.0 %collective-permute-start.18 = (f32[256,768]{1,0:T(8,128)}, f32[256,768]{1,0:T(8,128)}, u32[]{:S(2)}, u32[]{:S(2)}) collective-permute-start(f32[256,768]{1,0:T(8,128)} %collective-permute-done.17.refs_3_), channel_id=1, source_target_pairs={{0,2},{1,3},{2,0},{3,1},{4,6},{5,7},{6,4},{7,5},{8,10},{9,11},{10,... | collective-permute-start | bytes 2359304 | tf_op jit(solution)/shard_map/ppermute | solution.py:384
  241.3 4.2 %copy-start.7 = (f32[256,768]{1,0:T(8,128)}, f32[256,768]{1,0:T(8,128)S(1)}, u32[]{:S(2)}) copy-start(f32[256,768]{1,0:T(8,128)S(1)} %collective-permute-done.28.refs_6_) | copy-start | bytes 2359300
  241.3 67.7 %collective-permute-start.23 = (f32[256,768]{1,0:T(8,128)}, f32[256,768]{1,0:T(8,128)}, u32[]{:S(2)}, u32[]{:S(2)}) collective-permute-start(f32[256,768]{1,0:T(8,128)} %collective-permute-done.16.refs_3_), channel_id=1, source_target_pairs={{0,1},{1,0},{2,3},{3,2},{4,5},{5,4},{6,7},{7,6},{8,9},{9,8},{10,11... | collective-permute-start | bytes 2359304 | tf_op jit(solution)/shard_map/ppermute | solution.py:384
  245.5 63.6 %collective-permute-start.25 = (f32[256,768]{1,0:T(8,128)}, f32[256,768]{1,0:T(8,128)}, u32[]{:S(2)}, u32[]{:S(2)}) collective-permute-start(f32[256,768]{1,0:T(8,128)} %collective-permute-done.24.refs_5_), channel_id=1, source_target_pairs={{0,1},{1,0},{2,3},{3,2},{4,5},{5,4},{6,7},{7,6},{8,9},{9,8},{10,11... | collective-permute-start | bytes 2359304 | tf_op jit(solution)/shard_map/ppermute | solution.py:384
  245.5 1.0 copy-start.8
  245.5 81.2 %collective-permute-start.20 = (f32[256,768]{1,0:T(8,128)}, f32[256,768]{1,0:T(8,128)}, u32[]{:S(2)}, u32[]{:S(2)}) collective-permute-start(f32[256,768]{1,0:T(8,128)} %collective-permute-done.17.refs_3_), channel_id=1, source_target_pairs={{0,1},{1,0},{2,3},{3,2},{4,5},{5,4},{6,7},{7,6},{8,9},{9,8},{10,11... | collective-permute-start | bytes 2359304 | tf_op jit(solution)/shard_map/ppermute | solution.py:384
  262.3 64.4 %collective-permute-start.22 = (f32[256,768]{1,0:T(8,128)}, f32[256,768]{1,0:T(8,128)}, u32[]{:S(2)}, u32[]{:S(2)}) collective-permute-start(f32[256,768]{1,0:T(8,128)} %collective-permute-done.21.refs_5_), channel_id=1, source_target_pairs={{0,1},{1,0},{2,3},{3,2},{4,5},{5,4},{6,7},{7,6},{8,9},{9,8},{10,11... | collective-permute-start | bytes 2359304 | tf_op jit(solution)/shard_map/ppermute | solution.py:384
  278.7 65.7 %collective-permute-start.19 = (f32[256,768]{1,0:T(8,128)}, f32[256,768]{1,0:T(8,128)}, u32[]{:S(2)}, u32[]{:S(2)}) collective-permute-start(f32[256,768]{1,0:T(8,128)} %collective-permute-done.18.refs_3_), channel_id=1, source_target_pairs={{0,1},{1,0},{2,3},{3,2},{4,5},{5,4},{6,7},{7,6},{8,9},{9,8},{10,11... | collective-permute-start | bytes 2359304 | tf_op jit(solution)/shard_map/ppermute | solution.py:384

commit v7 on v6

--- a/solution.py
+++ b/solution.py
@@ -14,6 +14,7 @@
 VMEM_BYTES = 64 * 2**20
 LANES = 128
 SUB = 8
+PARTS = 4
 SLOTS = 4
 f32 = jnp.float32
 bf16 = jnp.bfloat16
@@ -74,8 +75,24 @@
     dy_ref,
     dyr_ref,
     cs_hbm,
-    keep_hbm,
-    send_hbm,
+    *refs,
+):
+    outs, scratch = refs[:PARTS], refs[PARTS:]
+    transform_parts(
+        col_ref, phase_ref, val_hbm, cond_ref, dz_ref, dy_ref, dyr_ref, cs_hbm, outs, *scratch
+    )
+
+
+def transform_parts(
+    col_ref,
+    phase_ref,
+    val_hbm,
+    cond_ref,
+    dz_ref,
+    dy_ref,
+    dyr_ref,
+    cs_hbm,
+    outs,
     val_scr,
     cs_scr,
     z_scr,
@@ -152,7 +169,8 @@
     m1 = (sub1 % 2) == 0
     kzs, kyq, _, _, _ = tab_scr.shape
     tab = tab_scr.reshape(kzs * kyq * 4 * SUB, lanes)
-    quads = keep_hbm.shape[0]
+    quads = outs[0].shape[0]
+    low4 = sub1 < 4
     phases.wait()
 
     def quad(q):
@@ -160,32 +178,26 @@
         for i in range(4):
             d = tab[pl.ds(pl.multiple_of(col_ref[q * 4 + i], SUB), SUB), :]
             at = pl.ds(pl.multiple_of(phase_ref[q * 4 + i], SUB), SUB)
-            t.append(d * cs_scr[0, at, :] + roll_sub(d, 4) * cs_scr[1, at, :])
+            p = cs_scr[at, :]
+            turned = roll_sub(p, 4)
+            t.append(d * jnp.where(low4, p, turned) + roll_sub(d, 4) * jnp.where(low4, turned, -p))
         v0 = jnp.where(m2, t[0], roll_sub(t[2], 2)) + jnp.where(m2, roll_sub(t[0], -2), t[2])
         v1 = jnp.where(m2, t[1], roll_sub(t[3], 2)) + jnp.where(m2, roll_sub(t[1], -2), t[3])
         out_scr[q] = jnp.where(m1, v0, roll_sub(v1, 1)) + jnp.where(m1, roll_sub(v0, -1), v1)
 
-    at_once = math.gcd(quads // 2, SUB)
     copies = []
-    for n, (out_hbm, first, at, size) in enumerate(
-        (
-            (send_hbm, quads, 0, quads),
-            (keep_hbm, 0, 0, quads // 2),
-            (keep_hbm, 0, quads // 2, quads // 2),
-        )
-    ):
-        in_steps(size, at_once, lambda q, start=first + at: quad(start + q))
+    for n in reversed(range(PARTS)):
+        first = n * quads
+        in_steps(quads, math.gcd(quads, SUB), lambda q, first=first: quad(first + q))
         copies.append(
-            pltpu.make_async_copy(
-                out_scr.at[pl.ds(first + at, size)], out_hbm.at[pl.ds(at, size)], out_sems.at[n]
-            )
+            pltpu.make_async_copy(out_scr.at[pl.ds(first, quads)], outs[n], out_sems.at[n])
         )
         copies[-1].start()
     for copy in copies:
         copy.wait()
 
 
-def transform(col, phase, val, cond, cs, num_g):
+def transform(col, phase, val, cond, c, cs, num_g):
     slots, size_y, size_z, lanes = val.shape
     dz = jnp.asarray(split_np(z_table(size_z)))
     full, real_only = y_tables(size_y)
@@ -195,9 +207,19 @@
     hbm = pl.BlockSpec(memory_space=pl.ANY)
     return pl.pallas_call(
         transform_kernel,
-        out_shape=(jax.ShapeDtypeStruct((num_g // 8, SUB, lanes), f32),) * 2,
-        in_specs=[smem, smem, hbm, vmem, vmem, vmem, vmem, hbm],
-        out_specs=(hbm, hbm),
+        grid=(1,),
+        out_shape=(jax.ShapeDtypeStruct((num_g // 4 // PARTS, SUB, lanes), f32),) * PARTS,
+        in_specs=[
+            smem,
+            smem,
+            hbm,
+            pl.BlockSpec((None,) + cond.shape[1:], lambda i: (c, 0, 0, 0, 0)),
+            vmem,
+            vmem,
+            vmem,
+            hbm,
+        ],
+        out_specs=(hbm,) * PARTS,
         scratch_shapes=[
             pltpu.VMEM(val.shape, f32),
             pltpu.VMEM(cs.shape, f32),
@@ -205,7 +227,7 @@
             pltpu.VMEM((size_z // 2 + 1, size_y // 4, 4, SUB, lanes), f32),
             pltpu.VMEM((num_g // 4, SUB, lanes), f32),
             pltpu.SemaphoreType.DMA((slots + 1,)),
-            pltpu.SemaphoreType.DMA((3,)),
+            pltpu.SemaphoreType.DMA((PARTS,)),
         ],
         compiler_params=pltpu.CompilerParams(vmem_limit_bytes=VMEM_BYTES),
         name="transform",
@@ -221,14 +243,18 @@
 def fill_left(w_ref, own_ref, left_scr):
     freqs = w_ref.shape[0]
     rows, pairs2 = own_ref.shape
+    pairs = pairs2 // 2
 
     def fill(w, carry):
         row = w_ref[pl.ds(w, 1), :]
-        high, low = split_lanes(own_ref[...] * jnp.concatenate([row, row], axis=1))
+        a = own_ref[:, :pairs] * row
+        b = own_ref[:, pairs:] * row
         at = pl.ds(pl.multiple_of(w * rows, rows), rows)
-        left_scr[at, :pairs2] = high
-        left_scr[at, pairs2 : 2 * pairs2] = high
-        left_scr[at, 2 * pairs2 :] = low
+        for n, side in enumerate((a + b, a, b)):
+            high, low = split_lanes(side)
+            left_scr[at, (3 * n) * pairs : (3 * n + 1) * pairs] = high
+            left_scr[at, (3 * n + 1) * pairs : (3 * n + 2) * pairs] = high
+            left_scr[at, (3 * n + 2) * pairs : (3 * n + 3) * pairs] = low
         return carry
 
     lax.fori_loop(0, freqs, fill, 0)
@@ -237,14 +263,21 @@
 def chi_tile(block, left_scr, real_ref, imag_ref):
     freqs, rows, _ = real_ref.shape
     pairs = block.shape[1] // 2
-    turned = jnp.concatenate([-block[:, pairs:], block[:, :pairs]], axis=1)
-    for value, out_ref in ((block, real_ref), (turned, imag_ref)):
-        high, low = split_lanes(value)
+    c, d = block[:, :pairs], block[:, pairs:]
+    got = []
+    for n, side in enumerate((c, c + d, c - d)):
+        high, low = split_lanes(side)
         right = jnp.concatenate([high, low, high], axis=1)
-        got = lax.dot_general(
-            left_scr[...], right, (((1,), (1,)), ((), ())), preferred_element_type=f32
+        got.append(
+            lax.dot_general(
+                left_scr[:, 3 * n * pairs : 3 * (n + 1) * pairs],
+                right,
+                (((1,), (1,)), ((), ())),
+                preferred_element_type=f32,
+            )
         )
-        out_ref[...] = got.reshape(freqs, rows, -1)
+    real_ref[...] = (got[0] - got[2]).reshape(freqs, rows, -1)
+    imag_ref[...] = (got[0] - got[1]).reshape(freqs, rows, -1)
 
 
 def chi_kernel(w_ref, own_ref, all_ref, real_ref, imag_ref, left_scr):
@@ -272,7 +305,7 @@
             pl.BlockSpec((tile, 2 * pairs), lambda t: (t, 0)),
         ],
         out_specs=(out_spec, out_spec),
-        scratch_shapes=[pltpu.VMEM((freqs * rows, 6 * pairs), bf16)],
+        scratch_shapes=[pltpu.VMEM((freqs * rows, 9 * pairs), bf16)],
         name="chi",
     )(weights, own, everyone)
 
@@ -333,7 +366,7 @@
             + [hbm] * (len(pieces) + len(olds)),
             out_specs=(out_spec, out_spec),
             scratch_shapes=[
-                pltpu.VMEM((freqs * rows, 6 * pairs), bf16),
+                pltpu.VMEM((freqs * rows, 9 * pairs), bf16),
                 pltpu.VMEM((len(blocks), rows, 2 * pairs), f32),
                 pltpu.SemaphoreType.DMA((len(pieces),)),
             ],
@@ -384,14 +417,14 @@
     return lax.ppermute(value, "blk", pairs)
 
 
-def reduce_scatter(keep, other, links, before):
-    half = keep.shape[0] // 2
-    got = send(other, links.core)
-    far = send(keep[half:] + got[half:], links.y)
+def reduce_scatter(near, far, near_other, far_other, links, before):
+    far = far + send(far_other, links.core)
+    got = send(near_other, links.core)
+    far = send(far, links.y)
     if before:
         far, *_ = lax.optimization_barrier((far, *before))
-    near = keep[:half] + got[:half] + far
-    block = half // 4
+    near = near + got + far
+    block = near.shape[0] // 4
     to_cw, to_ccw, next_cw, mine = lax.optimization_barrier(
         tuple(near[i * block : (i + 1) * block] for i in (2, 3, 1, 0))
     )
@@ -427,14 +460,10 @@
     ang = (k[:, None] * x[None, :] % size_x).astype(f32) * (2.0 * math.pi / size_x)
     live = (jnp.arange(SLOTS) < planes).astype(f32) * norm
     cos_t, sin_t = jnp.cos(ang) * live, jnp.sin(ang) * live
-    plain = jnp.stack(
-        [jnp.concatenate([cos_t, cos_t], 1), jnp.concatenate([sin_t, -sin_t], 1)]
+    table = jnp.stack(
+        [jnp.concatenate([cos_t, sin_t], axis=1), jnp.concatenate([cos_t, -sin_t], axis=1)]
     )
-    mirror = jnp.stack(
-        [jnp.concatenate([cos_t, -cos_t], 1), jnp.concatenate([-sin_t, -sin_t], 1)]
-    )
-    table = jnp.concatenate([plain, mirror], axis=1)
-    return jnp.broadcast_to(table.reshape(2, -1, 1), (2, table[0].size, LANES))
+    return jnp.broadcast_to(table.reshape(-1, 1), (table.size, LANES))
 
 
 def polarizability(psi_val, psi_cond, e_val, e_cond, occ, freq, gmap):
@@ -472,17 +501,21 @@
         ids = table[count:]
     owned = []
     for c in range(num_cond):
-        keep, other = transform(pick[0], pick[1], val, cond[c], cs, num_g)
+        made = transform(pick[0], pick[1], val, cond, c, cs, num_g)
         if links is None:
-            whole = jnp.concatenate([keep, other])
+            whole = jnp.concatenate(made)
             owned.append((lax.psum_scatter(whole, "blk", scatter_dimension=0, tiled=True),))
         else:
             before = owned[-1][1:] if c == num_cond - 1 else ()
-            owned.append(reduce_scatter(keep, other, links, before))
+            owned.append(reduce_scatter(*made, links, before))
     for c, parts in enumerate(owned):
         owned[c] = sum(parts[1:], parts[0])
     own = jnp.stack(owned).reshape(num_cond, -1, 2, 4, num_val)
-    own = jnp.transpose(own, (1, 3, 2, 0, 4)).reshape(-1, 2 * pairs)
+    rows = own.shape[1] * 4
+    turned = lax.dynamic_slice_in_dim(mirrored, lax.axis_index("blk") * rows, rows)
+    sign = jnp.where(turned, -1.0, 1.0).astype(f32)
+    signs = jnp.stack([jnp.ones_like(sign), sign], axis=1).reshape(-1, 4, 2, 1, 1)
+    own = (jnp.transpose(own, (1, 3, 2, 0, 4)) * signs).reshape(-1, 2 * pairs)
 
     gaps = e_val[None, :] - e_cond[:, None]
     gaps = gaps.reshape(1, pairs)

time: 357 us -> 346 us (0.969)
  starting transfers between devices: 40.6 us -> 32.2 us
  other arithmetic: 8.91 us -> 16.1 us
  Pallas kernels: 144 us -> 137 us
  waiting for transfers between devices: 150 us -> 146 us
    ppermute x30 -> x33, starting transfers between devices: 40.6 us -> 32.2 us  [send(): return lax.ppermute(value, 'blk', pairs)]
    pallas_call x5, Pallas kernels: 75.6 us -> 68.6 us  [chi_group(): pl.pallas_call(functools.partial(chi_group_kernel, counts, old is not Non...]
    ppermute x30 -> x33, waiting for transfers between devices: 150 us -> 146 us  [send(): return lax.ppermute(value, 'blk', pairs)]
  transfers between devices with their start and end apart: 30 -> 33, of which waited for: 15 -> 12; matrix products, arithmetic and copies ran while one was open for 2% -> 5% of each run, Pallas kernels for 31% -> 30%
where the time goes in v7:
time: 346 us; the launch traced here: 345 us
  waiting for transfers between devices  146 us (42%)
  Pallas kernels  137 us (40%)
  starting transfers between devices  32.2 us (9%)
  other arithmetic  16.1 us (5%)
  local copies, waits for them, and re-layouts  12 us (3%)
    ppermute x33, waiting for transfers between devices, send(): return lax.ppermute(value, 'blk', pairs)  146 us
    pallas_call x5, Pallas kernels, chi_group(): pl.pallas_call(functools.partial(chi_group_kernel, counts, old is not Non...  68.6 us
    pallas_call x3, Pallas kernels, transform(): pl.pallas_call(transform_kernel, grid=(1,), out_shape=(jax.ShapeDtypeStru...  68.3 us
    ppermute x33, starting transfers between devices, send(): return lax.ppermute(value, 'blk', pairs)  32.2 us
  transfers between devices with their start and end apart: 33, of which 12 were waited for; matrix products, arithmetic and copies ran while one was open for 5% of the time, Pallas kernels for 30%

profile of v7, /device:TPU:0, one launch (start us, length us, event | category | flops | bytes accessed | tf_op | source)
XLA Modules:
  0.0 344.9 jit_solution(13618820814735511284)
XLA Ops:
  1.0 0.7 constant_dynamic-slice_fusion
  1.7 0.6 copy-done.12
  2.3 0.8 fusion.2
  3.1 0.6 gather_fusion
  3.7 0.6 fusion.24
  4.3 3.1 copy.40
  7.4 1.0 broadcast_in_dim.20.cs_hbm
  8.4 22.8 %transform.4 = (f32[256,8,128]{2,1,0:T(8,128)}, f32[256,8,128]{2,1,0:T(8,128)}, f32[256,8,128]{2,1,0:T(8,128)}, f32[256,8,128]{2,1,0:T(8,128)}) custom-call(s32[4096]{0:T(1024)} %bitcast.45, s32[4096]{0:T(1024)} %bitcast.42, f32[4,64,64,128]{3,2,1,0:T(8,128)} %bitcast.31, f32[3,4,8,64,8]{4,3,2,1,0:T(8,128)} %bitcast.34, ...), custom_call_target="tpu_custom_call" | custom-call | tf_op jit(solution)/shard_map/transform/pallas_call | solution.py:208
  31.2 0.6 collective-permute-start.7
  31.8 22.8 %transform.3 = (f32[256,8,128]{2,1,0:T(8,128)}, f32[256,8,128]{2,1,0:T(8,128)}, f32[256,8,128]{2,1,0:T(8,128)}, f32[256,8,128]{2,1,0:T(8,128)}) custom-call(s32[4096]{0:T(1024)} %bitcast.46, s32[4096]{0:T(1024)} %bitcast.43, f32[4,64,64,128]{3,2,1,0:T(8,128)} %bitcast.32, f32[3,4,8,64,8]{4,3,2,1,0:T(8,128)} %bitcast.35, ...), custom_call_target="tpu_custom_call" | custom-call | tf_op jit(solution)/shard_map/transform/pallas_call | solution.py:208
  54.7 22.7 %transform.5 = (f32[256,8,128]{2,1,0:T(8,128)}, f32[256,8,128]{2,1,0:T(8,128)}, f32[256,8,128]{2,1,0:T(8,128)}, f32[256,8,128]{2,1,0:T(8,128)}) custom-call(s32[4096]{0:T(1024)} %bitcast.47, s32[4096]{0:T(1024)} %bitcast.44, f32[4,64,64,128]{3,2,1,0:T(8,128)} %bitcast.33, f32[3,4,8,64,8]{4,3,2,1,0:T(8,128)} %bitcast.36, ...), custom_call_target="tpu_custom_call" | custom-call | tf_op jit(solution)/shard_map/transform/pallas_call | solution.py:208
  77.5 0.6 collective-permute-start.13
  78.2 1.6 add.143
  79.9 2.9 collective-permute-start.8
  82.7 1.6 add.137
  84.6 0.4 collective-permute-start.12
  85.0 1.3 add.149
  86.4 1.7 collective-permute-start.14
  88.1 18.6 %collective-permute-done.8 = f32[256,8,128]{2,1,0:T(8,128)S(1)} collective-permute-done((f32[256,8,128]{2,1,0:T(8,128)S(1)}, f32[256,8,128]{2,1,0:T(8,128)S(1)}, u32[]{:S(2)}, u32[]{:S(2)}) %collective-permute-start.8) | collective-permute-done | bytes 1048608 | tf_op jit(solution)/shard_map/ppermute | solution.py:417
  106.7 1.4 add_add_fusion.1
  108.1 0.9 fusion.23
  109.0 3.2 collective-permute-start.10
  112.1 17.1 %collective-permute-done.2 = f32[256,8,128]{2,1,0:T(8,128)S(1)} collective-permute-done((f32[256,8,128]{2,1,0:T(8,128)S(1)}, f32[256,8,128]{2,1,0:T(8,128)S(1)}, u32[]{:S(2)}, u32[]{:S(2)}) %collective-permute-start.2) | collective-permute-done | bytes 1048608 | tf_op jit(solution)/shard_map/ppermute | solution.py:417
  129.2 1.4 add_add_fusion.2
  130.6 0.9 fusion.21
  131.5 3.2 collective-permute-start.4
  134.6 0.7 add.146
  135.4 2.9 collective-permute-start.11
  138.3 6.1 %collective-permute-done.4 = f32[64,8,128]{2,1,0:T(8,128)} collective-permute-done((f32[64,8,128]{2,1,0:T(8,128)}, f32[64,8,128]{2,1,0:T(8,128)}, u32[]{:S(2)}, u32[]{:S(2)}) %collective-permute-start.4) | collective-permute-done | bytes 262176 | tf_op jit(solution)/shard_map/ppermute | solution.py:417
  144.4 1.7 add.140
  146.1 5.1 %collective-permute-done.14 = f32[256,8,128]{2,1,0:T(8,128)} collective-permute-done((f32[256,8,128]{2,1,0:T(8,128)S(1)}, f32[256,8,128]{2,1,0:T(8,128)}, u32[]{:S(2)}, u32[]{:S(2)}) %collective-permute-start.14) | collective-permute-done | bytes 1048608 | tf_op jit(solution)/shard_map/ppermute | solution.py:417
  151.2 2.9 collective-permute-start.5
  154.1 1.4 add_add_fusion
  155.5 2.2 collective-permute-start.16
  158.2 11.8 %collective-permute-done.16 = f32[64,8,128]{2,1,0:T(8,128)S(1)} collective-permute-done((f32[64,8,128]{2,1,0:T(8,128)S(1)}, f32[64,8,128]{2,1,0:T(8,128)S(1)}, u32[]{:S(2)}, u32[]{:S(2)}) %collective-permute-start.16) | collective-permute-done | bytes 262176 | tf_op jit(solution)/shard_map/ppermute | solution.py:417
  170.0 2.8 collective-permute-start.17
  172.8 1.1 add_add_fusion.5
  173.9 0.3 copy.42
  174.1 1.2 add_add_fusion.4
  175.6 4.5 %collective-permute-done.17 = f32[64,8,128]{2,1,0:T(8,128)S(1)} collective-permute-done((f32[64,8,128]{2,1,0:T(8,128)S(1)}, f32[64,8,128]{2,1,0:T(8,128)S(1)}, u32[]{:S(2)}, u32[]{:S(2)}) %collective-permute-start.17) | collective-permute-done | bytes 262176 | tf_op jit(solution)/shard_map/ppermute | solution.py:417
  180.4 0.9 fusion
  181.3 0.4 reshape.110.refs_2_.refs_3_
  181.7 1.7 collective-permute-start.18
  183.4 17.8 %collective-permute-done.18.refs_5_ = f32[256,768]{1,0:T(8,128)S(1)} collective-permute-done((f32[256,768]{1,0:T(8,128)S(1)}, f32[256,768]{1,0:T(8,128)S(1)}, u32[]{:S(2)}, u32[]{:S(2)}) %collective-permute-start.18) | collective-permute-done | bytes 786464 | tf_op jit(solution)/shard_map/ppermute | solution.py:417
  201.2 0.8 collective-permute-start.19
  202.0 1.5 collective-permute-start.29
  203.6 17.3 %collective-permute-done.19.refs_3_ = f32[256,768]{1,0:T(8,128)} collective-permute-done((f32[256,768]{1,0:T(8,128)S(1)}, f32[256,768]{1,0:T(8,128)}, u32[]{:S(2)}, u32[]{:S(2)}) %collective-permute-start.19) | collective-permute-done | bytes 786464 | tf_op jit(solution)/shard_map/ppermute | solution.py:417
  220.8 1.5 collective-permute-start.27
  222.6 0.9 copy-done.2
  223.5 0.5 collective-permute-start.24
  224.1 14.6 %collective-permute-done.20.refs_3_ = f32[256,768]{1,0:T(8,128)} collective-permute-done((f32[256,768]{1,0:T(8,128)S(1)}, f32[256,768]{1,0:T(8,128)}, u32[]{:S(2)}, u32[]{:S(2)}) %collective-permute-start.20) | collective-permute-done | bytes 786464 | tf_op jit(solution)/shard_map/ppermute | solution.py:417
  238.7 1.5 collective-permute-start.21
  240.2 1.1 collective-permute-done.27.refs_5_
  241.4 0.6 collective-permute-start.23
  241.9 0.4 copy-done.6
  242.3 15.9 %collective-permute-done.24.refs_5_ = f32[256,768]{1,0:T(8,128)} collective-permute-done((f32[256,768]{1,0:T(8,128)}, f32[256,768]{1,0:T(8,128)}, u32[]{:S(2)}, u32[]{:S(2)}) %collective-permute-start.24) | collective-permute-done | bytes 786464 | tf_op jit(solution)/shard_map/ppermute | solution.py:417
  258.2 16.4 %collective-permute-done.21.refs_3_ = f32[256,768]{1,0:T(8,128)} collective-permute-done((f32[256,768]{1,0:T(8,128)}, f32[256,768]{1,0:T(8,128)}, u32[]{:S(2)}, u32[]{:S(2)}) %collective-permute-start.21) | collective-permute-done | bytes 786464 | tf_op jit(solution)/shard_map/ppermute | solution.py:417
  274.7 0.6 slice_bitcast_fusion.refs_0_
  275.3 0.7 divide_multiply_fusion.refs_1_
  276.0 10.3 %chi.5 = (f32[5,256,4096]{2,1,0:T(8,128)}, f32[5,256,4096]{2,1,0:T(8,128)}) custom-call(s32[16]{0:T(128)} %slice_bitcast_fusion.refs_0_, f32[5,384]{1,0:T(8,128)} %divide_multiply_fusion.refs_1_, f32[256,768]{1,0:T(8,128)} %copy-done, f32[256,768]{1,0:T(8,128)} %copy-done, f32[256,768]{1,0:T(8,128)} %copy-done.2), custom_call_target="tpu_custom_call" | custom-call | tf_op jit(solution)/shard_map/chi/pallas_call | solution.py:357
  286.3 15.9 %chi.6 = (f32[5,256,4096]{2,1,0:T(8,128)}, f32[5,256,4096]{2,1,0:T(8,128)}) custom-call(s32[16]{0:T(128)} %slice_bitcast_fusion.refs_0_, f32[5,384]{1,0:T(8,128)} %divide_multiply_fusion.refs_1_, f32[256,768]{1,0:T(8,128)} %copy-done, f32[256,768]{1,0:T(8,128)} %copy-done.4, f32[256,768]{1,0:T(8,128)} %copy-done.6, ...), custom_call_target="tpu_custom_call", output_to_operand_aliasing={{0}: (7, {}), {1}: (8, {})} | custom-call | tf_op jit(solution)/shard_map/chi/pallas_call | solution.py:357
  302.2 15.9 %chi.7 = (f32[5,256,4096]{2,1,0:T(8,128)}, f32[5,256,4096]{2,1,0:T(8,128)}) custom-call(s32[16]{0:T(128)} %slice_bitcast_fusion.refs_0_, f32[5,384]{1,0:T(8,128)} %divide_multiply_fusion.refs_1_, f32[256,768]{1,0:T(8,128)} %copy-done, f32[256,768]{1,0:T(8,128)} %collective-permute-done.19.refs_3_, ...), custom_call_target="tpu_custom_call", output_to_operand_aliasing={{0}: (7, {}), {1}: (8, {})} | custom-call | tf_op jit(solution)/shard_map/chi/pallas_call | solution.py:357
  318.2 15.9 %chi.8 = (f32[5,256,4096]{2,1,0:T(8,128)}, f32[5,256,4096]{2,1,0:T(8,128)}) custom-call(s32[16]{0:T(128)} %slice_bitcast_fusion.refs_0_, f32[5,384]{1,0:T(8,128)} %divide_multiply_fusion.refs_1_, f32[256,768]{1,0:T(8,128)} %copy-done, f32[256,768]{1,0:T(8,128)} %collective-permute-done.20.refs_3_, ...), custom_call_target="tpu_custom_call", output_to_operand_aliasing={{0}: (7, {}), {1}: (8, {})} | custom-call | tf_op jit(solution)/shard_map/chi/pallas_call | solution.py:357
  334.2 10.5 %chi.9 = (f32[5,256,4096]{2,1,0:T(8,128)}, f32[5,256,4096]{2,1,0:T(8,128)}) custom-call(s32[16]{0:T(128)} %slice_bitcast_fusion.refs_0_, f32[5,384]{1,0:T(8,128)} %divide_multiply_fusion.refs_1_, f32[256,768]{1,0:T(8,128)} %copy-done, f32[256,768]{1,0:T(8,128)} %collective-permute-done.21.refs_3_, ...), custom_call_target="tpu_custom_call", output_to_operand_aliasing={{0}: (5, {}), {1}: (6, {})} | custom-call | tf_op jit(solution)/shard_map/chi/pallas_call | solution.py:357
  (83 shorter events, 2.3 us)
Async XLA Ops:
  1.7 0.6 copy-start.12
  31.2 47.0 %collective-permute-start.7 = (f32[256,8,128]{2,1,0:T(8,128)}, f32[256,8,128]{2,1,0:T(8,128)}, u32[]{:S(2)}, u32[]{:S(2)}) collective-permute-start(f32[256,8,128]{2,1,0:T(8,128)} %get-tuple-element.50), channel_id=1, source_target_pairs={{0,1},{1,0},{2,3},{3,2},{4,5},{5,4},{6,7},{7,6},{8,9},{9,8},{10,11... | collective-permute-start | bytes 3145736 | tf_op jit(solution)/shard_map/ppermute | solution.py:417
  54.6 28.1 %collective-permute-start.1 = (f32[256,8,128]{2,1,0:T(8,128)}, f32[256,8,128]{2,1,0:T(8,128)}, u32[]{:S(2)}, u32[]{:S(2)}) collective-permute-start(f32[256,8,128]{2,1,0:T(8,128)} %get-tuple-element.42), channel_id=1, source_target_pairs={{0,1},{1,0},{2,3},{3,2},{4,5},{5,4},{6,7},{7,6},{8,9},{9,8},{10,11... | collective-permute-start | bytes 3145736 | tf_op jit(solution)/shard_map/ppermute | solution.py:417
  77.4 76.7 %copy-start.1 = (f32[256,8,128]{2,1,0:T(8,128)S(1)}, f32[256,8,128]{2,1,0:T(8,128)}, u32[]{:S(2)}) copy-start(f32[256,8,128]{2,1,0:T(8,128)} %get-tuple-element.55) | copy-start | bytes 3145732
  77.4 80.4 %copy-start.7 = (s32[4096]{0:T(1024)S(1)}, s32[4096]{0:T(1024)}, u32[]{:S(2)}) copy-start(s32[4096]{0:T(1024)} %param.23) | copy-start | bytes 49156
  77.4 197.2 %copy-start.10 = (s32[128]{0:T(128)S(1)}, s32[128]{0:T(128)}, u32[]{:S(2)}) copy-start(s32[128]{0:T(128)} %param.21) | copy-start | bytes 1540
  77.5 197.2 %copy-start.11 = (f32[5]{0:T(128)S(1)}, f32[5]{0:T(128)}, u32[]{:S(2)}) copy-start(f32[5]{0:T(128)} %param.22) | copy-start | bytes 64
  77.5 197.2 %copy-start.13 = (s32[1,32]{1,0:T(1,128)S(1)}, s32[1,32]{1,0:T(1,128)}, u32[]{:S(2)}) copy-start(s32[1,32]{1,0:T(1,128)} %copy-done.12) | copy-start | bytes 388
  77.5 197.8 %copy-start.8 = (f32[3]{0:T(128)S(1)}, f32[3]{0:T(128)}, u32[]{:S(2)}) copy-start(f32[3]{0:T(128)} %param.20) | copy-start | bytes 40
  77.5 197.7 %copy-start.9 = (f32[128]{0:T(128)S(1)}, f32[128]{0:T(128)}, u32[]{:S(2)}) copy-start(f32[128]{0:T(128)} %param.19) | copy-start | bytes 1540
  77.5 7.1 %collective-permute-start.13 = (f32[256,8,128]{2,1,0:T(8,128)}, f32[256,8,128]{2,1,0:T(8,128)S(1)}, u32[]{:S(2)}, u32[]{:S(2)}) collective-permute-start(f32[256,8,128]{2,1,0:T(8,128)} %get-tuple-element.58), channel_id=1, source_target_pairs={{0,1},{1,0},{2,3},{3,2},{4,5},{5,4},{6,7},{7,6},{8,9},{9,8},{10,11... | collective-permute-start | bytes 3145736 | tf_op jit(solution)/shard_map/ppermute | solution.py:417
  78.1 8.3 %collective-permute-start.6 = (f32[256,8,128]{2,1,0:T(8,128)}, f32[256,8,128]{2,1,0:T(8,128)S(1)}, u32[]{:S(2)}, u32[]{:S(2)}) collective-permute-start(f32[256,8,128]{2,1,0:T(8,128)} %get-tuple-element.48), channel_id=1, source_target_pairs={{0,1},{1,0},{2,3},{3,2},{4,5},{5,4},{6,7},{7,6},{8,9},{9,8},{10,11... | collective-permute-start | bytes 3145736 | tf_op jit(solution)/shard_map/ppermute | solution.py:417
  79.9 26.9 %collective-permute-start.8 = (f32[256,8,128]{2,1,0:T(8,128)S(1)}, f32[256,8,128]{2,1,0:T(8,128)S(1)}, u32[]{:S(2)}, u32[]{:S(2)}) collective-permute-start(f32[256,8,128]{2,1,0:T(8,128)S(1)} %add.143), channel_id=1, source_target_pairs={{0,2},{1,3},{2,0},{3,1},{4,6},{5,7},{6,4},{7,5},{8,10},{9,11},{10,... | collective-permute-start | bytes 3145736 | tf_op jit(solution)/shard_map/ppermute | solution.py:417
  82.7 29.4 %collective-permute-start = (f32[256,8,128]{2,1,0:T(8,128)}, f32[256,8,128]{2,1,0:T(8,128)S(1)}, u32[]{:S(2)}, u32[]{:S(2)}) collective-permute-start(f32[256,8,128]{2,1,0:T(8,128)} %get-tuple-element.40), channel_id=1, source_target_pairs={{0,1},{1,0},{2,3},{3,2},{4,5},{5,4},{6,7},{7,6},{8,9},{9,8},{10,11... | collective-permute-start | bytes 3145736 | tf_op jit(solution)/shard_map/ppermute | solution.py:417
  84.4 44.8 %collective-permute-start.2 = (f32[256,8,128]{2,1,0:T(8,128)S(1)}, f32[256,8,128]{2,1,0:T(8,128)S(1)}, u32[]{:S(2)}, u32[]{:S(2)}) collective-permute-start(f32[256,8,128]{2,1,0:T(8,128)S(1)} %add.137), channel_id=1, source_target_pairs={{0,2},{1,3},{2,0},{3,1},{4,6},{5,7},{6,4},{7,5},{8,10},{9,11},{10,... | collective-permute-start | bytes 3145736 | tf_op jit(solution)/shard_map/ppermute | solution.py:417
  84.6 69.5 %collective-permute-start.12 = (f32[256,8,128]{2,1,0:T(8,128)}, f32[256,8,128]{2,1,0:T(8,128)S(1)}, u32[]{:S(2)}, u32[]{:S(2)}) collective-permute-start(f32[256,8,128]{2,1,0:T(8,128)} %get-tuple-element.56), channel_id=1, source_target_pairs={{0,1},{1,0},{2,3},{3,2},{4,5},{5,4},{6,7},{7,6},{8,9},{9,8},{10,11... | collective-permute-start | bytes 3145736 | tf_op jit(solution)/shard_map/ppermute | solution.py:417
  86.4 64.8 %collective-permute-start.14 = (f32[256,8,128]{2,1,0:T(8,128)S(1)}, f32[256,8,128]{2,1,0:T(8,128)}, u32[]{:S(2)}, u32[]{:S(2)}) collective-permute-start(f32[256,8,128]{2,1,0:T(8,128)S(1)} %add.149), channel_id=1, source_target_pairs={{0,2},{1,3},{2,0},{3,1},{4,6},{5,7},{6,4},{7,5},{8,10},{9,11},{10,... | collective-permute-start | bytes 3145736 | tf_op jit(solution)/shard_map/ppermute | solution.py:417
  109.0 25.7 %collective-permute-start.10 = (f32[64,8,128]{2,1,0:T(8,128)S(1)}, f32[64,8,128]{2,1,0:T(8,128)S(1)}, u32[]{:S(2)}, u32[]{:S(2)}) collective-permute-start(f32[64,8,128]{2,1,0:T(8,128)S(1)} %get-tuple-element.54), channel_id=1, source_target_pairs={{0,8},{1,9},{2,10},{3,11},{4,0},{5,1},{6,2},{7,3},{8,12},{9,13},{1... | collective-permute-start | bytes 786440 | tf_op jit(solution)/shard_map/ppermute | solution.py:417
  131.5 12.9 %collective-permute-start.4 = (f32[64,8,128]{2,1,0:T(8,128)}, f32[64,8,128]{2,1,0:T(8,128)}, u32[]{:S(2)}, u32[]{:S(2)}) collective-permute-start(f32[64,8,128]{2,1,0:T(8,128)} %get-tuple-element.46), channel_id=1, source_target_pairs={{0,8},{1,9},{2,10},{3,11},{4,0},{5,1},{6,2},{7,3},{8,12},{9,13},{1... | collective-permute-start | bytes 786440 | tf_op jit(solution)/shard_map/ppermute | solution.py:417
  134.6 19.4 %collective-permute-start.9 = (f32[64,8,128]{2,1,0:T(8,128)}, f32[64,8,128]{2,1,0:T(8,128)}, u32[]{:S(2)}, u32[]{:S(2)}) collective-permute-start(f32[64,8,128]{2,1,0:T(8,128)} %get-tuple-element.52), channel_id=1, source_target_pairs={{0,4},{1,5},{2,6},{3,7},{4,12},{5,13},{6,14},{7,15},{8,0},{9,1},{1... | collective-permute-start | bytes 786440 | tf_op jit(solution)/shard_map/ppermute | solution.py:417
  135.4 18.7 %collective-permute-start.11 = (f32[64,8,128]{2,1,0:T(8,128)}, f32[64,8,128]{2,1,0:T(8,128)}, u32[]{:S(2)}, u32[]{:S(2)}) collective-permute-start(f32[64,8,128]{2,1,0:T(8,128)} %add.146), channel_id=1, source_target_pairs={{0,8},{1,9},{2,10},{3,11},{4,0},{5,1},{6,2},{7,3},{8,12},{9,13},{1... | collective-permute-start | bytes 786440 | tf_op jit(solution)/shard_map/ppermute | solution.py:417
  144.4 28.4 %collective-permute-start.3 = (f32[64,8,128]{2,1,0:T(8,128)}, f32[64,8,128]{2,1,0:T(8,128)}, u32[]{:S(2)}, u32[]{:S(2)}) collective-permute-start(f32[64,8,128]{2,1,0:T(8,128)} %get-tuple-element.44), channel_id=1, source_target_pairs={{0,4},{1,5},{2,6},{3,7},{4,12},{5,13},{6,14},{7,15},{8,0},{9,1},{1... | collective-permute-start | bytes 786440 | tf_op jit(solution)/shard_map/ppermute | solution.py:417
  151.2 21.6 %collective-permute-start.5 = (f32[64,8,128]{2,1,0:T(8,128)}, f32[64,8,128]{2,1,0:T(8,128)S(1)}, u32[]{:S(2)}, u32[]{:S(2)}) collective-permute-start(f32[64,8,128]{2,1,0:T(8,128)} %add.140), channel_id=1, source_target_pairs={{0,8},{1,9},{2,10},{3,11},{4,0},{5,1},{6,2},{7,3},{8,12},{9,13},{1... | collective-permute-start | bytes 786440 | tf_op jit(solution)/shard_map/ppermute | solution.py:417
  155.5 14.4 %collective-permute-start.16 = (f32[64,8,128]{2,1,0:T(8,128)S(1)}, f32[64,8,128]{2,1,0:T(8,128)S(1)}, u32[]{:S(2)}, u32[]{:S(2)}) collective-permute-start(f32[64,8,128]{2,1,0:T(8,128)S(1)} %get-tuple-element.63), channel_id=1, source_target_pairs={{0,8},{1,9},{2,10},{3,11},{4,0},{5,1},{6,2},{7,3},{8,12},{9,13},{1... | collective-permute-start | bytes 786440 | tf_op jit(solution)/shard_map/ppermute | solution.py:417
  158.1 17.4 %collective-permute-start.15 = (f32[64,8,128]{2,1,0:T(8,128)S(1)}, f32[64,8,128]{2,1,0:T(8,128)S(1)}, u32[]{:S(2)}, u32[]{:S(2)}) collective-permute-start(f32[64,8,128]{2,1,0:T(8,128)S(1)} %get-tuple-element.61), channel_id=1, source_target_pairs={{0,4},{1,5},{2,6},{3,7},{4,12},{5,13},{6,14},{7,15},{8,0},{9,1},{1... | collective-permute-start | bytes 786440 | tf_op jit(solution)/shard_map/ppermute | solution.py:417
  170.0 10.1 %collective-permute-start.17 = (f32[64,8,128]{2,1,0:T(8,128)S(1)}, f32[64,8,128]{2,1,0:T(8,128)S(1)}, u32[]{:S(2)}, u32[]{:S(2)}) collective-permute-start(f32[64,8,128]{2,1,0:T(8,128)S(1)} %add.152), channel_id=1, source_target_pairs={{0,8},{1,9},{2,10},{3,11},{4,0},{5,1},{6,2},{7,3},{8,12},{9,13},{1... | collective-permute-start | bytes 786440 | tf_op jit(solution)/shard_map/ppermute | solution.py:417
  181.7 21.9 %copy-start = (f32[256,768]{1,0:T(8,128)}, f32[256,768]{1,0:T(8,128)S(1)}, u32[]{:S(2)}) copy-start(f32[256,768]{1,0:T(8,128)S(1)} %reshape.110.refs_2_.refs_3_) | copy-start | bytes 2359300
  181.7 19.5 %collective-permute-start.18 = (f32[256,768]{1,0:T(8,128)S(1)}, f32[256,768]{1,0:T(8,128)S(1)}, u32[]{:S(2)}, u32[]{:S(2)}) collective-permute-start(f32[256,768]{1,0:T(8,128)S(1)} %reshape.110.refs_2_.refs_3_), channel_id=1, source_target_pairs={{0,8},{1,9},{2,10},{3,11},{4,0},{5,1},{6,2},{7,3},{8,12},{9,13},{1... | collective-permute-start | bytes 2359304 | tf_op jit(solution)/shard_map/ppermute | solution.py:417
  201.2 22.8 %copy-start.3 = (f32[256,768]{1,0:T(8,128)}, f32[256,768]{1,0:T(8,128)S(1)}, u32[]{:S(2)}) copy-start(f32[256,768]{1,0:T(8,128)S(1)} %collective-permute-done.18.refs_5_) | copy-start | bytes 2359300
  201.2 19.6 %collective-permute-start.19 = (f32[256,768]{1,0:T(8,128)S(1)}, f32[256,768]{1,0:T(8,128)}, u32[]{:S(2)}, u32[]{:S(2)}) collective-permute-start(f32[256,768]{1,0:T(8,128)S(1)} %reshape.110.refs_2_.refs_3_), channel_id=1, source_target_pairs={{0,4},{1,5},{2,6},{3,7},{4,12},{5,13},{6,14},{7,15},{8,0},{9,1},{1... | collective-permute-start | bytes 2359304 | tf_op jit(solution)/shard_map/ppermute | solution.py:417
  202.0 20.3 %collective-permute-start.29 = (f32[256,768]{1,0:T(8,128)S(1)}, f32[256,768]{1,0:T(8,128)S(1)}, u32[]{:S(2)}, u32[]{:S(2)}) collective-permute-start(f32[256,768]{1,0:T(8,128)S(1)} %reshape.110.refs_2_.refs_3_), channel_id=1, source_target_pairs={{0,2},{1,3},{2,0},{3,1},{4,6},{5,7},{6,4},{7,5},{8,10},{9,11},{10,... | collective-permute-start | bytes 2359304 | tf_op jit(solution)/shard_map/ppermute | solution.py:417
  203.5 19.1 %collective-permute-start.32 = (f32[256,768]{1,0:T(8,128)S(1)}, f32[256,768]{1,0:T(8,128)S(1)}, u32[]{:S(2)}, u32[]{:S(2)}) collective-permute-start(f32[256,768]{1,0:T(8,128)S(1)} %reshape.110.refs_2_.refs_3_), channel_id=1, source_target_pairs={{0,1},{1,0},{2,3},{3,2},{4,5},{5,4},{6,7},{7,6},{8,9},{9,8},{10,11... | collective-permute-start | bytes 2359304 | tf_op jit(solution)/shard_map/ppermute | solution.py:417
  220.8 17.9 %collective-permute-start.20 = (f32[256,768]{1,0:T(8,128)S(1)}, f32[256,768]{1,0:T(8,128)}, u32[]{:S(2)}, u32[]{:S(2)}) collective-permute-start(f32[256,768]{1,0:T(8,128)S(1)} %collective-permute-done.18.refs_5_), channel_id=1, source_target_pairs={{0,8},{1,9},{2,10},{3,11},{4,0},{5,1},{6,2},{7,3},{8,12},{9,13},{1... | collective-permute-start | bytes 2359304 | tf_op jit(solution)/shard_map/ppermute | solution.py:417
  220.8 19.4 %collective-permute-start.31 = (f32[256,768]{1,0:T(8,128)S(1)}, f32[256,768]{1,0:T(8,128)S(1)}, u32[]{:S(2)}, u32[]{:S(2)}) collective-permute-start(f32[256,768]{1,0:T(8,128)S(1)} %collective-permute-done.18.refs_5_), channel_id=1, source_target_pairs={{0,1},{1,0},{2,3},{3,2},{4,5},{5,4},{6,7},{7,6},{8,9},{9,8},{10,11... | collective-permute-start | bytes 2359304 | tf_op jit(solution)/shard_map/ppermute | solution.py:417
  220.8 20.5 %collective-permute-start.27 = (f32[256,768]{1,0:T(8,128)S(1)}, f32[256,768]{1,0:T(8,128)}, u32[]{:S(2)}, u32[]{:S(2)}) collective-permute-start(f32[256,768]{1,0:T(8,128)S(1)} %collective-permute-done.18.refs_5_), channel_id=1, source_target_pairs={{0,2},{1,3},{2,0},{3,1},{4,6},{5,7},{6,4},{7,5},{8,10},{9,11},{10,... | collective-permute-start | bytes 2359304 | tf_op jit(solution)/shard_map/ppermute | solution.py:417
  222.4 19.0 %copy-start.4 = (f32[256,768]{1,0:T(8,128)}, f32[256,768]{1,0:T(8,128)S(1)}, u32[]{:S(2)}) copy-start(f32[256,768]{1,0:T(8,128)S(1)} %collective-permute-done.29.refs_3_) | copy-start | bytes 2359300
  222.4 19.0 %collective-permute-start.30 = (f32[256,768]{1,0:T(8,128)S(1)}, f32[256,768]{1,0:T(8,128)S(1)}, u32[]{:S(2)}, u32[]{:S(2)}) collective-permute-start(f32[256,768]{1,0:T(8,128)S(1)} %collective-permute-done.29.refs_3_), channel_id=1, source_target_pairs={{0,1},{1,0},{2,3},{3,2},{4,5},{5,4},{6,7},{7,6},{8,9},{9,8},{10,11... | collective-permute-start | bytes 2359304 | tf_op jit(solution)/shard_map/ppermute | solution.py:417
  222.6 0.9 copy-start.2
  223.5 34.7 %collective-permute-start.24 = (f32[256,768]{1,0:T(8,128)}, f32[256,768]{1,0:T(8,128)}, u32[]{:S(2)}, u32[]{:S(2)}) collective-permute-start(f32[256,768]{1,0:T(8,128)} %collective-permute-done.19.refs_3_), channel_id=1, source_target_pairs={{0,2},{1,3},{2,0},{3,1},{4,6},{5,7},{6,4},{7,5},{8,10},{9,11},{10,... | collective-permute-start | bytes 2359304 | tf_op jit(solution)/shard_map/ppermute | solution.py:417
  238.7 35.9 %collective-permute-start.21 = (f32[256,768]{1,0:T(8,128)}, f32[256,768]{1,0:T(8,128)}, u32[]{:S(2)}, u32[]{:S(2)}) collective-permute-start(f32[256,768]{1,0:T(8,128)} %collective-permute-done.20.refs_3_), channel_id=1, source_target_pairs={{0,2},{1,3},{2,0},{3,1},{4,6},{5,7},{6,4},{7,5},{8,10},{9,11},{10,... | collective-permute-start | bytes 2359304 | tf_op jit(solution)/shard_map/ppermute | solution.py:417
  240.2 1.2 copy-start.5
  240.2 62.0 %collective-permute-start.26 = (f32[256,768]{1,0:T(8,128)}, f32[256,768]{1,0:T(8,128)}, u32[]{:S(2)}, u32[]{:S(2)}) collective-permute-start(f32[256,768]{1,0:T(8,128)} %collective-permute-done.19.refs_3_), channel_id=1, source_target_pairs={{0,1},{1,0},{2,3},{3,2},{4,5},{5,4},{6,7},{7,6},{8,9},{9,8},{10,11... | collective-permute-start | bytes 2359304 | tf_op jit(solution)/shard_map/ppermute | solution.py:417
  241.4 60.9 %collective-permute-start.28 = (f32[256,768]{1,0:T(8,128)}, f32[256,768]{1,0:T(8,128)}, u32[]{:S(2)}, u32[]{:S(2)}) collective-permute-start(f32[256,768]{1,0:T(8,128)} %collective-permute-done.27.refs_5_), channel_id=1, source_target_pairs={{0,1},{1,0},{2,3},{3,2},{4,5},{5,4},{6,7},{7,6},{8,9},{9,8},{10,11... | collective-permute-start | bytes 2359304 | tf_op jit(solution)/shard_map/ppermute | solution.py:417
  241.4 0.9 copy-start.6
  241.4 76.8 %collective-permute-start.23 = (f32[256,768]{1,0:T(8,128)}, f32[256,768]{1,0:T(8,128)}, u32[]{:S(2)}, u32[]{:S(2)}) collective-permute-start(f32[256,768]{1,0:T(8,128)} %collective-permute-done.20.refs_3_), channel_id=1, source_target_pairs={{0,1},{1,0},{2,3},{3,2},{4,5},{5,4},{6,7},{7,6},{8,9},{9,8},{10,11... | collective-permute-start | bytes 2359304 | tf_op jit(solution)/shard_map/ppermute | solution.py:417
  258.2 60.0 %collective-permute-start.25 = (f32[256,768]{1,0:T(8,128)}, f32[256,768]{1,0:T(8,128)}, u32[]{:S(2)}, u32[]{:S(2)}) collective-permute-start(f32[256,768]{1,0:T(8,128)} %collective-permute-done.24.refs_5_), channel_id=1, source_target_pairs={{0,1},{1,0},{2,3},{3,2},{4,5},{5,4},{6,7},{7,6},{8,9},{9,8},{10,11... | collective-permute-start | bytes 2359304 | tf_op jit(solution)/shard_map/ppermute | solution.py:417
  274.6 59.5 %collective-permute-start.22 = (f32[256,768]{1,0:T(8,128)}, f32[256,768]{1,0:T(8,128)}, u32[]{:S(2)}, u32[]{:S(2)}) collective-permute-start(f32[256,768]{1,0:T(8,128)} %collective-permute-done.21.refs_3_), channel_id=1, source_target_pairs={{0,1},{1,0},{2,3},{3,2},{4,5},{5,4},{6,7},{7,6},{8,9},{9,8},{10,11... | collective-permute-start | bytes 2359304 | tf_op jit(solution)/shard_map/ppermute | solution.py:417

commit v8 on v7

--- a/solution.py
+++ b/solution.py
@@ -115,11 +115,12 @@
     phases.start()
 
     def z_stage(x, yg):
-        cond = cond_ref[x, yg]
+        cond = cond_ref[x]
         parts = []
         for j in range(SUB):
             block = val_scr[x, yg * SUB + j]
-            parts.append(block * jnp.broadcast_to(cond[:, j : j + 1], (size_z, lanes)))
+            y = yg * SUB + j
+            parts.append(block * jnp.broadcast_to(cond[:, y : y + 1], (size_z, lanes)))
         rhs = split3(jnp.concatenate(parts, axis=1))
         got = jnp.dot(dz_ref[...], rhs, preferred_element_type=f32)
         for j in range(SUB):
@@ -128,7 +129,8 @@
 
     def z_plane(x, carry):
         plane(x).wait()
-        in_steps(groups_y, 4, functools.partial(z_stage, x))
+        for yg in range(groups_y):
+            z_stage(x, yg)
         return carry
 
     lax.fori_loop(0, slots, z_plane, 0)
@@ -162,7 +164,7 @@
         block = jnp.concatenate([rows(kz), rows(half + kz)], axis=0)
         put(kz, jnp.dot(dy_ref[...], split3(block), preferred_element_type=f32))
 
-    in_steps(half - 1, 3, y_stage)
+    in_steps(half - 1, 5, y_stage)
 
     sub1 = lax.broadcasted_iota(jnp.int32, (SUB, lanes), 0)
     m2 = (sub1 % 4) < 2
@@ -188,7 +190,7 @@
     copies = []
     for n in reversed(range(PARTS)):
         first = n * quads
-        in_steps(quads, math.gcd(quads, SUB), lambda q, first=first: quad(first + q))
+        in_steps(quads, math.gcd(quads, 2 * SUB), lambda q, first=first: quad(first + q))
         copies.append(
             pltpu.make_async_copy(out_scr.at[pl.ds(first, quads)], outs[n], out_sems.at[n])
         )
@@ -213,7 +215,7 @@
             smem,
             smem,
             hbm,
-            pl.BlockSpec((None,) + cond.shape[1:], lambda i: (c, 0, 0, 0, 0)),
+            pl.BlockSpec((None,) + cond.shape[1:], lambda i: (c, 0, 0, 0)),
             vmem,
             vmem,
             vmem,
@@ -418,16 +420,22 @@
 
 
 def reduce_scatter(near, far, near_other, far_other, links, before):
-    far = far + send(far_other, links.core)
-    got = send(near_other, links.core)
-    far = send(far, links.y)
+    block = near.shape[0] // 4
+    got_far = send(far_other, links.core)
+    got_near = send(near_other, links.core)
     if before:
-        far, *_ = lax.optimization_barrier((far, *before))
-    near = near + got + far
-    block = near.shape[0] // 4
-    to_cw, to_ccw, next_cw, mine = lax.optimization_barrier(
-        tuple(near[i * block : (i + 1) * block] for i in (2, 3, 1, 0))
-    )
+        cuts = ((2 * block, 4 * block), (0, 2 * block))
+        high, low = (send(far[i:j] + got_far[i:j], links.y) for i, j in cuts)
+        high, *_ = lax.optimization_barrier((high, *before))
+        high = near[2 * block :] + got_near[2 * block :] + high
+        to_cw, to_ccw, near = lax.optimization_barrier((high[:block], high[block:], near))
+        low = near[: 2 * block] + got_near[: 2 * block] + low
+        mine, next_cw = low[:block], low[block:]
+    else:
+        near = near + got_near + send(far + got_far, links.y)
+        to_cw, to_ccw, next_cw, mine = lax.optimization_barrier(
+            tuple(near[i * block : (i + 1) * block] for i in (2, 3, 1, 0))
+        )
     two_back = send(to_cw, links.cw)
     ahead = send(to_ccw, links.ccw)
     next_cw = next_cw + two_back
@@ -475,12 +483,10 @@
     norm = 1.0 / math.sqrt(size_x * size_y * size_z)
 
     val = jnp.transpose(psi_val, (1, 2, 3, 0))
-    cond = jnp.transpose(
-        psi_cond.reshape(num_cond, planes, size_y // SUB, SUB, size_z), (0, 1, 2, 4, 3)
-    )
+    cond = jnp.transpose(psi_cond, (0, 1, 3, 2))
     if planes < SLOTS:
         val = jnp.pad(val, ((0, SLOTS - planes), (0, 0), (0, 0), (0, 0)))
-        cond = jnp.pad(cond, ((0, 0), (0, SLOTS - planes), (0, 0), (0, 0), (0, 0)))
+        cond = jnp.pad(cond, ((0, 0), (0, SLOTS - planes), (0, 0), (0, 0)))
 
     kz = gmap % size_z
     ky = gmap // size_z % size_y

time: 346 us -> 350 us (1.012)
  the two profiles are of different devices: /device:TPU:0 before, /device:TPU:17 now
where the time goes in v8:
time: 350 us
  Pallas kernels  128 us (37%)
  waiting for transfers between devices  128 us (37%)
  starting transfers between devices  64.3 us (18%)
  other arithmetic  16.2 us (5%)
  local copies, waits for them, and re-layouts  11.1 us (3%)
    ppermute x34, waiting for transfers between devices, send(): return lax.ppermute(value, 'blk', pairs)  128 us
    pallas_call x5, Pallas kernels, chi_group(): pl.pallas_call(functools.partial(chi_group_kernel, counts, old is not Non...  68.6 us
    ppermute x34, starting transfers between devices, send(): return lax.ppermute(value, 'blk', pairs)  64.3 us
    pallas_call x3, Pallas kernels, transform(): pl.pallas_call(transform_kernel, grid=(1,), out_shape=(jax.ShapeDtypeStru...  59.9 us
  transfers between devices with their start and end apart: 34, of which 13 were waited for; matrix products, arithmetic and copies ran while one was open for 5% of the time, Pallas kernels for 28%

profile of v8, /device:TPU:17, one launch (start us, length us, event | category | flops | bytes accessed | tf_op | source)
XLA Modules:
  0.0 349.6 jit_solution(4676055587311863758)
XLA Ops:
  1.0 0.7 constant_dynamic-slice_fusion
  2.2 0.8 fusion.5
  3.1 0.6 gather_fusion
  3.6 0.6 fusion.27
  4.3 1.9 copy.41
  6.2 1.0 broadcast_in_dim.20.cs_hbm
  7.2 20.0 %transform.4 = (f32[256,8,128]{2,1,0:T(8,128)}, f32[256,8,128]{2,1,0:T(8,128)}, f32[256,8,128]{2,1,0:T(8,128)}, f32[256,8,128]{2,1,0:T(8,128)}) custom-call(s32[4096]{0:T(1024)} %bitcast.43, s32[4096]{0:T(1024)} %bitcast.40, f32[4,64,64,128]{3,2,1,0:T(8,128)} %bitcast.30, f32[3,4,64,64]{3,2,1,0:T(8,128)} %bitcast.33, ...), custom_call_target="tpu_custom_call" | custom-call | tf_op jit(solution)/shard_map/transform/pallas_call | solution.py:210
  27.1 0.7 collective-permute-start.7
  27.9 19.9 %transform.3 = (f32[256,8,128]{2,1,0:T(8,128)}, f32[256,8,128]{2,1,0:T(8,128)}, f32[256,8,128]{2,1,0:T(8,128)}, f32[256,8,128]{2,1,0:T(8,128)}) custom-call(s32[4096]{0:T(1024)} %bitcast.44, s32[4096]{0:T(1024)} %bitcast.41, f32[4,64,64,128]{3,2,1,0:T(8,128)} %bitcast.31, f32[3,4,64,64]{3,2,1,0:T(8,128)} %bitcast.34, ...), custom_call_target="tpu_custom_call" | custom-call | tf_op jit(solution)/shard_map/transform/pallas_call | solution.py:210
  47.9 19.9 %transform.5 = (f32[256,8,128]{2,1,0:T(8,128)}, f32[256,8,128]{2,1,0:T(8,128)}, f32[256,8,128]{2,1,0:T(8,128)}, f32[256,8,128]{2,1,0:T(8,128)}) custom-call(s32[4096]{0:T(1024)} %bitcast.45, s32[4096]{0:T(1024)} %bitcast.42, f32[4,64,64,128]{3,2,1,0:T(8,128)} %bitcast.32, f32[3,4,64,64]{3,2,1,0:T(8,128)} %bitcast.35, ...), custom_call_target="tpu_custom_call" | custom-call | tf_op jit(solution)/shard_map/transform/pallas_call | solution.py:210
  68.6 1.6 add.152
  70.2 1.3 collective-permute-start.8
  71.6 0.7 collective-permute-start
  72.3 1.6 add.146
  74.5 2.3 slice_add_fusion
  76.8 1.2 collective-permute-start.14
  78.1 16.5 %collective-permute-done.8 = f32[256,8,128]{2,1,0:T(8,128)S(1)} collective-permute-done((f32[256,8,128]{2,1,0:T(8,128)S(1)}, f32[256,8,128]{2,1,0:T(8,128)S(1)}, u32[]{:S(2)}, u32[]{:S(2)}) %collective-permute-start.8) | collective-permute-done | bytes 1048608 | tf_op jit(solution)/shard_map/ppermute | solution.py:419
  94.6 1.4 add_add_fusion
  96.0 0.9 fusion.25
  96.8 1.3 collective-permute-start.10
  98.1 18.9 %collective-permute-done.2 = f32[256,8,128]{2,1,0:T(8,128)S(1)} collective-permute-done((f32[256,8,128]{2,1,0:T(8,128)S(1)}, f32[256,8,128]{2,1,0:T(8,128)S(1)}, u32[]{:S(2)}, u32[]{:S(2)}) %collective-permute-start.2) | collective-permute-done | bytes 1048608 | tf_op jit(solution)/shard_map/ppermute | solution.py:419
  117.1 1.4 add_add_fusion.1
  118.4 0.9 fusion.24
  119.3 1.3 collective-permute-start.4
  120.6 1.1 collective-permute-start.9
  121.7 1.7 add.155
  123.8 2.4 collective-permute-done.4
  126.2 1.2 collective-permute-start.15
  127.8 0.6 collective-permute-done.14
  128.5 4.8 %collective-permute-done.9 = f32[64,8,128]{2,1,0:T(8,128)} collective-permute-done((f32[64,8,128]{2,1,0:T(8,128)}, f32[64,8,128]{2,1,0:T(8,128)}, u32[]{:S(2)}, u32[]{:S(2)}) %collective-permute-start.9) | collective-permute-done | bytes 262176 | tf_op jit(solution)/shard_map/ppermute | solution.py:419
  133.3 4.7 %collective-permute-start.5 = (f32[64,8,128]{2,1,0:T(8,128)S(1)}, f32[64,8,128]{2,1,0:T(8,128)S(1)}, u32[]{:S(2)}, u32[]{:S(2)}) collective-permute-start(f32[64,8,128]{2,1,0:T(8,128)S(1)} %add.149), channel_id=1, source_target_pairs={{0,8},{1,9},{2,10},{3,11},{4,0},{5,1},{6,2},{7,3},{8,12},{9,13},{1... | collective-permute-start | bytes 786440 | tf_op jit(solution)/shard_map/ppermute | solution.py:419
  138.0 1.1 fusion.2
  139.2 2.4 collective-permute-start.16
  141.6 1.1 fusion.1
  142.7 12.1 %collective-permute-done.17 = f32[64,8,128]{2,1,0:T(8,128)S(1)} collective-permute-done((f32[64,8,128]{2,1,0:T(8,128)S(1)}, f32[64,8,128]{2,1,0:T(8,128)S(1)}, u32[]{:S(2)}, u32[]{:S(2)}) %collective-permute-start.17) | collective-permute-done | bytes 262176 | tf_op jit(solution)/shard_map/ppermute | solution.py:419
  154.9 2.9 collective-permute-start.18
  158.1 1.1 add_add_fusion.2
  159.5 1.0 collective-permute-done.16
  160.5 5.5 %collective-permute-done.18 = f32[64,8,128]{2,1,0:T(8,128)S(1)} collective-permute-done((f32[64,8,128]{2,1,0:T(8,128)S(1)}, f32[64,8,128]{2,1,0:T(8,128)S(1)}, u32[]{:S(2)}, u32[]{:S(2)}) %collective-permute-start.18) | collective-permute-done | bytes 262176 | tf_op jit(solution)/shard_map/ppermute | solution.py:419
  166.3 0.9 fusion
  167.6 2.3 collective-permute-start.19
  169.9 15.5 %collective-permute-done.19.refs_5_ = f32[256,768]{1,0:T(8,128)S(1)} collective-permute-done((f32[256,768]{1,0:T(8,128)S(1)}, f32[256,768]{1,0:T(8,128)S(1)}, u32[]{:S(2)}, u32[]{:S(2)}) %collective-permute-start.19) | collective-permute-done | bytes 786464 | tf_op jit(solution)/shard_map/ppermute | solution.py:419
  185.3 1.2 collective-permute-start.30
  186.6 3.5 collective-permute-start.33
  190.1 12.8 %collective-permute-done.20.refs_3_ = f32[256,768]{1,0:T(8,128)} collective-permute-done((f32[256,768]{1,0:T(8,128)S(1)}, f32[256,768]{1,0:T(8,128)}, u32[]{:S(2)}, u32[]{:S(2)}) %collective-permute-start.20) | collective-permute-done | bytes 786464 | tf_op jit(solution)/shard_map/ppermute | solution.py:419
  202.8 2.5 collective-permute-start.21
  205.4 20.3 %collective-permute-start.32 = (f32[256,768]{1,0:T(8,128)S(1)}, f32[256,768]{1,0:T(8,128)S(1)}, u32[]{:S(2)}, u32[]{:S(2)}) collective-permute-start(f32[256,768]{1,0:T(8,128)S(1)} %collective-permute-done.19.refs_5_), channel_id=1, source_target_pairs={{0,1},{1,0},{2,3},{3,2},{4,5},{5,4},{6,7},{7,6},{8,9},{9,8},{10,11... | collective-permute-start | bytes 2359304 | tf_op jit(solution)/shard_map/ppermute | solution.py:419
  225.6 1.2 collective-permute-start.28
  227.2 0.9 copy-done.2
  228.3 1.2 collective-permute-start.22
  229.5 7.1 %collective-permute-start.27 = (f32[256,768]{1,0:T(8,128)}, f32[256,768]{1,0:T(8,128)}, u32[]{:S(2)}, u32[]{:S(2)}) collective-permute-start(f32[256,768]{1,0:T(8,128)} %collective-permute-done.20.refs_3_), channel_id=1, source_target_pairs={{0,1},{1,0},{2,3},{3,2},{4,5},{5,4},{6,7},{7,6},{8,9},{9,8},{10,11... | collective-permute-start | bytes 2359304 | tf_op jit(solution)/shard_map/ppermute | solution.py:419
  236.7 8.2 %collective-permute-done.28.refs_5_ = f32[256,768]{1,0:T(8,128)} collective-permute-done((f32[256,768]{1,0:T(8,128)S(1)}, f32[256,768]{1,0:T(8,128)}, u32[]{:S(2)}, u32[]{:S(2)}) %collective-permute-start.28) | collective-permute-done | bytes 786464 | tf_op jit(solution)/shard_map/ppermute | solution.py:419
  244.8 1.3 collective-permute-start.29
  246.3 0.9 copy-done.6
  247.1 14.6 %collective-permute-done.25.refs_5_ = f32[256,768]{1,0:T(8,128)} collective-permute-done((f32[256,768]{1,0:T(8,128)}, f32[256,768]{1,0:T(8,128)}, u32[]{:S(2)}, u32[]{:S(2)}) %collective-permute-start.25) | collective-permute-done | bytes 786464 | tf_op jit(solution)/shard_map/ppermute | solution.py:419
  261.7 1.3 collective-permute-start.26
  263.0 15.5 %collective-permute-done.22.refs_3_ = f32[256,768]{1,0:T(8,128)} collective-permute-done((f32[256,768]{1,0:T(8,128)}, f32[256,768]{1,0:T(8,128)}, u32[]{:S(2)}, u32[]{:S(2)}) %collective-permute-start.22) | collective-permute-done | bytes 786464 | tf_op jit(solution)/shard_map/ppermute | solution.py:419
  278.5 0.9 collective-permute-start.23
  280.1 0.7 divide_multiply_fusion.refs_1_
  280.7 10.3 %chi.5 = (f32[5,256,4096]{2,1,0:T(8,128)}, f32[5,256,4096]{2,1,0:T(8,128)}) custom-call(s32[16]{0:T(128)} %slice_bitcast_fusion.refs_0_, f32[5,384]{1,0:T(8,128)} %divide_multiply_fusion.refs_1_, f32[256,768]{1,0:T(8,128)} %copy-done, f32[256,768]{1,0:T(8,128)} %copy-done, f32[256,768]{1,0:T(8,128)} %copy-done.2), custom_call_target="tpu_custom_call" | custom-call | tf_op jit(solution)/shard_map/chi/pallas_call | solution.py:359
  291.0 15.9 %chi.6 = (f32[5,256,4096]{2,1,0:T(8,128)}, f32[5,256,4096]{2,1,0:T(8,128)}) custom-call(s32[16]{0:T(128)} %slice_bitcast_fusion.refs_0_, f32[5,384]{1,0:T(8,128)} %divide_multiply_fusion.refs_1_, f32[256,768]{1,0:T(8,128)} %copy-done, f32[256,768]{1,0:T(8,128)} %copy-done.4, f32[256,768]{1,0:T(8,128)} %copy-done.6, ...), custom_call_target="tpu_custom_call", output_to_operand_aliasing={{0}: (7, {}), {1}: (8, {})} | custom-call | tf_op jit(solution)/shard_map/chi/pallas_call | solution.py:359
  307.0 15.9 %chi.7 = (f32[5,256,4096]{2,1,0:T(8,128)}, f32[5,256,4096]{2,1,0:T(8,128)}) custom-call(s32[16]{0:T(128)} %slice_bitcast_fusion.refs_0_, f32[5,384]{1,0:T(8,128)} %divide_multiply_fusion.refs_1_, f32[256,768]{1,0:T(8,128)} %copy-done, f32[256,768]{1,0:T(8,128)} %collective-permute-done.20.refs_3_, ...), custom_call_target="tpu_custom_call", output_to_operand_aliasing={{0}: (7, {}), {1}: (8, {})} | custom-call | tf_op jit(solution)/shard_map/chi/pallas_call | solution.py:359
  323.0 15.9 %chi.8 = (f32[5,256,4096]{2,1,0:T(8,128)}, f32[5,256,4096]{2,1,0:T(8,128)}) custom-call(s32[16]{0:T(128)} %slice_bitcast_fusion.refs_0_, f32[5,384]{1,0:T(8,128)} %divide_multiply_fusion.refs_1_, f32[256,768]{1,0:T(8,128)} %copy-done, f32[256,768]{1,0:T(8,128)} %collective-permute-done.21.refs_3_, ...), custom_call_target="tpu_custom_call", output_to_operand_aliasing={{0}: (7, {}), {1}: (8, {})} | custom-call | tf_op jit(solution)/shard_map/chi/pallas_call | solution.py:359
  338.9 10.5 %chi.9 = (f32[5,256,4096]{2,1,0:T(8,128)}, f32[5,256,4096]{2,1,0:T(8,128)}) custom-call(s32[16]{0:T(128)} %slice_bitcast_fusion.refs_0_, f32[5,384]{1,0:T(8,128)} %divide_multiply_fusion.refs_1_, f32[256,768]{1,0:T(8,128)} %copy-done, f32[256,768]{1,0:T(8,128)} %collective-permute-done.22.refs_3_, ...), custom_call_target="tpu_custom_call", output_to_operand_aliasing={{0}: (5, {}), {1}: (6, {})} | custom-call | tf_op jit(solution)/shard_map/chi/pallas_call | solution.py:359
  (86 shorter events, 5.9 us)
Async XLA Ops:
  1.7 0.5 copy-start.12
  27.1 41.4 %collective-permute-start.7 = (f32[256,8,128]{2,1,0:T(8,128)}, f32[256,8,128]{2,1,0:T(8,128)}, u32[]{:S(2)}, u32[]{:S(2)}) collective-permute-start(f32[256,8,128]{2,1,0:T(8,128)} %get-tuple-element.49), channel_id=1, source_target_pairs={{0,1},{1,0},{2,3},{3,2},{4,5},{5,4},{6,7},{7,6},{8,9},{9,8},{10,11... | collective-permute-start | bytes 3145736 | tf_op jit(solution)/shard_map/ppermute | solution.py:419
  47.8 24.4 %collective-permute-start.1 = (f32[256,8,128]{2,1,0:T(8,128)}, f32[256,8,128]{2,1,0:T(8,128)}, u32[]{:S(2)}, u32[]{:S(2)}) collective-permute-start(f32[256,8,128]{2,1,0:T(8,128)} %get-tuple-element.41), channel_id=1, source_target_pairs={{0,1},{1,0},{2,3},{3,2},{4,5},{5,4},{6,7},{7,6},{8,9},{9,8},{10,11... | collective-permute-start | bytes 3145736 | tf_op jit(solution)/shard_map/ppermute | solution.py:419
  67.9 55.9 %copy-start.7 = (s32[4096]{0:T(1024)S(1)}, s32[4096]{0:T(1024)}, u32[]{:S(2)}) copy-start(s32[4096]{0:T(1024)} %param.23) | copy-start | bytes 49156
  67.9 70.1 %copy-start.1 = (f32[256,8,128]{2,1,0:T(8,128)S(1)}, f32[256,8,128]{2,1,0:T(8,128)}, u32[]{:S(2)}) copy-start(f32[256,8,128]{2,1,0:T(8,128)} %get-tuple-element.59) | copy-start | bytes 3145732
  67.9 211.5 %copy-start.10 = (s32[128]{0:T(128)S(1)}, s32[128]{0:T(128)}, u32[]{:S(2)}) copy-start(s32[128]{0:T(128)} %param.21) | copy-start | bytes 1540
  67.9 211.5 %copy-start.11 = (f32[5]{0:T(128)S(1)}, f32[5]{0:T(128)}, u32[]{:S(2)}) copy-start(f32[5]{0:T(128)} %param.22) | copy-start | bytes 64
  67.9 211.5 %copy-start.13 = (s32[1,32]{1,0:T(1,128)S(1)}, s32[1,32]{1,0:T(1,128)}, u32[]{:S(2)}) copy-start(s32[1,32]{1,0:T(1,128)} %copy-done.12) | copy-start | bytes 388
  67.9 212.0 %copy-start.8 = (f32[3]{0:T(128)S(1)}, f32[3]{0:T(128)}, u32[]{:S(2)}) copy-start(f32[3]{0:T(128)} %param.20) | copy-start | bytes 40
  67.9 212.0 %copy-start.9 = (f32[128]{0:T(128)S(1)}, f32[128]{0:T(128)}, u32[]{:S(2)}) copy-start(f32[128]{0:T(128)} %param.19) | copy-start | bytes 1540
  68.0 6.2 %collective-permute-start.13 = (f32[256,8,128]{2,1,0:T(8,128)}, f32[256,8,128]{2,1,0:T(8,128)S(1)}, u32[]{:S(2)}, u32[]{:S(2)}) collective-permute-start(f32[256,8,128]{2,1,0:T(8,128)} %get-tuple-element.57), channel_id=1, source_target_pairs={{0,1},{1,0},{2,3},{3,2},{4,5},{5,4},{6,7},{7,6},{8,9},{9,8},{10,11... | collective-permute-start | bytes 3145736 | tf_op jit(solution)/shard_map/ppermute | solution.py:419
  68.5 8.3 %collective-permute-start.6 = (f32[256,8,128]{2,1,0:T(8,128)}, f32[256,8,128]{2,1,0:T(8,128)S(1)}, u32[]{:S(2)}, u32[]{:S(2)}) collective-permute-start(f32[256,8,128]{2,1,0:T(8,128)} %get-tuple-element.47), channel_id=1, source_target_pairs={{0,1},{1,0},{2,3},{3,2},{4,5},{5,4},{6,7},{7,6},{8,9},{9,8},{10,11... | collective-permute-start | bytes 3145736 | tf_op jit(solution)/shard_map/ppermute | solution.py:419
  70.2 24.4 %collective-permute-start.8 = (f32[256,8,128]{2,1,0:T(8,128)S(1)}, f32[256,8,128]{2,1,0:T(8,128)S(1)}, u32[]{:S(2)}, u32[]{:S(2)}) collective-permute-start(f32[256,8,128]{2,1,0:T(8,128)S(1)} %add.152), channel_id=1, source_target_pairs={{0,2},{1,3},{2,0},{3,1},{4,6},{5,7},{6,4},{7,5},{8,10},{9,11},{10,... | collective-permute-start | bytes 3145736 | tf_op jit(solution)/shard_map/ppermute | solution.py:419
  71.6 26.6 %collective-permute-start = (f32[256,8,128]{2,1,0:T(8,128)}, f32[256,8,128]{2,1,0:T(8,128)S(1)}, u32[]{:S(2)}, u32[]{:S(2)}) collective-permute-start(f32[256,8,128]{2,1,0:T(8,128)} %get-tuple-element.39), channel_id=1, source_target_pairs={{0,1},{1,0},{2,3},{3,2},{4,5},{5,4},{6,7},{7,6},{8,9},{9,8},{10,11... | collective-permute-start | bytes 3145736 | tf_op jit(solution)/shard_map/ppermute | solution.py:419
  73.9 43.1 %collective-permute-start.2 = (f32[256,8,128]{2,1,0:T(8,128)S(1)}, f32[256,8,128]{2,1,0:T(8,128)S(1)}, u32[]{:S(2)}, u32[]{:S(2)}) collective-permute-start(f32[256,8,128]{2,1,0:T(8,128)S(1)} %add.146), channel_id=1, source_target_pairs={{0,2},{1,3},{2,0},{3,1},{4,6},{5,7},{6,4},{7,5},{8,10},{9,11},{10,... | collective-permute-start | bytes 3145736 | tf_op jit(solution)/shard_map/ppermute | solution.py:419
  74.2 63.8 %collective-permute-start.12 = (f32[256,8,128]{2,1,0:T(8,128)}, f32[256,8,128]{2,1,0:T(8,128)S(1)}, u32[]{:S(2)}, u32[]{:S(2)}) collective-permute-start(f32[256,8,128]{2,1,0:T(8,128)} %get-tuple-element.55), channel_id=1, source_target_pairs={{0,1},{1,0},{2,3},{3,2},{4,5},{5,4},{6,7},{7,6},{8,9},{9,8},{10,11... | collective-permute-start | bytes 3145736 | tf_op jit(solution)/shard_map/ppermute | solution.py:419
  76.8 51.6 %collective-permute-start.14 = (f32[128,8,128]{2,1,0:T(8,128)}, f32[128,8,128]{2,1,0:T(8,128)}, u32[]{:S(2)}, u32[]{:S(2)}) collective-permute-start(f32[128,8,128]{2,1,0:T(8,128)} %get-tuple-element.75), channel_id=1, source_target_pairs={{0,2},{1,3},{2,0},{3,1},{4,6},{5,7},{6,4},{7,5},{8,10},{9,11},{10,... | collective-permute-start | bytes 1572872 | tf_op jit(solution)/shard_map/ppermute | solution.py:419
  96.8 24.9 %collective-permute-start.10 = (f32[64,8,128]{2,1,0:T(8,128)}, f32[64,8,128]{2,1,0:T(8,128)}, u32[]{:S(2)}, u32[]{:S(2)}) collective-permute-start(f32[64,8,128]{2,1,0:T(8,128)} %get-tuple-element.53), channel_id=1, source_target_pairs={{0,8},{1,9},{2,10},{3,11},{4,0},{5,1},{6,2},{7,3},{8,12},{9,13},{1... | collective-permute-start | bytes 786440 | tf_op jit(solution)/shard_map/ppermute | solution.py:419
  119.3 6.9 %collective-permute-start.4 = (f32[64,8,128]{2,1,0:T(8,128)}, f32[64,8,128]{2,1,0:T(8,128)S(1)}, u32[]{:S(2)}, u32[]{:S(2)}) collective-permute-start(f32[64,8,128]{2,1,0:T(8,128)} %get-tuple-element.45), channel_id=1, source_target_pairs={{0,8},{1,9},{2,10},{3,11},{4,0},{5,1},{6,2},{7,3},{8,12},{9,13},{1... | collective-permute-start | bytes 786440 | tf_op jit(solution)/shard_map/ppermute | solution.py:419
  120.6 12.7 %collective-permute-start.9 = (f32[64,8,128]{2,1,0:T(8,128)}, f32[64,8,128]{2,1,0:T(8,128)}, u32[]{:S(2)}, u32[]{:S(2)}) collective-permute-start(f32[64,8,128]{2,1,0:T(8,128)} %get-tuple-element.51), channel_id=1, source_target_pairs={{0,4},{1,5},{2,6},{3,7},{4,12},{5,13},{6,14},{7,15},{8,0},{9,1},{1... | collective-permute-start | bytes 786440 | tf_op jit(solution)/shard_map/ppermute | solution.py:419
  123.3 14.7 %collective-permute-start.11 = (f32[64,8,128]{2,1,0:T(8,128)}, f32[64,8,128]{2,1,0:T(8,128)}, u32[]{:S(2)}, u32[]{:S(2)}) collective-permute-start(f32[64,8,128]{2,1,0:T(8,128)} %add.155), channel_id=1, source_target_pairs={{0,8},{1,9},{2,10},{3,11},{4,0},{5,1},{6,2},{7,3},{8,12},{9,13},{1... | collective-permute-start | bytes 786440 | tf_op jit(solution)/shard_map/ppermute | solution.py:419
  126.2 15.4 %collective-permute-start.15 = (f32[128,8,128]{2,1,0:T(8,128)}, f32[128,8,128]{2,1,0:T(8,128)}, u32[]{:S(2)}, u32[]{:S(2)}) collective-permute-start(f32[128,8,128]{2,1,0:T(8,128)} %get-tuple-element.74), channel_id=1, source_target_pairs={{0,2},{1,3},{2,0},{3,1},{4,6},{5,7},{6,4},{7,5},{8,10},{9,11},{10,... | collective-permute-start | bytes 1572872 | tf_op jit(solution)/shard_map/ppermute | solution.py:419
  128.4 29.4 %collective-permute-start.3 = (f32[64,8,128]{2,1,0:T(8,128)}, f32[64,8,128]{2,1,0:T(8,128)S(1)}, u32[]{:S(2)}, u32[]{:S(2)}) collective-permute-start(f32[64,8,128]{2,1,0:T(8,128)} %get-tuple-element.43), channel_id=1, source_target_pairs={{0,4},{1,5},{2,6},{3,7},{4,12},{5,13},{6,14},{7,15},{8,0},{9,1},{1... | collective-permute-start | bytes 786440 | tf_op jit(solution)/shard_map/ppermute | solution.py:419
  133.3 24.5 %collective-permute-start.5 = (f32[64,8,128]{2,1,0:T(8,128)S(1)}, f32[64,8,128]{2,1,0:T(8,128)S(1)}, u32[]{:S(2)}, u32[]{:S(2)}) collective-permute-start(f32[64,8,128]{2,1,0:T(8,128)S(1)} %add.149), channel_id=1, source_target_pairs={{0,8},{1,9},{2,10},{3,11},{4,0},{5,1},{6,2},{7,3},{8,12},{9,13},{1... | collective-permute-start | bytes 786440 | tf_op jit(solution)/shard_map/ppermute | solution.py:419
  139.2 15.7 %collective-permute-start.17 = (f32[64,8,128]{2,1,0:T(8,128)S(1)}, f32[64,8,128]{2,1,0:T(8,128)S(1)}, u32[]{:S(2)}, u32[]{:S(2)}) collective-permute-start(f32[64,8,128]{2,1,0:T(8,128)S(1)} %get-tuple-element.61), channel_id=1, source_target_pairs={{0,8},{1,9},{2,10},{3,11},{4,0},{5,1},{6,2},{7,3},{8,12},{9,13},{1... | collective-permute-start | bytes 786440 | tf_op jit(solution)/shard_map/ppermute | solution.py:419
  139.2 21.2 %collective-permute-start.16 = (f32[64,8,128]{2,1,0:T(8,128)S(1)}, f32[64,8,128]{2,1,0:T(8,128)S(1)}, u32[]{:S(2)}, u32[]{:S(2)}) collective-permute-start(f32[64,8,128]{2,1,0:T(8,128)S(1)} %get-tuple-element.60), channel_id=1, source_target_pairs={{0,4},{1,5},{2,6},{3,7},{4,12},{5,13},{6,14},{7,15},{8,0},{9,1},{1... | collective-permute-start | bytes 786440 | tf_op jit(solution)/shard_map/ppermute | solution.py:419
  154.9 11.1 %collective-permute-start.18 = (f32[64,8,128]{2,1,0:T(8,128)S(1)}, f32[64,8,128]{2,1,0:T(8,128)S(1)}, u32[]{:S(2)}, u32[]{:S(2)}) collective-permute-start(f32[64,8,128]{2,1,0:T(8,128)S(1)} %slice_add_fusion.4), channel_id=1, source_target_pairs={{0,8},{1,9},{2,10},{3,11},{4,0},{5,1},{6,2},{7,3},{8,12},{9,13},{1... | collective-permute-start | bytes 786440 | tf_op jit(solution)/shard_map/ppermute | solution.py:419
  167.6 19.0 %copy-start = (f32[256,768]{1,0:T(8,128)}, f32[256,768]{1,0:T(8,128)S(1)}, u32[]{:S(2)}) copy-start(f32[256,768]{1,0:T(8,128)S(1)} %reshape.106.refs_2_.refs_3_) | copy-start | bytes 2359300
  167.6 17.7 %collective-permute-start.19 = (f32[256,768]{1,0:T(8,128)S(1)}, f32[256,768]{1,0:T(8,128)S(1)}, u32[]{:S(2)}, u32[]{:S(2)}) collective-permute-start(f32[256,768]{1,0:T(8,128)S(1)} %reshape.106.refs_2_.refs_3_), channel_id=1, source_target_pairs={{0,8},{1,9},{2,10},{3,11},{4,0},{5,1},{6,2},{7,3},{8,12},{9,13},{1... | collective-permute-start | bytes 2359304 | tf_op jit(solution)/shard_map/ppermute | solution.py:419
  185.3 42.9 %copy-start.3 = (f32[256,768]{1,0:T(8,128)}, f32[256,768]{1,0:T(8,128)S(1)}, u32[]{:S(2)}) copy-start(f32[256,768]{1,0:T(8,128)S(1)} %collective-permute-done.19.refs_5_) | copy-start | bytes 2359300
  185.3 17.5 %collective-permute-start.20 = (f32[256,768]{1,0:T(8,128)S(1)}, f32[256,768]{1,0:T(8,128)}, u32[]{:S(2)}, u32[]{:S(2)}) collective-permute-start(f32[256,768]{1,0:T(8,128)S(1)} %reshape.106.refs_2_.refs_3_), channel_id=1, source_target_pairs={{0,4},{1,5},{2,6},{3,7},{4,12},{5,13},{6,14},{7,15},{8,0},{9,1},{1... | collective-permute-start | bytes 2359304 | tf_op jit(solution)/shard_map/ppermute | solution.py:419
  185.3 41.5 %collective-permute-start.30 = (f32[256,768]{1,0:T(8,128)S(1)}, f32[256,768]{1,0:T(8,128)S(1)}, u32[]{:S(2)}, u32[]{:S(2)}) collective-permute-start(f32[256,768]{1,0:T(8,128)S(1)} %reshape.106.refs_2_.refs_3_), channel_id=1, source_target_pairs={{0,2},{1,3},{2,0},{3,1},{4,6},{5,7},{6,4},{7,5},{8,10},{9,11},{10,... | collective-permute-start | bytes 2359304 | tf_op jit(solution)/shard_map/ppermute | solution.py:419
  186.6 40.6 %collective-permute-start.33 = (f32[256,768]{1,0:T(8,128)S(1)}, f32[256,768]{1,0:T(8,128)S(1)}, u32[]{:S(2)}, u32[]{:S(2)}) collective-permute-start(f32[256,768]{1,0:T(8,128)S(1)} %reshape.106.refs_2_.refs_3_), channel_id=1, source_target_pairs={{0,1},{1,0},{2,3},{3,2},{4,5},{5,4},{6,7},{7,6},{8,9},{9,8},{10,11... | collective-permute-start | bytes 2359304 | tf_op jit(solution)/shard_map/ppermute | solution.py:419
  202.8 25.5 %collective-permute-start.21 = (f32[256,768]{1,0:T(8,128)S(1)}, f32[256,768]{1,0:T(8,128)}, u32[]{:S(2)}, u32[]{:S(2)}) collective-permute-start(f32[256,768]{1,0:T(8,128)S(1)} %collective-permute-done.19.refs_5_), channel_id=1, source_target_pairs={{0,8},{1,9},{2,10},{3,11},{4,0},{5,1},{6,2},{7,3},{8,12},{9,13},{1... | collective-permute-start | bytes 2359304 | tf_op jit(solution)/shard_map/ppermute | solution.py:419
  205.4 24.2 %collective-permute-start.32 = (f32[256,768]{1,0:T(8,128)S(1)}, f32[256,768]{1,0:T(8,128)S(1)}, u32[]{:S(2)}, u32[]{:S(2)}) collective-permute-start(f32[256,768]{1,0:T(8,128)S(1)} %collective-permute-done.19.refs_5_), channel_id=1, source_target_pairs={{0,1},{1,0},{2,3},{3,2},{4,5},{5,4},{6,7},{7,6},{8,9},{9,8},{10,11... | collective-permute-start | bytes 2359304 | tf_op jit(solution)/shard_map/ppermute | solution.py:419
  225.6 19.2 %collective-permute-start.28 = (f32[256,768]{1,0:T(8,128)S(1)}, f32[256,768]{1,0:T(8,128)}, u32[]{:S(2)}, u32[]{:S(2)}) collective-permute-start(f32[256,768]{1,0:T(8,128)S(1)} %collective-permute-done.19.refs_5_), channel_id=1, source_target_pairs={{0,2},{1,3},{2,0},{3,1},{4,6},{5,7},{6,4},{7,5},{8,10},{9,11},{10,... | collective-permute-start | bytes 2359304 | tf_op jit(solution)/shard_map/ppermute | solution.py:419
  226.9 18.0 %copy-start.4 = (f32[256,768]{1,0:T(8,128)}, f32[256,768]{1,0:T(8,128)S(1)}, u32[]{:S(2)}) copy-start(f32[256,768]{1,0:T(8,128)S(1)} %collective-permute-done.30.refs_3_) | copy-start | bytes 2359300
  226.9 19.3 %collective-permute-start.31 = (f32[256,768]{1,0:T(8,128)S(1)}, f32[256,768]{1,0:T(8,128)S(1)}, u32[]{:S(2)}, u32[]{:S(2)}) collective-permute-start(f32[256,768]{1,0:T(8,128)S(1)} %collective-permute-done.30.refs_3_), channel_id=1, source_target_pairs={{0,1},{1,0},{2,3},{3,2},{4,5},{5,4},{6,7},{7,6},{8,9},{9,8},{10,11... | collective-permute-start | bytes 2359304 | tf_op jit(solution)/shard_map/ppermute | solution.py:419
  227.2 0.9 copy-start.2
  228.1 33.6 %collective-permute-start.25 = (f32[256,768]{1,0:T(8,128)}, f32[256,768]{1,0:T(8,128)}, u32[]{:S(2)}, u32[]{:S(2)}) collective-permute-start(f32[256,768]{1,0:T(8,128)} %collective-permute-done.20.refs_3_), channel_id=1, source_target_pairs={{0,2},{1,3},{2,0},{3,1},{4,6},{5,7},{6,4},{7,5},{8,10},{9,11},{10,... | collective-permute-start | bytes 2359304 | tf_op jit(solution)/shard_map/ppermute | solution.py:419
  228.3 50.3 %collective-permute-start.22 = (f32[256,768]{1,0:T(8,128)}, f32[256,768]{1,0:T(8,128)}, u32[]{:S(2)}, u32[]{:S(2)}) collective-permute-start(f32[256,768]{1,0:T(8,128)} %collective-permute-done.21.refs_3_), channel_id=1, source_target_pairs={{0,2},{1,3},{2,0},{3,1},{4,6},{5,7},{6,4},{7,5},{8,10},{9,11},{10,... | collective-permute-start | bytes 2359304 | tf_op jit(solution)/shard_map/ppermute | solution.py:419
  229.5 16.6 %copy-start.5 = (f32[256,768]{1,0:T(8,128)}, f32[256,768]{1,0:T(8,128)S(1)}, u32[]{:S(2)}) copy-start(f32[256,768]{1,0:T(8,128)S(1)} %collective-permute-done.32.refs_6_) | copy-start | bytes 2359300
  229.5 77.4 %collective-permute-start.27 = (f32[256,768]{1,0:T(8,128)}, f32[256,768]{1,0:T(8,128)}, u32[]{:S(2)}, u32[]{:S(2)}) collective-permute-start(f32[256,768]{1,0:T(8,128)} %collective-permute-done.20.refs_3_), channel_id=1, source_target_pairs={{0,1},{1,0},{2,3},{3,2},{4,5},{5,4},{6,7},{7,6},{8,9},{9,8},{10,11... | collective-permute-start | bytes 2359304 | tf_op jit(solution)/shard_map/ppermute | solution.py:419
  244.8 62.2 %collective-permute-start.29 = (f32[256,768]{1,0:T(8,128)}, f32[256,768]{1,0:T(8,128)}, u32[]{:S(2)}, u32[]{:S(2)}) collective-permute-start(f32[256,768]{1,0:T(8,128)} %collective-permute-done.28.refs_5_), channel_id=1, source_target_pairs={{0,1},{1,0},{2,3},{3,2},{4,5},{5,4},{6,7},{7,6},{8,9},{9,8},{10,11... | collective-permute-start | bytes 2359304 | tf_op jit(solution)/shard_map/ppermute | solution.py:419
  246.2 1.0 copy-start.6
  246.2 76.8 %collective-permute-start.24 = (f32[256,768]{1,0:T(8,128)}, f32[256,768]{1,0:T(8,128)}, u32[]{:S(2)}, u32[]{:S(2)}) collective-permute-start(f32[256,768]{1,0:T(8,128)} %collective-permute-done.21.refs_3_), channel_id=1, source_target_pairs={{0,1},{1,0},{2,3},{3,2},{4,5},{5,4},{6,7},{7,6},{8,9},{9,8},{10,11... | collective-permute-start | bytes 2359304 | tf_op jit(solution)/shard_map/ppermute | solution.py:419
  261.7 61.3 %collective-permute-start.26 = (f32[256,768]{1,0:T(8,128)}, f32[256,768]{1,0:T(8,128)}, u32[]{:S(2)}, u32[]{:S(2)}) collective-permute-start(f32[256,768]{1,0:T(8,128)} %collective-permute-done.25.refs_5_), channel_id=1, source_target_pairs={{0,1},{1,0},{2,3},{3,2},{4,5},{5,4},{6,7},{7,6},{8,9},{9,8},{10,11... | collective-permute-start | bytes 2359304 | tf_op jit(solution)/shard_map/ppermute | solution.py:419
  278.5 60.4 %collective-permute-start.23 = (f32[256,768]{1,0:T(8,128)}, f32[256,768]{1,0:T(8,128)}, u32[]{:S(2)}, u32[]{:S(2)}) collective-permute-start(f32[256,768]{1,0:T(8,128)} %collective-permute-done.22.refs_3_), channel_id=1, source_target_pairs={{0,1},{1,0},{2,3},{3,2},{4,5},{5,4},{6,7},{7,6},{8,9},{9,8},{10,11... | collective-permute-start | bytes 2359304 | tf_op jit(solution)/shard_map/ppermute | solution.py:419

commit v9 on v8

--- a/solution.py
+++ b/solution.py
@@ -423,19 +423,14 @@
     block = near.shape[0] // 4
     got_far = send(far_other, links.core)
     got_near = send(near_other, links.core)
+    cuts = ((2 * block, 4 * block), (0, 2 * block))
+    high, low = (send(far[i:j] + got_far[i:j], links.y) for i, j in cuts)
     if before:
-        cuts = ((2 * block, 4 * block), (0, 2 * block))
-        high, low = (send(far[i:j] + got_far[i:j], links.y) for i, j in cuts)
         high, *_ = lax.optimization_barrier((high, *before))
-        high = near[2 * block :] + got_near[2 * block :] + high
-        to_cw, to_ccw, near = lax.optimization_barrier((high[:block], high[block:], near))
-        low = near[: 2 * block] + got_near[: 2 * block] + low
-        mine, next_cw = low[:block], low[block:]
-    else:
-        near = near + got_near + send(far + got_far, links.y)
-        to_cw, to_ccw, next_cw, mine = lax.optimization_barrier(
-            tuple(near[i * block : (i + 1) * block] for i in (2, 3, 1, 0))
-        )
+    high = near[2 * block :] + got_near[2 * block :] + high
+    to_cw, to_ccw, near = lax.optimization_barrier((high[:block], high[block:], near))
+    low = near[: 2 * block] + got_near[: 2 * block] + low
+    mine, next_cw = low[:block], low[block:]
     two_back = send(to_cw, links.cw)
     ahead = send(to_ccw, links.ccw)
     next_cw = next_cw + two_back

time: 350 us -> 334 us (0.954)
  the two profiles are of different devices: /device:TPU:17 before, /device:TPU:0 now
where the time goes in v9:
time: 334 us; the launch traced here: 333 us
  waiting for transfers between devices  149 us (45%)
  Pallas kernels  129 us (39%)
  starting transfers between devices  32.6 us (10%)
  other arithmetic  13.1 us (4%)
  local copies, waits for them, and re-layouts  9.06 us (3%)
    ppermute x36, waiting for transfers between devices, send(): return lax.ppermute(value, 'blk', pairs)  149 us
    pallas_call x5, Pallas kernels, chi_group(): pl.pallas_call(functools.partial(chi_group_kernel, counts, old is not Non...  68.6 us
    pallas_call x3, Pallas kernels, transform(): pl.pallas_call(transform_kernel, grid=(1,), out_shape=(jax.ShapeDtypeStru...  59.9 us
    ppermute x36, starting transfers between devices, send(): return lax.ppermute(value, 'blk', pairs)  32.6 us
  transfers between devices with their start and end apart: 36, of which 15 were waited for; matrix products, arithmetic and copies ran while one was open for 4% of the time, Pallas kernels for 29%

profile of v9, /device:TPU:0, one launch (start us, length us, event | category | flops | bytes accessed | tf_op | source)
XLA Modules:
  0.0 333.3 jit_solution(17194900943611973831)
XLA Ops:
  1.0 0.7 constant_dynamic-slice_fusion
  1.7 0.6 copy-done.11
  2.3 0.8 fusion.11
  3.1 0.6 gather_fusion
  3.7 0.6 fusion.33
  4.3 1.9 copy.41
  6.3 1.0 broadcast_in_dim.20.cs_hbm
  7.2 20.0 %transform.3 = (f32[256,8,128]{2,1,0:T(8,128)}, f32[256,8,128]{2,1,0:T(8,128)}, f32[256,8,128]{2,1,0:T(8,128)}, f32[256,8,128]{2,1,0:T(8,128)}) custom-call(s32[4096]{0:T(1024)} %bitcast.43, s32[4096]{0:T(1024)} %bitcast.40, f32[4,64,64,128]{3,2,1,0:T(8,128)} %bitcast.30, f32[3,4,64,64]{3,2,1,0:T(8,128)} %bitcast.33, ...), custom_call_target="tpu_custom_call" | custom-call | tf_op jit(solution)/shard_map/transform/pallas_call | solution.py:210
  27.2 0.6 collective-permute-start.1
  27.8 20.0 %transform.4 = (f32[256,8,128]{2,1,0:T(8,128)}, f32[256,8,128]{2,1,0:T(8,128)}, f32[256,8,128]{2,1,0:T(8,128)}, f32[256,8,128]{2,1,0:T(8,128)}) custom-call(s32[4096]{0:T(1024)} %bitcast.44, s32[4096]{0:T(1024)} %bitcast.41, f32[4,64,64,128]{3,2,1,0:T(8,128)} %bitcast.31, f32[3,4,64,64]{3,2,1,0:T(8,128)} %bitcast.34, ...), custom_call_target="tpu_custom_call" | custom-call | tf_op jit(solution)/shard_map/transform/pallas_call | solution.py:210
  47.8 19.9 %transform.5 = (f32[256,8,128]{2,1,0:T(8,128)}, f32[256,8,128]{2,1,0:T(8,128)}, f32[256,8,128]{2,1,0:T(8,128)}, f32[256,8,128]{2,1,0:T(8,128)}) custom-call(s32[4096]{0:T(1024)} %bitcast.45, s32[4096]{0:T(1024)} %bitcast.42, f32[4,64,64,128]{3,2,1,0:T(8,128)} %bitcast.32, f32[3,4,64,64]{3,2,1,0:T(8,128)} %bitcast.35, ...), custom_call_target="tpu_custom_call" | custom-call | tf_op jit(solution)/shard_map/transform/pallas_call | solution.py:210
  67.9 0.6 collective-permute-start.15
  68.5 0.4 collective-permute-start.7
  68.9 0.7 fusion.19
  70.1 1.6 slice_add_fusion.8
  71.8 3.0 collective-permute-start.2
  74.8 1.6 slice_add_fusion.4
  76.5 1.3 slice_add_fusion
  77.8 2.1 collective-permute-start.3
  79.9 7.7 %collective-permute-done.2 = f32[128,8,128]{2,1,0:T(8,128)S(1)} collective-permute-done((f32[128,8,128]{2,1,0:T(8,128)S(1)}, f32[128,8,128]{2,1,0:T(8,128)S(1)}, u32[]{:S(2)}, u32[]{:S(2)}) %collective-permute-start.2) | collective-permute-done | bytes 524320 | tf_op jit(solution)/shard_map/ppermute | solution.py:419
  87.6 2.0 collective-permute-start.10
  89.6 1.1 fusion.6
  90.8 8.0 %collective-permute-done.9 = f32[128,8,128]{2,1,0:T(8,128)S(1)} collective-permute-done((f32[128,8,128]{2,1,0:T(8,128)S(1)}, f32[128,8,128]{2,1,0:T(8,128)S(1)}, u32[]{:S(2)}, u32[]{:S(2)}) %collective-permute-start.9) | collective-permute-done | bytes 524320 | tf_op jit(solution)/shard_map/ppermute | solution.py:419
  98.8 3.1 collective-permute-start.5
  101.9 1.3 fusion.4
  103.2 18.1 %collective-permute-done.10 = f32[128,8,128]{2,1,0:T(8,128)S(1)} collective-permute-done((f32[128,8,128]{2,1,0:T(8,128)S(1)}, f32[128,8,128]{2,1,0:T(8,128)S(1)}, u32[]{:S(2)}, u32[]{:S(2)}) %collective-permute-start.10) | collective-permute-done | bytes 524320 | tf_op jit(solution)/shard_map/ppermute | solution.py:419
  121.3 3.1 collective-permute-start.12
  124.4 1.3 fusion.3
  125.6 2.8 collective-permute-done.12
  128.4 2.4 collective-permute-start.11
  130.8 1.1 collective-permute-start.13
  131.9 1.1 fusion.5
  133.1 1.6 collective-permute-start.17
  134.7 1.0 collective-permute-start.4
  135.7 5.8 %collective-permute-done.11 = f32[64,8,128]{2,1,0:T(8,128)S(1)} collective-permute-done((f32[64,8,128]{2,1,0:T(8,128)S(1)}, f32[64,8,128]{2,1,0:T(8,128)S(1)}, u32[]{:S(2)}, u32[]{:S(2)}) %collective-permute-start.11) | collective-permute-done | bytes 262176 | tf_op jit(solution)/shard_map/ppermute | solution.py:419
  141.5 4.1 %collective-permute-done.13 = f32[64,8,128]{2,1,0:T(8,128)S(1)} collective-permute-done((f32[64,8,128]{2,1,0:T(8,128)S(1)}, f32[64,8,128]{2,1,0:T(8,128)S(1)}, u32[]{:S(2)}, u32[]{:S(2)}) %collective-permute-start.13) | collective-permute-done | bytes 262176 | tf_op jit(solution)/shard_map/ppermute | solution.py:419
  145.8 1.0 collective-permute-start.19
  146.8 1.1 collective-permute-start.18
  147.9 13.9 %collective-permute-done.19 = f32[64,8,128]{2,1,0:T(8,128)S(1)} collective-permute-done((f32[64,8,128]{2,1,0:T(8,128)S(1)}, f32[64,8,128]{2,1,0:T(8,128)S(1)}, u32[]{:S(2)}, u32[]{:S(2)}) %collective-permute-start.19) | collective-permute-done | bytes 262176 | tf_op jit(solution)/shard_map/ppermute | solution.py:419
  161.9 1.1 collective-permute-start.20
  163.7 1.6 collective-permute-done.18
  165.3 5.0 %collective-permute-done.20 = f32[64,8,128]{2,1,0:T(8,128)S(1)} collective-permute-done((f32[64,8,128]{2,1,0:T(8,128)S(1)}, f32[64,8,128]{2,1,0:T(8,128)S(1)}, u32[]{:S(2)}, u32[]{:S(2)}) %collective-permute-start.20) | collective-permute-done | bytes 262176 | tf_op jit(solution)/shard_map/ppermute | solution.py:419
  170.6 0.9 fusion
  171.9 1.1 collective-permute-start.21
  173.0 17.5 %collective-permute-done.21.refs_5_ = f32[256,768]{1,0:T(8,128)S(1)} collective-permute-done((f32[256,768]{1,0:T(8,128)S(1)}, f32[256,768]{1,0:T(8,128)S(1)}, u32[]{:S(2)}, u32[]{:S(2)}) %collective-permute-start.21) | collective-permute-done | bytes 786464 | tf_op jit(solution)/shard_map/ppermute | solution.py:419
  190.5 1.0 collective-permute-start.22
  191.5 1.5 collective-permute-start.32
  193.0 16.1 %collective-permute-done.22.refs_3_ = f32[256,768]{1,0:T(8,128)} collective-permute-done((f32[256,768]{1,0:T(8,128)S(1)}, f32[256,768]{1,0:T(8,128)}, u32[]{:S(2)}, u32[]{:S(2)}) %collective-permute-start.22) | collective-permute-done | bytes 786464 | tf_op jit(solution)/shard_map/ppermute | solution.py:419
  209.3 1.5 collective-permute-start.30
  211.0 0.9 copy-done.2
  211.9 0.5 collective-permute-start.27
  212.4 13.6 %collective-permute-done.23.refs_3_ = f32[256,768]{1,0:T(8,128)} collective-permute-done((f32[256,768]{1,0:T(8,128)S(1)}, f32[256,768]{1,0:T(8,128)}, u32[]{:S(2)}, u32[]{:S(2)}) %collective-permute-start.23) | collective-permute-done | bytes 786464 | tf_op jit(solution)/shard_map/ppermute | solution.py:419
  226.0 1.5 collective-permute-start.24
  227.6 2.2 collective-permute-done.30.refs_5_
  229.8 0.6 collective-permute-start.26
  230.8 15.9 %collective-permute-done.27.refs_5_ = f32[256,768]{1,0:T(8,128)} collective-permute-done((f32[256,768]{1,0:T(8,128)}, f32[256,768]{1,0:T(8,128)}, u32[]{:S(2)}, u32[]{:S(2)}) %collective-permute-start.27) | collective-permute-done | bytes 786464 | tf_op jit(solution)/shard_map/ppermute | solution.py:419
  246.6 16.4 %collective-permute-done.24.refs_3_ = f32[256,768]{1,0:T(8,128)} collective-permute-done((f32[256,768]{1,0:T(8,128)}, f32[256,768]{1,0:T(8,128)}, u32[]{:S(2)}, u32[]{:S(2)}) %collective-permute-start.24) | collective-permute-done | bytes 786464 | tf_op jit(solution)/shard_map/ppermute | solution.py:419
  263.1 0.6 slice_bitcast_fusion.refs_0_
  263.7 0.7 divide_multiply_fusion.refs_1_
  264.4 10.3 %chi.5 = (f32[5,256,4096]{2,1,0:T(8,128)}, f32[5,256,4096]{2,1,0:T(8,128)}) custom-call(s32[16]{0:T(128)} %slice_bitcast_fusion.refs_0_, f32[5,384]{1,0:T(8,128)} %divide_multiply_fusion.refs_1_, f32[256,768]{1,0:T(8,128)} %copy-done, f32[256,768]{1,0:T(8,128)} %copy-done, f32[256,768]{1,0:T(8,128)} %copy-done.2), custom_call_target="tpu_custom_call" | custom-call | tf_op jit(solution)/shard_map/chi/pallas_call | solution.py:359
  274.7 15.9 %chi.6 = (f32[5,256,4096]{2,1,0:T(8,128)}, f32[5,256,4096]{2,1,0:T(8,128)}) custom-call(s32[16]{0:T(128)} %slice_bitcast_fusion.refs_0_, f32[5,384]{1,0:T(8,128)} %divide_multiply_fusion.refs_1_, f32[256,768]{1,0:T(8,128)} %copy-done, f32[256,768]{1,0:T(8,128)} %copy-done.4, f32[256,768]{1,0:T(8,128)} %copy-done.6, ...), custom_call_target="tpu_custom_call", output_to_operand_aliasing={{0}: (7, {}), {1}: (8, {})} | custom-call | tf_op jit(solution)/shard_map/chi/pallas_call | solution.py:359
  290.6 15.9 %chi.7 = (f32[5,256,4096]{2,1,0:T(8,128)}, f32[5,256,4096]{2,1,0:T(8,128)}) custom-call(s32[16]{0:T(128)} %slice_bitcast_fusion.refs_0_, f32[5,384]{1,0:T(8,128)} %divide_multiply_fusion.refs_1_, f32[256,768]{1,0:T(8,128)} %copy-done, f32[256,768]{1,0:T(8,128)} %collective-permute-done.22.refs_3_, ...), custom_call_target="tpu_custom_call", output_to_operand_aliasing={{0}: (7, {}), {1}: (8, {})} | custom-call | tf_op jit(solution)/shard_map/chi/pallas_call | solution.py:359
  306.6 15.9 %chi.8 = (f32[5,256,4096]{2,1,0:T(8,128)}, f32[5,256,4096]{2,1,0:T(8,128)}) custom-call(s32[16]{0:T(128)} %slice_bitcast_fusion.refs_0_, f32[5,384]{1,0:T(8,128)} %divide_multiply_fusion.refs_1_, f32[256,768]{1,0:T(8,128)} %copy-done, f32[256,768]{1,0:T(8,128)} %collective-permute-done.23.refs_3_, ...), custom_call_target="tpu_custom_call", output_to_operand_aliasing={{0}: (7, {}), {1}: (8, {})} | custom-call | tf_op jit(solution)/shard_map/chi/pallas_call | solution.py:359
  322.6 10.5 %chi.9 = (f32[5,256,4096]{2,1,0:T(8,128)}, f32[5,256,4096]{2,1,0:T(8,128)}) custom-call(s32[16]{0:T(128)} %slice_bitcast_fusion.refs_0_, f32[5,384]{1,0:T(8,128)} %divide_multiply_fusion.refs_1_, f32[256,768]{1,0:T(8,128)} %copy-done, f32[256,768]{1,0:T(8,128)} %collective-permute-done.24.refs_3_, ...), custom_call_target="tpu_custom_call", output_to_operand_aliasing={{0}: (5, {}), {1}: (6, {})} | custom-call | tf_op jit(solution)/shard_map/chi/pallas_call | solution.py:359
  (90 shorter events, 3.8 us)
Async XLA Ops:
  1.7 0.6 copy-start.11
  27.2 42.8 %collective-permute-start.1 = (f32[256,8,128]{2,1,0:T(8,128)}, f32[256,8,128]{2,1,0:T(8,128)}, u32[]{:S(2)}, u32[]{:S(2)}) collective-permute-start(f32[256,8,128]{2,1,0:T(8,128)} %get-tuple-element.39), channel_id=1, source_target_pairs={{0,1},{1,0},{2,3},{3,2},{4,5},{5,4},{6,7},{7,6},{8,9},{9,8},{10,11... | collective-permute-start | bytes 3145736 | tf_op jit(solution)/shard_map/ppermute | solution.py:419
  47.8 24.0 %collective-permute-start.8 = (f32[256,8,128]{2,1,0:T(8,128)}, f32[256,8,128]{2,1,0:T(8,128)}, u32[]{:S(2)}, u32[]{:S(2)}) collective-permute-start(f32[256,8,128]{2,1,0:T(8,128)} %get-tuple-element.46), channel_id=1, source_target_pairs={{0,1},{1,0},{2,3},{3,2},{4,5},{5,4},{6,7},{7,6},{8,9},{9,8},{10,11... | collective-permute-start | bytes 3145736 | tf_op jit(solution)/shard_map/ppermute | solution.py:419
  67.8 77.8 %copy-start.1 = (f32[256,8,128]{2,1,0:T(8,128)S(1)}, f32[256,8,128]{2,1,0:T(8,128)}, u32[]{:S(2)}) copy-start(f32[256,8,128]{2,1,0:T(8,128)} %get-tuple-element.55) | copy-start | bytes 3145732
  67.8 195.2 %copy-start.9 = (s32[128]{0:T(128)S(1)}, s32[128]{0:T(128)}, u32[]{:S(2)}) copy-start(s32[128]{0:T(128)} %param.21) | copy-start | bytes 1540
  67.8 195.2 %copy-start.10 = (f32[5]{0:T(128)S(1)}, f32[5]{0:T(128)}, u32[]{:S(2)}) copy-start(f32[5]{0:T(128)} %param.22) | copy-start | bytes 64
  67.8 195.2 %copy-start.12 = (s32[1,32]{1,0:T(1,128)S(1)}, s32[1,32]{1,0:T(1,128)}, u32[]{:S(2)}) copy-start(s32[1,32]{1,0:T(1,128)} %copy-done.11) | copy-start | bytes 388
  67.8 195.8 %copy-start.7 = (f32[3]{0:T(128)S(1)}, f32[3]{0:T(128)}, u32[]{:S(2)}) copy-start(f32[3]{0:T(128)} %param.20) | copy-start | bytes 40
  67.8 195.8 %copy-start.8 = (f32[128]{0:T(128)S(1)}, f32[128]{0:T(128)}, u32[]{:S(2)}) copy-start(f32[128]{0:T(128)} %param.19) | copy-start | bytes 1540
  67.9 8.5 %collective-permute-start.15 = (f32[256,8,128]{2,1,0:T(8,128)}, f32[256,8,128]{2,1,0:T(8,128)S(1)}, u32[]{:S(2)}, u32[]{:S(2)}) collective-permute-start(f32[256,8,128]{2,1,0:T(8,128)} %get-tuple-element.53), channel_id=1, source_target_pairs={{0,1},{1,0},{2,3},{3,2},{4,5},{5,4},{6,7},{7,6},{8,9},{9,8},{10,11... | collective-permute-start | bytes 3145736 | tf_op jit(solution)/shard_map/ppermute | solution.py:419
  68.4 9.4 %collective-permute-start = (f32[256,8,128]{2,1,0:T(8,128)}, f32[256,8,128]{2,1,0:T(8,128)S(1)}, u32[]{:S(2)}, u32[]{:S(2)}) collective-permute-start(f32[256,8,128]{2,1,0:T(8,128)} %get-tuple-element.37), channel_id=1, source_target_pairs={{0,1},{1,0},{2,3},{3,2},{4,5},{5,4},{6,7},{7,6},{8,9},{9,8},{10,11... | collective-permute-start | bytes 3145736 | tf_op jit(solution)/shard_map/ppermute | solution.py:419
  68.5 22.3 %collective-permute-start.7 = (f32[256,8,128]{2,1,0:T(8,128)}, f32[256,8,128]{2,1,0:T(8,128)}, u32[]{:S(2)}, u32[]{:S(2)}) collective-permute-start(f32[256,8,128]{2,1,0:T(8,128)} %get-tuple-element.44), channel_id=1, source_target_pairs={{0,1},{1,0},{2,3},{3,2},{4,5},{5,4},{6,7},{7,6},{8,9},{9,8},{10,11... | collective-permute-start | bytes 3145736 | tf_op jit(solution)/shard_map/ppermute | solution.py:419
  70.0 75.6 %collective-permute-start.14 = (f32[256,8,128]{2,1,0:T(8,128)}, f32[256,8,128]{2,1,0:T(8,128)S(1)}, u32[]{:S(2)}, u32[]{:S(2)}) collective-permute-start(f32[256,8,128]{2,1,0:T(8,128)} %get-tuple-element.51), channel_id=1, source_target_pairs={{0,1},{1,0},{2,3},{3,2},{4,5},{5,4},{6,7},{7,6},{8,9},{9,8},{10,11... | collective-permute-start | bytes 3145736 | tf_op jit(solution)/shard_map/ppermute | solution.py:419
  71.8 15.8 %collective-permute-start.2 = (f32[128,8,128]{2,1,0:T(8,128)S(1)}, f32[128,8,128]{2,1,0:T(8,128)S(1)}, u32[]{:S(2)}, u32[]{:S(2)}) collective-permute-start(f32[128,8,128]{2,1,0:T(8,128)S(1)} %get-tuple-element.71), channel_id=1, source_target_pairs={{0,2},{1,3},{2,0},{3,1},{4,6},{5,7},{6,4},{7,5},{8,10},{9,11},{10,... | collective-permute-start | bytes 1572872 | tf_op jit(solution)/shard_map/ppermute | solution.py:419
  76.4 22.4 %collective-permute-start.9 = (f32[128,8,128]{2,1,0:T(8,128)S(1)}, f32[128,8,128]{2,1,0:T(8,128)S(1)}, u32[]{:S(2)}, u32[]{:S(2)}) collective-permute-start(f32[128,8,128]{2,1,0:T(8,128)S(1)} %get-tuple-element.75), channel_id=1, source_target_pairs={{0,2},{1,3},{2,0},{3,1},{4,6},{5,7},{6,4},{7,5},{8,10},{9,11},{10,... | collective-permute-start | bytes 1572872 | tf_op jit(solution)/shard_map/ppermute | solution.py:419
  77.8 53.0 %collective-permute-start.3 = (f32[128,8,128]{2,1,0:T(8,128)S(1)}, f32[128,8,128]{2,1,0:T(8,128)S(1)}, u32[]{:S(2)}, u32[]{:S(2)}) collective-permute-start(f32[128,8,128]{2,1,0:T(8,128)S(1)} %get-tuple-element.70), channel_id=1, source_target_pairs={{0,2},{1,3},{2,0},{3,1},{4,6},{5,7},{6,4},{7,5},{8,10},{9,11},{10,... | collective-permute-start | bytes 1572872 | tf_op jit(solution)/shard_map/ppermute | solution.py:419
  87.6 33.7 %collective-permute-start.10 = (f32[128,8,128]{2,1,0:T(8,128)S(1)}, f32[128,8,128]{2,1,0:T(8,128)S(1)}, u32[]{:S(2)}, u32[]{:S(2)}) collective-permute-start(f32[128,8,128]{2,1,0:T(8,128)S(1)} %get-tuple-element.74), channel_id=1, source_target_pairs={{0,2},{1,3},{2,0},{3,1},{4,6},{5,7},{6,4},{7,5},{8,10},{9,11},{10,... | collective-permute-start | bytes 1572872 | tf_op jit(solution)/shard_map/ppermute | solution.py:419
  90.8 43.9 %collective-permute-start.16 = (f32[128,8,128]{2,1,0:T(8,128)S(1)}, f32[128,8,128]{2,1,0:T(8,128)S(1)}, u32[]{:S(2)}, u32[]{:S(2)}) collective-permute-start(f32[128,8,128]{2,1,0:T(8,128)S(1)} %get-tuple-element.73), channel_id=1, source_target_pairs={{0,2},{1,3},{2,0},{3,1},{4,6},{5,7},{6,4},{7,5},{8,10},{9,11},{10,... | collective-permute-start | bytes 1572872 | tf_op jit(solution)/shard_map/ppermute | solution.py:419
  98.8 34.3 %collective-permute-start.5 = (f32[64,8,128]{2,1,0:T(8,128)S(1)}, f32[64,8,128]{2,1,0:T(8,128)S(1)}, u32[]{:S(2)}, u32[]{:S(2)}) collective-permute-start(f32[64,8,128]{2,1,0:T(8,128)S(1)} %get-tuple-element.42), channel_id=1, source_target_pairs={{0,8},{1,9},{2,10},{3,11},{4,0},{5,1},{6,2},{7,3},{8,12},{9,13},{1... | collective-permute-start | bytes 786440 | tf_op jit(solution)/shard_map/ppermute | solution.py:419
  121.3 7.2 %collective-permute-start.12 = (f32[64,8,128]{2,1,0:T(8,128)S(1)}, f32[64,8,128]{2,1,0:T(8,128)S(1)}, u32[]{:S(2)}, u32[]{:S(2)}) collective-permute-start(f32[64,8,128]{2,1,0:T(8,128)S(1)} %get-tuple-element.49), channel_id=1, source_target_pairs={{0,8},{1,9},{2,10},{3,11},{4,0},{5,1},{6,2},{7,3},{8,12},{9,13},{1... | collective-permute-start | bytes 786440 | tf_op jit(solution)/shard_map/ppermute | solution.py:419
  128.4 13.1 %collective-permute-start.11 = (f32[64,8,128]{2,1,0:T(8,128)S(1)}, f32[64,8,128]{2,1,0:T(8,128)S(1)}, u32[]{:S(2)}, u32[]{:S(2)}) collective-permute-start(f32[64,8,128]{2,1,0:T(8,128)S(1)} %get-tuple-element.48), channel_id=1, source_target_pairs={{0,4},{1,5},{2,6},{3,7},{4,12},{5,13},{6,14},{7,15},{8,0},{9,1},{1... | collective-permute-start | bytes 786440 | tf_op jit(solution)/shard_map/ppermute | solution.py:419
  130.8 14.8 %collective-permute-start.13 = (f32[64,8,128]{2,1,0:T(8,128)S(1)}, f32[64,8,128]{2,1,0:T(8,128)S(1)}, u32[]{:S(2)}, u32[]{:S(2)}) collective-permute-start(f32[64,8,128]{2,1,0:T(8,128)S(1)} %slice_add_fusion.14), channel_id=1, source_target_pairs={{0,8},{1,9},{2,10},{3,11},{4,0},{5,1},{6,2},{7,3},{8,12},{9,13},{1... | collective-permute-start | bytes 786440 | tf_op jit(solution)/shard_map/ppermute | solution.py:419
  133.1 14.8 %collective-permute-start.17 = (f32[128,8,128]{2,1,0:T(8,128)S(1)}, f32[128,8,128]{2,1,0:T(8,128)S(1)}, u32[]{:S(2)}, u32[]{:S(2)}) collective-permute-start(f32[128,8,128]{2,1,0:T(8,128)S(1)} %get-tuple-element.72), channel_id=1, source_target_pairs={{0,2},{1,3},{2,0},{3,1},{4,6},{5,7},{6,4},{7,5},{8,10},{9,11},{10,... | collective-permute-start | bytes 1572872 | tf_op jit(solution)/shard_map/ppermute | solution.py:419
  134.7 28.3 %collective-permute-start.4 = (f32[64,8,128]{2,1,0:T(8,128)S(1)}, f32[64,8,128]{2,1,0:T(8,128)S(1)}, u32[]{:S(2)}, u32[]{:S(2)}) collective-permute-start(f32[64,8,128]{2,1,0:T(8,128)S(1)} %get-tuple-element.41), channel_id=1, source_target_pairs={{0,4},{1,5},{2,6},{3,7},{4,12},{5,13},{6,14},{7,15},{8,0},{9,1},{1... | collective-permute-start | bytes 786440 | tf_op jit(solution)/shard_map/ppermute | solution.py:419
  141.5 21.5 %collective-permute-start.6 = (f32[64,8,128]{2,1,0:T(8,128)S(1)}, f32[64,8,128]{2,1,0:T(8,128)S(1)}, u32[]{:S(2)}, u32[]{:S(2)}) collective-permute-start(f32[64,8,128]{2,1,0:T(8,128)S(1)} %slice_add_fusion.16), channel_id=1, source_target_pairs={{0,8},{1,9},{2,10},{3,11},{4,0},{5,1},{6,2},{7,3},{8,12},{9,13},{1... | collective-permute-start | bytes 786440 | tf_op jit(solution)/shard_map/ppermute | solution.py:419
  145.8 16.1 %collective-permute-start.19 = (f32[64,8,128]{2,1,0:T(8,128)S(1)}, f32[64,8,128]{2,1,0:T(8,128)S(1)}, u32[]{:S(2)}, u32[]{:S(2)}) collective-permute-start(f32[64,8,128]{2,1,0:T(8,128)S(1)} %get-tuple-element.57), channel_id=1, source_target_pairs={{0,8},{1,9},{2,10},{3,11},{4,0},{5,1},{6,2},{7,3},{8,12},{9,13},{1... | collective-permute-start | bytes 786440 | tf_op jit(solution)/shard_map/ppermute | solution.py:419
  146.8 18.5 %collective-permute-start.18 = (f32[64,8,128]{2,1,0:T(8,128)S(1)}, f32[64,8,128]{2,1,0:T(8,128)S(1)}, u32[]{:S(2)}, u32[]{:S(2)}) collective-permute-start(f32[64,8,128]{2,1,0:T(8,128)S(1)} %get-tuple-element.56), channel_id=1, source_target_pairs={{0,4},{1,5},{2,6},{3,7},{4,12},{5,13},{6,14},{7,15},{8,0},{9,1},{1... | collective-permute-start | bytes 786440 | tf_op jit(solution)/shard_map/ppermute | solution.py:419
  161.9 8.4 %collective-permute-start.20 = (f32[64,8,128]{2,1,0:T(8,128)S(1)}, f32[64,8,128]{2,1,0:T(8,128)S(1)}, u32[]{:S(2)}, u32[]{:S(2)}) collective-permute-start(f32[64,8,128]{2,1,0:T(8,128)S(1)} %slice_add_fusion.12), channel_id=1, source_target_pairs={{0,8},{1,9},{2,10},{3,11},{4,0},{5,1},{6,2},{7,3},{8,12},{9,13},{1... | collective-permute-start | bytes 786440 | tf_op jit(solution)/shard_map/ppermute | solution.py:419
  171.9 21.1 %copy-start = (f32[256,768]{1,0:T(8,128)}, f32[256,768]{1,0:T(8,128)S(1)}, u32[]{:S(2)}) copy-start(f32[256,768]{1,0:T(8,128)S(1)} %reshape.106.refs_2_.refs_3_) | copy-start | bytes 2359300
  171.9 18.6 %collective-permute-start.21 = (f32[256,768]{1,0:T(8,128)S(1)}, f32[256,768]{1,0:T(8,128)S(1)}, u32[]{:S(2)}, u32[]{:S(2)}) collective-permute-start(f32[256,768]{1,0:T(8,128)S(1)} %reshape.106.refs_2_.refs_3_), channel_id=1, source_target_pairs={{0,8},{1,9},{2,10},{3,11},{4,0},{5,1},{6,2},{7,3},{8,12},{9,13},{1... | collective-permute-start | bytes 2359304 | tf_op jit(solution)/shard_map/ppermute | solution.py:419
  190.5 22.0 %copy-start.3 = (f32[256,768]{1,0:T(8,128)}, f32[256,768]{1,0:T(8,128)S(1)}, u32[]{:S(2)}) copy-start(f32[256,768]{1,0:T(8,128)S(1)} %collective-permute-done.21.refs_5_) | copy-start | bytes 2359300
  190.5 18.7 %collective-permute-start.22 = (f32[256,768]{1,0:T(8,128)S(1)}, f32[256,768]{1,0:T(8,128)}, u32[]{:S(2)}, u32[]{:S(2)}) collective-permute-start(f32[256,768]{1,0:T(8,128)S(1)} %reshape.106.refs_2_.refs_3_), channel_id=1, source_target_pairs={{0,4},{1,5},{2,6},{3,7},{4,12},{5,13},{6,14},{7,15},{8,0},{9,1},{1... | collective-permute-start | bytes 2359304 | tf_op jit(solution)/shard_map/ppermute | solution.py:419
  191.5 19.3 %collective-permute-start.32 = (f32[256,768]{1,0:T(8,128)S(1)}, f32[256,768]{1,0:T(8,128)S(1)}, u32[]{:S(2)}, u32[]{:S(2)}) collective-permute-start(f32[256,768]{1,0:T(8,128)S(1)} %reshape.106.refs_2_.refs_3_), channel_id=1, source_target_pairs={{0,2},{1,3},{2,0},{3,1},{4,6},{5,7},{6,4},{7,5},{8,10},{9,11},{10,... | collective-permute-start | bytes 2359304 | tf_op jit(solution)/shard_map/ppermute | solution.py:419
  193.0 18.0 %collective-permute-start.35 = (f32[256,768]{1,0:T(8,128)S(1)}, f32[256,768]{1,0:T(8,128)S(1)}, u32[]{:S(2)}, u32[]{:S(2)}) collective-permute-start(f32[256,768]{1,0:T(8,128)S(1)} %reshape.106.refs_2_.refs_3_), channel_id=1, source_target_pairs={{0,1},{1,0},{2,3},{3,2},{4,5},{5,4},{6,7},{7,6},{8,9},{9,8},{10,11... | collective-permute-start | bytes 2359304 | tf_op jit(solution)/shard_map/ppermute | solution.py:419
  209.1 16.9 %collective-permute-start.23 = (f32[256,768]{1,0:T(8,128)S(1)}, f32[256,768]{1,0:T(8,128)}, u32[]{:S(2)}, u32[]{:S(2)}) collective-permute-start(f32[256,768]{1,0:T(8,128)S(1)} %collective-permute-done.21.refs_5_), channel_id=1, source_target_pairs={{0,8},{1,9},{2,10},{3,11},{4,0},{5,1},{6,2},{7,3},{8,12},{9,13},{1... | collective-permute-start | bytes 2359304 | tf_op jit(solution)/shard_map/ppermute | solution.py:419
  209.3 18.3 %collective-permute-start.34 = (f32[256,768]{1,0:T(8,128)S(1)}, f32[256,768]{1,0:T(8,128)S(1)}, u32[]{:S(2)}, u32[]{:S(2)}) collective-permute-start(f32[256,768]{1,0:T(8,128)S(1)} %collective-permute-done.21.refs_5_), channel_id=1, source_target_pairs={{0,1},{1,0},{2,3},{3,2},{4,5},{5,4},{6,7},{7,6},{8,9},{9,8},{10,11... | collective-permute-start | bytes 2359304 | tf_op jit(solution)/shard_map/ppermute | solution.py:419
  209.3 20.5 %collective-permute-start.30 = (f32[256,768]{1,0:T(8,128)S(1)}, f32[256,768]{1,0:T(8,128)}, u32[]{:S(2)}, u32[]{:S(2)}) collective-permute-start(f32[256,768]{1,0:T(8,128)S(1)} %collective-permute-done.21.refs_5_), channel_id=1, source_target_pairs={{0,2},{1,3},{2,0},{3,1},{4,6},{5,7},{6,4},{7,5},{8,10},{9,11},{10,... | collective-permute-start | bytes 2359304 | tf_op jit(solution)/shard_map/ppermute | solution.py:419
  210.8 19.0 %copy-start.4 = (f32[256,768]{1,0:T(8,128)}, f32[256,768]{1,0:T(8,128)S(1)}, u32[]{:S(2)}) copy-start(f32[256,768]{1,0:T(8,128)S(1)} %collective-permute-done.32.refs_3_) | copy-start | bytes 2359300
  210.8 19.0 %collective-permute-start.33 = (f32[256,768]{1,0:T(8,128)S(1)}, f32[256,768]{1,0:T(8,128)S(1)}, u32[]{:S(2)}, u32[]{:S(2)}) collective-permute-start(f32[256,768]{1,0:T(8,128)S(1)} %collective-permute-done.32.refs_3_), channel_id=1, source_target_pairs={{0,1},{1,0},{2,3},{3,2},{4,5},{5,4},{6,7},{7,6},{8,9},{9,8},{10,11... | collective-permute-start | bytes 2359304 | tf_op jit(solution)/shard_map/ppermute | solution.py:419
  211.0 0.9 copy-start.2
  211.9 34.7 %collective-permute-start.27 = (f32[256,768]{1,0:T(8,128)}, f32[256,768]{1,0:T(8,128)}, u32[]{:S(2)}, u32[]{:S(2)}) collective-permute-start(f32[256,768]{1,0:T(8,128)} %collective-permute-done.22.refs_3_), channel_id=1, source_target_pairs={{0,2},{1,3},{2,0},{3,1},{4,6},{5,7},{6,4},{7,5},{8,10},{9,11},{10,... | collective-permute-start | bytes 2359304 | tf_op jit(solution)/shard_map/ppermute | solution.py:419
  226.0 37.0 %collective-permute-start.24 = (f32[256,768]{1,0:T(8,128)}, f32[256,768]{1,0:T(8,128)}, u32[]{:S(2)}, u32[]{:S(2)}) collective-permute-start(f32[256,768]{1,0:T(8,128)} %collective-permute-done.23.refs_3_), channel_id=1, source_target_pairs={{0,2},{1,3},{2,0},{3,1},{4,6},{5,7},{6,4},{7,5},{8,10},{9,11},{10,... | collective-permute-start | bytes 2359304 | tf_op jit(solution)/shard_map/ppermute | solution.py:419
  227.6 2.2 copy-start.5
  227.6 63.1 %collective-permute-start.29 = (f32[256,768]{1,0:T(8,128)}, f32[256,768]{1,0:T(8,128)}, u32[]{:S(2)}, u32[]{:S(2)}) collective-permute-start(f32[256,768]{1,0:T(8,128)} %collective-permute-done.22.refs_3_), channel_id=1, source_target_pairs={{0,1},{1,0},{2,3},{3,2},{4,5},{5,4},{6,7},{7,6},{8,9},{9,8},{10,11... | collective-permute-start | bytes 2359304 | tf_op jit(solution)/shard_map/ppermute | solution.py:419
  229.8 60.8 %collective-permute-start.31 = (f32[256,768]{1,0:T(8,128)}, f32[256,768]{1,0:T(8,128)}, u32[]{:S(2)}, u32[]{:S(2)}) collective-permute-start(f32[256,768]{1,0:T(8,128)} %collective-permute-done.30.refs_5_), channel_id=1, source_target_pairs={{0,1},{1,0},{2,3},{3,2},{4,5},{5,4},{6,7},{7,6},{8,9},{9,8},{10,11... | collective-permute-start | bytes 2359304 | tf_op jit(solution)/shard_map/ppermute | solution.py:419
  229.8 1.0 copy-start.6
  229.8 76.8 %collective-permute-start.26 = (f32[256,768]{1,0:T(8,128)}, f32[256,768]{1,0:T(8,128)}, u32[]{:S(2)}, u32[]{:S(2)}) collective-permute-start(f32[256,768]{1,0:T(8,128)} %collective-permute-done.23.refs_3_), channel_id=1, source_target_pairs={{0,1},{1,0},{2,3},{3,2},{4,5},{5,4},{6,7},{7,6},{8,9},{9,8},{10,11... | collective-permute-start | bytes 2359304 | tf_op jit(solution)/shard_map/ppermute | solution.py:419
  246.6 60.0 %collective-permute-start.28 = (f32[256,768]{1,0:T(8,128)}, f32[256,768]{1,0:T(8,128)}, u32[]{:S(2)}, u32[]{:S(2)}) collective-permute-start(f32[256,768]{1,0:T(8,128)} %collective-permute-done.27.refs_5_), channel_id=1, source_target_pairs={{0,1},{1,0},{2,3},{3,2},{4,5},{5,4},{6,7},{7,6},{8,9},{9,8},{10,11... | collective-permute-start | bytes 2359304 | tf_op jit(solution)/shard_map/ppermute | solution.py:419
  263.0 59.5 %collective-permute-start.25 = (f32[256,768]{1,0:T(8,128)}, f32[256,768]{1,0:T(8,128)}, u32[]{:S(2)}, u32[]{:S(2)}) collective-permute-start(f32[256,768]{1,0:T(8,128)} %collective-permute-done.24.refs_3_), channel_id=1, source_target_pairs={{0,1},{1,0},{2,3},{3,2},{4,5},{5,4},{6,7},{7,6},{8,9},{9,8},{10,11... | collective-permute-start | bytes 2359304 | tf_op jit(solution)/shard_map/ppermute | solution.py:419

commit v10 on v9

--- a/solution.py
+++ b/solution.py
@@ -443,15 +443,19 @@
     later, cw = lax.optimization_barrier((own, cw))
     ccw = send(later, links.ccw)
     cw_later, ccw = lax.optimization_barrier((cw, ccw))
-    mine = {(0, 0): own, (0, 3): cw, (0, 1): ccw, (0, 2): send(cw_later, links.cw)}
-    for r in range(4):
-        mine[1, r] = send(mine[0, r], links.y)
+    mine = {(0, 0): [own], (0, 3): [cw], (0, 1): [ccw]}
+    mine[0, 2] = [send(cw_later, links.cw)]
+    for r in (0, 3, 1):
+        mine[1, r] = [send(mine[0, r][0], links.y)]
+    half = own.shape[0] // 2
+    mine[1, 2] = [send(mine[0, 2][0][:half], links.y), send(mine[1, 1][0][half:], links.ccw)]
     old = None
     first = 0
     for group in GROUPS:
         blocks = []
         for b, r in group:
-            blocks += [[mine[b, r]], [send(mine[b, r], links.core)]]
+            twins = [send(piece, links.core) for piece in mine[b, r]]
+            blocks += [mine[b, r], twins]
         old = chi_group(weights, own, blocks, ids, first, num_g, old)
         first += len(blocks)
     return old

time: 334 us -> 334 us (level)
  waiting for transfers between devices: 149 us -> 136 us
  starting transfers between devices: 32.6 us -> 42.6 us
    ppermute x36 -> x38, waiting for transfers between devices: 149 us -> 136 us  [send(): return lax.ppermute(value, 'blk', pairs)]
    ppermute x36 -> x38, starting transfers between devices: 32.6 us -> 42.6 us  [send(): return lax.ppermute(value, 'blk', pairs)]
  transfers between devices with their start and end apart: 36 -> 38, of which waited for: 15 -> 16; matrix products, arithmetic and copies ran while one was open for 4% -> 4% of each run, Pallas kernels for 29% -> 29%
where the time goes in v10:
time: 334 us; the launch traced here: 333 us
  waiting for transfers between devices  136 us (41%)
  Pallas kernels  129 us (39%)
  starting transfers between devices  42.6 us (13%)
  other arithmetic  13.1 us (4%)
  local copies, waits for them, and re-layouts  11.5 us (3%)
    ppermute x38, waiting for transfers between devices, send(): return lax.ppermute(value, 'blk', pairs)  136 us
    pallas_call x5, Pallas kernels, chi_group(): pl.pallas_call(functools.partial(chi_group_kernel, counts, old is not Non...  68.7 us
    pallas_call x3, Pallas kernels, transform(): pl.pallas_call(transform_kernel, grid=(1,), out_shape=(jax.ShapeDtypeStru...  59.9 us
    ppermute x38, starting transfers between devices, send(): return lax.ppermute(value, 'blk', pairs)  42.6 us
  transfers between devices with their start and end apart: 38, of which 16 were waited for; matrix products, arithmetic and copies ran while one was open for 4% of the time, Pallas kernels for 29%

profile of v10, /device:TPU:0, one launch (start us, length us, event | category | flops | bytes accessed | tf_op | source)
XLA Modules:
  0.0 333.4 jit_solution(16778230196060023972)
XLA Ops:
  1.0 0.7 constant_dynamic-slice_fusion
  2.3 0.8 fusion.11
  3.1 0.6 gather_fusion
  3.7 0.6 fusion.33
  4.3 1.9 copy.41
  6.2 1.0 broadcast_in_dim.20.cs_hbm
  7.2 20.0 %transform.3 = (f32[256,8,128]{2,1,0:T(8,128)}, f32[256,8,128]{2,1,0:T(8,128)}, f32[256,8,128]{2,1,0:T(8,128)}, f32[256,8,128]{2,1,0:T(8,128)}) custom-call(s32[4096]{0:T(1024)} %bitcast.43, s32[4096]{0:T(1024)} %bitcast.40, f32[4,64,64,128]{3,2,1,0:T(8,128)} %bitcast.30, f32[3,4,64,64]{3,2,1,0:T(8,128)} %bitcast.33, ...), custom_call_target="tpu_custom_call" | custom-call | tf_op jit(solution)/shard_map/transform/pallas_call | solution.py:210
  27.2 0.6 collective-permute-start.1
  27.8 19.9 %transform.4 = (f32[256,8,128]{2,1,0:T(8,128)}, f32[256,8,128]{2,1,0:T(8,128)}, f32[256,8,128]{2,1,0:T(8,128)}, f32[256,8,128]{2,1,0:T(8,128)}) custom-call(s32[4096]{0:T(1024)} %bitcast.44, s32[4096]{0:T(1024)} %bitcast.41, f32[4,64,64,128]{3,2,1,0:T(8,128)} %bitcast.31, f32[3,4,64,64]{3,2,1,0:T(8,128)} %bitcast.34, ...), custom_call_target="tpu_custom_call" | custom-call | tf_op jit(solution)/shard_map/transform/pallas_call | solution.py:210
  47.8 20.0 %transform.5 = (f32[256,8,128]{2,1,0:T(8,128)}, f32[256,8,128]{2,1,0:T(8,128)}, f32[256,8,128]{2,1,0:T(8,128)}, f32[256,8,128]{2,1,0:T(8,128)}) custom-call(s32[4096]{0:T(1024)} %bitcast.45, s32[4096]{0:T(1024)} %bitcast.42, f32[4,64,64,128]{3,2,1,0:T(8,128)} %bitcast.32, f32[3,4,64,64]{3,2,1,0:T(8,128)} %bitcast.35, ...), custom_call_target="tpu_custom_call" | custom-call | tf_op jit(solution)/shard_map/transform/pallas_call | solution.py:210
  68.9 0.7 fusion.19
  70.1 1.6 slice_add_fusion.8
  71.8 3.0 collective-permute-start.2
  74.8 1.6 slice_add_fusion.4
  76.5 1.3 slice_add_fusion
  77.8 2.1 collective-permute-start.3
  79.9 7.7 %collective-permute-done.2 = f32[128,8,128]{2,1,0:T(8,128)S(1)} collective-permute-done((f32[128,8,128]{2,1,0:T(8,128)S(1)}, f32[128,8,128]{2,1,0:T(8,128)S(1)}, u32[]{:S(2)}, u32[]{:S(2)}) %collective-permute-start.2) | collective-permute-done | bytes 524320 | tf_op jit(solution)/shard_map/ppermute | solution.py:419
  87.5 2.0 collective-permute-start.10
  89.6 1.1 fusion.6
  90.8 8.0 %collective-permute-done.9 = f32[128,8,128]{2,1,0:T(8,128)S(1)} collective-permute-done((f32[128,8,128]{2,1,0:T(8,128)S(1)}, f32[128,8,128]{2,1,0:T(8,128)S(1)}, u32[]{:S(2)}, u32[]{:S(2)}) %collective-permute-start.9) | collective-permute-done | bytes 524320 | tf_op jit(solution)/shard_map/ppermute | solution.py:419
  98.8 3.1 collective-permute-start.5
  101.9 1.3 fusion.4
  103.2 18.1 %collective-permute-done.10 = f32[128,8,128]{2,1,0:T(8,128)S(1)} collective-permute-done((f32[128,8,128]{2,1,0:T(8,128)S(1)}, f32[128,8,128]{2,1,0:T(8,128)S(1)}, u32[]{:S(2)}, u32[]{:S(2)}) %collective-permute-start.10) | collective-permute-done | bytes 524320 | tf_op jit(solution)/shard_map/ppermute | solution.py:419
  121.2 3.1 collective-permute-start.12
  124.3 1.3 fusion.3
  125.6 2.8 collective-permute-done.12
  128.4 2.4 collective-permute-start.11
  130.8 1.1 collective-permute-start.13
  131.9 1.1 fusion.5
  133.1 1.6 collective-permute-start.17
  134.7 1.0 collective-permute-start.4
  135.7 5.8 %collective-permute-done.11 = f32[64,8,128]{2,1,0:T(8,128)S(1)} collective-permute-done((f32[64,8,128]{2,1,0:T(8,128)S(1)}, f32[64,8,128]{2,1,0:T(8,128)S(1)}, u32[]{:S(2)}, u32[]{:S(2)}) %collective-permute-start.11) | collective-permute-done | bytes 262176 | tf_op jit(solution)/shard_map/ppermute | solution.py:419
  141.5 4.1 %collective-permute-done.13 = f32[64,8,128]{2,1,0:T(8,128)S(1)} collective-permute-done((f32[64,8,128]{2,1,0:T(8,128)S(1)}, f32[64,8,128]{2,1,0:T(8,128)S(1)}, u32[]{:S(2)}, u32[]{:S(2)}) %collective-permute-start.13) | collective-permute-done | bytes 262176 | tf_op jit(solution)/shard_map/ppermute | solution.py:419
  145.7 1.0 collective-permute-start.19
  146.8 1.1 collective-permute-start.18
  147.9 13.9 %collective-permute-done.19 = f32[64,8,128]{2,1,0:T(8,128)S(1)} collective-permute-done((f32[64,8,128]{2,1,0:T(8,128)S(1)}, f32[64,8,128]{2,1,0:T(8,128)S(1)}, u32[]{:S(2)}, u32[]{:S(2)}) %collective-permute-start.19) | collective-permute-done | bytes 262176 | tf_op jit(solution)/shard_map/ppermute | solution.py:419
  161.9 1.1 collective-permute-start.20
  163.7 1.6 collective-permute-done.18
  165.3 4.9 %collective-permute-done.20 = f32[64,8,128]{2,1,0:T(8,128)S(1)} collective-permute-done((f32[64,8,128]{2,1,0:T(8,128)S(1)}, f32[64,8,128]{2,1,0:T(8,128)S(1)}, u32[]{:S(2)}, u32[]{:S(2)}) %collective-permute-start.20) | collective-permute-done | bytes 262176 | tf_op jit(solution)/shard_map/ppermute | solution.py:419
  170.6 0.9 fusion
  171.9 1.1 collective-permute-start.21
  173.0 17.5 %collective-permute-done.21.refs_5_ = f32[256,768]{1,0:T(8,128)S(1)} collective-permute-done((f32[256,768]{1,0:T(8,128)S(1)}, f32[256,768]{1,0:T(8,128)S(1)}, u32[]{:S(2)}, u32[]{:S(2)}) %collective-permute-start.21) | collective-permute-done | bytes 786464 | tf_op jit(solution)/shard_map/ppermute | solution.py:419
  190.5 1.0 collective-permute-start.22
  191.5 1.5 collective-permute-start.34
  193.0 16.0 %collective-permute-done.22.refs_3_ = f32[256,768]{1,0:T(8,128)S(1)} collective-permute-done((f32[256,768]{1,0:T(8,128)S(1)}, f32[256,768]{1,0:T(8,128)S(1)}, u32[]{:S(2)}, u32[]{:S(2)}) %collective-permute-start.22) | collective-permute-done | bytes 786464 | tf_op jit(solution)/shard_map/ppermute | solution.py:419
  209.1 1.5 collective-permute-start.25
  211.7 14.3 %collective-permute-done.23.refs_3_ = f32[256,768]{1,0:T(8,128)} collective-permute-done((f32[256,768]{1,0:T(8,128)S(1)}, f32[256,768]{1,0:T(8,128)}, u32[]{:S(2)}, u32[]{:S(2)}) %collective-permute-start.23) | collective-permute-done | bytes 786464 | tf_op jit(solution)/shard_map/ppermute | solution.py:419
  226.0 3.7 %collective-permute-done.25.refs_5_ = f32[256,768]{1,0:T(8,128)} collective-permute-done((f32[256,768]{1,0:T(8,128)S(1)}, f32[256,768]{1,0:T(8,128)}, u32[]{:S(2)}, u32[]{:S(2)}) %collective-permute-start.25) | collective-permute-done | bytes 786464 | tf_op jit(solution)/shard_map/ppermute | solution.py:419
  229.7 1.0 slice.210
  230.7 1.0 slice.211
  231.7 0.9 copy-done.2
  232.6 1.5 collective-permute-start.24
  234.1 9.6 %collective-permute-start.26 = (f32[128,768]{1,0:T(8,128)S(1)}, f32[128,768]{1,0:T(8,128)}, u32[]{:S(2)}, u32[]{:S(2)}) collective-permute-start(f32[128,768]{1,0:T(8,128)S(1)} %slice.211), channel_id=1, source_target_pairs={{0,4},{1,5},{2,6},{3,7},{4,12},{5,13},{6,14},{7,15},{8,0},{9,1},{1... | collective-permute-start | bytes 1179656 | tf_op jit(solution)/shard_map/ppermute | solution.py:419
  243.7 2.8 collective-permute-done.32.refs_5_
  247.2 0.8 copy-done.7
  248.0 3.2 collective-permute-done.24.refs_3_
  251.2 11.9 %collective-permute-done.26.refs_4_ = f32[128,768]{1,0:T(8,128)} collective-permute-done((f32[128,768]{1,0:T(8,128)S(1)}, f32[128,768]{1,0:T(8,128)}, u32[]{:S(2)}, u32[]{:S(2)}) %collective-permute-start.26) | collective-permute-done | bytes 393248 | tf_op jit(solution)/shard_map/ppermute | solution.py:419
  263.1 0.6 slice_bitcast_fusion.refs_0_
  263.8 0.7 divide_multiply_fusion.refs_1_
  264.4 10.3 %chi.5 = (f32[5,256,4096]{2,1,0:T(8,128)}, f32[5,256,4096]{2,1,0:T(8,128)}) custom-call(s32[16]{0:T(128)} %slice_bitcast_fusion.refs_0_, f32[5,384]{1,0:T(8,128)} %divide_multiply_fusion.refs_1_, f32[256,768]{1,0:T(8,128)} %copy-done, f32[256,768]{1,0:T(8,128)} %copy-done, f32[256,768]{1,0:T(8,128)} %copy-done.2), custom_call_target="tpu_custom_call" | custom-call | tf_op jit(solution)/shard_map/chi/pallas_call | solution.py:359
  274.7 15.9 %chi.6 = (f32[5,256,4096]{2,1,0:T(8,128)}, f32[5,256,4096]{2,1,0:T(8,128)}) custom-call(s32[16]{0:T(128)} %slice_bitcast_fusion.refs_0_, f32[5,384]{1,0:T(8,128)} %divide_multiply_fusion.refs_1_, f32[256,768]{1,0:T(8,128)} %copy-done, f32[256,768]{1,0:T(8,128)} %copy-done.5, f32[256,768]{1,0:T(8,128)} %copy-done.8, ...), custom_call_target="tpu_custom_call", output_to_operand_aliasing={{0}: (7, {}), {1}: (8, {})} | custom-call | tf_op jit(solution)/shard_map/chi/pallas_call | solution.py:359
  290.7 15.9 %chi.7 = (f32[5,256,4096]{2,1,0:T(8,128)}, f32[5,256,4096]{2,1,0:T(8,128)}) custom-call(s32[16]{0:T(128)} %slice_bitcast_fusion.refs_0_, f32[5,384]{1,0:T(8,128)} %divide_multiply_fusion.refs_1_, f32[256,768]{1,0:T(8,128)} %copy-done, f32[256,768]{1,0:T(8,128)} %copy-done.3, f32[256,768]{1,0:T(8,128)} %copy-done.7, ...), custom_call_target="tpu_custom_call", output_to_operand_aliasing={{0}: (7, {}), {1}: (8, {})} | custom-call | tf_op jit(solution)/shard_map/chi/pallas_call | solution.py:359
  306.6 15.9 %chi.8 = (f32[5,256,4096]{2,1,0:T(8,128)}, f32[5,256,4096]{2,1,0:T(8,128)}) custom-call(s32[16]{0:T(128)} %slice_bitcast_fusion.refs_0_, f32[5,384]{1,0:T(8,128)} %divide_multiply_fusion.refs_1_, f32[256,768]{1,0:T(8,128)} %copy-done, f32[256,768]{1,0:T(8,128)} %collective-permute-done.23.refs_3_, ...), custom_call_target="tpu_custom_call", output_to_operand_aliasing={{0}: (7, {}), {1}: (8, {})} | custom-call | tf_op jit(solution)/shard_map/chi/pallas_call | solution.py:359
  322.6 10.6 %chi.9 = (f32[5,256,4096]{2,1,0:T(8,128)}, f32[5,256,4096]{2,1,0:T(8,128)}) custom-call(s32[16]{0:T(128)} %slice_bitcast_fusion.refs_0_, f32[5,384]{1,0:T(8,128)} %divide_multiply_fusion.refs_1_, f32[256,768]{1,0:T(8,128)} %copy-done, f32[128,768]{1,0:T(8,128)} %collective-permute-done.24.refs_3_, ...), custom_call_target="tpu_custom_call", output_to_operand_aliasing={{0}: (7, {}), {1}: (8, {})} | custom-call | tf_op jit(solution)/shard_map/chi/pallas_call | solution.py:359
  (100 shorter events, 6.4 us)
Async XLA Ops:
  1.7 0.6 copy-start.13
  27.2 42.8 %collective-permute-start.1 = (f32[256,8,128]{2,1,0:T(8,128)}, f32[256,8,128]{2,1,0:T(8,128)}, u32[]{:S(2)}, u32[]{:S(2)}) collective-permute-start(f32[256,8,128]{2,1,0:T(8,128)} %get-tuple-element.39), channel_id=1, source_target_pairs={{0,1},{1,0},{2,3},{3,2},{4,5},{5,4},{6,7},{7,6},{8,9},{9,8},{10,11... | collective-permute-start | bytes 3145736 | tf_op jit(solution)/shard_map/ppermute | solution.py:419
  47.7 24.0 %collective-permute-start.8 = (f32[256,8,128]{2,1,0:T(8,128)}, f32[256,8,128]{2,1,0:T(8,128)}, u32[]{:S(2)}, u32[]{:S(2)}) collective-permute-start(f32[256,8,128]{2,1,0:T(8,128)} %get-tuple-element.46), channel_id=1, source_target_pairs={{0,1},{1,0},{2,3},{3,2},{4,5},{5,4},{6,7},{7,6},{8,9},{9,8},{10,11... | collective-permute-start | bytes 3145736 | tf_op jit(solution)/shard_map/ppermute | solution.py:419
  67.8 77.8 %copy-start.1 = (f32[256,8,128]{2,1,0:T(8,128)S(1)}, f32[256,8,128]{2,1,0:T(8,128)}, u32[]{:S(2)}) copy-start(f32[256,8,128]{2,1,0:T(8,128)} %get-tuple-element.55) | copy-start | bytes 3145732
  67.8 179.4 %copy-start.11 = (s32[128]{0:T(128)S(1)}, s32[128]{0:T(128)}, u32[]{:S(2)}) copy-start(s32[128]{0:T(128)} %param.21) | copy-start | bytes 1540
  67.8 179.4 %copy-start.12 = (f32[5]{0:T(128)S(1)}, f32[5]{0:T(128)}, u32[]{:S(2)}) copy-start(f32[5]{0:T(128)} %param.22) | copy-start | bytes 64
  67.8 180.2 %copy-start.9 = (f32[3]{0:T(128)S(1)}, f32[3]{0:T(128)}, u32[]{:S(2)}) copy-start(f32[3]{0:T(128)} %param.20) | copy-start | bytes 40
  67.8 180.1 %copy-start.10 = (f32[128]{0:T(128)S(1)}, f32[128]{0:T(128)}, u32[]{:S(2)}) copy-start(f32[128]{0:T(128)} %param.19) | copy-start | bytes 1540
  67.8 195.3 %copy-start.14 = (s32[1,32]{1,0:T(1,128)S(1)}, s32[1,32]{1,0:T(1,128)}, u32[]{:S(2)}) copy-start(s32[1,32]{1,0:T(1,128)} %copy-done.13) | copy-start | bytes 388
  67.9 8.5 %collective-permute-start.15 = (f32[256,8,128]{2,1,0:T(8,128)}, f32[256,8,128]{2,1,0:T(8,128)S(1)}, u32[]{:S(2)}, u32[]{:S(2)}) collective-permute-start(f32[256,8,128]{2,1,0:T(8,128)} %get-tuple-element.53), channel_id=1, source_target_pairs={{0,1},{1,0},{2,3},{3,2},{4,5},{5,4},{6,7},{7,6},{8,9},{9,8},{10,11... | collective-permute-start | bytes 3145736 | tf_op jit(solution)/shard_map/ppermute | solution.py:419
  68.4 9.4 %collective-permute-start = (f32[256,8,128]{2,1,0:T(8,128)}, f32[256,8,128]{2,1,0:T(8,128)S(1)}, u32[]{:S(2)}, u32[]{:S(2)}) collective-permute-start(f32[256,8,128]{2,1,0:T(8,128)} %get-tuple-element.37), channel_id=1, source_target_pairs={{0,1},{1,0},{2,3},{3,2},{4,5},{5,4},{6,7},{7,6},{8,9},{9,8},{10,11... | collective-permute-start | bytes 3145736 | tf_op jit(solution)/shard_map/ppermute | solution.py:419
  68.5 22.2 %collective-permute-start.7 = (f32[256,8,128]{2,1,0:T(8,128)}, f32[256,8,128]{2,1,0:T(8,128)}, u32[]{:S(2)}, u32[]{:S(2)}) collective-permute-start(f32[256,8,128]{2,1,0:T(8,128)} %get-tuple-element.44), channel_id=1, source_target_pairs={{0,1},{1,0},{2,3},{3,2},{4,5},{5,4},{6,7},{7,6},{8,9},{9,8},{10,11... | collective-permute-start | bytes 3145736 | tf_op jit(solution)/shard_map/ppermute | solution.py:419
  70.0 75.6 %collective-permute-start.14 = (f32[256,8,128]{2,1,0:T(8,128)}, f32[256,8,128]{2,1,0:T(8,128)S(1)}, u32[]{:S(2)}, u32[]{:S(2)}) collective-permute-start(f32[256,8,128]{2,1,0:T(8,128)} %get-tuple-element.51), channel_id=1, source_target_pairs={{0,1},{1,0},{2,3},{3,2},{4,5},{5,4},{6,7},{7,6},{8,9},{9,8},{10,11... | collective-permute-start | bytes 3145736 | tf_op jit(solution)/shard_map/ppermute | solution.py:419
  71.8 15.8 %collective-permute-start.2 = (f32[128,8,128]{2,1,0:T(8,128)S(1)}, f32[128,8,128]{2,1,0:T(8,128)S(1)}, u32[]{:S(2)}, u32[]{:S(2)}) collective-permute-start(f32[128,8,128]{2,1,0:T(8,128)S(1)} %get-tuple-element.71), channel_id=1, source_target_pairs={{0,2},{1,3},{2,0},{3,1},{4,6},{5,7},{6,4},{7,5},{8,10},{9,11},{10,... | collective-permute-start | bytes 1572872 | tf_op jit(solution)/shard_map/ppermute | solution.py:419
  76.4 22.4 %collective-permute-start.9 = (f32[128,8,128]{2,1,0:T(8,128)S(1)}, f32[128,8,128]{2,1,0:T(8,128)S(1)}, u32[]{:S(2)}, u32[]{:S(2)}) collective-permute-start(f32[128,8,128]{2,1,0:T(8,128)S(1)} %get-tuple-element.75), channel_id=1, source_target_pairs={{0,2},{1,3},{2,0},{3,1},{4,6},{5,7},{6,4},{7,5},{8,10},{9,11},{10,... | collective-permute-start | bytes 1572872 | tf_op jit(solution)/shard_map/ppermute | solution.py:419
  77.8 53.0 %collective-permute-start.3 = (f32[128,8,128]{2,1,0:T(8,128)S(1)}, f32[128,8,128]{2,1,0:T(8,128)S(1)}, u32[]{:S(2)}, u32[]{:S(2)}) collective-permute-start(f32[128,8,128]{2,1,0:T(8,128)S(1)} %get-tuple-element.70), channel_id=1, source_target_pairs={{0,2},{1,3},{2,0},{3,1},{4,6},{5,7},{6,4},{7,5},{8,10},{9,11},{10,... | collective-permute-start | bytes 1572872 | tf_op jit(solution)/shard_map/ppermute | solution.py:419
  87.5 33.7 %collective-permute-start.10 = (f32[128,8,128]{2,1,0:T(8,128)S(1)}, f32[128,8,128]{2,1,0:T(8,128)S(1)}, u32[]{:S(2)}, u32[]{:S(2)}) collective-permute-start(f32[128,8,128]{2,1,0:T(8,128)S(1)} %get-tuple-element.74), channel_id=1, source_target_pairs={{0,2},{1,3},{2,0},{3,1},{4,6},{5,7},{6,4},{7,5},{8,10},{9,11},{10,... | collective-permute-start | bytes 1572872 | tf_op jit(solution)/shard_map/ppermute | solution.py:419
  90.7 43.9 %collective-permute-start.16 = (f32[128,8,128]{2,1,0:T(8,128)S(1)}, f32[128,8,128]{2,1,0:T(8,128)S(1)}, u32[]{:S(2)}, u32[]{:S(2)}) collective-permute-start(f32[128,8,128]{2,1,0:T(8,128)S(1)} %get-tuple-element.73), channel_id=1, source_target_pairs={{0,2},{1,3},{2,0},{3,1},{4,6},{5,7},{6,4},{7,5},{8,10},{9,11},{10,... | collective-permute-start | bytes 1572872 | tf_op jit(solution)/shard_map/ppermute | solution.py:419
  98.8 34.3 %collective-permute-start.5 = (f32[64,8,128]{2,1,0:T(8,128)S(1)}, f32[64,8,128]{2,1,0:T(8,128)S(1)}, u32[]{:S(2)}, u32[]{:S(2)}) collective-permute-start(f32[64,8,128]{2,1,0:T(8,128)S(1)} %get-tuple-element.42), channel_id=1, source_target_pairs={{0,8},{1,9},{2,10},{3,11},{4,0},{5,1},{6,2},{7,3},{8,12},{9,13},{1... | collective-permute-start | bytes 786440 | tf_op jit(solution)/shard_map/ppermute | solution.py:419
  121.2 7.2 %collective-permute-start.12 = (f32[64,8,128]{2,1,0:T(8,128)S(1)}, f32[64,8,128]{2,1,0:T(8,128)S(1)}, u32[]{:S(2)}, u32[]{:S(2)}) collective-permute-start(f32[64,8,128]{2,1,0:T(8,128)S(1)} %get-tuple-element.49), channel_id=1, source_target_pairs={{0,8},{1,9},{2,10},{3,11},{4,0},{5,1},{6,2},{7,3},{8,12},{9,13},{1... | collective-permute-start | bytes 786440 | tf_op jit(solution)/shard_map/ppermute | solution.py:419
  128.4 13.1 %collective-permute-start.11 = (f32[64,8,128]{2,1,0:T(8,128)S(1)}, f32[64,8,128]{2,1,0:T(8,128)S(1)}, u32[]{:S(2)}, u32[]{:S(2)}) collective-permute-start(f32[64,8,128]{2,1,0:T(8,128)S(1)} %get-tuple-element.48), channel_id=1, source_target_pairs={{0,4},{1,5},{2,6},{3,7},{4,12},{5,13},{6,14},{7,15},{8,0},{9,1},{1... | collective-permute-start | bytes 786440 | tf_op jit(solution)/shard_map/ppermute | solution.py:419
  130.8 14.8 %collective-permute-start.13 = (f32[64,8,128]{2,1,0:T(8,128)S(1)}, f32[64,8,128]{2,1,0:T(8,128)S(1)}, u32[]{:S(2)}, u32[]{:S(2)}) collective-permute-start(f32[64,8,128]{2,1,0:T(8,128)S(1)} %slice_add_fusion.14), channel_id=1, source_target_pairs={{0,8},{1,9},{2,10},{3,11},{4,0},{5,1},{6,2},{7,3},{8,12},{9,13},{1... | collective-permute-start | bytes 786440 | tf_op jit(solution)/shard_map/ppermute | solution.py:419
  133.1 14.8 %collective-permute-start.17 = (f32[128,8,128]{2,1,0:T(8,128)S(1)}, f32[128,8,128]{2,1,0:T(8,128)S(1)}, u32[]{:S(2)}, u32[]{:S(2)}) collective-permute-start(f32[128,8,128]{2,1,0:T(8,128)S(1)} %get-tuple-element.72), channel_id=1, source_target_pairs={{0,2},{1,3},{2,0},{3,1},{4,6},{5,7},{6,4},{7,5},{8,10},{9,11},{10,... | collective-permute-start | bytes 1572872 | tf_op jit(solution)/shard_map/ppermute | solution.py:419
  134.7 28.3 %collective-permute-start.4 = (f32[64,8,128]{2,1,0:T(8,128)S(1)}, f32[64,8,128]{2,1,0:T(8,128)S(1)}, u32[]{:S(2)}, u32[]{:S(2)}) collective-permute-start(f32[64,8,128]{2,1,0:T(8,128)S(1)} %get-tuple-element.41), channel_id=1, source_target_pairs={{0,4},{1,5},{2,6},{3,7},{4,12},{5,13},{6,14},{7,15},{8,0},{9,1},{1... | collective-permute-start | bytes 786440 | tf_op jit(solution)/shard_map/ppermute | solution.py:419
  141.5 21.5 %collective-permute-start.6 = (f32[64,8,128]{2,1,0:T(8,128)S(1)}, f32[64,8,128]{2,1,0:T(8,128)S(1)}, u32[]{:S(2)}, u32[]{:S(2)}) collective-permute-start(f32[64,8,128]{2,1,0:T(8,128)S(1)} %slice_add_fusion.16), channel_id=1, source_target_pairs={{0,8},{1,9},{2,10},{3,11},{4,0},{5,1},{6,2},{7,3},{8,12},{9,13},{1... | collective-permute-start | bytes 786440 | tf_op jit(solution)/shard_map/ppermute | solution.py:419
  145.7 16.1 %collective-permute-start.19 = (f32[64,8,128]{2,1,0:T(8,128)S(1)}, f32[64,8,128]{2,1,0:T(8,128)S(1)}, u32[]{:S(2)}, u32[]{:S(2)}) collective-permute-start(f32[64,8,128]{2,1,0:T(8,128)S(1)} %get-tuple-element.57), channel_id=1, source_target_pairs={{0,8},{1,9},{2,10},{3,11},{4,0},{5,1},{6,2},{7,3},{8,12},{9,13},{1... | collective-permute-start | bytes 786440 | tf_op jit(solution)/shard_map/ppermute | solution.py:419
  146.8 18.5 %collective-permute-start.18 = (f32[64,8,128]{2,1,0:T(8,128)S(1)}, f32[64,8,128]{2,1,0:T(8,128)S(1)}, u32[]{:S(2)}, u32[]{:S(2)}) collective-permute-start(f32[64,8,128]{2,1,0:T(8,128)S(1)} %get-tuple-element.56), channel_id=1, source_target_pairs={{0,4},{1,5},{2,6},{3,7},{4,12},{5,13},{6,14},{7,15},{8,0},{9,1},{1... | collective-permute-start | bytes 786440 | tf_op jit(solution)/shard_map/ppermute | solution.py:419
  161.9 8.4 %collective-permute-start.20 = (f32[64,8,128]{2,1,0:T(8,128)S(1)}, f32[64,8,128]{2,1,0:T(8,128)S(1)}, u32[]{:S(2)}, u32[]{:S(2)}) collective-permute-start(f32[64,8,128]{2,1,0:T(8,128)S(1)} %slice_add_fusion.12), channel_id=1, source_target_pairs={{0,8},{1,9},{2,10},{3,11},{4,0},{5,1},{6,2},{7,3},{8,12},{9,13},{1... | collective-permute-start | bytes 786440 | tf_op jit(solution)/shard_map/ppermute | solution.py:419
  171.9 38.8 %copy-start = (f32[256,768]{1,0:T(8,128)}, f32[256,768]{1,0:T(8,128)S(1)}, u32[]{:S(2)}) copy-start(f32[256,768]{1,0:T(8,128)S(1)} %reshape.106.refs_2_.refs_3_) | copy-start | bytes 2359300
  171.9 18.6 %collective-permute-start.21 = (f32[256,768]{1,0:T(8,128)S(1)}, f32[256,768]{1,0:T(8,128)S(1)}, u32[]{:S(2)}, u32[]{:S(2)}) collective-permute-start(f32[256,768]{1,0:T(8,128)S(1)} %reshape.106.refs_2_.refs_3_), channel_id=1, source_target_pairs={{0,8},{1,9},{2,10},{3,11},{4,0},{5,1},{6,2},{7,3},{8,12},{9,13},{1... | collective-permute-start | bytes 2359304 | tf_op jit(solution)/shard_map/ppermute | solution.py:419
  190.5 56.6 %copy-start.4 = (f32[256,768]{1,0:T(8,128)}, f32[256,768]{1,0:T(8,128)S(1)}, u32[]{:S(2)}) copy-start(f32[256,768]{1,0:T(8,128)S(1)} %collective-permute-done.21.refs_5_) | copy-start | bytes 2359300
  190.5 18.6 %collective-permute-start.22 = (f32[256,768]{1,0:T(8,128)S(1)}, f32[256,768]{1,0:T(8,128)S(1)}, u32[]{:S(2)}, u32[]{:S(2)}) collective-permute-start(f32[256,768]{1,0:T(8,128)S(1)} %reshape.106.refs_2_.refs_3_), channel_id=1, source_target_pairs={{0,4},{1,5},{2,6},{3,7},{4,12},{5,13},{6,14},{7,15},{8,0},{9,1},{1... | collective-permute-start | bytes 2359304 | tf_op jit(solution)/shard_map/ppermute | solution.py:419
  191.5 19.7 %collective-permute-start.34 = (f32[256,768]{1,0:T(8,128)S(1)}, f32[256,768]{1,0:T(8,128)S(1)}, u32[]{:S(2)}, u32[]{:S(2)}) collective-permute-start(f32[256,768]{1,0:T(8,128)S(1)} %reshape.106.refs_2_.refs_3_), channel_id=1, source_target_pairs={{0,2},{1,3},{2,0},{3,1},{4,6},{5,7},{6,4},{7,5},{8,10},{9,11},{10,... | collective-permute-start | bytes 2359304 | tf_op jit(solution)/shard_map/ppermute | solution.py:419
  209.0 25.1 %copy-start.3 = (f32[256,768]{1,0:T(8,128)}, f32[256,768]{1,0:T(8,128)S(1)}, u32[]{:S(2)}) copy-start(f32[256,768]{1,0:T(8,128)S(1)} %collective-permute-done.22.refs_3_) | copy-start | bytes 2359300
  209.0 17.0 %collective-permute-start.23 = (f32[256,768]{1,0:T(8,128)S(1)}, f32[256,768]{1,0:T(8,128)}, u32[]{:S(2)}, u32[]{:S(2)}) collective-permute-start(f32[256,768]{1,0:T(8,128)S(1)} %collective-permute-done.21.refs_5_), channel_id=1, source_target_pairs={{0,8},{1,9},{2,10},{3,11},{4,0},{5,1},{6,2},{7,3},{8,12},{9,13},{1... | collective-permute-start | bytes 2359304 | tf_op jit(solution)/shard_map/ppermute | solution.py:419
  209.1 20.5 %collective-permute-start.25 = (f32[256,768]{1,0:T(8,128)S(1)}, f32[256,768]{1,0:T(8,128)}, u32[]{:S(2)}, u32[]{:S(2)}) collective-permute-start(f32[256,768]{1,0:T(8,128)S(1)} %collective-permute-done.22.refs_3_), channel_id=1, source_target_pairs={{0,2},{1,3},{2,0},{3,1},{4,6},{5,7},{6,4},{7,5},{8,10},{9,11},{10,... | collective-permute-start | bytes 2359304 | tf_op jit(solution)/shard_map/ppermute | solution.py:419
  210.7 21.1 %collective-permute-start.37 = (f32[256,768]{1,0:T(8,128)S(1)}, f32[256,768]{1,0:T(8,128)S(1)}, u32[]{:S(2)}, u32[]{:S(2)}) collective-permute-start(f32[256,768]{1,0:T(8,128)S(1)} %reshape.106.refs_2_.refs_3_), channel_id=1, source_target_pairs={{0,1},{1,0},{2,3},{3,2},{4,5},{5,4},{6,7},{7,6},{8,9},{9,8},{10,11... | collective-permute-start | bytes 2359304 | tf_op jit(solution)/shard_map/ppermute | solution.py:419
  210.7 23.5 %collective-permute-start.36 = (f32[256,768]{1,0:T(8,128)S(1)}, f32[256,768]{1,0:T(8,128)S(1)}, u32[]{:S(2)}, u32[]{:S(2)}) collective-permute-start(f32[256,768]{1,0:T(8,128)S(1)} %collective-permute-done.21.refs_5_), channel_id=1, source_target_pairs={{0,1},{1,0},{2,3},{3,2},{4,5},{5,4},{6,7},{7,6},{8,9},{9,8},{10,11... | collective-permute-start | bytes 2359304 | tf_op jit(solution)/shard_map/ppermute | solution.py:419
  211.2 36.0 %copy-start.5 = (f32[256,768]{1,0:T(8,128)}, f32[256,768]{1,0:T(8,128)S(1)}, u32[]{:S(2)}) copy-start(f32[256,768]{1,0:T(8,128)S(1)} %collective-permute-done.34.refs_3_) | copy-start | bytes 2359300
  211.2 35.3 %collective-permute-start.32 = (f32[256,768]{1,0:T(8,128)S(1)}, f32[256,768]{1,0:T(8,128)}, u32[]{:S(2)}, u32[]{:S(2)}) collective-permute-start(f32[256,768]{1,0:T(8,128)S(1)} %collective-permute-done.21.refs_5_), channel_id=1, source_target_pairs={{0,2},{1,3},{2,0},{3,1},{4,6},{5,7},{6,4},{7,5},{8,10},{9,11},{10,... | collective-permute-start | bytes 2359304 | tf_op jit(solution)/shard_map/ppermute | solution.py:419
  226.0 20.5 %collective-permute-start.35 = (f32[256,768]{1,0:T(8,128)S(1)}, f32[256,768]{1,0:T(8,128)S(1)}, u32[]{:S(2)}, u32[]{:S(2)}) collective-permute-start(f32[256,768]{1,0:T(8,128)S(1)} %collective-permute-done.34.refs_3_), channel_id=1, source_target_pairs={{0,1},{1,0},{2,3},{3,2},{4,5},{5,4},{6,7},{7,6},{8,9},{9,8},{10,11... | collective-permute-start | bytes 2359304 | tf_op jit(solution)/shard_map/ppermute | solution.py:419
  229.7 17.4 %collective-permute-start.31 = (f32[256,768]{1,0:T(8,128)S(1)}, f32[256,768]{1,0:T(8,128)S(1)}, u32[]{:S(2)}, u32[]{:S(2)}) collective-permute-start(f32[256,768]{1,0:T(8,128)S(1)} %collective-permute-done.22.refs_3_), channel_id=1, source_target_pairs={{0,1},{1,0},{2,3},{3,2},{4,5},{5,4},{6,7},{7,6},{8,9},{9,8},{10,11... | collective-permute-start | bytes 2359304 | tf_op jit(solution)/shard_map/ppermute | solution.py:419
  231.7 0.9 copy-start.2
  232.6 18.6 %collective-permute-start.24 = (f32[128,768]{1,0:T(8,128)S(1)}, f32[128,768]{1,0:T(8,128)}, u32[]{:S(2)}, u32[]{:S(2)}) collective-permute-start(f32[128,768]{1,0:T(8,128)S(1)} %slice.210), channel_id=1, source_target_pairs={{0,2},{1,3},{2,0},{3,1},{4,6},{5,7},{6,4},{7,5},{8,10},{9,11},{10,... | collective-permute-start | bytes 1179656 | tf_op jit(solution)/shard_map/ppermute | solution.py:419
  234.1 13.1 %copy-start.6 = (f32[256,768]{1,0:T(8,128)}, f32[256,768]{1,0:T(8,128)S(1)}, u32[]{:S(2)}) copy-start(f32[256,768]{1,0:T(8,128)S(1)} %collective-permute-done.36.refs_6_) | copy-start | bytes 2359300
  234.1 29.0 %collective-permute-start.26 = (f32[128,768]{1,0:T(8,128)S(1)}, f32[128,768]{1,0:T(8,128)}, u32[]{:S(2)}, u32[]{:S(2)}) collective-permute-start(f32[128,768]{1,0:T(8,128)S(1)} %slice.211), channel_id=1, source_target_pairs={{0,4},{1,5},{2,6},{3,7},{4,12},{5,13},{6,14},{7,15},{8,0},{9,1},{1... | collective-permute-start | bytes 1179656 | tf_op jit(solution)/shard_map/ppermute | solution.py:419
  246.5 44.1 %collective-permute-start.33 = (f32[256,768]{1,0:T(8,128)}, f32[256,768]{1,0:T(8,128)}, u32[]{:S(2)}, u32[]{:S(2)}) collective-permute-start(f32[256,768]{1,0:T(8,128)} %collective-permute-done.32.refs_5_), channel_id=1, source_target_pairs={{0,1},{1,0},{2,3},{3,2},{4,5},{5,4},{6,7},{7,6},{8,9},{9,8},{10,11... | collective-permute-start | bytes 2359304 | tf_op jit(solution)/shard_map/ppermute | solution.py:419
  246.5 1.5 copy-start.8
  246.5 60.1 %collective-permute-start.29 = (f32[256,768]{1,0:T(8,128)}, f32[256,768]{1,0:T(8,128)}, u32[]{:S(2)}, u32[]{:S(2)}) collective-permute-start(f32[256,768]{1,0:T(8,128)} %collective-permute-done.23.refs_3_), channel_id=1, source_target_pairs={{0,1},{1,0},{2,3},{3,2},{4,5},{5,4},{6,7},{7,6},{8,9},{9,8},{10,11... | collective-permute-start | bytes 2359304 | tf_op jit(solution)/shard_map/ppermute | solution.py:419
  247.0 0.9 copy-start.7
  247.0 59.6 %collective-permute-start.30 = (f32[256,768]{1,0:T(8,128)}, f32[256,768]{1,0:T(8,128)}, u32[]{:S(2)}, u32[]{:S(2)}) collective-permute-start(f32[256,768]{1,0:T(8,128)} %collective-permute-done.25.refs_5_), channel_id=1, source_target_pairs={{0,1},{1,0},{2,3},{3,2},{4,5},{5,4},{6,7},{7,6},{8,9},{9,8},{10,11... | collective-permute-start | bytes 2359304 | tf_op jit(solution)/shard_map/ppermute | solution.py:419
  251.2 71.4 %collective-permute-start.27 = (f32[128,768]{1,0:T(8,128)}, f32[128,768]{1,0:T(8,128)}, u32[]{:S(2)}, u32[]{:S(2)}) collective-permute-start(f32[128,768]{1,0:T(8,128)} %collective-permute-done.24.refs_3_), channel_id=1, source_target_pairs={{0,1},{1,0},{2,3},{3,2},{4,5},{5,4},{6,7},{7,6},{8,9},{9,8},{10,11... | collective-permute-start | bytes 1179656 | tf_op jit(solution)/shard_map/ppermute | solution.py:419
  263.1 59.5 %collective-permute-start.28 = (f32[128,768]{1,0:T(8,128)}, f32[128,768]{1,0:T(8,128)}, u32[]{:S(2)}, u32[]{:S(2)}) collective-permute-start(f32[128,768]{1,0:T(8,128)} %collective-permute-done.26.refs_4_), channel_id=1, source_target_pairs={{0,1},{1,0},{2,3},{3,2},{4,5},{5,4},{6,7},{7,6},{8,9},{9,8},{10,11... | collective-permute-start | bytes 1179656 | tf_op jit(solution)/shard_map/ppermute | solution.py:419

commit v11 on v9

--- a/solution.py
+++ b/solution.py
@@ -190,7 +190,7 @@
     copies = []
     for n in reversed(range(PARTS)):
         first = n * quads
-        in_steps(quads, math.gcd(quads, 2 * SUB), lambda q, first=first: quad(first + q))
+        in_steps(quads, math.gcd(quads, 4 * SUB), lambda q, first=first: quad(first + q))
         copies.append(
             pltpu.make_async_copy(out_scr.at[pl.ds(first, quads)], outs[n], out_sems.at[n])
         )
@@ -419,14 +419,12 @@
     return lax.ppermute(value, "blk", pairs)
 
 
-def reduce_scatter(near, far, near_other, far_other, links, before):
+def reduce_scatter(near, far, near_other, far_other, links):
     block = near.shape[0] // 4
     got_far = send(far_other, links.core)
     got_near = send(near_other, links.core)
     cuts = ((2 * block, 4 * block), (0, 2 * block))
     high, low = (send(far[i:j] + got_far[i:j], links.y) for i, j in cuts)
-    if before:
-        high, *_ = lax.optimization_barrier((high, *before))
     high = near[2 * block :] + got_near[2 * block :] + high
     to_cw, to_ccw, near = lax.optimization_barrier((high[:block], high[block:], near))
     low = near[: 2 * block] + got_near[: 2 * block] + low
@@ -507,8 +505,7 @@
             whole = jnp.concatenate(made)
             owned.append((lax.psum_scatter(whole, "blk", scatter_dimension=0, tiled=True),))
         else:
-            before = owned[-1][1:] if c == num_cond - 1 else ()
-            owned.append(reduce_scatter(*made, links, before))
+            owned.append(reduce_scatter(*made, links))
     for c, parts in enumerate(owned):
         owned[c] = sum(parts[1:], parts[0])
     own = jnp.stack(owned).reshape(num_cond, -1, 2, 4, num_val)

time: 334 us -> 338 us (1.012)
  starting transfers between devices: 32.6 us -> 46.4 us
  waiting for transfers between devices: 149 us -> 139 us
    ppermute x36, starting transfers between devices: 32.6 us -> 46.4 us  [send(): return lax.ppermute(value, 'blk', pairs)]
    ppermute x36, waiting for transfers between devices: 149 us -> 139 us  [send(): return lax.ppermute(value, 'blk', pairs)]
where the time goes in v11:
time: 338 us
  waiting for transfers between devices  139 us (41%)
  Pallas kernels  127 us (38%)
  starting transfers between devices  46.4 us (14%)
  other arithmetic  14.3 us (4%)
  local copies, waits for them, and re-layouts  9.15 us (3%)
    ppermute x36, waiting for transfers between devices, send(): return lax.ppermute(value, 'blk', pairs)  139 us
    pallas_call x5, Pallas kernels, chi_group(): pl.pallas_call(functools.partial(chi_group_kernel, counts, old is not Non...  68.6 us
    pallas_call x3, Pallas kernels, transform(): pl.pallas_call(transform_kernel, grid=(1,), out_shape=(jax.ShapeDtypeStru...  58.7 us
    ppermute x36, starting transfers between devices, send(): return lax.ppermute(value, 'blk', pairs)  46.4 us
  transfers between devices with their start and end apart: 36, of which 15 were waited for; matrix products, arithmetic and copies ran while one was open for 4% of the time, Pallas kernels for 29%

profile of v11, /device:TPU:0, one launch (start us, length us, event | category | flops | bytes accessed | tf_op | source)
XLA Modules:
  0.0 337.5 jit_solution(17715518177358053059)
XLA Ops:
  1.0 0.7 constant_dynamic-slice_fusion
  1.7 0.6 copy-done.12
  2.3 0.8 fusion.11
  3.1 0.6 gather_fusion
  3.7 0.6 fusion.33
  4.3 1.9 copy.41
  6.2 1.0 broadcast_in_dim.20.cs_hbm
  7.2 19.6 %transform.3 = (f32[256,8,128]{2,1,0:T(8,128)}, f32[256,8,128]{2,1,0:T(8,128)}, f32[256,8,128]{2,1,0:T(8,128)}, f32[256,8,128]{2,1,0:T(8,128)}) custom-call(s32[4096]{0:T(1024)} %bitcast.43, s32[4096]{0:T(1024)} %bitcast.40, f32[4,64,64,128]{3,2,1,0:T(8,128)} %bitcast.30, f32[3,4,64,64]{3,2,1,0:T(8,128)} %bitcast.33, ...), custom_call_target="tpu_custom_call" | custom-call | tf_op jit(solution)/shard_map/transform/pallas_call | solution.py:210
  26.8 0.6 collective-permute-start.1
  27.4 19.6 %transform.4 = (f32[256,8,128]{2,1,0:T(8,128)}, f32[256,8,128]{2,1,0:T(8,128)}, f32[256,8,128]{2,1,0:T(8,128)}, f32[256,8,128]{2,1,0:T(8,128)}) custom-call(s32[4096]{0:T(1024)} %bitcast.44, s32[4096]{0:T(1024)} %bitcast.41, f32[4,64,64,128]{3,2,1,0:T(8,128)} %bitcast.31, f32[3,4,64,64]{3,2,1,0:T(8,128)} %bitcast.34, ...), custom_call_target="tpu_custom_call" | custom-call | tf_op jit(solution)/shard_map/transform/pallas_call | solution.py:210
  47.0 19.5 %transform.5 = (f32[256,8,128]{2,1,0:T(8,128)}, f32[256,8,128]{2,1,0:T(8,128)}, f32[256,8,128]{2,1,0:T(8,128)}, f32[256,8,128]{2,1,0:T(8,128)}) custom-call(s32[4096]{0:T(1024)} %bitcast.45, s32[4096]{0:T(1024)} %bitcast.42, f32[4,64,64,128]{3,2,1,0:T(8,128)} %bitcast.32, f32[3,4,64,64]{3,2,1,0:T(8,128)} %bitcast.35, ...), custom_call_target="tpu_custom_call" | custom-call | tf_op jit(solution)/shard_map/transform/pallas_call | solution.py:210
  66.6 0.6 collective-permute-start.15
  67.7 0.7 fusion.19
  68.9 1.6 slice_add_fusion.8
  70.6 3.0 collective-permute-start.2
  73.6 1.6 slice_add_fusion.4
  75.3 1.3 slice_add_fusion
  76.6 2.1 collective-permute-start.3
  78.7 7.7 %collective-permute-done.2 = f32[128,8,128]{2,1,0:T(8,128)S(1)} collective-permute-done((f32[128,8,128]{2,1,0:T(8,128)S(1)}, f32[128,8,128]{2,1,0:T(8,128)S(1)}, u32[]{:S(2)}, u32[]{:S(2)}) %collective-permute-start.2) | collective-permute-done | bytes 524320 | tf_op jit(solution)/shard_map/ppermute | solution.py:419
  86.3 2.0 collective-permute-start.16
  88.4 1.3 fusion.6
  89.8 7.8 %collective-permute-done.9 = f32[128,8,128]{2,1,0:T(8,128)S(1)} collective-permute-done((f32[128,8,128]{2,1,0:T(8,128)S(1)}, f32[128,8,128]{2,1,0:T(8,128)S(1)}, u32[]{:S(2)}, u32[]{:S(2)}) %collective-permute-start.9) | collective-permute-done | bytes 524320 | tf_op jit(solution)/shard_map/ppermute | solution.py:419
  97.6 2.0 collective-permute-start.17
  99.6 1.3 fusion.4
  100.9 2.6 collective-permute-start.5
  103.5 16.5 %collective-permute-done.16 = f32[128,8,128]{2,1,0:T(8,128)S(1)} collective-permute-done((f32[128,8,128]{2,1,0:T(8,128)S(1)}, f32[128,8,128]{2,1,0:T(8,128)S(1)}, u32[]{:S(2)}, u32[]{:S(2)}) %collective-permute-start.16) | collective-permute-done | bytes 524320 | tf_op jit(solution)/shard_map/ppermute | solution.py:419
  120.0 2.1 collective-permute-start.4
  122.1 1.1 fusion.2
  123.3 1.1 collective-permute-start.12
  124.4 1.3 fusion.5
  125.7 5.6 %collective-permute-done.10 = f32[128,8,128]{2,1,0:T(8,128)S(1)} collective-permute-done((f32[128,8,128]{2,1,0:T(8,128)S(1)}, f32[128,8,128]{2,1,0:T(8,128)S(1)}, u32[]{:S(2)}, u32[]{:S(2)}) %collective-permute-start.10) | collective-permute-done | bytes 524320 | tf_op jit(solution)/shard_map/ppermute | solution.py:419
  131.3 2.1 collective-permute-start.11
  133.4 1.1 fusion.3
  134.5 7.4 %collective-permute-done.17 = f32[128,8,128]{2,1,0:T(8,128)S(1)} collective-permute-done((f32[128,8,128]{2,1,0:T(8,128)S(1)}, f32[128,8,128]{2,1,0:T(8,128)S(1)}, u32[]{:S(2)}, u32[]{:S(2)}) %collective-permute-start.17) | collective-permute-done | bytes 524320 | tf_op jit(solution)/shard_map/ppermute | solution.py:419
  141.9 2.8 collective-permute-start.19
  144.9 3.1 collective-permute-start.6
  148.1 4.4 %collective-permute-done.19 = f32[64,8,128]{2,1,0:T(8,128)S(1)} collective-permute-done((f32[64,8,128]{2,1,0:T(8,128)S(1)}, f32[64,8,128]{2,1,0:T(8,128)S(1)}, u32[]{:S(2)}, u32[]{:S(2)}) %collective-permute-start.19) | collective-permute-done | bytes 262176 | tf_op jit(solution)/shard_map/ppermute | solution.py:419
  152.5 4.7 %collective-permute-start.13 = (f32[64,8,128]{2,1,0:T(8,128)S(1)}, f32[64,8,128]{2,1,0:T(8,128)S(1)}, u32[]{:S(2)}, u32[]{:S(2)}) collective-permute-start(f32[64,8,128]{2,1,0:T(8,128)S(1)} %slice_add_fusion.14), channel_id=1, source_target_pairs={{0,8},{1,9},{2,10},{3,11},{4,0},{5,1},{6,2},{7,3},{8,12},{9,13},{1... | collective-permute-start | bytes 786440 | tf_op jit(solution)/shard_map/ppermute | solution.py:419
  157.2 3.0 collective-permute-start.20
  160.2 2.5 collective-permute-done.6
  163.0 5.3 %collective-permute-done.13 = f32[64,8,128]{2,1,0:T(8,128)S(1)} collective-permute-done((f32[64,8,128]{2,1,0:T(8,128)S(1)}, f32[64,8,128]{2,1,0:T(8,128)S(1)}, u32[]{:S(2)}, u32[]{:S(2)}) %collective-permute-start.13) | collective-permute-done | bytes 262176 | tf_op jit(solution)/shard_map/ppermute | solution.py:419
  168.6 3.5 %collective-permute-done.20 = f32[64,8,128]{2,1,0:T(8,128)S(1)} collective-permute-done((f32[64,8,128]{2,1,0:T(8,128)S(1)}, f32[64,8,128]{2,1,0:T(8,128)S(1)}, u32[]{:S(2)}, u32[]{:S(2)}) %collective-permute-start.20) | collective-permute-done | bytes 262176 | tf_op jit(solution)/shard_map/ppermute | solution.py:419
  172.5 0.9 fusion
  173.8 3.4 %collective-permute-start.21 = (f32[256,768]{1,0:T(8,128)S(1)}, f32[256,768]{1,0:T(8,128)S(1)}, u32[]{:S(2)}, u32[]{:S(2)}) collective-permute-start(f32[256,768]{1,0:T(8,128)S(1)} %reshape.106.refs_2_.refs_3_), channel_id=1, source_target_pairs={{0,8},{1,9},{2,10},{3,11},{4,0},{5,1},{6,2},{7,3},{8,12},{9,13},{1... | collective-permute-start | bytes 2359304 | tf_op jit(solution)/shard_map/ppermute | solution.py:419
  177.3 15.3 %collective-permute-done.21.refs_5_ = f32[256,768]{1,0:T(8,128)S(1)} collective-permute-done((f32[256,768]{1,0:T(8,128)S(1)}, f32[256,768]{1,0:T(8,128)S(1)}, u32[]{:S(2)}, u32[]{:S(2)}) %collective-permute-start.21) | collective-permute-done | bytes 786464 | tf_op jit(solution)/shard_map/ppermute | solution.py:419
  192.6 2.4 collective-permute-start.22
  195.0 1.5 collective-permute-start.32
  196.5 14.9 %collective-permute-done.22.refs_3_ = f32[256,768]{1,0:T(8,128)} collective-permute-done((f32[256,768]{1,0:T(8,128)S(1)}, f32[256,768]{1,0:T(8,128)}, u32[]{:S(2)}, u32[]{:S(2)}) %collective-permute-start.22) | collective-permute-done | bytes 786464 | tf_op jit(solution)/shard_map/ppermute | solution.py:419
  211.4 2.0 collective-permute-start.23
  213.4 1.5 collective-permute-start.30
  215.2 0.9 copy-done.3
  216.6 11.6 %collective-permute-done.23.refs_3_ = f32[256,768]{1,0:T(8,128)} collective-permute-done((f32[256,768]{1,0:T(8,128)S(1)}, f32[256,768]{1,0:T(8,128)}, u32[]{:S(2)}, u32[]{:S(2)}) %collective-permute-start.23) | collective-permute-done | bytes 786464 | tf_op jit(solution)/shard_map/ppermute | solution.py:419
  228.2 1.5 collective-permute-start.24
  229.7 4.2 %collective-permute-done.30.refs_5_ = f32[256,768]{1,0:T(8,128)} collective-permute-done((f32[256,768]{1,0:T(8,128)S(1)}, f32[256,768]{1,0:T(8,128)}, u32[]{:S(2)}, u32[]{:S(2)}) %collective-permute-start.30) | collective-permute-done | bytes 786464 | tf_op jit(solution)/shard_map/ppermute | solution.py:419
  234.0 0.6 collective-permute-start.26
  234.9 15.9 %collective-permute-done.27.refs_5_ = f32[256,768]{1,0:T(8,128)} collective-permute-done((f32[256,768]{1,0:T(8,128)}, f32[256,768]{1,0:T(8,128)}, u32[]{:S(2)}, u32[]{:S(2)}) %collective-permute-start.27) | collective-permute-done | bytes 786464 | tf_op jit(solution)/shard_map/ppermute | solution.py:419
  250.8 16.4 %collective-permute-done.24.refs_3_ = f32[256,768]{1,0:T(8,128)} collective-permute-done((f32[256,768]{1,0:T(8,128)}, f32[256,768]{1,0:T(8,128)}, u32[]{:S(2)}, u32[]{:S(2)}) %collective-permute-start.24) | collective-permute-done | bytes 786464 | tf_op jit(solution)/shard_map/ppermute | solution.py:419
  267.2 0.6 slice_bitcast_fusion.refs_0_
  268.0 0.7 divide_multiply_fusion.refs_1_
  268.6 10.3 %chi.5 = (f32[5,256,4096]{2,1,0:T(8,128)}, f32[5,256,4096]{2,1,0:T(8,128)}) custom-call(s32[16]{0:T(128)} %slice_bitcast_fusion.refs_0_, f32[5,384]{1,0:T(8,128)} %divide_multiply_fusion.refs_1_, f32[256,768]{1,0:T(8,128)} %copy-done, f32[256,768]{1,0:T(8,128)} %copy-done, f32[256,768]{1,0:T(8,128)} %copy-done.3), custom_call_target="tpu_custom_call" | custom-call | tf_op jit(solution)/shard_map/chi/pallas_call | solution.py:359
  278.9 15.9 %chi.6 = (f32[5,256,4096]{2,1,0:T(8,128)}, f32[5,256,4096]{2,1,0:T(8,128)}) custom-call(s32[16]{0:T(128)} %slice_bitcast_fusion.refs_0_, f32[5,384]{1,0:T(8,128)} %divide_multiply_fusion.refs_1_, f32[256,768]{1,0:T(8,128)} %copy-done, f32[256,768]{1,0:T(8,128)} %copy-done.5, f32[256,768]{1,0:T(8,128)} %copy-done.7, ...), custom_call_target="tpu_custom_call", output_to_operand_aliasing={{0}: (7, {}), {1}: (8, {})} | custom-call | tf_op jit(solution)/shard_map/chi/pallas_call | solution.py:359
  294.9 15.9 %chi.7 = (f32[5,256,4096]{2,1,0:T(8,128)}, f32[5,256,4096]{2,1,0:T(8,128)}) custom-call(s32[16]{0:T(128)} %slice_bitcast_fusion.refs_0_, f32[5,384]{1,0:T(8,128)} %divide_multiply_fusion.refs_1_, f32[256,768]{1,0:T(8,128)} %copy-done, f32[256,768]{1,0:T(8,128)} %collective-permute-done.22.refs_3_, ...), custom_call_target="tpu_custom_call", output_to_operand_aliasing={{0}: (7, {}), {1}: (8, {})} | custom-call | tf_op jit(solution)/shard_map/chi/pallas_call | solution.py:359
  310.9 15.9 %chi.8 = (f32[5,256,4096]{2,1,0:T(8,128)}, f32[5,256,4096]{2,1,0:T(8,128)}) custom-call(s32[16]{0:T(128)} %slice_bitcast_fusion.refs_0_, f32[5,384]{1,0:T(8,128)} %divide_multiply_fusion.refs_1_, f32[256,768]{1,0:T(8,128)} %copy-done, f32[256,768]{1,0:T(8,128)} %collective-permute-done.23.refs_3_, ...), custom_call_target="tpu_custom_call", output_to_operand_aliasing={{0}: (7, {}), {1}: (8, {})} | custom-call | tf_op jit(solution)/shard_map/chi/pallas_call | solution.py:359
  326.8 10.5 %chi.9 = (f32[5,256,4096]{2,1,0:T(8,128)}, f32[5,256,4096]{2,1,0:T(8,128)}) custom-call(s32[16]{0:T(128)} %slice_bitcast_fusion.refs_0_, f32[5,384]{1,0:T(8,128)} %divide_multiply_fusion.refs_1_, f32[256,768]{1,0:T(8,128)} %copy-done, f32[256,768]{1,0:T(8,128)} %collective-permute-done.24.refs_3_, ...), custom_call_target="tpu_custom_call", output_to_operand_aliasing={{0}: (5, {}), {1}: (6, {})} | custom-call | tf_op jit(solution)/shard_map/chi/pallas_call | solution.py:359
  (92 shorter events, 4.6 us)
Async XLA Ops:
  1.7 0.6 copy-start.12
  26.8 42.0 %collective-permute-start.1 = (f32[256,8,128]{2,1,0:T(8,128)}, f32[256,8,128]{2,1,0:T(8,128)}, u32[]{:S(2)}, u32[]{:S(2)}) collective-permute-start(f32[256,8,128]{2,1,0:T(8,128)} %get-tuple-element.38), channel_id=1, source_target_pairs={{0,1},{1,0},{2,3},{3,2},{4,5},{5,4},{6,7},{7,6},{8,9},{9,8},{10,11... | collective-permute-start | bytes 3145736 | tf_op jit(solution)/shard_map/ppermute | solution.py:419
  46.9 23.6 %collective-permute-start.8 = (f32[256,8,128]{2,1,0:T(8,128)}, f32[256,8,128]{2,1,0:T(8,128)}, u32[]{:S(2)}, u32[]{:S(2)}) collective-permute-start(f32[256,8,128]{2,1,0:T(8,128)} %get-tuple-element.45), channel_id=1, source_target_pairs={{0,1},{1,0},{2,3},{3,2},{4,5},{5,4},{6,7},{7,6},{8,9},{9,8},{10,11... | collective-permute-start | bytes 3145736 | tf_op jit(solution)/shard_map/ppermute | solution.py:419
  66.6 66.8 %copy-start.2 = (f32[256,8,128]{2,1,0:T(8,128)S(1)}, f32[256,8,128]{2,1,0:T(8,128)}, u32[]{:S(2)}) copy-start(f32[256,8,128]{2,1,0:T(8,128)} %get-tuple-element.46) | copy-start | bytes 3145732
  66.6 78.1 %copy-start.1 = (f32[256,8,128]{2,1,0:T(8,128)S(1)}, f32[256,8,128]{2,1,0:T(8,128)}, u32[]{:S(2)}) copy-start(f32[256,8,128]{2,1,0:T(8,128)} %get-tuple-element.53) | copy-start | bytes 3145732
  66.6 200.6 %copy-start.10 = (s32[128]{0:T(128)S(1)}, s32[128]{0:T(128)}, u32[]{:S(2)}) copy-start(s32[128]{0:T(128)} %param.21) | copy-start | bytes 1540
  66.6 200.6 %copy-start.11 = (f32[5]{0:T(128)S(1)}, f32[5]{0:T(128)}, u32[]{:S(2)}) copy-start(f32[5]{0:T(128)} %param.22) | copy-start | bytes 64
  66.6 200.6 %copy-start.13 = (s32[1,32]{1,0:T(1,128)S(1)}, s32[1,32]{1,0:T(1,128)}, u32[]{:S(2)}) copy-start(s32[1,32]{1,0:T(1,128)} %copy-done.12) | copy-start | bytes 388
  66.6 201.3 %copy-start.8 = (f32[3]{0:T(128)S(1)}, f32[3]{0:T(128)}, u32[]{:S(2)}) copy-start(f32[3]{0:T(128)} %param.20) | copy-start | bytes 40
  66.6 201.2 %copy-start.9 = (f32[128]{0:T(128)S(1)}, f32[128]{0:T(128)}, u32[]{:S(2)}) copy-start(f32[128]{0:T(128)} %param.19) | copy-start | bytes 1540
  66.6 8.5 %collective-permute-start.15 = (f32[256,8,128]{2,1,0:T(8,128)}, f32[256,8,128]{2,1,0:T(8,128)S(1)}, u32[]{:S(2)}, u32[]{:S(2)}) collective-permute-start(f32[256,8,128]{2,1,0:T(8,128)} %get-tuple-element.52), channel_id=1, source_target_pairs={{0,1},{1,0},{2,3},{3,2},{4,5},{5,4},{6,7},{7,6},{8,9},{9,8},{10,11... | collective-permute-start | bytes 3145736 | tf_op jit(solution)/shard_map/ppermute | solution.py:419
  67.2 9.4 %collective-permute-start = (f32[256,8,128]{2,1,0:T(8,128)}, f32[256,8,128]{2,1,0:T(8,128)}, u32[]{:S(2)}, u32[]{:S(2)}) collective-permute-start(f32[256,8,128]{2,1,0:T(8,128)} %get-tuple-element.36), channel_id=1, source_target_pairs={{0,1},{1,0},{2,3},{3,2},{4,5},{5,4},{6,7},{7,6},{8,9},{9,8},{10,11... | collective-permute-start | bytes 3145736 | tf_op jit(solution)/shard_map/ppermute | solution.py:419
  67.3 22.4 %collective-permute-start.7 = (f32[256,8,128]{2,1,0:T(8,128)}, f32[256,8,128]{2,1,0:T(8,128)}, u32[]{:S(2)}, u32[]{:S(2)}) collective-permute-start(f32[256,8,128]{2,1,0:T(8,128)} %get-tuple-element.43), channel_id=1, source_target_pairs={{0,1},{1,0},{2,3},{3,2},{4,5},{5,4},{6,7},{7,6},{8,9},{9,8},{10,11... | collective-permute-start | bytes 3145736 | tf_op jit(solution)/shard_map/ppermute | solution.py:419
  68.8 32.1 %collective-permute-start.14 = (f32[256,8,128]{2,1,0:T(8,128)}, f32[256,8,128]{2,1,0:T(8,128)S(1)}, u32[]{:S(2)}, u32[]{:S(2)}) collective-permute-start(f32[256,8,128]{2,1,0:T(8,128)} %get-tuple-element.50), channel_id=1, source_target_pairs={{0,1},{1,0},{2,3},{3,2},{4,5},{5,4},{6,7},{7,6},{8,9},{9,8},{10,11... | collective-permute-start | bytes 3145736 | tf_op jit(solution)/shard_map/ppermute | solution.py:419
  70.6 15.8 %collective-permute-start.2 = (f32[128,8,128]{2,1,0:T(8,128)S(1)}, f32[128,8,128]{2,1,0:T(8,128)S(1)}, u32[]{:S(2)}, u32[]{:S(2)}) collective-permute-start(f32[128,8,128]{2,1,0:T(8,128)S(1)} %get-tuple-element.69), channel_id=1, source_target_pairs={{0,2},{1,3},{2,0},{3,1},{4,6},{5,7},{6,4},{7,5},{8,10},{9,11},{10,... | collective-permute-start | bytes 1572872 | tf_op jit(solution)/shard_map/ppermute | solution.py:419
  75.2 22.4 %collective-permute-start.9 = (f32[128,8,128]{2,1,0:T(8,128)S(1)}, f32[128,8,128]{2,1,0:T(8,128)S(1)}, u32[]{:S(2)}, u32[]{:S(2)}) collective-permute-start(f32[128,8,128]{2,1,0:T(8,128)S(1)} %get-tuple-element.71), channel_id=1, source_target_pairs={{0,2},{1,3},{2,0},{3,1},{4,6},{5,7},{6,4},{7,5},{8,10},{9,11},{10,... | collective-permute-start | bytes 1572872 | tf_op jit(solution)/shard_map/ppermute | solution.py:419
  76.6 46.7 %collective-permute-start.3 = (f32[128,8,128]{2,1,0:T(8,128)S(1)}, f32[128,8,128]{2,1,0:T(8,128)S(1)}, u32[]{:S(2)}, u32[]{:S(2)}) collective-permute-start(f32[128,8,128]{2,1,0:T(8,128)S(1)} %get-tuple-element.68), channel_id=1, source_target_pairs={{0,2},{1,3},{2,0},{3,1},{4,6},{5,7},{6,4},{7,5},{8,10},{9,11},{10,... | collective-permute-start | bytes 1572872 | tf_op jit(solution)/shard_map/ppermute | solution.py:419
  86.3 33.7 %collective-permute-start.16 = (f32[128,8,128]{2,1,0:T(8,128)S(1)}, f32[128,8,128]{2,1,0:T(8,128)S(1)}, u32[]{:S(2)}, u32[]{:S(2)}) collective-permute-start(f32[128,8,128]{2,1,0:T(8,128)S(1)} %get-tuple-element.73), channel_id=1, source_target_pairs={{0,2},{1,3},{2,0},{3,1},{4,6},{5,7},{6,4},{7,5},{8,10},{9,11},{10,... | collective-permute-start | bytes 1572872 | tf_op jit(solution)/shard_map/ppermute | solution.py:419
  89.7 41.6 %collective-permute-start.10 = (f32[128,8,128]{2,1,0:T(8,128)S(1)}, f32[128,8,128]{2,1,0:T(8,128)S(1)}, u32[]{:S(2)}, u32[]{:S(2)}) collective-permute-start(f32[128,8,128]{2,1,0:T(8,128)S(1)} %get-tuple-element.70), channel_id=1, source_target_pairs={{0,2},{1,3},{2,0},{3,1},{4,6},{5,7},{6,4},{7,5},{8,10},{9,11},{10,... | collective-permute-start | bytes 1572872 | tf_op jit(solution)/shard_map/ppermute | solution.py:419
  97.6 44.3 %collective-permute-start.17 = (f32[128,8,128]{2,1,0:T(8,128)S(1)}, f32[128,8,128]{2,1,0:T(8,128)S(1)}, u32[]{:S(2)}, u32[]{:S(2)}) collective-permute-start(f32[128,8,128]{2,1,0:T(8,128)S(1)} %get-tuple-element.72), channel_id=1, source_target_pairs={{0,2},{1,3},{2,0},{3,1},{4,6},{5,7},{6,4},{7,5},{8,10},{9,11},{10,... | collective-permute-start | bytes 1572872 | tf_op jit(solution)/shard_map/ppermute | solution.py:419
  100.9 43.9 %collective-permute-start.5 = (f32[64,8,128]{2,1,0:T(8,128)S(1)}, f32[64,8,128]{2,1,0:T(8,128)S(1)}, u32[]{:S(2)}, u32[]{:S(2)}) collective-permute-start(f32[64,8,128]{2,1,0:T(8,128)S(1)} %get-tuple-element.41), channel_id=1, source_target_pairs={{0,8},{1,9},{2,10},{3,11},{4,0},{5,1},{6,2},{7,3},{8,12},{9,13},{1... | collective-permute-start | bytes 786440 | tf_op jit(solution)/shard_map/ppermute | solution.py:419
  120.0 37.2 %collective-permute-start.4 = (f32[64,8,128]{2,1,0:T(8,128)S(1)}, f32[64,8,128]{2,1,0:T(8,128)S(1)}, u32[]{:S(2)}, u32[]{:S(2)}) collective-permute-start(f32[64,8,128]{2,1,0:T(8,128)S(1)} %get-tuple-element.40), channel_id=1, source_target_pairs={{0,4},{1,5},{2,6},{3,7},{4,12},{5,13},{6,14},{7,15},{8,0},{9,1},{1... | collective-permute-start | bytes 786440 | tf_op jit(solution)/shard_map/ppermute | solution.py:419
  123.3 21.6 %collective-permute-start.12 = (f32[64,8,128]{2,1,0:T(8,128)S(1)}, f32[64,8,128]{2,1,0:T(8,128)S(1)}, u32[]{:S(2)}, u32[]{:S(2)}) collective-permute-start(f32[64,8,128]{2,1,0:T(8,128)S(1)} %get-tuple-element.48), channel_id=1, source_target_pairs={{0,8},{1,9},{2,10},{3,11},{4,0},{5,1},{6,2},{7,3},{8,12},{9,13},{1... | collective-permute-start | bytes 786440 | tf_op jit(solution)/shard_map/ppermute | solution.py:419
  131.3 31.7 %collective-permute-start.11 = (f32[64,8,128]{2,1,0:T(8,128)S(1)}, f32[64,8,128]{2,1,0:T(8,128)S(1)}, u32[]{:S(2)}, u32[]{:S(2)}) collective-permute-start(f32[64,8,128]{2,1,0:T(8,128)S(1)} %get-tuple-element.47), channel_id=1, source_target_pairs={{0,4},{1,5},{2,6},{3,7},{4,12},{5,13},{6,14},{7,15},{8,0},{9,1},{1... | collective-permute-start | bytes 786440 | tf_op jit(solution)/shard_map/ppermute | solution.py:419
  141.9 10.6 %collective-permute-start.19 = (f32[64,8,128]{2,1,0:T(8,128)S(1)}, f32[64,8,128]{2,1,0:T(8,128)S(1)}, u32[]{:S(2)}, u32[]{:S(2)}) collective-permute-start(f32[64,8,128]{2,1,0:T(8,128)S(1)} %get-tuple-element.55), channel_id=1, source_target_pairs={{0,8},{1,9},{2,10},{3,11},{4,0},{5,1},{6,2},{7,3},{8,12},{9,13},{1... | collective-permute-start | bytes 786440 | tf_op jit(solution)/shard_map/ppermute | solution.py:419
  144.8 23.8 %collective-permute-start.18 = (f32[64,8,128]{2,1,0:T(8,128)S(1)}, f32[64,8,128]{2,1,0:T(8,128)S(1)}, u32[]{:S(2)}, u32[]{:S(2)}) collective-permute-start(f32[64,8,128]{2,1,0:T(8,128)S(1)} %get-tuple-element.54), channel_id=1, source_target_pairs={{0,4},{1,5},{2,6},{3,7},{4,12},{5,13},{6,14},{7,15},{8,0},{9,1},{1... | collective-permute-start | bytes 786440 | tf_op jit(solution)/shard_map/ppermute | solution.py:419
  144.9 17.8 %collective-permute-start.6 = (f32[64,8,128]{2,1,0:T(8,128)S(1)}, f32[64,8,128]{2,1,0:T(8,128)S(1)}, u32[]{:S(2)}, u32[]{:S(2)}) collective-permute-start(f32[64,8,128]{2,1,0:T(8,128)S(1)} %slice_add_fusion.16), channel_id=1, source_target_pairs={{0,8},{1,9},{2,10},{3,11},{4,0},{5,1},{6,2},{7,3},{8,12},{9,13},{1... | collective-permute-start | bytes 786440 | tf_op jit(solution)/shard_map/ppermute | solution.py:419
  152.5 15.8 %collective-permute-start.13 = (f32[64,8,128]{2,1,0:T(8,128)S(1)}, f32[64,8,128]{2,1,0:T(8,128)S(1)}, u32[]{:S(2)}, u32[]{:S(2)}) collective-permute-start(f32[64,8,128]{2,1,0:T(8,128)S(1)} %slice_add_fusion.14), channel_id=1, source_target_pairs={{0,8},{1,9},{2,10},{3,11},{4,0},{5,1},{6,2},{7,3},{8,12},{9,13},{1... | collective-permute-start | bytes 786440 | tf_op jit(solution)/shard_map/ppermute | solution.py:419
  157.2 15.0 %collective-permute-start.20 = (f32[64,8,128]{2,1,0:T(8,128)S(1)}, f32[64,8,128]{2,1,0:T(8,128)S(1)}, u32[]{:S(2)}, u32[]{:S(2)}) collective-permute-start(f32[64,8,128]{2,1,0:T(8,128)S(1)} %slice_add_fusion.12), channel_id=1, source_target_pairs={{0,8},{1,9},{2,10},{3,11},{4,0},{5,1},{6,2},{7,3},{8,12},{9,13},{1... | collective-permute-start | bytes 786440 | tf_op jit(solution)/shard_map/ppermute | solution.py:419
  173.8 22.7 %copy-start = (f32[256,768]{1,0:T(8,128)}, f32[256,768]{1,0:T(8,128)S(1)}, u32[]{:S(2)}) copy-start(f32[256,768]{1,0:T(8,128)S(1)} %reshape.106.refs_2_.refs_3_) | copy-start | bytes 2359300
  173.8 18.8 %collective-permute-start.21 = (f32[256,768]{1,0:T(8,128)S(1)}, f32[256,768]{1,0:T(8,128)S(1)}, u32[]{:S(2)}, u32[]{:S(2)}) collective-permute-start(f32[256,768]{1,0:T(8,128)S(1)} %reshape.106.refs_2_.refs_3_), channel_id=1, source_target_pairs={{0,8},{1,9},{2,10},{3,11},{4,0},{5,1},{6,2},{7,3},{8,12},{9,13},{1... | collective-permute-start | bytes 2359304 | tf_op jit(solution)/shard_map/ppermute | solution.py:419
  192.6 24.0 %copy-start.4 = (f32[256,768]{1,0:T(8,128)}, f32[256,768]{1,0:T(8,128)S(1)}, u32[]{:S(2)}) copy-start(f32[256,768]{1,0:T(8,128)S(1)} %collective-permute-done.21.refs_5_) | copy-start | bytes 2359300
  192.6 18.8 %collective-permute-start.22 = (f32[256,768]{1,0:T(8,128)S(1)}, f32[256,768]{1,0:T(8,128)}, u32[]{:S(2)}, u32[]{:S(2)}) collective-permute-start(f32[256,768]{1,0:T(8,128)S(1)} %reshape.106.refs_2_.refs_3_), channel_id=1, source_target_pairs={{0,4},{1,5},{2,6},{3,7},{4,12},{5,13},{6,14},{7,15},{8,0},{9,1},{1... | collective-permute-start | bytes 2359304 | tf_op jit(solution)/shard_map/ppermute | solution.py:419
  195.0 20.0 %collective-permute-start.32 = (f32[256,768]{1,0:T(8,128)S(1)}, f32[256,768]{1,0:T(8,128)S(1)}, u32[]{:S(2)}, u32[]{:S(2)}) collective-permute-start(f32[256,768]{1,0:T(8,128)S(1)} %reshape.106.refs_2_.refs_3_), channel_id=1, source_target_pairs={{0,2},{1,3},{2,0},{3,1},{4,6},{5,7},{6,4},{7,5},{8,10},{9,11},{10,... | collective-permute-start | bytes 2359304 | tf_op jit(solution)/shard_map/ppermute | solution.py:419
  196.5 18.7 %collective-permute-start.35 = (f32[256,768]{1,0:T(8,128)S(1)}, f32[256,768]{1,0:T(8,128)S(1)}, u32[]{:S(2)}, u32[]{:S(2)}) collective-permute-start(f32[256,768]{1,0:T(8,128)S(1)} %reshape.106.refs_2_.refs_3_), channel_id=1, source_target_pairs={{0,1},{1,0},{2,3},{3,2},{4,5},{5,4},{6,7},{7,6},{8,9},{9,8},{10,11... | collective-permute-start | bytes 2359304 | tf_op jit(solution)/shard_map/ppermute | solution.py:419
  211.4 16.8 %collective-permute-start.23 = (f32[256,768]{1,0:T(8,128)S(1)}, f32[256,768]{1,0:T(8,128)}, u32[]{:S(2)}, u32[]{:S(2)}) collective-permute-start(f32[256,768]{1,0:T(8,128)S(1)} %collective-permute-done.21.refs_5_), channel_id=1, source_target_pairs={{0,8},{1,9},{2,10},{3,11},{4,0},{5,1},{6,2},{7,3},{8,12},{9,13},{1... | collective-permute-start | bytes 2359304 | tf_op jit(solution)/shard_map/ppermute | solution.py:419
  213.4 16.3 %collective-permute-start.34 = (f32[256,768]{1,0:T(8,128)S(1)}, f32[256,768]{1,0:T(8,128)S(1)}, u32[]{:S(2)}, u32[]{:S(2)}) collective-permute-start(f32[256,768]{1,0:T(8,128)S(1)} %collective-permute-done.21.refs_5_), channel_id=1, source_target_pairs={{0,1},{1,0},{2,3},{3,2},{4,5},{5,4},{6,7},{7,6},{8,9},{9,8},{10,11... | collective-permute-start | bytes 2359304 | tf_op jit(solution)/shard_map/ppermute | solution.py:419
  213.4 20.5 %collective-permute-start.30 = (f32[256,768]{1,0:T(8,128)S(1)}, f32[256,768]{1,0:T(8,128)}, u32[]{:S(2)}, u32[]{:S(2)}) collective-permute-start(f32[256,768]{1,0:T(8,128)S(1)} %collective-permute-done.21.refs_5_), channel_id=1, source_target_pairs={{0,2},{1,3},{2,0},{3,1},{4,6},{5,7},{6,4},{7,5},{8,10},{9,11},{10,... | collective-permute-start | bytes 2359304 | tf_op jit(solution)/shard_map/ppermute | solution.py:419
  214.9 19.0 %copy-start.5 = (f32[256,768]{1,0:T(8,128)}, f32[256,768]{1,0:T(8,128)S(1)}, u32[]{:S(2)}) copy-start(f32[256,768]{1,0:T(8,128)S(1)} %collective-permute-done.32.refs_3_) | copy-start | bytes 2359300
  214.9 19.0 %collective-permute-start.33 = (f32[256,768]{1,0:T(8,128)S(1)}, f32[256,768]{1,0:T(8,128)S(1)}, u32[]{:S(2)}, u32[]{:S(2)}) collective-permute-start(f32[256,768]{1,0:T(8,128)S(1)} %collective-permute-done.32.refs_3_), channel_id=1, source_target_pairs={{0,1},{1,0},{2,3},{3,2},{4,5},{5,4},{6,7},{7,6},{8,9},{9,8},{10,11... | collective-permute-start | bytes 2359304 | tf_op jit(solution)/shard_map/ppermute | solution.py:419
  215.2 0.9 copy-start.3
  216.1 34.7 %collective-permute-start.27 = (f32[256,768]{1,0:T(8,128)}, f32[256,768]{1,0:T(8,128)}, u32[]{:S(2)}, u32[]{:S(2)}) collective-permute-start(f32[256,768]{1,0:T(8,128)} %collective-permute-done.22.refs_3_), channel_id=1, source_target_pairs={{0,2},{1,3},{2,0},{3,1},{4,6},{5,7},{6,4},{7,5},{8,10},{9,11},{10,... | collective-permute-start | bytes 2359304 | tf_op jit(solution)/shard_map/ppermute | solution.py:419
  228.2 39.0 %collective-permute-start.24 = (f32[256,768]{1,0:T(8,128)}, f32[256,768]{1,0:T(8,128)}, u32[]{:S(2)}, u32[]{:S(2)}) collective-permute-start(f32[256,768]{1,0:T(8,128)} %collective-permute-done.23.refs_3_), channel_id=1, source_target_pairs={{0,2},{1,3},{2,0},{3,1},{4,6},{5,7},{6,4},{7,5},{8,10},{9,11},{10,... | collective-permute-start | bytes 2359304 | tf_op jit(solution)/shard_map/ppermute | solution.py:419
  229.7 4.2 %copy-start.6 = (f32[256,768]{1,0:T(8,128)}, f32[256,768]{1,0:T(8,128)S(1)}, u32[]{:S(2)}) copy-start(f32[256,768]{1,0:T(8,128)S(1)} %collective-permute-done.34.refs_6_) | copy-start | bytes 2359300
  229.7 65.1 %collective-permute-start.29 = (f32[256,768]{1,0:T(8,128)}, f32[256,768]{1,0:T(8,128)}, u32[]{:S(2)}, u32[]{:S(2)}) collective-permute-start(f32[256,768]{1,0:T(8,128)} %collective-permute-done.22.refs_3_), channel_id=1, source_target_pairs={{0,1},{1,0},{2,3},{3,2},{4,5},{5,4},{6,7},{7,6},{8,9},{9,8},{10,11... | collective-permute-start | bytes 2359304 | tf_op jit(solution)/shard_map/ppermute | solution.py:419
  233.9 60.9 %collective-permute-start.31 = (f32[256,768]{1,0:T(8,128)}, f32[256,768]{1,0:T(8,128)}, u32[]{:S(2)}, u32[]{:S(2)}) collective-permute-start(f32[256,768]{1,0:T(8,128)} %collective-permute-done.30.refs_5_), channel_id=1, source_target_pairs={{0,1},{1,0},{2,3},{3,2},{4,5},{5,4},{6,7},{7,6},{8,9},{9,8},{10,11... | collective-permute-start | bytes 2359304 | tf_op jit(solution)/shard_map/ppermute | solution.py:419
  234.0 1.0 copy-start.7
  234.0 76.9 %collective-permute-start.26 = (f32[256,768]{1,0:T(8,128)}, f32[256,768]{1,0:T(8,128)}, u32[]{:S(2)}, u32[]{:S(2)}) collective-permute-start(f32[256,768]{1,0:T(8,128)} %collective-permute-done.23.refs_3_), channel_id=1, source_target_pairs={{0,1},{1,0},{2,3},{3,2},{4,5},{5,4},{6,7},{7,6},{8,9},{9,8},{10,11... | collective-permute-start | bytes 2359304 | tf_op jit(solution)/shard_map/ppermute | solution.py:419
  250.8 60.0 %collective-permute-start.28 = (f32[256,768]{1,0:T(8,128)}, f32[256,768]{1,0:T(8,128)}, u32[]{:S(2)}, u32[]{:S(2)}) collective-permute-start(f32[256,768]{1,0:T(8,128)} %collective-permute-done.27.refs_5_), channel_id=1, source_target_pairs={{0,1},{1,0},{2,3},{3,2},{4,5},{5,4},{6,7},{7,6},{8,9},{9,8},{10,11... | collective-permute-start | bytes 2359304 | tf_op jit(solution)/shard_map/ppermute | solution.py:419
  267.2 59.6 %collective-permute-start.25 = (f32[256,768]{1,0:T(8,128)}, f32[256,768]{1,0:T(8,128)}, u32[]{:S(2)}, u32[]{:S(2)}) collective-permute-start(f32[256,768]{1,0:T(8,128)} %collective-permute-done.24.refs_3_), channel_id=1, source_target_pairs={{0,1},{1,0},{2,3},{3,2},{4,5},{5,4},{6,7},{7,6},{8,9},{9,8},{10,11... | collective-permute-start | bytes 2359304 | tf_op jit(solution)/shard_map/ppermute | solution.py:419
